TPU v7x, 32 devices: a whole 2x2x4 slice. The times are simulated.
32 devices in a mesh: dp: 4 (over x, core), fsdp: 8 (over z, y).
Axes of the slice: x: 2, y: 2, z: 4, core: 2. Of those that a mesh axis runs over, the one named last changes fastest.
Arguments:
- inputs: bfloat16 [8192, 384], P(('dp', 'fsdp')), may hold values from -6 to 6
- cotangent: bfloat16 [8192, 384], P(('dp', 'fsdp')), may hold values from -6 to 6
- master: float32 [1774848], P(('dp', 'fsdp'))
- first_moment: float32 [1774848], P(('dp', 'fsdp')), may hold values from -1.5 to 1.5
- second_moment: float32 [1774848], P(('dp', 'fsdp')), may hold values from 0.005 to 0.2
- image_ids: int32 [8192], replicated, may hold values from 0 to 6, as said below
- spans: int32 [32, 2], replicated, may hold values from 0 to 31, as said below
Outputs:
- block_out: bfloat16 [8192, 384], P(('dp', 'fsdp'))
- input_grad: float32 [8192, 384], P(('dp', 'fsdp'))
- weight_grad: float32 [1774848], P(('dp', 'fsdp'))
- grad_norm: float32 [1], replicated
- new_first: float32 [1774848], P(('dp', 'fsdp'))
- new_second: float32 [1774848], P(('dp', 'fsdp'))
- new_master: float32 [1774848], P(('dp', 'fsdp'))
Inputs may be any that keep to these rules, and one draw needn't show every extreme that they name: `image_ids`: image numbers start at 0 and never fall; they rise by one at the first token of each image; every image has exactly 1370 tokens except the first and the last, which may have fewer; the largest image number is the same in every draw. `spans`: row d holds the first and the last device whose tokens belong to an image that also has tokens on device d.
All inputs are finite; a program needn't handle non-finite values.
Results may differ from a plain program's by a relative error of at most 0.011.
Values may be sent and summed in bfloat16 or wider, within the bound.
No kernel may reach another device: no remote copies, remote signals or barrier semaphores. Data moves between devices by JAX's collectives and lax.ppermute only.
A program may use at most 192 MiB of HBM per device.

v0:
```python
import math

import jax
import jax.numpy as jnp
from jax import lax
from jax.sharding import PartitionSpec as P

D = 384
HEADS = 6
HEAD_DIM = 64
FF = 1536
IMG = 1370


LN_EPS = 1e-06
BETA_ONE = 0.5
BETA_TWO = 0.6
LEARN_RATE = 0.01
WEIGHT_DECAY = 0.05
ADAM_EPS = 1e-08
CLIP_RATIO = 0.25
MASKED = -1e30
GROUP = 2


def passed_along(x, axis, by):
    devices = lax.axis_size(axis)
    pairs = [(i, i + by) for i in range(devices) if 0 <= i + by < devices]
    return lax.ppermute(x, axis, pairs)


def shapes(width, hidden):
    return [
        (width,),
        (width,),
        (width, 3 * width),
        (2 * width,),
        (width, width),
        (width,),
        (width,),
        (width,),
        (width,),
        (width, hidden),
        (hidden,),
        (hidden, width),
        (width,),
        (width,),
    ]


def unpack(flat, width, hidden):
    pieces = []
    offset = 0
    for shape in shapes(width, hidden):
        count = math.prod(shape)
        pieces.append(flat[offset : offset + count].reshape(shape))
        offset += count
    return pieces


def layer_norm(values, gain, shift):
    center = values - jnp.mean(values, axis=-1, keepdims=True)
    spread = jnp.mean(center * center, axis=-1, keepdims=True)
    return center * lax.rsqrt(spread + LN_EPS) * gain + shift


def gelu_exact(values):
    return jax.nn.gelu(values, approximate=False)


def heads_first(values, heads):
    length = values.shape[0]
    return values.reshape(length, heads // GROUP, GROUP, -1).transpose(1, 0, 2, 3)


def heads_back(values):
    groups, length, inner, width = values.shape
    return values.transpose(1, 0, 2, 3).reshape(length, groups * inner * width)


def group_scores(query, keys, mask, scale):
    scores = jnp.einsum("thd,khd->htk", query, keys, preferred_element_type=jnp.float32) * scale
    return jnp.where(mask[None], scores, MASKED)


def group_forward(query, keys, values, mask, scale):
    scores = group_scores(query, keys, mask, scale)
    top = jnp.max(scores, axis=-1, keepdims=True)
    expo = jnp.exp(scores - top)
    total = jnp.sum(expo, axis=-1, keepdims=True)
    weights = (expo / total).astype(jnp.bfloat16)
    mixed = jnp.einsum("htk,khd->thd", weights, values, preferred_element_type=jnp.float32)
    return (mixed, (top + jnp.log(total))[..., 0])


def group_backward(query, keys, values, upstream, log_total, mask, scale):
    scores = group_scores(query, keys, mask, scale)
    probs = jnp.exp(scores - log_total[..., None])
    grad_probs = jnp.einsum("thd,khd->htk", upstream, values, preferred_element_type=jnp.float32)
    inner = jnp.sum(probs * grad_probs, axis=-1, keepdims=True)
    grad_scores = (probs * (grad_probs - inner)).astype(jnp.bfloat16)
    grad_query = (
        jnp.einsum("htk,khd->thd", grad_scores, keys, preferred_element_type=jnp.float32) * scale
    )
    grad_keys = (
        jnp.einsum("htk,thd->khd", grad_scores, query, preferred_element_type=jnp.float32) * scale
    )
    grad_values = jnp.einsum(
        "htk,thd->khd", probs.astype(jnp.bfloat16), upstream, preferred_element_type=jnp.float32
    )
    return (grad_query, grad_keys, grad_values)


def visibility(image_ids, spans, rows, reach):
    device = lax.axis_index(("dp", "fsdp"))
    start = device * rows
    query_ids = lax.dynamic_slice_in_dim(image_ids, start, rows, 0)
    padded = jnp.pad(image_ids, (reach * rows, reach * rows), constant_values=-1)
    window = (2 * reach + 1) * rows
    key_ids = lax.dynamic_slice_in_dim(padded, start, window, 0)
    key_device = device - reach + jnp.arange(window, dtype=jnp.int32) // rows
    bounds = lax.dynamic_index_in_dim(spans, device, 0, keepdims=False)
    return (
        (query_ids[:, None] == key_ids[None, :])
        & (key_device >= bounds[0])[None, :]
        & (key_device <= bounds[1])[None, :]
    )


def gather_window(pair, reach):
    below = []
    above = []
    for distance in range(1, reach + 1):
        below.append(passed_along(pair, ("dp", "fsdp"), distance))
        above.append(passed_along(pair, ("dp", "fsdp"), -distance))
    return jnp.concatenate(below[::-1] + [pair] + above, axis=0)


def return_grads(window_grads, rows, reach):
    own = window_grads[reach * rows : (reach + 1) * rows]
    for distance in range(1, reach + 1):
        lower = window_grads[(reach - distance) * rows : (reach - distance + 1) * rows]
        upper = window_grads[(reach + distance) * rows : (reach + distance + 1) * rows]
        own = own + passed_along(lower.astype(jnp.bfloat16), ("dp", "fsdp"), -distance).astype(
            lower.dtype
        )
        own = own + passed_along(upper.astype(jnp.bfloat16), ("dp", "fsdp"), distance).astype(
            upper.dtype
        )
    return own


def forward(flat, values, mask, reach):
    (
        first_gain,
        first_shift,
        triple_weight,
        triple_bias,
        output_weight,
        output_bias,
        first_scale,
        second_gain,
        second_shift,
        up_weight,
        up_bias,
        down_weight,
        down_bias,
        second_scale,
    ) = unpack(flat, D, FF)
    normed_one, pull_one = jax.vjp(
        layer_norm, values, first_gain.astype(jnp.float32), first_shift.astype(jnp.float32)
    )
    normed_one_low = normed_one.astype(jnp.bfloat16)
    bias_full = jnp.concatenate(
        [triple_bias[:D], jnp.zeros((D,), jnp.bfloat16), triple_bias[D:]]
    ).astype(jnp.float32)
    triple = (
        jnp.dot(normed_one_low, triple_weight, preferred_element_type=jnp.float32) + bias_full
    ).astype(jnp.bfloat16)
    query = triple[:, :D]
    window = gather_window(triple[:, D:], reach)
    scale = HEAD_DIM ** (-0.5)
    query_heads = heads_first(query, HEADS)
    key_heads = heads_first(window[:, :D], HEADS)
    value_heads = heads_first(window[:, D:], HEADS)
    mixed, log_total = lax.map(
        lambda group: group_forward(group[0], group[1], group[2], mask, scale),
        (query_heads, key_heads, value_heads),
    )
    attended = heads_back(mixed).astype(jnp.bfloat16)
    branch_one = jnp.dot(
        attended, output_weight, preferred_element_type=jnp.float32
    ) + output_bias.astype(jnp.float32)
    middle = values + first_scale.astype(jnp.float32) * branch_one
    normed_two, pull_two = jax.vjp(
        layer_norm, middle, second_gain.astype(jnp.float32), second_shift.astype(jnp.float32)
    )
    normed_two_low = normed_two.astype(jnp.bfloat16)
    pre_act = jnp.dot(
        normed_two_low, up_weight, preferred_element_type=jnp.float32
    ) + up_bias.astype(jnp.float32)
    activated, pull_act = jax.vjp(gelu_exact, pre_act)
    activated_low = activated.astype(jnp.bfloat16)
    branch_two = jnp.dot(
        activated_low, down_weight, preferred_element_type=jnp.float32
    ) + down_bias.astype(jnp.float32)
    result = middle + second_scale.astype(jnp.float32) * branch_two
    saved = (
        pull_one,
        normed_one_low,
        triple_weight,
        query_heads,
        key_heads,
        value_heads,
        log_total,
        attended,
        output_weight,
        first_scale,
        branch_one,
        pull_two,
        normed_two_low,
        up_weight,
        pull_act,
        activated_low,
        down_weight,
        second_scale,
        branch_two,
    )
    return (result, saved)


def backward(saved, upstream, mask, rows, reach):
    (
        pull_one,
        normed_one_low,
        triple_weight,
        query_heads,
        key_heads,
        value_heads,
        log_total,
        attended,
        output_weight,
        first_scale,
        branch_one,
        pull_two,
        normed_two_low,
        up_weight,
        pull_act,
        activated_low,
        down_weight,
        second_scale,
        branch_two,
    ) = saved
    scale = HEAD_DIM ** (-0.5)
    grad_scale_two = jnp.sum(upstream * branch_two, axis=0)
    grad_branch_two = (second_scale.astype(jnp.float32) * upstream).astype(jnp.bfloat16)
    grad_down_bias = jnp.sum(grad_branch_two.astype(jnp.float32), axis=0)
    grad_down = jnp.einsum(
        "tf,td->fd", activated_low, grad_branch_two, preferred_element_type=jnp.float32
    )
    grad_activated = jnp.einsum(
        "td,fd->tf", grad_branch_two, down_weight, preferred_element_type=jnp.float32
    )
    grad_pre = pull_act(grad_activated)[0].astype(jnp.bfloat16)
    grad_up_bias = jnp.sum(grad_pre.astype(jnp.float32), axis=0)
    grad_up = jnp.einsum("td,tf->df", normed_two_low, grad_pre, preferred_element_type=jnp.float32)
    grad_normed_two = jnp.einsum(
        "tf,df->td", grad_pre, up_weight, preferred_element_type=jnp.float32
    )
    grad_middle_part, grad_second_gain, grad_second_shift = pull_two(grad_normed_two)
    grad_middle = upstream + grad_middle_part
    grad_scale_one = jnp.sum(grad_middle * branch_one, axis=0)
    grad_branch_one = (first_scale.astype(jnp.float32) * grad_middle).astype(jnp.bfloat16)
    grad_output_bias = jnp.sum(grad_branch_one.astype(jnp.float32), axis=0)
    grad_output = jnp.einsum(
        "td,te->de", attended, grad_branch_one, preferred_element_type=jnp.float32
    )
    grad_attended = jnp.einsum(
        "te,de->td", grad_branch_one, output_weight, preferred_element_type=jnp.float32
    ).astype(jnp.bfloat16)
    upstream_heads = heads_first(grad_attended, HEADS)
    grad_query, grad_keys, grad_values = lax.map(
        lambda group: group_backward(group[0], group[1], group[2], group[3], group[4], mask, scale),
        (query_heads, key_heads, value_heads, upstream_heads, log_total),
    )
    grad_query_low = heads_back(grad_query).astype(jnp.bfloat16)
    window_grads = jnp.concatenate([heads_back(grad_keys), heads_back(grad_values)], axis=1)
    grad_pair_low = return_grads(window_grads, rows, reach).astype(jnp.bfloat16)
    grad_triple = jnp.concatenate([grad_query_low, grad_pair_low], axis=1)
    grad_triple_bias = jnp.concatenate(
        [
            jnp.sum(grad_query_low.astype(jnp.float32), axis=0),
            jnp.sum(grad_pair_low[:, D:].astype(jnp.float32), axis=0),
        ]
    )
    grad_triple_weight = jnp.einsum(
        "td,te->de", normed_one_low, grad_triple, preferred_element_type=jnp.float32
    )
    grad_normed_one = jnp.einsum(
        "te,de->td", grad_triple, triple_weight, preferred_element_type=jnp.float32
    )
    grad_input_part, grad_first_gain, grad_first_shift = pull_one(grad_normed_one)
    input_grad = grad_middle + grad_input_part
    full_grad = jnp.concatenate(
        [
            grad_first_gain,
            grad_first_shift,
            grad_triple_weight.reshape(-1),
            grad_triple_bias,
            grad_output.reshape(-1),
            grad_output_bias,
            grad_scale_one,
            grad_second_gain,
            grad_second_shift,
            grad_up.reshape(-1),
            grad_up_bias,
            grad_down.reshape(-1),
            grad_down_bias,
            grad_scale_two,
        ]
    )
    return (input_grad, full_grad)


def per_device(inputs, cotangent, master, first_moment, second_moment, image_ids, spans):
    rows = inputs.shape[0]
    reach = (IMG - 2 + rows) // rows
    values = inputs.astype(jnp.float32)
    mask = visibility(image_ids, spans, rows, reach)
    master_low = master.astype(jnp.bfloat16)
    weights = lax.all_gather(master_low, ("dp", "fsdp"), axis=0, tiled=True)
    result, unused = forward(weights, values, mask, reach)
    weights_back = lax.all_gather(master_low, ("dp", "fsdp"), axis=0, tiled=True)
    recomputed, saved = forward(weights_back, values, mask, reach)
    input_grad, full_grad = backward(saved, cotangent.astype(jnp.float32), mask, rows, reach)
    grad_shard = lax.psum_scatter(full_grad, ("dp", "fsdp"), scatter_dimension=0, tiled=True)
    total_square = lax.psum(jnp.sum(grad_shard * grad_shard), ("dp", "fsdp"))
    grad_norm = jnp.sqrt(total_square)
    ceiling = CLIP_RATIO * math.sqrt(full_grad.shape[0])
    factor = ceiling / jnp.maximum(grad_norm, ceiling)
    clipped = grad_shard * factor
    new_first = BETA_ONE * first_moment + (1.0 - BETA_ONE) * clipped
    new_second = BETA_TWO * second_moment + (1.0 - BETA_TWO) * clipped * clipped
    new_master = master - LEARN_RATE * (
        new_first / (jnp.sqrt(new_second) + ADAM_EPS) + WEIGHT_DECAY * master
    )
    return (
        result.astype(jnp.bfloat16),
        input_grad,
        grad_shard,
        grad_norm.reshape(1),
        new_first,
        new_second,
        new_master,
    )


def solution(mesh):
    in_specs = (
        P(("dp", "fsdp"), None),
        P(("dp", "fsdp"), None),
        P(("dp", "fsdp")),
        P(("dp", "fsdp")),
        P(("dp", "fsdp")),
        P(),
        P(),
    )
    out_specs = (
        P(("dp", "fsdp"), None),
        P(("dp", "fsdp"), None),
        P(("dp", "fsdp")),
        P(),
        P(("dp", "fsdp")),
        P(("dp", "fsdp")),
        P(("dp", "fsdp")),
    )
    return jax.shard_map(
        per_device, mesh=mesh, in_specs=in_specs, out_specs=out_specs, check_vma=False
    )
```

profile of v0, /device:TPU:0, one launch (start us, length us, event | category | flops | bytes accessed | tf_op | source)
XLA Modules:
  0.0 818.8 jit_solution(1039286945937886592)
XLA Ops:
  16.2 139.6 %all-reduce.6.cloned.1.call-done = bf16[1774848]{0:T(1024)(128)(2,1)} async-done(((bf16[1774848]{0:T(1024)(128)(2,1)}), bf16[1774848]{0:T(1024)(128)(2,1)}) %all-reduce.6.cloned.1.call-update) | async-done | bytes 3549712
  161.1 5.2 collective-permute-start
  172.2 4.7 collective-permute-start.3
  202.0 4.7 collective-permute-done.4
  211.9 29.1 %collective-permute-done.7 = bf16[256,768]{1,0:T(8,128)(2,1)S(1)} collective-permute-done((bf16[256,768]{1,0:T(8,128)(2,1)}, bf16[256,768]{1,0:T(8,128)(2,1)S(1)}, u32[]{:S(2)}, u32[]{:S(2)}) %collective-permute-start.7) | collective-permute-done | bytes 393248 | tf_op jit(solution)/shard_map/ppermute | solution.py:29
  241.0 9.3 %collective-permute-done.8 = bf16[256,768]{1,0:T(8,128)(2,1)S(1)} collective-permute-done((bf16[256,768]{1,0:T(8,128)(2,1)}, bf16[256,768]{1,0:T(8,128)(2,1)S(1)}, u32[]{:S(2)}, u32[]{:S(2)}) %collective-permute-start.8) | collective-permute-done | bytes 393248 | tf_op jit(solution)/shard_map/ppermute | solution.py:29
  250.4 40.0 %collective-permute-done.9 = bf16[256,768]{1,0:T(8,128)(2,1)S(1)} collective-permute-done((bf16[256,768]{1,0:T(8,128)(2,1)}, bf16[256,768]{1,0:T(8,128)(2,1)S(1)}, u32[]{:S(2)}, u32[]{:S(2)}) %collective-permute-start.9) | collective-permute-done | bytes 393248 | tf_op jit(solution)/shard_map/ppermute | solution.py:29
  301.0 21.4 %while.40 = (s32[]{:T(128)}, bf16[3,256,2,64]{1,3,2,0:T(8,128)(2,1)S(1)}, f32[3,2,256]{2,1,0:T(2,128)S(1)}, bf16[3,3328,2,64]{1,3,2,0:T(8,128)(2,1)}, bf16[3,256...) while((s32[]{:T(128)}, ...), condition=%wide.region_11.12_spmd.clone, body=%wide.region_8.11_spmd.clone.sunk | while | flops 452394496 | bytes 24091256 | solution.py:186
  323.8 4.8 multiply_convert_fusion.1
  334.9 57.4 %while.41 = (s32[]{:T(128)}, bf16[3,256,2,64]{1,3,2,0:T(8,128)(2,1)}, f32[3,3328,2,64]{1,3,2,0:T(8,128)}, f32[3,3328,2,64]{1,3,2,0:T(8,128)}, bf16[3,3328,2,64]{...) while((s32[]{:T(128)}, ...), condition=%wide.region_18.19_spmd.clone, body=%wide.region_16.18_spmd.clone.sunk | while | flops 1108868608 | bytes 72847016 | solution.py:282
  392.3 6.7 fusion.91
  399.1 4.6 fusion.243
  418.3 10.6 %collective-permute-done.22 = bf16[256,768]{0,1:T(8,128)(2,1)} collective-permute-done((bf16[256,768]{0,1:T(8,128)(2,1)}, bf16[256,768]{0,1:T(8,128)(2,1)}, u32[]{:S(2)}, u32[]{:S(2)}) %collective-permute-start.22) | collective-permute-done | bytes 393248 | tf_op jit(solution)/shard_map/ppermute | solution.py:29
  440.8 35.3 %collective-permute-done.20 = bf16[256,768]{0,1:T(8,128)(2,1)} collective-permute-done((bf16[256,768]{0,1:T(8,128)(2,1)}, bf16[256,768]{0,1:T(8,128)(2,1)}, u32[]{:S(2)}, u32[]{:S(2)}) %collective-permute-start.20) | collective-permute-done | bytes 393248 | tf_op jit(solution)/shard_map/ppermute | solution.py:29
  479.4 25.6 %collective-permute-done.18 = bf16[256,768]{0,1:T(8,128)(2,1)} collective-permute-done((bf16[256,768]{0,1:T(8,128)(2,1)}, bf16[256,768]{0,1:T(8,128)(2,1)}, u32[]{:S(2)}, u32[]{:S(2)}) %collective-permute-start.18) | collective-permute-done | bytes 393248 | tf_op jit(solution)/shard_map/ppermute | solution.py:29
  517.3 6.6 collective-permute-done.14
  537.5 16.3 %dynamic-update-slice.3 = f32[1774848]{0:T(1024)} dynamic-update-slice(f32[1774848]{0:T(1024)} %constant_dynamic-update-slice_fusion.25, f32[442368]{0:T(1024)} %reshape.248, s32[]{} %constant.217) | dynamic-update-slice | bytes 3538948
  568.1 21.1 %dynamic-update-slice.13 = f32[1774848]{0:T(1024)} dynamic-update-slice(f32[1774848]{0:T(1024)} %constant_dynamic-update-slice_fusion.16, f32[589824]{0:T(1024)} %reshape.251, s32[]{} %constant.227) | dynamic-update-slice | bytes 4718596
  592.6 26.5 %while.39 = (s32[]{:T(128)}, bf16[3,256,2,64]{1,3,2,0:T(8,128)(2,1)}, bf16[3,3328,2,64]{1,3,2,0:T(8,128)(2,1)}, bf16[3,256,2,64]{1,3,2,0:T(8,128)(2,1)}, bf16[3,...) while((s32[]{:T(128)}, ...), condition=%wide.region_5.6_spmd.clone, body=%wide.region_2.5_spmd.clone.sunk | while | flops 672209920 | bytes 5402221 | solution.py:186
  605.5 4.6 fusion.301
  614.3 4.7 fusion.301
  621.0 6.6 fusion.114
  627.6 139.5 %all-reduce.8.cloned.1.call-done = f32[1774848]{0:T(1024)} async-done(((f32[1774848]{0:T(1024)}), f32[1774848]{0:T(1024)}) %all-reduce.8.cloned.1.call-update) | async-done | bytes 7099408
  768.7 40.2 %psum.7 = f32[]{:T(128)} all-reduce(f32[]{:T(128)} %get-tuple-element.295), channel_id=1, replica_groups=mesh['dp'=4,'fsdp'=8] {'dp','fsdp'}, use_global_device_ids=true, to_apply=%region_34.35 | all-reduce | flops 1 | bytes 8 | tf_op jit(solution)/shard_map/psum | solution.py:337
  (301 shorter events, 241.4 us)
Async XLA Ops:
  7.2 148.7 %all-reduce.6.cloned.1.call-start = ((), (), s32[]{:S(2)}) async-start(), calls=%async_computation | async-start | bytes 7102464
  13.1 754.0 %all-reduce.8.cloned.1.call-start = ((), (), s32[]{:S(2)}) async-start(), calls=%async_computation.1 | async-start | bytes 14204928
  161.1 27.4 %collective-permute-start = (bf16[256,768]{1,0:T(8,128)(2,1)}, bf16[256,768]{1,0:T(8,128)(2,1)}, u32[]{:S(2)}, u32[]{:S(2)}) collective-permute-start(bf16[256,768]{1,0:T(8,128)(2,1)} %slice.205), channel_id=1, source_target_pairs={{0,6},{1,7},{2,8},{3,9},{4,10},{5,11},{6,12},{7,13},{8,14},{9,15},... | collective-permute-start | bytes 1179656 | tf_op jit(solution)/shard_map/ppermute | solution.py:29
  166.3 25.3 %collective-permute-start.1 = (bf16[256,768]{1,0:T(8,128)(2,1)}, bf16[256,768]{1,0:T(8,128)(2,1)}, u32[]{:S(2)}, u32[]{:S(2)}) collective-permute-start(bf16[256,768]{1,0:T(8,128)(2,1)} %slice.205), channel_id=1, source_target_pairs={{0,5},{1,6},{2,7},{3,8},{4,9},{5,10},{6,11},{7,12},{8,13},{9,14},{... | collective-permute-start | bytes 1179656 | tf_op jit(solution)/shard_map/ppermute | solution.py:29
  168.7 25.2 %collective-permute-start.2 = (bf16[256,768]{1,0:T(8,128)(2,1)}, bf16[256,768]{1,0:T(8,128)(2,1)}, u32[]{:S(2)}, u32[]{:S(2)}) collective-permute-start(bf16[256,768]{1,0:T(8,128)(2,1)} %slice.205), channel_id=1, source_target_pairs={{0,4},{1,5},{2,6},{3,7},{4,8},{5,9},{6,10},{7,11},{8,12},{9,13},{1... | collective-permute-start | bytes 1179656 | tf_op jit(solution)/shard_map/ppermute | solution.py:29
  172.2 27.5 %collective-permute-start.3 = (bf16[256,768]{1,0:T(8,128)(2,1)}, bf16[256,768]{1,0:T(8,128)(2,1)}, u32[]{:S(2)}, u32[]{:S(2)}) collective-permute-start(bf16[256,768]{1,0:T(8,128)(2,1)} %slice.205), channel_id=1, source_target_pairs={{0,3},{1,4},{2,5},{3,6},{4,7},{5,8},{6,9},{7,10},{8,11},{9,12},{10... | collective-permute-start | bytes 1179656 | tf_op jit(solution)/shard_map/ppermute | solution.py:29
  176.9 29.8 %collective-permute-start.4 = (bf16[256,768]{1,0:T(8,128)(2,1)}, bf16[256,768]{1,0:T(8,128)(2,1)}, u32[]{:S(2)}, u32[]{:S(2)}) collective-permute-start(bf16[256,768]{1,0:T(8,128)(2,1)} %slice.205), channel_id=1, source_target_pairs={{0,2},{1,3},{2,4},{3,5},{4,6},{5,7},{6,8},{7,9},{8,10},{9,11},{10,... | collective-permute-start | bytes 1179656 | tf_op jit(solution)/shard_map/ppermute | solution.py:29
  188.5 20.5 %collective-permute-start.5 = (bf16[256,768]{1,0:T(8,128)(2,1)}, bf16[256,768]{1,0:T(8,128)(2,1)S(1)}, u32[]{:S(2)}, u32[]{:S(2)}) collective-permute-start(bf16[256,768]{1,0:T(8,128)(2,1)} %slice.205), channel_id=1, source_target_pairs={{0,1},{1,2},{2,3},{3,4},{4,5},{5,6},{6,7},{7,8},{8,9},{9,10},{10,1... | collective-permute-start | bytes 1179656 | tf_op jit(solution)/shard_map/ppermute | solution.py:29
  191.6 18.8 %collective-permute-start.6 = (bf16[256,768]{1,0:T(8,128)(2,1)}, bf16[256,768]{1,0:T(8,128)(2,1)S(1)}, u32[]{:S(2)}, u32[]{:S(2)}) collective-permute-start(bf16[256,768]{1,0:T(8,128)(2,1)} %slice.205), channel_id=1, source_target_pairs={{1,0},{2,1},{3,2},{4,3},{5,4},{6,5},{7,6},{8,7},{9,8},{10,9},{11,1... | collective-permute-start | bytes 1179656 | tf_op jit(solution)/shard_map/ppermute | solution.py:29
  193.9 47.1 %collective-permute-start.7 = (bf16[256,768]{1,0:T(8,128)(2,1)}, bf16[256,768]{1,0:T(8,128)(2,1)S(1)}, u32[]{:S(2)}, u32[]{:S(2)}) collective-permute-start(bf16[256,768]{1,0:T(8,128)(2,1)} %slice.205), channel_id=1, source_target_pairs={{2,0},{3,1},{4,2},{5,3},{6,4},{7,5},{8,6},{9,7},{10,8},{11,9},{12,... | collective-permute-start | bytes 1179656 | tf_op jit(solution)/shard_map/ppermute | solution.py:29
  199.7 50.6 %collective-permute-start.8 = (bf16[256,768]{1,0:T(8,128)(2,1)}, bf16[256,768]{1,0:T(8,128)(2,1)S(1)}, u32[]{:S(2)}, u32[]{:S(2)}) collective-permute-start(bf16[256,768]{1,0:T(8,128)(2,1)} %slice.205), channel_id=1, source_target_pairs={{3,0},{4,1},{5,2},{6,3},{7,4},{8,5},{9,6},{10,7},{11,8},{12,9},{13... | collective-permute-start | bytes 1179656 | tf_op jit(solution)/shard_map/ppermute | solution.py:29
  206.7 83.7 %collective-permute-start.9 = (bf16[256,768]{1,0:T(8,128)(2,1)}, bf16[256,768]{1,0:T(8,128)(2,1)S(1)}, u32[]{:S(2)}, u32[]{:S(2)}) collective-permute-start(bf16[256,768]{1,0:T(8,128)(2,1)} %slice.205), channel_id=1, source_target_pairs={{4,0},{5,1},{6,2},{7,3},{8,4},{9,5},{10,6},{11,7},{12,8},{13,9},{1... | collective-permute-start | bytes 1179656 | tf_op jit(solution)/shard_map/ppermute | solution.py:29
  209.0 82.3 %collective-permute-start.10 = (bf16[256,768]{1,0:T(8,128)(2,1)}, bf16[256,768]{1,0:T(8,128)(2,1)S(1)}, u32[]{:S(2)}, u32[]{:S(2)}) collective-permute-start(bf16[256,768]{1,0:T(8,128)(2,1)} %slice.205), channel_id=1, source_target_pairs={{5,0},{6,1},{7,2},{8,3},{9,4},{10,5},{11,6},{12,7},{13,8},{14,9},{... | collective-permute-start | bytes 1179656 | tf_op jit(solution)/shard_map/ppermute | solution.py:29
  210.4 80.9 %collective-permute-start.11 = (bf16[256,768]{1,0:T(8,128)(2,1)}, bf16[256,768]{1,0:T(8,128)(2,1)S(1)}, u32[]{:S(2)}, u32[]{:S(2)}) collective-permute-start(bf16[256,768]{1,0:T(8,128)(2,1)} %slice.205), channel_id=1, source_target_pairs={{6,0},{7,1},{8,2},{9,3},{10,4},{11,5},{12,6},{13,7},{14,8},{15,9},... | collective-permute-start | bytes 1179656 | tf_op jit(solution)/shard_map/ppermute | solution.py:29
  405.9 23.0 %collective-permute-start.22 = (bf16[256,768]{0,1:T(8,128)(2,1)}, bf16[256,768]{0,1:T(8,128)(2,1)}, u32[]{:S(2)}, u32[]{:S(2)}) collective-permute-start(bf16[256,768]{0,1:T(8,128)(2,1)} %get-tuple-element.311), channel_id=1, source_target_pairs={{6,0},{7,1},{8,2},{9,3},{10,4},{11,5},{12,6},{13,7},{14,8},{15,9},... | collective-permute-start | bytes 1179656 | tf_op jit(solution)/shard_map/ppermute | solution.py:29
  407.2 32.3 %collective-permute-start.21 = (bf16[256,768]{0,1:T(8,128)(2,1)}, bf16[256,768]{0,1:T(8,128)(2,1)}, u32[]{:S(2)}, u32[]{:S(2)}) collective-permute-start(bf16[256,768]{0,1:T(8,128)(2,1)} %get-tuple-element.312), channel_id=1, source_target_pairs={{0,5},{1,6},{2,7},{3,8},{4,9},{5,10},{6,11},{7,12},{8,13},{9,14},{... | collective-permute-start | bytes 1179656 | tf_op jit(solution)/shard_map/ppermute | solution.py:29
  409.5 66.5 %collective-permute-start.20 = (bf16[256,768]{0,1:T(8,128)(2,1)}, bf16[256,768]{0,1:T(8,128)(2,1)}, u32[]{:S(2)}, u32[]{:S(2)}) collective-permute-start(bf16[256,768]{0,1:T(8,128)(2,1)} %get-tuple-element.313), channel_id=1, source_target_pairs={{5,0},{6,1},{7,2},{8,3},{9,4},{10,5},{11,6},{12,7},{13,8},{14,9},{... | collective-permute-start | bytes 1179656 | tf_op jit(solution)/shard_map/ppermute | solution.py:29
  410.8 67.3 %collective-permute-start.19 = (bf16[256,768]{0,1:T(8,128)(2,1)}, bf16[256,768]{0,1:T(8,128)(2,1)}, u32[]{:S(2)}, u32[]{:S(2)}) collective-permute-start(bf16[256,768]{0,1:T(8,128)(2,1)} %get-tuple-element.314), channel_id=1, source_target_pairs={{0,4},{1,5},{2,6},{3,7},{4,8},{5,9},{6,10},{7,11},{8,12},{9,13},{1... | collective-permute-start | bytes 1179656 | tf_op jit(solution)/shard_map/ppermute | solution.py:29
  417.0 88.0 %collective-permute-start.18 = (bf16[256,768]{0,1:T(8,128)(2,1)}, bf16[256,768]{0,1:T(8,128)(2,1)}, u32[]{:S(2)}, u32[]{:S(2)}) collective-permute-start(bf16[256,768]{0,1:T(8,128)(2,1)} %get-tuple-element.315), channel_id=1, source_target_pairs={{4,0},{5,1},{6,2},{7,3},{8,4},{9,5},{10,6},{11,7},{12,8},{13,9},{1... | collective-permute-start | bytes 1179656 | tf_op jit(solution)/shard_map/ppermute | solution.py:29
  428.9 78.1 %collective-permute-start.17 = (bf16[256,768]{0,1:T(8,128)(2,1)}, bf16[256,768]{0,1:T(8,128)(2,1)}, u32[]{:S(2)}, u32[]{:S(2)}) collective-permute-start(bf16[256,768]{0,1:T(8,128)(2,1)} %get-tuple-element.316), channel_id=1, source_target_pairs={{0,3},{1,4},{2,5},{3,6},{4,7},{5,8},{6,9},{7,10},{8,11},{9,12},{10... | collective-permute-start | bytes 1179656 | tf_op jit(solution)/shard_map/ppermute | solution.py:29
  439.5 77.8 %collective-permute-start.16 = (bf16[256,768]{0,1:T(8,128)(2,1)}, bf16[256,768]{0,1:T(8,128)(2,1)}, u32[]{:S(2)}, u32[]{:S(2)}) collective-permute-start(bf16[256,768]{0,1:T(8,128)(2,1)} %get-tuple-element.317), channel_id=1, source_target_pairs={{3,0},{4,1},{5,2},{6,3},{7,4},{8,5},{9,6},{10,7},{11,8},{12,9},{13... | collective-permute-start | bytes 1179656 | tf_op jit(solution)/shard_map/ppermute | solution.py:29
  476.1 41.3 %collective-permute-start.15 = (bf16[256,768]{0,1:T(8,128)(2,1)}, bf16[256,768]{0,1:T(8,128)(2,1)}, u32[]{:S(2)}, u32[]{:S(2)}) collective-permute-start(bf16[256,768]{0,1:T(8,128)(2,1)} %get-tuple-element.318), channel_id=1, source_target_pairs={{0,2},{1,3},{2,4},{3,5},{4,6},{5,7},{6,8},{7,9},{8,10},{9,11},{10,... | collective-permute-start | bytes 1179656 | tf_op jit(solution)/shard_map/ppermute | solution.py:29
  478.1 45.8 %collective-permute-start.14 = (bf16[256,768]{0,1:T(8,128)(2,1)}, bf16[256,768]{0,1:T(8,128)(2,1)}, u32[]{:S(2)}, u32[]{:S(2)}) collective-permute-start(bf16[256,768]{0,1:T(8,128)(2,1)} %get-tuple-element.319), channel_id=1, source_target_pairs={{2,0},{3,1},{4,2},{5,3},{6,4},{7,5},{8,6},{9,7},{10,8},{11,9},{12,... | collective-permute-start | bytes 1179656 | tf_op jit(solution)/shard_map/ppermute | solution.py:29
  505.0 18.9 %collective-permute-start.13 = (bf16[256,768]{0,1:T(8,128)(2,1)}, bf16[256,768]{0,1:T(8,128)(2,1)}, u32[]{:S(2)}, u32[]{:S(2)}) collective-permute-start(bf16[256,768]{0,1:T(8,128)(2,1)} %get-tuple-element.320), channel_id=1, source_target_pairs={{0,1},{1,2},{2,3},{3,4},{4,5},{5,6},{6,7},{7,8},{8,9},{9,10},{10,1... | collective-permute-start | bytes 1179656 | tf_op jit(solution)/shard_map/ppermute | solution.py:29
  (59 other events, 2682.2 us)
Sparse Core Ops, SparseCore 0:
  13.6 142.1 all-reduce.5
  592.0 174.9 all-reduce.7
where the time goes:
time: 829 us; the launch traced here: 819 us
  waiting for transfers between devices  444 us (54%)
  matrix products  116 us (14%)
  local copies, waits for them, and re-layouts  108 us (13%)
  starting transfers between devices  51.9 us (6%)
  other arithmetic  40.2 us (5%)
  blocking collectives  40.2 us (5%)
  between operations  17 us (2%)
    unnamed x4, waiting for transfers between devices  279 us
    ppermute x24, waiting for transfers between devices, passed_along(): return lax.ppermute(x, axis, pairs)  165 us
    unnamed x136, local copies, waits for them, and re-layouts  67.4 us
    ppermute x24, starting transfers between devices, passed_along(): return lax.ppermute(x, axis, pairs)  51.8 us
    psum x1, blocking collectives, per_device(): total_square = lax.psum(jnp.sum(grad_shard * grad_shard), ('dp', 'fsdp'))  40.2 us
    dot_general x6, matrix products, group_forward(): jnp.einsum('htk,khd->thd', weights, values, preferred_element_type=jnp.fl...  22 us
    dot_general x6, matrix products, group_scores(): jnp.einsum('thd,khd->htk', query, keys, preferred_element_type=jnp.float32)  18.3 us
  transfers between devices with their start and end apart: 26, of which 12 were waited for; matrix products, arithmetic and copies ran while one was open for 9% of the time, Pallas kernels for 0%

commit v1 on v0

v1 whole, which is shorter than its diff:
```python
import math

import jax
import jax.numpy as jnp
from jax import lax
from jax.experimental import pallas as pl
from jax.experimental.pallas import tpu as pltpu
from jax.sharding import PartitionSpec as P

D = 384
HEADS = 6
HEAD_DIM = 64
FF = 1536
IMG = 1370
LANES = 128

LN_EPS = 1e-06
BETA_ONE = 0.5
BETA_TWO = 0.6
LEARN_RATE = 0.01
WEIGHT_DECAY = 0.05
ADAM_EPS = 1e-08
CLIP_RATIO = 0.25
MASKED = -1e30
BOTH = ("dp", "fsdp")
LOW = jnp.bfloat16
WIDE = jnp.float32
SCALE = HEAD_DIM ** (-0.5)

NT = (((1,), (1,)), ((), ()))
NN = (((1,), (0,)), ((), ()))
TN = (((0,), (0,)), ((), ()))

PIECES = [
    ("gain1", D),
    ("shift1", D),
    ("triple", 3 * D * D),
    ("tbias", 2 * D),
    ("out", D * D),
    ("obias", D),
    ("scale1", D),
    ("gain2", D),
    ("shift2", D),
    ("up", D * FF),
    ("ubias", FF),
    ("down", FF * D),
    ("dbias", D),
    ("scale2", D),
]
AT = {}
_row = 0
for _name, _count in PIECES:
    AT[_name] = _row
    _row += _count // LANES
ALL_ROWS = _row


def dot(a, b, dims):
    return lax.dot_general(a, b, dims, preferred_element_type=WIDE)


class Plan:
    def __init__(self, dp, fsdp, share, tokens):
        self.count = dp * fsdp
        self.share = share
        self.rows = -(-(2 * (LANES - 1) + share) // LANES)
        self.rows = -(-self.rows // 16) * 16
        self.start = [e * share // LANES for e in range(self.count)]
        self.tokens = tokens
        self.reach = (IMG - 2 + tokens) // tokens
        self.window = 2 * self.reach + 1
        self.grouped = dp == 4 and fsdp == 8 and self.reach <= 6
        if self.grouped:
            self.stages = [[2, 4, 6], [16, 1, 17], [8]]
        else:
            bits = [1 << k for k in range(self.count.bit_length() - 1)]
            bits = [b for b in bits if b != fsdp] + [fsdp]
            self.stages = [[b] for b in bits]
        masks = [0]
        for stage in self.stages:
            masks = masks + [m ^ s for s in stage for m in masks]
        self.bits = [masks[1 << k] for k in range(self.count.bit_length() - 1)]
        self.first_late = next(e for e in range(self.count) if self.start[e] >= AT["out"])
        self.flat_rows = -(-(self.start[-1] + self.rows) // 8) * 8

    def send(self, x, mask):
        return lax.ppermute(x, BOTH, [(i, i ^ mask) for i in range(self.count)])

    def spread(self, own):
        buf = own[None]
        for stage in self.stages[:-1]:
            buf = jnp.concatenate([buf] + [self.send(buf, m) for m in stage], axis=0)
        return buf, self.send(buf, self.stages[-1][0])

    def reduce_parts(self, blocks):
        buf = blocks
        for stage in reversed(self.stages):
            split = buf.reshape((len(stage) + 1, -1) + buf.shape[1:])
            parts = [split[0]] + [self.send(split[k + 1], m) for k, m in enumerate(stage)]
            if stage is self.stages[0]:
                return [part[0] for part in parts]
            total = parts[0].astype(WIDE)
            for part in parts[1:]:
                total = total + part.astype(WIDE)
            buf = total.astype(LOW)

    def total(self, value):
        for stage in self.stages:
            got = [value] + [self.send(value, m) for m in stage]
            while len(got) > 1:
                got = [got[k] + got[k + 1] for k in range(0, len(got), 2)]
            value = got[0]
        return value

    def exchange(self, block):
        own = block[None]
        if self.grouped:
            column = jnp.concatenate([own] + [self.send(own, m) for m in (2, 4, 6)], axis=0)
            beside = self.send(column, 1)
            across = [(8 + j, 16 + j) for j in range(8)] + [(16 + j, 8 + j) for j in range(8)]
            far_column = lax.ppermute(column, BOTH, across)
            far_beside = lax.ppermute(beside, BOTH, across)
            row = jnp.concatenate([column, beside], axis=0)
            return [row, self.send(row, 8), far_column, far_beside]
        slots = []
        for slot in range(self.window):
            by = self.reach - slot
            pairs = [(i, i + by) for i in range(self.count) if 0 <= i + by < self.count]
            slots.append(own if by == 0 else lax.ppermute(own, BOTH, pairs))
        return [jnp.concatenate(slots, axis=0)]

    def table(self, device, spans):
        e = jnp.arange(self.count, dtype=jnp.int32)
        rel = e ^ device
        where = jnp.zeros_like(e)
        for k, bit in enumerate(self.bits):
            where = where + jnp.where((rel & bit) != 0, 1 << k, 0)
        slot = jnp.arange(self.window, dtype=jnp.int32)
        if self.grouped:
            other = device - self.reach + slot
            pos = ((other ^ device) & 7) >> 1
            pos = pos + 4 * ((other ^ device) & 1)
            cross = (other >> 3) ^ (device >> 3)
            source = jnp.where(cross == 0, 0, jnp.where(cross == 1, 1, 2 + (pos >> 2)))
            index = jnp.where(source >= 2, pos & 3, pos)
        else:
            source = jnp.zeros_like(slot)
            index = slot
        bounds = lax.dynamic_index_in_dim(spans, device, 0, keepdims=False)
        ends = jnp.clip(bounds - device + self.reach, 0, self.window - 1)
        shift = ((device * self.share) % LANES).reshape(1)
        return jnp.concatenate([where, source, index, ends, shift]).astype(jnp.int32)

    def source_at(self, slot):
        return self.count + slot

    def index_at(self, slot):
        return self.count + self.window + slot

    def low_at(self):
        return self.count + 2 * self.window

    def shift_at(self):
        return self.count + 2 * self.window + 2


def fetch_window(plan, table, sources, dest, sems, lo, hi, wait):
    def step(slot, carry):
        for k, source in enumerate(sources):

            @pl.when(table[plan.source_at(slot)] == k)
            def _(source=source):
                copy = pltpu.make_async_copy(
                    source.at[table[plan.index_at(slot)]], dest.at[slot], sems.at[slot]
                )
                if wait:
                    copy.wait()
                else:
                    copy.start()

        return carry

    lax.fori_loop(lo, hi + 1, step, 0)


def normalized(x):
    center = x - jnp.mean(x, axis=-1, keepdims=True)
    spread = jnp.mean(center * center, axis=-1, keepdims=True)
    r = lax.rsqrt(spread + LN_EPS)
    return center * r, r


def norm_back(grad, gain, n, r):
    g = grad * gain
    inner = jnp.mean(g, axis=-1, keepdims=True)
    outer = jnp.mean(g * n, axis=-1, keepdims=True)
    return r * (g - inner - n * outer)


def vector(ref, row, width):
    return jnp.concatenate([ref[row + j : row + j + 1, :] for j in range(width // LANES)], axis=1)


def put_vector(ref, row, value):
    for j in range(value.shape[1] // LANES):
        ref[row + j : row + j + 1, :] = value[:, LANES * j : LANES * (j + 1)]


def column_sum(x):
    return jnp.sum(x, axis=0, keepdims=True)


def shift_kernel(plan):
    def kernel(table, x_ref, out_ref, pad):
        s = table[plan.shift_at()]
        x = x_ref[...]
        y = pltpu.roll(x, s, 1)
        pad[0:8, :] = jnp.zeros((8, LANES), WIDE)
        pad[8:, :] = y
        lane = lax.broadcasted_iota(jnp.int32, y.shape, 1)
        out_ref[...] = jnp.where(lane >= s, y, pad[7 : 7 + plan.rows, :]).astype(LOW)

    return kernel


def unshift_kernel(plan):
    def kernel(table, *refs):
        parts, (out_ref, sq_ref, pad) = refs[:-3], refs[-3:]
        s = table[plan.shift_at()]
        got = [p[...].astype(WIDE) for p in parts]
        while len(got) > 1:
            got = [got[k] + got[k + 1] for k in range(0, len(got), 2)]
        y = pltpu.roll(got[0], LANES - s, 1)
        pad[0 : plan.rows, :] = y
        pad[plan.rows :, :] = jnp.zeros((8, LANES), WIDE)
        lane = lax.broadcasted_iota(jnp.int32, y.shape, 1)
        row = lax.broadcasted_iota(jnp.int32, y.shape, 0)
        out = jnp.where(lane < LANES - s, y, pad[1 : 1 + plan.rows, :])
        out = jnp.where(row * LANES + lane < plan.share, out, 0.0)
        out_ref[...] = out
        sq = jnp.sum(jnp.sum(out * out, axis=0, keepdims=True), axis=1, keepdims=True)
        sq_ref[...] = jnp.broadcast_to(sq, (8, LANES))

    return kernel


def forward_kernel(plan, sources):
    T = plan.tokens
    W = plan.window
    own = plan.reach
    half = plan.count // 2

    def kernel(table, *refs):
        near, core = refs[:2]
        wins = refs[2 : 2 + sources]
        cot_ref, col_ref, row_ref = refs[2 + sources : 5 + sources]
        (
            out_ref,
            msg_ref,
            q_ref,
            k_ref,
            v_ref,
            triple_ref,
            normed_ref,
            mid_ref,
            act_ref,
            pre_ref,
            gbt_ref,
            n2_ref,
            att_ref,
            gbo_ref,
            vec_ref,
            stat_ref,
            gain_ref,
            kown_ref,
            vown_ref,
        ) = refs[5 + sources : 24 + sources]
        wbuf, flat, xwin, wo, wup, wdn, scores, wsem, xsem = refs[24 + sources :]
        lo = table[plan.low_at()]
        hi = table[plan.low_at() + 1]

        def weight_copy(e, wait):
            t = table[e]

            @pl.when(t < half)
            def _():
                c = pltpu.make_async_copy(near.at[t], wbuf.at[e], wsem.at[e])
                c.wait() if wait else c.start()

            @pl.when(t >= half)
            def _():
                c = pltpu.make_async_copy(core.at[t - half], wbuf.at[e], wsem.at[e])
                c.wait() if wait else c.start()

        def start_one(e, carry):
            weight_copy(e, False)
            return carry

        lax.fori_loop(0, plan.count, start_one, 0)
        fetch_window(plan, table, wins, xwin, xsem, lo, hi, False)

        def wait_one(e, carry):
            weight_copy(e, True)
            return carry

        lax.fori_loop(0, plan.count, wait_one, 0)
        for e in range(plan.count):
            r0 = plan.start[e]
            block = wbuf[e].astype(WIDE)
            if e:
                before = flat[r0 : r0 + 1, :]
                flat[r0 : r0 + plan.rows, :] = block
                flat[r0 : r0 + 1, :] = before + block[0:1, :]
            else:
                flat[r0 : r0 + plan.rows, :] = block

        def unfold(dest, name, height, width):
            wide = width // LANES
            step = min(height, 384)
            for j in range(wide):
                for i in range(0, height, step):
                    dest[i : i + step, LANES * j : LANES * (j + 1)] = flat[
                        pl.ds(AT[name] + i * wide + j, step, stride=wide), :
                    ].astype(LOW)

        unfold(triple_ref, "triple", D, 3 * D)
        gain1 = vector(flat, AT["gain1"], D)
        shift1 = vector(flat, AT["shift1"], D)
        gain_ref[...] = jnp.broadcast_to(gain1, (8, D))
        tbias = vector(flat, AT["tbias"], 2 * D)
        fetch_window(plan, table, wins, xwin, xsem, lo, hi, True)

        def project(w, carry):
            n, _ = normalized(xwin[w].astype(WIDE))
            low = (n * gain1 + shift1).astype(LOW)

            @pl.when(w == own)
            def _():
                normed_ref[...] = low

            q = dot(low, triple_ref[:, :D], NN) + tbias[:, :D]
            q_ref[w] = (q.astype(LOW).astype(WIDE) * SCALE).astype(LOW)
            k_ref[w] = dot(low, triple_ref[:, D : 2 * D], NN).astype(LOW)
            v_ref[w] = (dot(low, triple_ref[:, 2 * D :], NN) + tbias[:, D:]).astype(LOW)
            return carry

        lax.fori_loop(lo, hi + 1, project, 0)
        kown_ref[...] = k_ref[own]
        vown_ref[...] = v_ref[own]

        unfold(wo, "out", D, D)
        unfold(wup, "up", D, FF)
        unfold(wdn, "down", FF, D)

        lane = lax.broadcasted_iota(jnp.int32, (T, LANES), 1)
        left = lane < HEAD_DIM
        ids = jnp.concatenate([col_ref[...]] * (T // LANES), axis=1)
        mixed = []
        stats = jnp.zeros((T, LANES), WIDE)
        for p in range(HEADS // 2):
            cols = slice(LANES * p, LANES * (p + 1))
            q = q_ref[own, :, cols]
            qs = [jnp.where(left, q, 0), jnp.where(left, 0, q)]

            def first(w, tops, qs=qs, cols=cols):
                key = k_ref[w, :, cols]
                seen = ids == row_ref[pl.ds(w, 1), :]
                new = []
                for i in range(2):
                    s = jnp.where(seen, dot(qs[i], key, NT), MASKED)
                    scores[i, w] = s
                    top = tops[i]
                    for c in range(0, T, LANES):
                        top = jnp.maximum(top, s[:, c : c + LANES])
                    new.append(top)
                return tuple(new)

            start = jnp.full((T, LANES), MASKED, WIDE)
            tops = lax.fori_loop(lo, hi + 1, first, (start, start))
            tops = [jnp.max(t, axis=1, keepdims=True) for t in tops]

            def second(w, carry, tops=tops, cols=cols):
                value = v_ref[w, :, cols]
                new = []
                for i in range(2):
                    total, acc = carry[2 * i], carry[2 * i + 1]
                    e = jnp.exp(scores[i, w] - tops[i])
                    for c in range(0, T, LANES):
                        total = total + e[:, c : c + LANES]
                    new += [total, acc + dot(e.astype(LOW), value, NN)]
                return tuple(new)

            zero = jnp.zeros((T, LANES), WIDE)
            got = lax.fori_loop(lo, hi + 1, second, (zero,) * 4)
            sums = [jnp.sum(got[2 * i], axis=1, keepdims=True) for i in range(2)]
            mixed.append(jnp.where(left, got[1] / sums[0], got[3] / sums[1]))
            for i in range(2):
                stats = jnp.where(lane == 2 * p + i, tops[i] + jnp.log(sums[i]), stats)
        att = jnp.concatenate(mixed, axis=1)
        att_low = att.astype(LOW)
        att_ref[...] = att_low
        x = xwin[own].astype(WIDE)
        scale1 = vector(flat, AT["scale1"], D)
        scale2 = vector(flat, AT["scale2"], D)
        gain2 = vector(flat, AT["gain2"], D)
        branch_one = dot(att_low, wo[...], NN) + vector(flat, AT["obias"], D)
        middle = x + scale1 * branch_one
        n2, r2 = normalized(middle)
        n2_low = (n2 * gain2 + vector(flat, AT["shift2"], D)).astype(LOW)
        n2_ref[...] = n2_low
        pre = dot(n2_low, wup[...], NN) + vector(flat, AT["ubias"], FF)
        cdf = 0.5 * (1.0 + lax.erf(pre * math.sqrt(0.5)))
        act_low = (pre * cdf).astype(LOW)
        act_ref[...] = act_low
        slope = cdf + pre * (jnp.exp(-0.5 * pre * pre) * (1.0 / math.sqrt(2.0 * math.pi)))
        branch_two = dot(act_low, wdn[...], NN) + vector(flat, AT["dbias"], D)
        out_ref[...] = (middle + scale2 * branch_two).astype(LOW)

        up = cot_ref[...].astype(WIDE)
        gbt = (scale2 * up).astype(LOW)
        gbt_ref[...] = gbt
        gpre = (dot(gbt, wdn[...], NT) * slope).astype(LOW)
        pre_ref[...] = gpre
        gn2 = dot(gpre, wup[...], NT)
        gmid = up + norm_back(gn2, gain2, n2, r2)
        mid_ref[...] = gmid
        gbo = (scale1 * gmid).astype(LOW)
        gbo_ref[...] = gbo
        gatt = dot(gbo, wo[...], NT).astype(LOW)
        msg_ref[0:T, :] = gatt
        inner = gatt.astype(WIDE) * att
        for p in range(HEADS // 2):
            part = inner[:, LANES * p : LANES * (p + 1)]
            one = jnp.sum(jnp.where(left, part, 0.0), axis=1, keepdims=True)
            two = jnp.sum(jnp.where(left, 0.0, part), axis=1, keepdims=True)
            stats = jnp.where(lane == HEADS + 2 * p, one, stats)
            stats = jnp.where(lane == HEADS + 2 * p + 1, two, stats)
        stat_ref[...] = stats
        flipped = jnp.transpose(stats)[0:16, :]
        hi16 = flipped.astype(LOW)
        rest = flipped - hi16.astype(WIDE)
        mid16 = rest.astype(LOW)
        low16 = (rest - mid16.astype(WIDE)).astype(LOW)
        packed = jnp.concatenate([hi16, mid16[:, : D - T]], axis=1)
        msg_ref[T : T + 16, :] = packed
        packed = jnp.concatenate([mid16[:, D - T :], low16], axis=1)
        msg_ref[T + 16 : T + 32, :] = packed

        vec_ref[...] = jnp.zeros(vec_ref.shape, WIDE)
        vec_ref[0:1, :D] = column_sum(up * branch_two)
        vec_ref[1:2, :D] = column_sum(gbt.astype(WIDE))
        vec_ref[2:3, :] = column_sum(gpre.astype(WIDE))
        vec_ref[3:4, :D] = column_sum(gn2 * n2)
        vec_ref[4:5, :D] = column_sum(gn2)
        vec_ref[5:6, :D] = column_sum(gmid * branch_one)
        vec_ref[6:7, :D] = column_sum(gbo.astype(WIDE))

    return kernel


def fold(dest, row, left, right, width):
    wide = width // LANES
    height = left.shape[1]
    for i in range(0, height, 384):
        part = dot(left[:, i : i + 384], right[...], TN)
        for j in range(wide):
            dest[pl.ds(row + i * wide + j, 384, stride=wide), :] = part[
                :, LANES * j : LANES * (j + 1)
            ]


def middle_kernel(plan):
    T = plan.tokens
    own = plan.reach
    base = AT["out"]

    def kernel(
        table,
        q_ref,
        k_ref,
        v_ref,
        msg_ref,
        stat_ref,
        col_ref,
        row_ref,
        act_ref,
        pre_ref,
        gbt_ref,
        n2_ref,
        att_ref,
        gbo_ref,
        vec_ref,
        gq_ref,
        blocks_ref,
        tail_ref,
        flat,
    ):
        lo = table[plan.low_at()]
        hi = table[plan.low_at() + 1]
        fold(flat, AT["down"] - base, act_ref, gbt_ref, D)
        fold(flat, AT["up"] - base, n2_ref, pre_ref, FF)
        fold(flat, AT["out"] - base, att_ref, gbo_ref, D)
        put_vector(flat, AT["scale2"] - base, vec_ref[0:1, :D])
        put_vector(flat, AT["dbias"] - base, vec_ref[1:2, :D])
        put_vector(flat, AT["ubias"] - base, vec_ref[2:3, :])
        put_vector(flat, AT["gain2"] - base, vec_ref[3:4, :D])
        put_vector(flat, AT["shift2"] - base, vec_ref[4:5, :D])
        put_vector(flat, AT["scale1"] - base, vec_ref[5:6, :D])
        put_vector(flat, AT["obias"] - base, vec_ref[6:7, :D])
        end = ALL_ROWS - base
        flat[end:, :] = jnp.zeros((flat.shape[0] - end, LANES), WIDE)
        tail_ref[...] = flat[0 : plan.rows, :]
        for e in range(plan.first_late, plan.count):
            r0 = plan.start[e] - base
            blocks_ref[table[e]] = flat[r0 : r0 + plan.rows, :].astype(LOW)

        lane = lax.broadcasted_iota(jnp.int32, (T, LANES), 1)
        left = lane < HEAD_DIM
        ids = jnp.concatenate([col_ref[...]] * (T // LANES), axis=1)
        for p in range(HEADS // 2):
            cols = slice(LANES * p, LANES * (p + 1))
            q = q_ref[own, :, cols]
            g = msg_ref[0:T, cols]
            qs = [jnp.where(left, q, 0), jnp.where(left, 0, q)]
            gs = [jnp.where(left, g, 0), jnp.where(left, 0, g)]
            logs = [stat_ref[:, 2 * p + i : 2 * p + i + 1] for i in range(2)]
            inner = [stat_ref[:, HEADS + 2 * p + i : HEADS + 2 * p + i + 1] for i in range(2)]

            def step(w, carry, qs=qs, gs=gs, logs=logs, inner=inner, cols=cols):
                key = k_ref[w, :, cols]
                value = v_ref[w, :, cols]
                seen = ids == row_ref[pl.ds(w, 1), :]
                new = []
                for i in range(2):
                    s = jnp.where(seen, dot(qs[i], key, NT), MASKED)
                    prob = jnp.exp(s - logs[i])
                    gs_i = prob * (dot(gs[i], value, NT) - inner[i])
                    new.append(carry[i] + dot(gs_i.astype(LOW), key, NN))
                return tuple(new)

            zero = jnp.zeros((T, LANES), WIDE)
            got = lax.fori_loop(lo, hi + 1, step, (zero, zero))
            gq_ref[:, cols] = (jnp.where(left, got[0], got[1]) * SCALE).astype(LOW)

    return kernel


def last_kernel(plan, sources):
    T = plan.tokens
    own = plan.reach
    early = plan.first_late

    def kernel(table, *refs):
        wins = refs[:sources]
        (
            q_ref,
            k_ref,
            v_ref,
            col_ref,
            row_ref,
            gq_ref,
            normed_ref,
            triple_ref,
            x_ref,
            mid_ref,
            gain_ref,
            tail_ref,
            _,
            grad_ref,
            blocks_ref,
        ) = refs[sources : sources + 15]
        mwin, flat, gt, stage, msem, osem = refs[sources + 15 :]
        lo = table[plan.low_at()]
        hi = table[plan.low_at() + 1]
        fetch_window(plan, table, wins, mwin, msem, lo, hi, False)
        fetch_window(plan, table, wins, mwin, msem, lo, hi, True)
        lane = lax.broadcasted_iota(jnp.int32, (T, LANES), 1)
        left = lane < HEAD_DIM
        ids = jnp.concatenate([col_ref[...]] * (T // LANES), axis=1)
        for p in range(HEADS // 2):
            cols = slice(LANES * p, LANES * (p + 1))
            k = k_ref[:, cols]
            v = v_ref[:, cols]
            ks = [jnp.where(left, k, 0), jnp.where(left, 0, k)]
            vs = [jnp.where(left, v, 0), jnp.where(left, 0, v)]

            def step(w, carry, ks=ks, vs=vs, cols=cols, p=p):
                q = q_ref[w, :, cols]
                g = mwin[w, 0:T, cols]
                one = mwin[w, T : T + 16, :].astype(WIDE)
                two = mwin[w, T + 16 : T + 32, :].astype(WIDE)
                stats = one[:, :T] + jnp.concatenate(
                    [one[:, T:], two[:, : 2 * T - D]], axis=1
                )
                stats = stats + two[:, 2 * T - D :]
                seen = ids == row_ref[pl.ds(w, 1), :]
                new = []
                for i in range(2):
                    h = 2 * p + i
                    s = jnp.where(seen, dot(ks[i], q, NT), MASKED)
                    prob = jnp.exp(s - stats[h : h + 1, :])
                    gs_i = prob * (dot(vs[i], g, NT) - stats[HEADS + h : HEADS + h + 1, :])
                    new.append(carry[2 * i] + dot(gs_i.astype(LOW), q, NN))
                    new.append(carry[2 * i + 1] + dot(prob.astype(LOW), g, NN))
                return tuple(new)

            zero = jnp.zeros((T, LANES), WIDE)
            got = lax.fori_loop(lo, hi + 1, step, (zero,) * 4)
            gt[:, D + LANES * p : D + LANES * (p + 1)] = jnp.where(left, got[0], got[2]).astype(LOW)
            gt[:, 2 * D + LANES * p : 2 * D + LANES * (p + 1)] = jnp.where(
                left, got[1], got[3]
            ).astype(LOW)
        gt[:, :D] = gq_ref[...]
        fold(flat, AT["triple"], normed_ref, gt, 3 * D)
        put_vector(flat, AT["tbias"], column_sum(gt[:, :D].astype(WIDE)))
        put_vector(flat, AT["tbias"] + D // LANES, column_sum(gt[:, 2 * D :].astype(WIDE)))
        gn = dot(gt[...], triple_ref[...], NT)
        n, r = normalized(x_ref[...].astype(WIDE))
        put_vector(flat, AT["gain1"], column_sum(gn * n))
        put_vector(flat, AT["shift1"], column_sum(gn))
        flat[AT["out"] : AT["out"] + plan.rows, :] = tail_ref[...]
        for e in range(early):
            r0 = plan.start[e]
            stage[e] = flat[r0 : r0 + plan.rows, :].astype(LOW)
            pltpu.make_async_copy(stage.at[e], blocks_ref.at[table[e]], osem.at[e]).start()
        grad_ref[...] = mid_ref[...] + norm_back(gn, gain_ref[0:1, :], n, r)
        for e in range(early):
            pltpu.make_async_copy(stage.at[e], blocks_ref.at[table[e]], osem.at[e]).wait()

    return kernel


def shape(dims, kind):
    return jax.ShapeDtypeStruct(dims, kind)


SMEM = pl.BlockSpec(memory_space=pltpu.SMEM)
VMEM = pl.BlockSpec(memory_space=pltpu.VMEM)
ANY = pl.BlockSpec(memory_space=pl.ANY)


def build(plan):
    T = plan.tokens
    W = plan.window
    R = plan.rows
    N = plan.count
    limit = pltpu.CompilerParams(vmem_limit_bytes=60 * 1024 * 1024)

    def per_device(inputs, cotangent, master, first_moment, second_moment, image_ids, spans):
        device = lax.axis_index(BOTH).astype(jnp.int32)
        table = plan.table(device, spans)
        padded = jnp.pad(image_ids, (plan.reach * T, plan.reach * T), constant_values=-1)
        key_ids = lax.dynamic_slice_in_dim(padded, device * T, W * T, 0).reshape(W, T)
        own_ids = key_ids[plan.reach]
        columns = jnp.broadcast_to(own_ids[:, None], (T, LANES))

        shifted = pl.pallas_call(
            shift_kernel(plan),
            in_specs=[SMEM, VMEM],
            out_specs=VMEM,
            out_shape=shape((R, LANES), LOW),
            scratch_shapes=[pltpu.VMEM((R + 8, LANES), WIDE)],
            name="shift",
        )(table, jnp.pad(master, (0, R * LANES - plan.share)).reshape(R, LANES))
        near, core = plan.spread(shifted)
        wins = plan.exchange(inputs)
        sources = len(wins)

        outs = pl.pallas_call(
            forward_kernel(plan, sources),
            in_specs=[SMEM, ANY, ANY] + [ANY] * sources + [VMEM] * 3,
            out_specs=[VMEM] * 19,
            out_shape=[
                shape((T, D), LOW),
                shape((T + 32, D), LOW),
                shape((W, T, D), LOW),
                shape((W, T, D), LOW),
                shape((W, T, D), LOW),
                shape((D, 3 * D), LOW),
                shape((T, D), LOW),
                shape((T, D), WIDE),
                shape((T, FF), LOW),
                shape((T, FF), LOW),
                shape((T, D), LOW),
                shape((T, D), LOW),
                shape((T, D), LOW),
                shape((T, D), LOW),
                shape((8, FF), WIDE),
                shape((T, LANES), WIDE),
                shape((8, D), WIDE),
                shape((T, D), LOW),
                shape((T, D), LOW),
            ],
            scratch_shapes=[
                pltpu.VMEM((N, R, LANES), LOW),
                pltpu.VMEM((plan.flat_rows, LANES), WIDE),
                pltpu.VMEM((W, T, D), LOW),
                pltpu.VMEM((D, D), LOW),
                pltpu.VMEM((D, FF), LOW),
                pltpu.VMEM((FF, D), LOW),
                pltpu.VMEM((2, W, T, T), WIDE),
                pltpu.SemaphoreType.DMA((N,)),
                pltpu.SemaphoreType.DMA((W,)),
            ],
            compiler_params=limit,
            name="forward",
        )(table, near, core, *wins, cotangent, columns, key_ids)
        (
            result,
            message,
            q,
            k,
            v,
            triple,
            normed,
            gmid,
            act,
            gpre,
            gbt,
            n2,
            att,
            gbo,
            vec,
            stat,
            gain,
            k_own,
            v_own,
        ) = outs
        messages = plan.exchange(message)

        gq, blocks, tail = pl.pallas_call(
            middle_kernel(plan),
            in_specs=[SMEM] + [VMEM] * 14,
            out_specs=[VMEM] * 3,
            out_shape=[
                shape((T, D), LOW),
                shape((N, R, LANES), LOW),
                shape((R, LANES), WIDE),
            ],
            scratch_shapes=[
                pltpu.VMEM((plan.flat_rows - AT["out"] + 8, LANES), WIDE),
            ],
            compiler_params=limit,
            name="middle",
        )(table, q, k, v, message, stat, columns, key_ids, act, gpre, gbt, n2, att, gbo, vec)

        late = plan.first_late
        input_grad, blocks = pl.pallas_call(
            last_kernel(plan, sources),
            in_specs=[SMEM]
            + [ANY] * sources
            + [VMEM] * 12
            + [ANY],
            out_specs=[VMEM, ANY],
            out_shape=[shape((T, D), WIDE), shape((N, R, LANES), LOW)],
            scratch_shapes=[
                pltpu.VMEM((W, T + 32, D), LOW),
                pltpu.VMEM((AT["out"] + R + 8, LANES), WIDE),
                pltpu.VMEM((T, 3 * D), LOW),
                pltpu.VMEM((late, R, LANES), LOW),
                pltpu.SemaphoreType.DMA((W,)),
                pltpu.SemaphoreType.DMA((late,)),
            ],
            input_output_aliases={13 + sources: 1},
            compiler_params=limit,
            name="last",
        )(
            table,
            *messages,
            q,
            k_own,
            v_own,
            columns,
            key_ids,
            gq,
            normed,
            triple,
            inputs,
            gmid,
            gain,
            tail,
            blocks,
        )

        parts = plan.reduce_parts(blocks)
        grad, square = pl.pallas_call(
            unshift_kernel(plan),
            in_specs=[SMEM] + [VMEM] * len(parts),
            out_specs=[VMEM, VMEM],
            out_shape=[shape((R, LANES), WIDE), shape((8, LANES), WIDE)],
            scratch_shapes=[pltpu.VMEM((R + 8, LANES), WIDE)],
            name="unshift",
        )(table, *parts)
        grad_shard = grad.reshape(-1)[: plan.share]
        grad_norm = jnp.sqrt(plan.total(square)[0, 0])
        ceiling = CLIP_RATIO * math.sqrt(plan.share * N)
        factor = ceiling / jnp.maximum(grad_norm, ceiling)
        clipped = grad_shard * factor
        new_first = BETA_ONE * first_moment + (1.0 - BETA_ONE) * clipped
        new_second = BETA_TWO * second_moment + (1.0 - BETA_TWO) * clipped * clipped
        new_master = master - LEARN_RATE * (
            new_first / (jnp.sqrt(new_second) + ADAM_EPS) + WEIGHT_DECAY * master
        )
        return (
            result,
            input_grad,
            grad_shard,
            grad_norm.reshape(1),
            new_first,
            new_second,
            new_master,
        )

    return per_device


def solution(mesh):
    dp = mesh.shape["dp"]
    fsdp = mesh.shape["fsdp"]
    row = P(BOTH, None)
    flat = P(BOTH)
    in_specs = (row, row, flat, flat, flat, P(), P())
    out_specs = (row, row, flat, P(), flat, flat, flat)

    def per_device(*args):
        inputs, master = args[0], args[2]
        plan = Plan(dp, fsdp, master.shape[0], inputs.shape[0])
        return build(plan)(*args)

    return jax.shard_map(
        per_device, mesh=mesh, in_specs=in_specs, out_specs=out_specs, check_vma=False
    )
```

time: 829 us -> 289 us (0.35); the launches traced: 819 us -> 287 us
  waiting for transfers between devices: 444 us -> 95.2 us
  matrix products: 116 us -> 0 us
  local copies, waits for them, and re-layouts: 108 us -> 13.8 us
  starting transfers between devices: 51.9 us -> 126 us
  Pallas kernels: 0 us -> 41.5 us
  blocking collectives: 40.2 us -> 0 us
  other arithmetic: 40.2 us -> 8.17 us
  between operations: 17 us -> 2.89 us
    unnamed x4 -> x0, waiting for transfers between devices: 279 us -> none
    dot_general x38 -> x0, matrix products: 106 us -> none  [the longest x6 22 us: group_forward(): jnp.einsum('htk,khd->thd', weights, values, preferred_element_type=jnp.fl...]
    ppermute x24 -> x35, starting transfers between devices: 51.8 us -> 126 us  [the longest x31 119 us: send(): return lax.ppermute(x, BOTH, [(i, i ^ mask) for i in range(self.count)])]
    ppermute x24 -> x35, waiting for transfers between devices: 165 us -> 95.2 us  [the longest x31 95.2 us: send(): return lax.ppermute(x, BOTH, [(i, i ^ mask) for i in range(self.count)])]
    unnamed x136 -> x42, local copies, waits for them, and re-layouts: 67.4 us -> 4.25 us
    pallas_call x0 -> x5, Pallas kernels: none -> 41.5 us  [the longest x1 15.8 us: per_device(): pl.pallas_call(forward_kernel(plan, sources), in_specs=[SMEM, ANY, ANY] +...]
    psum x1 -> x0, blocking collectives: 40.2 us -> none  [per_device(): total_square = lax.psum(jnp.sum(grad_shard * grad_shard), ('dp', 'fsdp'))]
    slice x13 -> x5, local copies, waits for them, and re-layouts: 22.2 us -> 3.14 us  [the longest x3 2.55 us: reduce_parts(): split[k + 1]]
  transfers between devices with their start and end apart: 26 -> 35, of which waited for: 12 -> 16; matrix products, arithmetic and copies ran while one was open for 9% -> 2% of each run, Pallas kernels for 0% -> 4%
where the time goes in v1:
time: 289 us; the launch traced here: 287 us
  starting transfers between devices  126 us (44%)
  waiting for transfers between devices  95.2 us (33%)
  Pallas kernels  41.5 us (14%)
  local copies, waits for them, and re-layouts  13.8 us (5%)
  other arithmetic  8.17 us (3%)
  between operations  2.89 us (1%)
    ppermute x31, starting transfers between devices, send(): return lax.ppermute(x, BOTH, [(i, i ^ mask) for i in range(self.count)])  119 us
    ppermute x31, waiting for transfers between devices, send(): return lax.ppermute(x, BOTH, [(i, i ^ mask) for i in range(self.count)])  95.2 us
    pallas_call x1, Pallas kernels, per_device(): pl.pallas_call(forward_kernel(plan, sources), in_specs=[SMEM, ANY, ANY] +...  15.8 us
    pallas_call x1, Pallas kernels, per_device(): pl.pallas_call(middle_kernel(plan), in_specs=[SMEM] + [VMEM] * 14, out_sp...  11.3 us
    pallas_call x1, Pallas kernels, per_device(): pl.pallas_call(last_kernel(plan, sources), in_specs=[SMEM] + [ANY] * sour...  10.7 us
  transfers between devices with their start and end apart: 35, of which 16 were waited for; matrix products, arithmetic and copies ran while one was open for 2% of the time, Pallas kernels for 4%

profile of v1, /device:TPU:0, one launch (start us, length us, event | category | flops | bytes accessed | tf_op | source)
XLA Modules:
  0.0 287.1 jit_solution(358591401069504212)
XLA Ops:
  5.6 3.1 %collective-permute-start = (bf16[1,448,128]{2,1,0:T(8,128)(2,1)}, bf16[1,448,128]{2,1,0:T(8,128)(2,1)S(1)}, u32[]{:S(2)}, u32[]{:S(2)}) collective-permute-start(bf16[1,448,128]{2,1,0:T(8,128)(2,1)} %bitcast.25), channel_id=1, source_target_pairs={{0,2},{1,3},{2,0},{3,1},{4,6},{5,7},{6,4},{7,5},{8,10},{9,11},{10,... | collective-permute-start | bytes 344072 | tf_op jit(solution)/shard_map/ppermute | solution.py:87
  8.6 2.6 collective-permute-start.1
  12.1 3.5 %collective-permute-start.8 = (bf16[1,256,384]{2,1,0:T(8,128)(2,1)}, bf16[1,256,384]{2,1,0:T(8,128)(2,1)S(1)}, u32[]{:S(2)}, u32[]{:S(2)}) collective-permute-start(bf16[1,256,384]{2,1,0:T(8,128)(2,1)} %bitcast.22), channel_id=1, source_target_pairs={{0,4},{1,5},{2,6},{3,7},{4,0},{5,1},{6,2},{7,3},{8,12},{9,13},{10,... | collective-permute-start | bytes 589832 | tf_op jit(solution)/shard_map/ppermute | solution.py:87
  17.6 3.0 %collective-permute-done.1 = bf16[1,448,128]{2,1,0:T(8,128)(2,1)S(1)} collective-permute-done((bf16[1,448,128]{2,1,0:T(8,128)(2,1)}, bf16[1,448,128]{2,1,0:T(8,128)(2,1)S(1)}, u32[]{:S(2)}, u32[]{:S(2)}) %collective-permute-start.1) | collective-permute-done | bytes 114720 | tf_op jit(solution)/shard_map/ppermute | solution.py:87
  25.2 10.5 %collective-permute-done.8 = bf16[1,256,384]{2,1,0:T(8,128)(2,1)S(1)} collective-permute-done((bf16[1,256,384]{2,1,0:T(8,128)(2,1)}, bf16[1,256,384]{2,1,0:T(8,128)(2,1)S(1)}, u32[]{:S(2)}, u32[]{:S(2)}) %collective-permute-start.8) | collective-permute-done | bytes 196640 | tf_op jit(solution)/shard_map/ppermute | solution.py:87
  38.4 4.5 %collective-permute-done.4 = bf16[4,448,128]{2,1,0:T(8,128)(2,1)S(1)} collective-permute-done((bf16[4,448,128]{2,1,0:T(8,128)(2,1)S(1)}, bf16[4,448,128]{2,1,0:T(8,128)(2,1)S(1)}, u32[]{:S(2)}, u32[]{:S(2)}) %collective-permute-start.4) | collective-permute-done | bytes 458784 | tf_op jit(solution)/shard_map/ppermute | solution.py:87
  43.2 16.4 %collective-permute-done.10 = bf16[4,256,384]{2,1,0:T(8,128)(2,1)} collective-permute-done((bf16[4,256,384]{2,1,0:T(8,128)(2,1)}, bf16[4,256,384]{2,1,0:T(8,128)(2,1)}, u32[]{:S(2)}, u32[]{:S(2)}) %collective-permute-start.10) | collective-permute-done | bytes 786464 | tf_op jit(solution)/shard_map/ppermute | solution.py:87
  65.6 15.8 %forward.1 = (bf16[256,384]{1,0:T(8,128)(2,1)}, bf16[288,384]{1,0:T(8,128)(2,1)}, bf16[13,256,384]{2,1,0:T(8,128)(2,1)}, bf16[13,256,384]{2,1,0:T(8,128)(2,1)}, ...) custom-call(s32[61]{0:T(128)} %concatenate.24.table, ...), custom_call_target="tpu_custom_call" | custom-call | tf_op jit(solution)/shard_map/forward/pallas_call | solution.py:669
  81.4 13.7 %collective-permute-start.14 = (bf16[1,288,384]{2,1,0:T(8,128)(2,1)}, bf16[1,288,384]{2,1,0:T(8,128)(2,1)S(1)}, u32[]{:S(2)}, u32[]{:S(2)}) collective-permute-start(bf16[1,288,384]{2,1,0:T(8,128)(2,1)} %bitcast.17), channel_id=1, source_target_pairs={{0,2},{1,3},{2,0},{3,1},{4,6},{5,7},{6,4},{7,5},{8,10},{9,11},{10,... | collective-permute-start | bytes 663560 | tf_op jit(solution)/shard_map/ppermute | solution.py:87
  95.1 9.3 %collective-permute-start.15 = (bf16[1,288,384]{2,1,0:T(8,128)(2,1)}, bf16[1,288,384]{2,1,0:T(8,128)(2,1)S(1)}, u32[]{:S(2)}, u32[]{:S(2)}) collective-permute-start(bf16[1,288,384]{2,1,0:T(8,128)(2,1)} %bitcast.18), channel_id=1, source_target_pairs={{0,4},{1,5},{2,6},{3,7},{4,0},{5,1},{6,2},{7,3},{8,12},{9,13},{10,... | collective-permute-start | bytes 663560 | tf_op jit(solution)/shard_map/ppermute | solution.py:87
  104.5 8.9 %collective-permute-done.15 = bf16[1,288,384]{2,1,0:T(8,128)(2,1)S(1)} collective-permute-done((bf16[1,288,384]{2,1,0:T(8,128)(2,1)}, bf16[1,288,384]{2,1,0:T(8,128)(2,1)S(1)}, u32[]{:S(2)}, u32[]{:S(2)}) %collective-permute-start.15) | collective-permute-done | bytes 221216 | tf_op jit(solution)/shard_map/ppermute | solution.py:87
  115.5 13.2 %collective-permute-done.17 = bf16[4,288,384]{2,1,0:T(8,128)(2,1)} collective-permute-done((bf16[4,288,384]{2,1,0:T(8,128)(2,1)}, bf16[4,288,384]{2,1,0:T(8,128)(2,1)}, u32[]{:S(2)}, u32[]{:S(2)}) %collective-permute-start.17) | collective-permute-done | bytes 884768 | tf_op jit(solution)/shard_map/ppermute | solution.py:87
  130.1 23.3 %collective-permute-start.18 = (bf16[8,288,384]{2,1,0:T(8,128)(2,1)S(1)}, bf16[8,288,384]{2,1,0:T(8,128)(2,1)S(1)}, u32[]{:S(2)}, u32[]{:S(2)}) collective-permute-start(bf16[8,288,384]{2,1,0:T(8,128)(2,1)S(1)} %constant_dynamic-update-slice_fusion.12.refs_0_), channel_id=1, source_target_pairs={{0,8},{1,9},{2,10},{3,11},{4,12},{5,13},{6,14},{7,15},{8,0},{9,1},... | collective-permute-start | bytes 5308424 | tf_op jit(solution)/shard_map/ppermute | solution.py:87
  156.5 11.3 %middle.1 = (bf16[256,384]{1,0:T(8,128)(2,1)}, bf16[32,448,128]{2,1,0:T(8,128)(2,1)}, f32[448,128]{1,0:T(8,128)}) custom-call(s32[61]{0:T(128)} %concatenate.24.table, bf16[13,256,384]{2,1,0:T(8,128)(2,1)} %get-tuple-element.35.q_ref.refs_4_, bf16[13,256,384]{2,1,0:T(8,128)(2,1)} %get-tuple-element.38.k_ref, bf16[13,256,384]{2,1,0:T(8,128)(2,1)} %get-tuple-element.39.v_ref, ...), custom_call_target="tpu_custom_call" | custom-call | tf_op jit(solution)/shard_map/middle/pallas_call | solution.py:731
  169.1 10.7 %last.1 = (f32[256,384]{1,0:T(8,128)}, bf16[32,448,128]{2,1,0:T(8,128)(2,1)}) custom-call(s32[61]{0:T(128)} %concatenate.24.table, bf16[8,288,384]{2,1,0:T(8,128)(2,1)} %copy-done.1, bf16[8,288,384]{2,1,0:T(8,128)(2,1)} %copy-done.5, bf16[4,288,384]{2,1,0:T(8,128)(2,1)} %collective-permute-done.19.refs_2_, ...), custom_call_target="tpu_custom_call", output_to_operand_aliasing={{1}: (17, {})} | custom-call | tf_op jit(solution)/shard_map/last/pallas_call | solution.py:748
  181.6 17.9 %collective-permute-start.21 = (bf16[16,448,128]{2,1,0:T(8,128)(2,1)S(1)}, bf16[16,448,128]{2,1,0:T(8,128)(2,1)S(1)}, u32[]{:S(2)}, u32[]{:S(2)}) collective-permute-start(bf16[16,448,128]{2,1,0:T(8,128)(2,1)S(1)} %slice.52), channel_id=1, source_target_pairs={{0,8},{1,9},{2,10},{3,11},{4,12},{5,13},{6,14},{7,15},{8,0},{9,1},... | collective-permute-start | bytes 5505032 | tf_op jit(solution)/shard_map/ppermute | solution.py:87
  199.5 3.4 %collective-permute-done.21 = bf16[16,448,128]{2,1,0:T(8,128)(2,1)S(1)} collective-permute-done((bf16[16,448,128]{2,1,0:T(8,128)(2,1)S(1)}, bf16[16,448,128]{2,1,0:T(8,128)(2,1)S(1)}, u32[]{:S(2)}, u32[]{:S(2)}) %collective-permute-start.21) | collective-permute-done | bytes 1835040 | tf_op jit(solution)/shard_map/ppermute | solution.py:87
  203.5 3.7 %collective-permute-start.22 = (bf16[4,448,128]{2,1,0:T(8,128)(2,1)S(1)}, bf16[4,448,128]{2,1,0:T(8,128)(2,1)S(1)}, u32[]{:S(2)}, u32[]{:S(2)}) collective-permute-start(bf16[4,448,128]{2,1,0:T(8,128)(2,1)S(1)} %get-tuple-element.63), channel_id=1, source_target_pairs={{0,16},{1,17},{2,18},{3,19},{4,20},{5,21},{6,22},{7,23},{8,24},{9,... | collective-permute-start | bytes 1376264 | tf_op jit(solution)/shard_map/ppermute | solution.py:87
  207.2 20.4 %collective-permute-start.23 = (bf16[4,448,128]{2,1,0:T(8,128)(2,1)S(1)}, bf16[4,448,128]{2,1,0:T(8,128)(2,1)S(1)}, u32[]{:S(2)}, u32[]{:S(2)}) collective-permute-start(bf16[4,448,128]{2,1,0:T(8,128)(2,1)S(1)} %get-tuple-element.65), channel_id=1, source_target_pairs={{0,1},{1,0},{2,3},{3,2},{4,5},{5,4},{6,7},{7,6},{8,9},{9,8},{10,11... | collective-permute-start | bytes 1376264 | tf_op jit(solution)/shard_map/ppermute | solution.py:87
  227.7 20.3 %collective-permute-done.23 = bf16[4,448,128]{2,1,0:T(8,128)(2,1)S(1)} collective-permute-done((bf16[4,448,128]{2,1,0:T(8,128)(2,1)S(1)}, bf16[4,448,128]{2,1,0:T(8,128)(2,1)S(1)}, u32[]{:S(2)}, u32[]{:S(2)}) %collective-permute-start.23) | collective-permute-done | bytes 458784 | tf_op jit(solution)/shard_map/ppermute | solution.py:87
  248.9 4.4 %collective-permute-start.25 = (bf16[1,448,128]{2,1,0:T(8,128)(2,1)S(1)}, bf16[1,448,128]{2,1,0:T(8,128)(2,1)S(1)}, u32[]{:S(2)}, u32[]{:S(2)}) collective-permute-start(bf16[1,448,128]{2,1,0:T(8,128)(2,1)S(1)} %get-tuple-element.68), channel_id=1, source_target_pairs={{0,2},{1,3},{2,0},{3,1},{4,6},{5,7},{6,4},{7,5},{8,10},{9,11},{10,... | collective-permute-start | bytes 344072 | tf_op jit(solution)/shard_map/ppermute | solution.py:87
  256.9 6.4 %collective-permute-done.26 = bf16[1,448,128]{2,1,0:T(8,128)(2,1)S(1)} collective-permute-done((bf16[1,448,128]{2,1,0:T(8,128)(2,1)S(1)}, bf16[1,448,128]{2,1,0:T(8,128)(2,1)S(1)}, u32[]{:S(2)}, u32[]{:S(2)}) %collective-permute-start.26) | collective-permute-done | bytes 114720 | tf_op jit(solution)/shard_map/ppermute | solution.py:87
  265.9 2.9 %collective-permute-start.28 = (f32[8,128]{1,0:T(8,128)}, f32[8,128]{1,0:T(8,128)S(1)}, u32[]{:S(2)}, u32[]{:S(2)}) collective-permute-start(f32[8,128]{1,0:T(8,128)} %get-tuple-element.58), channel_id=1, source_target_pairs={{0,2},{1,3},{2,0},{3,1},{4,6},{5,7},{6,4},{7,5},{8,10},{9,11},{10,... | collective-permute-start | bytes 12296 | tf_op jit(solution)/shard_map/ppermute | solution.py:87
  268.8 2.4 collective-permute-start.30
  (118 shorter events, 52.7 us)
Async XLA Ops:
  5.6 11.9 %collective-permute-start = (bf16[1,448,128]{2,1,0:T(8,128)(2,1)}, bf16[1,448,128]{2,1,0:T(8,128)(2,1)S(1)}, u32[]{:S(2)}, u32[]{:S(2)}) collective-permute-start(bf16[1,448,128]{2,1,0:T(8,128)(2,1)} %bitcast.25), channel_id=1, source_target_pairs={{0,2},{1,3},{2,0},{3,1},{4,6},{5,7},{6,4},{7,5},{8,10},{9,11},{10,... | collective-permute-start | bytes 344072 | tf_op jit(solution)/shard_map/ppermute | solution.py:87
  8.6 11.9 %collective-permute-start.1 = (bf16[1,448,128]{2,1,0:T(8,128)(2,1)}, bf16[1,448,128]{2,1,0:T(8,128)(2,1)S(1)}, u32[]{:S(2)}, u32[]{:S(2)}) collective-permute-start(bf16[1,448,128]{2,1,0:T(8,128)(2,1)} %bitcast.26), channel_id=1, source_target_pairs={{0,4},{1,5},{2,6},{3,7},{4,0},{5,1},{6,2},{7,3},{8,12},{9,13},{10,... | collective-permute-start | bytes 344072 | tf_op jit(solution)/shard_map/ppermute | solution.py:87
  11.2 9.3 %collective-permute-start.2 = (bf16[1,448,128]{2,1,0:T(8,128)(2,1)}, bf16[1,448,128]{2,1,0:T(8,128)(2,1)S(1)}, u32[]{:S(2)}, u32[]{:S(2)}) collective-permute-start(bf16[1,448,128]{2,1,0:T(8,128)(2,1)} %bitcast.27), channel_id=1, source_target_pairs={{0,6},{1,7},{2,4},{3,5},{4,2},{5,3},{6,0},{7,1},{8,14},{9,15},{10,... | collective-permute-start | bytes 344072 | tf_op jit(solution)/shard_map/ppermute | solution.py:87
  11.2 13.4 %collective-permute-start.7 = (bf16[1,256,384]{2,1,0:T(8,128)(2,1)}, bf16[1,256,384]{2,1,0:T(8,128)(2,1)S(1)}, u32[]{:S(2)}, u32[]{:S(2)}) collective-permute-start(bf16[1,256,384]{2,1,0:T(8,128)(2,1)} %bitcast.21), channel_id=1, source_target_pairs={{0,2},{1,3},{2,0},{3,1},{4,6},{5,7},{6,4},{7,5},{8,10},{9,11},{10,... | collective-permute-start | bytes 589832 | tf_op jit(solution)/shard_map/ppermute | solution.py:87
  12.1 23.5 %collective-permute-start.8 = (bf16[1,256,384]{2,1,0:T(8,128)(2,1)}, bf16[1,256,384]{2,1,0:T(8,128)(2,1)S(1)}, u32[]{:S(2)}, u32[]{:S(2)}) collective-permute-start(bf16[1,256,384]{2,1,0:T(8,128)(2,1)} %bitcast.22), channel_id=1, source_target_pairs={{0,4},{1,5},{2,6},{3,7},{4,0},{5,1},{6,2},{7,3},{8,12},{9,13},{10,... | collective-permute-start | bytes 589832 | tf_op jit(solution)/shard_map/ppermute | solution.py:87
  17.5 18.1 %collective-permute-start.9 = (bf16[1,256,384]{2,1,0:T(8,128)(2,1)}, bf16[1,256,384]{2,1,0:T(8,128)(2,1)S(1)}, u32[]{:S(2)}, u32[]{:S(2)}) collective-permute-start(bf16[1,256,384]{2,1,0:T(8,128)(2,1)} %bitcast.23), channel_id=1, source_target_pairs={{0,6},{1,7},{2,4},{3,5},{4,2},{5,3},{6,0},{7,1},{8,14},{9,15},{10,... | collective-permute-start | bytes 589832 | tf_op jit(solution)/shard_map/ppermute | solution.py:87
  21.5 16.7 %collective-permute-start.3 = (bf16[4,448,128]{2,1,0:T(8,128)(2,1)S(1)}, bf16[4,448,128]{2,1,0:T(8,128)(2,1)S(1)}, u32[]{:S(2)}, u32[]{:S(2)}) collective-permute-start(bf16[4,448,128]{2,1,0:T(8,128)(2,1)S(1)} %pad_maximum_fusion.2), channel_id=1, source_target_pairs={{0,16},{1,17},{2,18},{3,19},{4,20},{5,21},{6,22},{7,23},{8,24},{9,... | collective-permute-start | bytes 1376264 | tf_op jit(solution)/shard_map/ppermute | solution.py:87
  23.1 19.8 %collective-permute-start.4 = (bf16[4,448,128]{2,1,0:T(8,128)(2,1)S(1)}, bf16[4,448,128]{2,1,0:T(8,128)(2,1)S(1)}, u32[]{:S(2)}, u32[]{:S(2)}) collective-permute-start(bf16[4,448,128]{2,1,0:T(8,128)(2,1)S(1)} %pad_maximum_fusion.2), channel_id=1, source_target_pairs={{0,1},{1,0},{2,3},{3,2},{4,5},{5,4},{6,7},{7,6},{8,9},{9,8},{10,11... | collective-permute-start | bytes 1376264 | tf_op jit(solution)/shard_map/ppermute | solution.py:87
  24.7 18.3 %collective-permute-start.5 = (bf16[4,448,128]{2,1,0:T(8,128)(2,1)S(1)}, bf16[4,448,128]{2,1,0:T(8,128)(2,1)S(1)}, u32[]{:S(2)}, u32[]{:S(2)}) collective-permute-start(bf16[4,448,128]{2,1,0:T(8,128)(2,1)S(1)} %pad_maximum_fusion.2), channel_id=1, source_target_pairs={{0,17},{1,16},{2,19},{3,18},{4,21},{5,20},{6,23},{7,22},{8,25},{9,... | collective-permute-start | bytes 1376264 | tf_op jit(solution)/shard_map/ppermute | solution.py:87
  36.7 22.9 %collective-permute-start.10 = (bf16[4,256,384]{2,1,0:T(8,128)(2,1)}, bf16[4,256,384]{2,1,0:T(8,128)(2,1)}, u32[]{:S(2)}, u32[]{:S(2)}) collective-permute-start(bf16[4,256,384]{2,1,0:T(8,128)(2,1)} %pad_maximum_fusion.1), channel_id=1, source_target_pairs={{0,1},{1,0},{2,3},{3,2},{4,5},{5,4},{6,7},{7,6},{8,9},{9,8},{10,11... | collective-permute-start | bytes 2359304 | tf_op jit(solution)/shard_map/ppermute | solution.py:87
  43.0 21.8 %collective-permute-start.6 = (bf16[16,448,128]{2,1,0:T(8,128)(2,1)S(1)}, bf16[16,448,128]{2,1,0:T(8,128)(2,1)}, u32[]{:S(2)}, u32[]{:S(2)}) collective-permute-start(bf16[16,448,128]{2,1,0:T(8,128)(2,1)S(1)} %constant_dynamic-update-slice_fusion.refs_0_), channel_id=1, source_target_pairs={{0,8},{1,9},{2,10},{3,11},{4,12},{5,13},{6,14},{7,15},{8,0},{9,1},... | collective-permute-start | bytes 5505032 | tf_op jit(solution)/shard_map/ppermute | solution.py:87
  81.4 23.0 %collective-permute-start.14 = (bf16[1,288,384]{2,1,0:T(8,128)(2,1)}, bf16[1,288,384]{2,1,0:T(8,128)(2,1)S(1)}, u32[]{:S(2)}, u32[]{:S(2)}) collective-permute-start(bf16[1,288,384]{2,1,0:T(8,128)(2,1)} %bitcast.17), channel_id=1, source_target_pairs={{0,2},{1,3},{2,0},{3,1},{4,6},{5,7},{6,4},{7,5},{8,10},{9,11},{10,... | collective-permute-start | bytes 663560 | tf_op jit(solution)/shard_map/ppermute | solution.py:87
  95.1 18.2 %collective-permute-start.15 = (bf16[1,288,384]{2,1,0:T(8,128)(2,1)}, bf16[1,288,384]{2,1,0:T(8,128)(2,1)S(1)}, u32[]{:S(2)}, u32[]{:S(2)}) collective-permute-start(bf16[1,288,384]{2,1,0:T(8,128)(2,1)} %bitcast.18), channel_id=1, source_target_pairs={{0,4},{1,5},{2,6},{3,7},{4,0},{5,1},{6,2},{7,3},{8,12},{9,13},{10,... | collective-permute-start | bytes 663560 | tf_op jit(solution)/shard_map/ppermute | solution.py:87
  104.5 8.9 %collective-permute-start.16 = (bf16[1,288,384]{2,1,0:T(8,128)(2,1)}, bf16[1,288,384]{2,1,0:T(8,128)(2,1)S(1)}, u32[]{:S(2)}, u32[]{:S(2)}) collective-permute-start(bf16[1,288,384]{2,1,0:T(8,128)(2,1)} %bitcast.19), channel_id=1, source_target_pairs={{0,6},{1,7},{2,4},{3,5},{4,2},{5,3},{6,0},{7,1},{8,14},{9,15},{10,... | collective-permute-start | bytes 663560 | tf_op jit(solution)/shard_map/ppermute | solution.py:87
  115.3 13.4 %collective-permute-start.17 = (bf16[4,288,384]{2,1,0:T(8,128)(2,1)}, bf16[4,288,384]{2,1,0:T(8,128)(2,1)}, u32[]{:S(2)}, u32[]{:S(2)}) collective-permute-start(bf16[4,288,384]{2,1,0:T(8,128)(2,1)} %pad_maximum_fusion), channel_id=1, source_target_pairs={{0,1},{1,0},{2,3},{3,2},{4,5},{5,4},{6,7},{7,6},{8,9},{9,8},{10,11... | collective-permute-start | bytes 2654216 | tf_op jit(solution)/shard_map/ppermute | solution.py:87
  130.1 37.8 %collective-permute-start.18 = (bf16[8,288,384]{2,1,0:T(8,128)(2,1)S(1)}, bf16[8,288,384]{2,1,0:T(8,128)(2,1)S(1)}, u32[]{:S(2)}, u32[]{:S(2)}) collective-permute-start(bf16[8,288,384]{2,1,0:T(8,128)(2,1)S(1)} %constant_dynamic-update-slice_fusion.12.refs_0_), channel_id=1, source_target_pairs={{0,8},{1,9},{2,10},{3,11},{4,12},{5,13},{6,14},{7,15},{8,0},{9,1},... | collective-permute-start | bytes 5308424 | tf_op jit(solution)/shard_map/ppermute | solution.py:87
  153.3 14.5 %collective-permute-start.19 = (bf16[4,288,384]{2,1,0:T(8,128)(2,1)}, bf16[4,288,384]{2,1,0:T(8,128)(2,1)}, u32[]{:S(2)}, u32[]{:S(2)}) collective-permute-start(bf16[4,288,384]{2,1,0:T(8,128)(2,1)} %pad_maximum_fusion), channel_id=1, source_target_pairs={{8,16},{9,17},{10,18},{11,19},{12,20},{13,21},{14,22},{15,23},{16,... | collective-permute-start | bytes 2654216 | tf_op jit(solution)/shard_map/ppermute | solution.py:121
  154.9 12.9 %collective-permute-start.20 = (bf16[4,288,384]{2,1,0:T(8,128)(2,1)}, bf16[4,288,384]{2,1,0:T(8,128)(2,1)}, u32[]{:S(2)}, u32[]{:S(2)}) collective-permute-start(bf16[4,288,384]{2,1,0:T(8,128)(2,1)} %collective-permute-done.17), channel_id=1, source_target_pairs={{8,16},{9,17},{10,18},{11,19},{12,20},{13,21},{14,22},{15,23},{16,... | collective-permute-start | bytes 2654216 | tf_op jit(solution)/shard_map/ppermute | solution.py:122
  181.6 21.3 %collective-permute-start.21 = (bf16[16,448,128]{2,1,0:T(8,128)(2,1)S(1)}, bf16[16,448,128]{2,1,0:T(8,128)(2,1)S(1)}, u32[]{:S(2)}, u32[]{:S(2)}) collective-permute-start(bf16[16,448,128]{2,1,0:T(8,128)(2,1)S(1)} %slice.52), channel_id=1, source_target_pairs={{0,8},{1,9},{2,10},{3,11},{4,12},{5,13},{6,14},{7,15},{8,0},{9,1},... | collective-permute-start | bytes 5505032 | tf_op jit(solution)/shard_map/ppermute | solution.py:87
  203.5 24.2 %collective-permute-start.22 = (bf16[4,448,128]{2,1,0:T(8,128)(2,1)S(1)}, bf16[4,448,128]{2,1,0:T(8,128)(2,1)S(1)}, u32[]{:S(2)}, u32[]{:S(2)}) collective-permute-start(bf16[4,448,128]{2,1,0:T(8,128)(2,1)S(1)} %get-tuple-element.63), channel_id=1, source_target_pairs={{0,16},{1,17},{2,18},{3,19},{4,20},{5,21},{6,22},{7,23},{8,24},{9,... | collective-permute-start | bytes 1376264 | tf_op jit(solution)/shard_map/ppermute | solution.py:87
  207.2 40.8 %collective-permute-start.23 = (bf16[4,448,128]{2,1,0:T(8,128)(2,1)S(1)}, bf16[4,448,128]{2,1,0:T(8,128)(2,1)S(1)}, u32[]{:S(2)}, u32[]{:S(2)}) collective-permute-start(bf16[4,448,128]{2,1,0:T(8,128)(2,1)S(1)} %get-tuple-element.65), channel_id=1, source_target_pairs={{0,1},{1,0},{2,3},{3,2},{4,5},{5,4},{6,7},{7,6},{8,9},{9,8},{10,11... | collective-permute-start | bytes 1376264 | tf_op jit(solution)/shard_map/ppermute | solution.py:87
  227.6 20.4 %collective-permute-start.24 = (bf16[4,448,128]{2,1,0:T(8,128)(2,1)S(1)}, bf16[4,448,128]{2,1,0:T(8,128)(2,1)S(1)}, u32[]{:S(2)}, u32[]{:S(2)}) collective-permute-start(bf16[4,448,128]{2,1,0:T(8,128)(2,1)S(1)} %get-tuple-element.64), channel_id=1, source_target_pairs={{0,17},{1,16},{2,19},{3,18},{4,21},{5,20},{6,23},{7,22},{8,25},{9,... | collective-permute-start | bytes 1376264 | tf_op jit(solution)/shard_map/ppermute | solution.py:87
  253.3 9.9 %collective-permute-start.26 = (bf16[1,448,128]{2,1,0:T(8,128)(2,1)S(1)}, bf16[1,448,128]{2,1,0:T(8,128)(2,1)S(1)}, u32[]{:S(2)}, u32[]{:S(2)}) collective-permute-start(bf16[1,448,128]{2,1,0:T(8,128)(2,1)S(1)} %get-tuple-element.67), channel_id=1, source_target_pairs={{0,4},{1,5},{2,6},{3,7},{4,0},{5,1},{6,2},{7,3},{8,12},{9,13},{10,... | collective-permute-start | bytes 344072 | tf_op jit(solution)/shard_map/ppermute | solution.py:87
  253.3 9.9 %collective-permute-start.27 = (bf16[1,448,128]{2,1,0:T(8,128)(2,1)S(1)}, bf16[1,448,128]{2,1,0:T(8,128)(2,1)S(1)}, u32[]{:S(2)}, u32[]{:S(2)}) collective-permute-start(bf16[1,448,128]{2,1,0:T(8,128)(2,1)S(1)} %get-tuple-element.66), channel_id=1, source_target_pairs={{0,6},{1,7},{2,4},{3,5},{4,2},{5,3},{6,0},{7,1},{8,14},{9,15},{10,... | collective-permute-start | bytes 344072 | tf_op jit(solution)/shard_map/ppermute | solution.py:87
  (25 other events, 398.2 us)

commit v2 on v1

--- a/solution.py
+++ b/solution.py
@@ -6,6 +6,7 @@
 from jax.experimental import pallas as pl
 from jax.experimental.pallas import tpu as pltpu
 from jax.sharding import PartitionSpec as P
+
 
 D = 384
 HEADS = 6
@@ -67,6 +68,7 @@
         self.rows = -(-self.rows // 16) * 16
         self.start = [e * share // LANES for e in range(self.count)]
         self.tokens = tokens
+        self.part = tokens
         self.reach = (IMG - 2 + tokens) // tokens
         self.window = 2 * self.reach + 1
         self.grouped = dp == 4 and fsdp == 8 and self.reach <= 6
@@ -112,24 +114,31 @@
             value = got[0]
         return value
 
-    def exchange(self, block):
+    def exchange(self, block, extra=()):
         own = block[None]
         if self.grouped:
-            column = jnp.concatenate([own] + [self.send(own, m) for m in (2, 4, 6)], axis=0)
-            beside = self.send(column, 1)
+            hops = []
+            for m in (1, 2, 3, 4, 6):
+                hops.append(self.send(own, m))
+            one, two, three, four, six = hops
+            pair = jnp.concatenate([four, six], axis=0)
+            quad = jnp.concatenate([two, three, four, six], axis=0)
+            pair, quad, extra = lax.optimization_barrier((pair, quad, extra))
             across = [(8 + j, 16 + j) for j in range(8)] + [(16 + j, 8 + j) for j in range(8)]
-            far_column = lax.ppermute(column, BOTH, across)
-            far_beside = lax.ppermute(beside, BOTH, across)
-            row = jnp.concatenate([column, beside], axis=0)
-            return [row, self.send(row, 8), far_column, far_beside]
+            skew = [(a, b ^ 1) for a, b in across]
+            far = lax.ppermute(quad, BOTH, across)
+            far_beside = lax.ppermute(pair, BOTH, skew)
+            beside = self.send(pair, 1)
+            row = jnp.concatenate([own, one, quad, beside], axis=0)
+            return [row, self.send(row, 8), far, far_beside], extra
         slots = []
         for slot in range(self.window):
             by = self.reach - slot
             pairs = [(i, i + by) for i in range(self.count) if 0 <= i + by < self.count]
             slots.append(own if by == 0 else lax.ppermute(own, BOTH, pairs))
-        return [jnp.concatenate(slots, axis=0)]
-
-    def table(self, device, spans):
+        return [jnp.concatenate(slots, axis=0)], extra
+
+    def table(self, device, spans, key_ids):
         e = jnp.arange(self.count, dtype=jnp.int32)
         rel = e ^ device
         where = jnp.zeros_like(e)
@@ -138,18 +147,24 @@
         slot = jnp.arange(self.window, dtype=jnp.int32)
         if self.grouped:
             other = device - self.reach + slot
-            pos = ((other ^ device) & 7) >> 1
-            pos = pos + 4 * ((other ^ device) & 1)
+            mask = (other ^ device) & 7
+            pos = jnp.where(mask == 6, 5, jnp.where(mask == 5, 6, mask))
             cross = (other >> 3) ^ (device >> 3)
-            source = jnp.where(cross == 0, 0, jnp.where(cross == 1, 1, 2 + (pos >> 2)))
-            index = jnp.where(source >= 2, pos & 3, pos)
+            late = pos >= 6
+            source = jnp.where(cross == 0, 0, jnp.where(cross == 1, 1, jnp.where(late, 3, 2)))
+            index = jnp.where(source >= 2, jnp.where(late, pos - 6, pos - 2), pos)
         else:
             source = jnp.zeros_like(slot)
             index = slot
         bounds = lax.dynamic_index_in_dim(spans, device, 0, keepdims=False)
         ends = jnp.clip(bounds - device + self.reach, 0, self.window - 1)
-        shift = ((device * self.share) % LANES).reshape(1)
-        return jnp.concatenate([where, source, index, ends, shift]).astype(jnp.int32)
+        own = key_ids[self.reach]
+        low, high = own[:: self.part], own[self.part - 1 :: self.part]
+        seen = (key_ids[:, -1][None] >= low[:, None]) & (key_ids[:, 0][None] <= high[:, None])
+        seen = seen & (slot >= ends[0])[None] & (slot <= ends[1])[None]
+        begin = jnp.min(jnp.where(seen, slot[None], self.window), axis=1)
+        finish = jnp.max(jnp.where(seen, slot[None], -1), axis=1)
+        return jnp.concatenate([where, source, index, ends, begin, finish]).astype(jnp.int32)
 
     def source_at(self, slot):
         return self.count + slot
@@ -160,8 +175,9 @@
     def low_at(self):
         return self.count + 2 * self.window
 
-    def shift_at(self):
-        return self.count + 2 * self.window + 2
+    def range_at(self, quarter):
+        at = self.count + 2 * self.window + 2 + quarter
+        return at, at + self.tokens // self.part
 
 
 def fetch_window(plan, table, sources, dest, sems, lo, hi, wait):
@@ -206,13 +222,29 @@
         ref[row + j : row + j + 1, :] = value[:, LANES * j : LANES * (j + 1)]
 
 
+def stacked(x):
+    left = lax.broadcasted_iota(jnp.int32, x.shape, 1) < HEAD_DIM
+    return jnp.concatenate([jnp.where(left, x, 0), jnp.where(left, 0, x)], axis=0)
+
+
+def unstacked(x):
+    half = x.shape[0] // 2
+    left = lax.broadcasted_iota(jnp.int32, (half, LANES), 1) < HEAD_DIM
+    return jnp.where(left, x[:half], x[half:])
+
+
+def tiled(ids, width):
+    ids = jnp.concatenate([ids] * (width // LANES), axis=1)
+    return jnp.concatenate([ids, ids], axis=0)
+
+
 def column_sum(x):
     return jnp.sum(x, axis=0, keepdims=True)
 
 
 def shift_kernel(plan):
     def kernel(table, x_ref, out_ref, pad):
-        s = table[plan.shift_at()]
+        s = table[0]
         x = x_ref[...]
         y = pltpu.roll(x, s, 1)
         pad[0:8, :] = jnp.zeros((8, LANES), WIDE)
@@ -226,7 +258,7 @@
 def unshift_kernel(plan):
     def kernel(table, *refs):
         parts, (out_ref, sq_ref, pad) = refs[:-3], refs[-3:]
-        s = table[plan.shift_at()]
+        s = table[0]
         got = [p[...].astype(WIDE) for p in parts]
         while len(got) > 1:
             got = [got[k] + got[k + 1] for k in range(0, len(got), 2)]
@@ -246,9 +278,10 @@
 
 def forward_kernel(plan, sources):
     T = plan.tokens
-    W = plan.window
     own = plan.reach
     half = plan.count // 2
+    part = plan.part
+    pairs = HEADS // 2
 
     def kernel(table, *refs):
         near, core = refs[:2]
@@ -275,7 +308,7 @@
             kown_ref,
             vown_ref,
         ) = refs[5 + sources : 24 + sources]
-        wbuf, flat, xwin, wo, wup, wdn, scores, wsem, xsem = refs[24 + sources :]
+        wbuf, flat, xwin, wo, wup, wdn, scores, tops, sums, accs, mix, wsem, xsem = refs[24 + sources :]
         lo = table[plan.low_at()]
         hi = table[plan.low_at() + 1]
 
@@ -352,51 +385,58 @@
         unfold(wup, "up", D, FF)
         unfold(wdn, "down", FF, D)
 
-        lane = lax.broadcasted_iota(jnp.int32, (T, LANES), 1)
-        left = lane < HEAD_DIM
-        ids = jnp.concatenate([col_ref[...]] * (T // LANES), axis=1)
-        mixed = []
-        stats = jnp.zeros((T, LANES), WIDE)
-        for p in range(HEADS // 2):
-            cols = slice(LANES * p, LANES * (p + 1))
-            q = q_ref[own, :, cols]
-            qs = [jnp.where(left, q, 0), jnp.where(left, 0, q)]
-
-            def first(w, tops, qs=qs, cols=cols):
-                key = k_ref[w, :, cols]
+        lane = lax.broadcasted_iota(jnp.int32, (part, LANES), 1)
+        for c in range(T // part):
+            rows = slice(part * c, part * (c + 1))
+            at, to = plan.range_at(c)
+            begin, finish = table[at], table[to] + 1
+            qs = [stacked(q_ref[own, rows, LANES * p : LANES * (p + 1)]) for p in range(pairs)]
+            ids = tiled(col_ref[rows, :], T)
+            for p in range(pairs):
+                tops[p] = jnp.full((2 * part, LANES), MASKED, WIDE)
+                sums[p] = jnp.zeros((2 * part, LANES), WIDE)
+                accs[p] = jnp.zeros((2 * part, LANES), WIDE)
+
+            def first(w, carry, qs=qs, ids=ids):
                 seen = ids == row_ref[pl.ds(w, 1), :]
-                new = []
-                for i in range(2):
-                    s = jnp.where(seen, dot(qs[i], key, NT), MASKED)
-                    scores[i, w] = s
-                    top = tops[i]
-                    for c in range(0, T, LANES):
-                        top = jnp.maximum(top, s[:, c : c + LANES])
-                    new.append(top)
-                return tuple(new)
-
-            start = jnp.full((T, LANES), MASKED, WIDE)
-            tops = lax.fori_loop(lo, hi + 1, first, (start, start))
-            tops = [jnp.max(t, axis=1, keepdims=True) for t in tops]
-
-            def second(w, carry, tops=tops, cols=cols):
-                value = v_ref[w, :, cols]
-                new = []
-                for i in range(2):
-                    total, acc = carry[2 * i], carry[2 * i + 1]
-                    e = jnp.exp(scores[i, w] - tops[i])
-                    for c in range(0, T, LANES):
-                        total = total + e[:, c : c + LANES]
-                    new += [total, acc + dot(e.astype(LOW), value, NN)]
-                return tuple(new)
-
-            zero = jnp.zeros((T, LANES), WIDE)
-            got = lax.fori_loop(lo, hi + 1, second, (zero,) * 4)
-            sums = [jnp.sum(got[2 * i], axis=1, keepdims=True) for i in range(2)]
-            mixed.append(jnp.where(left, got[1] / sums[0], got[3] / sums[1]))
-            for i in range(2):
-                stats = jnp.where(lane == 2 * p + i, tops[i] + jnp.log(sums[i]), stats)
-        att = jnp.concatenate(mixed, axis=1)
+                for p in range(pairs):
+                    s = dot(qs[p], k_ref[w, :, LANES * p : LANES * (p + 1)], NT)
+                    s = jnp.where(seen, s, MASKED)
+                    scores[p, w] = s
+                    top = tops[p]
+                    for j in range(0, T, LANES):
+                        top = jnp.maximum(top, s[:, j : j + LANES])
+                    tops[p] = top
+                return carry
+
+            lax.fori_loop(begin, finish, first, 0)
+            for p in range(pairs):
+                top = jnp.max(tops[p], axis=1, keepdims=True)
+                tops[p] = jnp.broadcast_to(top, (2 * part, LANES))
+
+            def second(w, carry):
+                for p in range(pairs):
+                    top = jnp.concatenate([tops[p]] * (T // LANES), axis=1)
+                    e = jnp.exp(scores[p, w] - top)
+                    total = sums[p]
+                    for j in range(0, T, LANES):
+                        total = total + e[:, j : j + LANES]
+                    sums[p] = total
+                    value = v_ref[w, :, LANES * p : LANES * (p + 1)]
+                    accs[p] = accs[p] + dot(e.astype(LOW), value, NN)
+                return carry
+
+            lax.fori_loop(begin, finish, second, 0)
+            stats = jnp.zeros((part, LANES), WIDE)
+            for p in range(pairs):
+                total = jnp.sum(sums[p], axis=1, keepdims=True)
+                mixed = accs[p] / total
+                mix[rows, LANES * p : LANES * (p + 1)] = unstacked(mixed)
+                log = tops[p] + jnp.log(total)
+                stats = jnp.where(lane == 2 * p, log[:part], stats)
+                stats = jnp.where(lane == 2 * p + 1, log[part:], stats)
+            stat_ref[rows, :] = stats
+        att = mix[...]
         att_low = att.astype(LOW)
         att_ref[...] = att_low
         x = xwin[own].astype(WIDE)
@@ -429,10 +469,13 @@
         gatt = dot(gbo, wo[...], NT).astype(LOW)
         msg_ref[0:T, :] = gatt
         inner = gatt.astype(WIDE) * att
+        stats = stat_ref[...]
+        lane = lax.broadcasted_iota(jnp.int32, (T, LANES), 1)
+        left = lane < HEAD_DIM
         for p in range(HEADS // 2):
-            part = inner[:, LANES * p : LANES * (p + 1)]
-            one = jnp.sum(jnp.where(left, part, 0.0), axis=1, keepdims=True)
-            two = jnp.sum(jnp.where(left, 0.0, part), axis=1, keepdims=True)
+            piece = inner[:, LANES * p : LANES * (p + 1)]
+            one = jnp.sum(jnp.where(left, piece, 0.0), axis=1, keepdims=True)
+            two = jnp.sum(jnp.where(left, 0.0, piece), axis=1, keepdims=True)
             stats = jnp.where(lane == HEADS + 2 * p, one, stats)
             stats = jnp.where(lane == HEADS + 2 * p + 1, two, stats)
         stat_ref[...] = stats
@@ -473,6 +516,8 @@
     T = plan.tokens
     own = plan.reach
     base = AT["out"]
+    part = plan.part
+    pairs = HEADS // 2
 
     def kernel(
         table,
@@ -494,9 +539,10 @@
         blocks_ref,
         tail_ref,
         flat,
+        logs,
+        dots,
+        accs,
     ):
-        lo = table[plan.low_at()]
-        hi = table[plan.low_at() + 1]
         fold(flat, AT["down"] - base, act_ref, gbt_ref, D)
         fold(flat, AT["up"] - base, n2_ref, pre_ref, FF)
         fold(flat, AT["out"] - base, att_ref, gbo_ref, D)
@@ -514,41 +560,46 @@
             r0 = plan.start[e] - base
             blocks_ref[table[e]] = flat[r0 : r0 + plan.rows, :].astype(LOW)
 
-        lane = lax.broadcasted_iota(jnp.int32, (T, LANES), 1)
-        left = lane < HEAD_DIM
-        ids = jnp.concatenate([col_ref[...]] * (T // LANES), axis=1)
-        for p in range(HEADS // 2):
-            cols = slice(LANES * p, LANES * (p + 1))
-            q = q_ref[own, :, cols]
-            g = msg_ref[0:T, cols]
-            qs = [jnp.where(left, q, 0), jnp.where(left, 0, q)]
-            gs = [jnp.where(left, g, 0), jnp.where(left, 0, g)]
-            logs = [stat_ref[:, 2 * p + i : 2 * p + i + 1] for i in range(2)]
-            inner = [stat_ref[:, HEADS + 2 * p + i : HEADS + 2 * p + i + 1] for i in range(2)]
-
-            def step(w, carry, qs=qs, gs=gs, logs=logs, inner=inner, cols=cols):
-                key = k_ref[w, :, cols]
-                value = v_ref[w, :, cols]
+        for c in range(T // part):
+            rows = slice(part * c, part * (c + 1))
+            at, to = plan.range_at(c)
+            begin, finish = table[at], table[to] + 1
+            qs = [stacked(q_ref[own, rows, LANES * p : LANES * (p + 1)]) for p in range(pairs)]
+            gs = [stacked(msg_ref[rows, LANES * p : LANES * (p + 1)]) for p in range(pairs)]
+            ids = tiled(col_ref[rows, :], T)
+            for p in range(pairs):
+                for k in range(2):
+                    h = 2 * p + k
+                    half = slice(part * k, part * (k + 1))
+                    logs[p, half, :] = jnp.broadcast_to(stat_ref[rows, h : h + 1], (part, LANES))
+                    h = h + HEADS
+                    dots[p, half, :] = jnp.broadcast_to(stat_ref[rows, h : h + 1], (part, LANES))
+                accs[p] = jnp.zeros((2 * part, LANES), WIDE)
+
+            def step(w, carry, qs=qs, gs=gs, ids=ids):
                 seen = ids == row_ref[pl.ds(w, 1), :]
-                new = []
-                for i in range(2):
-                    s = jnp.where(seen, dot(qs[i], key, NT), MASKED)
-                    prob = jnp.exp(s - logs[i])
-                    gs_i = prob * (dot(gs[i], value, NT) - inner[i])
-                    new.append(carry[i] + dot(gs_i.astype(LOW), key, NN))
-                return tuple(new)
-
-            zero = jnp.zeros((T, LANES), WIDE)
-            got = lax.fori_loop(lo, hi + 1, step, (zero, zero))
-            gq_ref[:, cols] = (jnp.where(left, got[0], got[1]) * SCALE).astype(LOW)
+                for p in range(pairs):
+                    cols = slice(LANES * p, LANES * (p + 1))
+                    key = k_ref[w, :, cols]
+                    s = jnp.where(seen, dot(qs[p], key, NT), MASKED)
+                    prob = jnp.exp(s - jnp.concatenate([logs[p]] * (T // LANES), axis=1))
+                    inner = jnp.concatenate([dots[p]] * (T // LANES), axis=1)
+                    grad = prob * (dot(gs[p], v_ref[w, :, cols], NT) - inner)
+                    accs[p] = accs[p] + dot(grad.astype(LOW), key, NN)
+                return carry
+
+            lax.fori_loop(begin, finish, step, 0)
+            for p in range(pairs):
+                gq_ref[rows, LANES * p : LANES * (p + 1)] = (unstacked(accs[p]) * SCALE).astype(LOW)
 
     return kernel
 
 
 def last_kernel(plan, sources):
     T = plan.tokens
-    own = plan.reach
     early = plan.first_late
+    part = plan.part
+    pairs = HEADS // 2
 
     def kernel(table, *refs):
         wins = refs[:sources]
@@ -569,47 +620,60 @@
             grad_ref,
             blocks_ref,
         ) = refs[sources : sources + 15]
-        mwin, flat, gt, stage, msem, osem = refs[sources + 15 :]
+        mwin, flat, gt, stage, stats, acck, accv, msem, osem = refs[sources + 15 :]
         lo = table[plan.low_at()]
         hi = table[plan.low_at() + 1]
         fetch_window(plan, table, wins, mwin, msem, lo, hi, False)
         fetch_window(plan, table, wins, mwin, msem, lo, hi, True)
-        lane = lax.broadcasted_iota(jnp.int32, (T, LANES), 1)
-        left = lane < HEAD_DIM
-        ids = jnp.concatenate([col_ref[...]] * (T // LANES), axis=1)
-        for p in range(HEADS // 2):
-            cols = slice(LANES * p, LANES * (p + 1))
-            k = k_ref[:, cols]
-            v = v_ref[:, cols]
-            ks = [jnp.where(left, k, 0), jnp.where(left, 0, k)]
-            vs = [jnp.where(left, v, 0), jnp.where(left, 0, v)]
-
-            def step(w, carry, ks=ks, vs=vs, cols=cols, p=p):
-                q = q_ref[w, :, cols]
-                g = mwin[w, 0:T, cols]
-                one = mwin[w, T : T + 16, :].astype(WIDE)
-                two = mwin[w, T + 16 : T + 32, :].astype(WIDE)
-                stats = one[:, :T] + jnp.concatenate(
-                    [one[:, T:], two[:, : 2 * T - D]], axis=1
+
+        def unpack(w, carry):
+            one = mwin[w, T : T + 16, :].astype(WIDE)
+            two = mwin[w, T + 16 : T + 32, :].astype(WIDE)
+            middle = jnp.concatenate([one[:, T:], two[:, : 2 * T - D]], axis=1)
+            stats[w] = (one[:, :T] + middle) + two[:, 2 * T - D :]
+            return carry
+
+        lax.fori_loop(lo, hi + 1, unpack, 0)
+        for c in range(T // part):
+            rows = slice(part * c, part * (c + 1))
+            at, to = plan.range_at(c)
+            begin, finish = table[at], table[to] + 1
+            ks = [stacked(k_ref[rows, LANES * p : LANES * (p + 1)]) for p in range(pairs)]
+            vs = [stacked(v_ref[rows, LANES * p : LANES * (p + 1)]) for p in range(pairs)]
+            ids = tiled(col_ref[rows, :], T)
+            for p in range(pairs):
+                acck[p] = jnp.zeros((2 * part, LANES), WIDE)
+                accv[p] = jnp.zeros((2 * part, LANES), WIDE)
+
+            def step(w, carry, ks=ks, vs=vs, ids=ids):
+                seen = ids == row_ref[pl.ds(w, 1), :]
+
+                def pair_rows(h):
+                    return jnp.concatenate(
+                        [
+                            jnp.broadcast_to(stats[w, h + k : h + k + 1, :], (part, T))
+                            for k in range(2)
+                        ],
+                        axis=0,
+                    )
+
+                for p in range(pairs):
+                    cols = slice(LANES * p, LANES * (p + 1))
+                    q = q_ref[w, :, cols]
+                    g = mwin[w, 0:T, cols]
+                    s = jnp.where(seen, dot(ks[p], q, NT), MASKED)
+                    prob = jnp.exp(s - pair_rows(2 * p))
+                    grad = prob * (dot(vs[p], g, NT) - pair_rows(HEADS + 2 * p))
+                    acck[p] = acck[p] + dot(grad.astype(LOW), q, NN)
+                    accv[p] = accv[p] + dot(prob.astype(LOW), g, NN)
+                return carry
+
+            lax.fori_loop(begin, finish, step, 0)
+            for p in range(pairs):
+                gt[rows, D + LANES * p : D + LANES * (p + 1)] = unstacked(acck[p]).astype(LOW)
+                gt[rows, 2 * D + LANES * p : 2 * D + LANES * (p + 1)] = unstacked(accv[p]).astype(
+                    LOW
                 )
-                stats = stats + two[:, 2 * T - D :]
-                seen = ids == row_ref[pl.ds(w, 1), :]
-                new = []
-                for i in range(2):
-                    h = 2 * p + i
-                    s = jnp.where(seen, dot(ks[i], q, NT), MASKED)
-                    prob = jnp.exp(s - stats[h : h + 1, :])
-                    gs_i = prob * (dot(vs[i], g, NT) - stats[HEADS + h : HEADS + h + 1, :])
-                    new.append(carry[2 * i] + dot(gs_i.astype(LOW), q, NN))
-                    new.append(carry[2 * i + 1] + dot(prob.astype(LOW), g, NN))
-                return tuple(new)
-
-            zero = jnp.zeros((T, LANES), WIDE)
-            got = lax.fori_loop(lo, hi + 1, step, (zero,) * 4)
-            gt[:, D + LANES * p : D + LANES * (p + 1)] = jnp.where(left, got[0], got[2]).astype(LOW)
-            gt[:, 2 * D + LANES * p : 2 * D + LANES * (p + 1)] = jnp.where(
-                left, got[1], got[3]
-            ).astype(LOW)
         gt[:, :D] = gq_ref[...]
         fold(flat, AT["triple"], normed_ref, gt, 3 * D)
         put_vector(flat, AT["tbias"], column_sum(gt[:, :D].astype(WIDE)))
@@ -648,9 +712,10 @@
 
     def per_device(inputs, cotangent, master, first_moment, second_moment, image_ids, spans):
         device = lax.axis_index(BOTH).astype(jnp.int32)
-        table = plan.table(device, spans)
+        shift = ((device * plan.share) % LANES).reshape(1).astype(jnp.int32)
         padded = jnp.pad(image_ids, (plan.reach * T, plan.reach * T), constant_values=-1)
         key_ids = lax.dynamic_slice_in_dim(padded, device * T, W * T, 0).reshape(W, T)
+        table = plan.table(device, spans, key_ids)
         own_ids = key_ids[plan.reach]
         columns = jnp.broadcast_to(own_ids[:, None], (T, LANES))
 
@@ -661,9 +726,9 @@
             out_shape=shape((R, LANES), LOW),
             scratch_shapes=[pltpu.VMEM((R + 8, LANES), WIDE)],
             name="shift",
-        )(table, jnp.pad(master, (0, R * LANES - plan.share)).reshape(R, LANES))
+        )(shift, jnp.pad(master, (0, R * LANES - plan.share)).reshape(R, LANES))
         near, core = plan.spread(shifted)
-        wins = plan.exchange(inputs)
+        wins, (table, columns, key_ids) = plan.exchange(inputs, (table, columns, key_ids))
         sources = len(wins)
 
         outs = pl.pallas_call(
@@ -698,7 +763,11 @@
                 pltpu.VMEM((D, D), LOW),
                 pltpu.VMEM((D, FF), LOW),
                 pltpu.VMEM((FF, D), LOW),
-                pltpu.VMEM((2, W, T, T), WIDE),
+                pltpu.VMEM((HEADS // 2, W, 2 * plan.part, T), WIDE),
+                pltpu.VMEM((HEADS // 2, 2 * plan.part, LANES), WIDE),
+                pltpu.VMEM((HEADS // 2, 2 * plan.part, LANES), WIDE),
+                pltpu.VMEM((HEADS // 2, 2 * plan.part, LANES), WIDE),
+                pltpu.VMEM((T, D), WIDE),
                 pltpu.SemaphoreType.DMA((N,)),
                 pltpu.SemaphoreType.DMA((W,)),
             ],
@@ -726,9 +795,9 @@
             k_own,
             v_own,
         ) = outs
-        messages = plan.exchange(message)
-
-        gq, blocks, tail = pl.pallas_call(
+        messages, _ = plan.exchange(message)
+
+        middle_call = pl.pallas_call(
             middle_kernel(plan),
             in_specs=[SMEM] + [VMEM] * 14,
             out_specs=[VMEM] * 3,
@@ -739,10 +808,16 @@
             ],
             scratch_shapes=[
                 pltpu.VMEM((plan.flat_rows - AT["out"] + 8, LANES), WIDE),
+                pltpu.VMEM((HEADS // 2, 2 * plan.part, LANES), WIDE),
+                pltpu.VMEM((HEADS // 2, 2 * plan.part, LANES), WIDE),
+                pltpu.VMEM((HEADS // 2, 2 * plan.part, LANES), WIDE),
             ],
             compiler_params=limit,
             name="middle",
-        )(table, q, k, v, message, stat, columns, key_ids, act, gpre, gbt, n2, att, gbo, vec)
+        )
+        gq, blocks, tail = middle_call(
+            table, q, k, v, message, stat, columns, key_ids, act, gpre, gbt, n2, att, gbo, vec
+        )
 
         late = plan.first_late
         input_grad, blocks = pl.pallas_call(
@@ -758,6 +833,9 @@
                 pltpu.VMEM((AT["out"] + R + 8, LANES), WIDE),
                 pltpu.VMEM((T, 3 * D), LOW),
                 pltpu.VMEM((late, R, LANES), LOW),
+                pltpu.VMEM((W, 16, T), WIDE),
+                pltpu.VMEM((HEADS // 2, 2 * plan.part, LANES), WIDE),
+                pltpu.VMEM((HEADS // 2, 2 * plan.part, LANES), WIDE),
                 pltpu.SemaphoreType.DMA((W,)),
                 pltpu.SemaphoreType.DMA((late,)),
             ],
@@ -790,7 +868,7 @@
             out_shape=[shape((R, LANES), WIDE), shape((8, LANES), WIDE)],
             scratch_shapes=[pltpu.VMEM((R + 8, LANES), WIDE)],
             name="unshift",
-        )(table, *parts)
+        )(shift, *parts)
         grad_shard = grad.reshape(-1)[: plan.share]
         grad_norm = jnp.sqrt(plan.total(square)[0, 0])
         ceiling = CLIP_RATIO * math.sqrt(plan.share * N)

time: 289 us -> 256 us (0.89)
  starting transfers between devices: 126 us -> 89 us
    ppermute x31 -> x35, starting transfers between devices: 119 us -> 85.5 us  [send(): return lax.ppermute(x, BOTH, [(i, i ^ mask) for i in range(self.count)])]
    ppermute x31 -> x35, waiting for transfers between devices: 95.2 us -> 95.1 us  [send(): return lax.ppermute(x, BOTH, [(i, i ^ mask) for i in range(self.count)])]
  transfers between devices with their start and end apart: 35 -> 39, of which waited for: 16 -> 22; matrix products, arithmetic and copies ran while one was open for 2% -> 5% of each run, Pallas kernels for 4% -> 5%
where the time goes in v2:
time: 256 us; the launch traced here: 255 us
  waiting for transfers between devices  95.1 us (37%)
  starting transfers between devices  89 us (35%)
  Pallas kernels  43.6 us (17%)
  local copies, waits for them, and re-layouts  14.9 us (6%)
  other arithmetic  9.38 us (4%)
  between operations  2.95 us (1%)
    ppermute x35, waiting for transfers between devices, send(): return lax.ppermute(x, BOTH, [(i, i ^ mask) for i in range(self.count)])  95.1 us
    ppermute x35, starting transfers between devices, send(): return lax.ppermute(x, BOTH, [(i, i ^ mask) for i in range(self.count)])  85.5 us
    pallas_call x1, Pallas kernels, per_device(): pl.pallas_call(forward_kernel(plan, sources), in_specs=[SMEM, ANY, ANY] +...  17.1 us
    pallas_call x1, Pallas kernels, per_device(): middle_call(table, q, k, v, message, stat, columns, key_ids, act, gpre, g...  11.9 us
    pallas_call x1, Pallas kernels, per_device(): pl.pallas_call(last_kernel(plan, sources), in_specs=[SMEM] + [ANY] * sour...  10.9 us
  transfers between devices with their start and end apart: 39, of which 22 were waited for; matrix products, arithmetic and copies ran while one was open for 5% of the time, Pallas kernels for 5%

profile of v2, /device:TPU:0, one launch (start us, length us, event | category | flops | bytes accessed | tf_op | source)
XLA Modules:
  0.0 254.9 jit_solution(6280792317190164897)
XLA Ops:
  4.1 3.1 %collective-permute-start.4 = (bf16[1,448,128]{2,1,0:T(8,128)(2,1)}, bf16[1,448,128]{2,1,0:T(8,128)(2,1)S(1)}, u32[]{:S(2)}, u32[]{:S(2)}) collective-permute-start(bf16[1,448,128]{2,1,0:T(8,128)(2,1)} %bitcast.29), channel_id=1, source_target_pairs={{0,2},{1,3},{2,0},{3,1},{4,6},{5,7},{6,4},{7,5},{8,10},{9,11},{10,... | collective-permute-start | bytes 344072 | tf_op jit(solution)/shard_map/ppermute | solution.py:89
  7.1 2.6 %collective-permute-start.5 = (bf16[1,448,128]{2,1,0:T(8,128)(2,1)}, bf16[1,448,128]{2,1,0:T(8,128)(2,1)S(1)}, u32[]{:S(2)}, u32[]{:S(2)}) collective-permute-start(bf16[1,448,128]{2,1,0:T(8,128)(2,1)} %bitcast.30), channel_id=1, source_target_pairs={{0,4},{1,5},{2,6},{3,7},{4,0},{5,1},{6,2},{7,3},{8,12},{9,13},{10,... | collective-permute-start | bytes 344072 | tf_op jit(solution)/shard_map/ppermute | solution.py:89
  24.7 2.8 %collective-permute-done.5 = bf16[1,448,128]{2,1,0:T(8,128)(2,1)S(1)} collective-permute-done((bf16[1,448,128]{2,1,0:T(8,128)(2,1)}, bf16[1,448,128]{2,1,0:T(8,128)(2,1)S(1)}, u32[]{:S(2)}, u32[]{:S(2)}) %collective-permute-start.5) | collective-permute-done | bytes 114720 | tf_op jit(solution)/shard_map/ppermute | solution.py:89
  30.7 3.4 %collective-permute-done = bf16[1,256,384]{2,1,0:T(8,128)(2,1)S(1)} collective-permute-done((bf16[1,256,384]{2,1,0:T(8,128)(2,1)}, bf16[1,256,384]{2,1,0:T(8,128)(2,1)S(1)}, u32[]{:S(2)}, u32[]{:S(2)}) %collective-permute-start) | collective-permute-done | bytes 196640 | tf_op jit(solution)/shard_map/ppermute | solution.py:89
  38.8 4.2 %collective-permute-done.3 = bf16[1,256,384]{2,1,0:T(8,128)(2,1)S(1)} collective-permute-done((bf16[1,256,384]{2,1,0:T(8,128)(2,1)}, bf16[1,256,384]{2,1,0:T(8,128)(2,1)S(1)}, u32[]{:S(2)}, u32[]{:S(2)}) %collective-permute-start.3) | collective-permute-done | bytes 196640 | tf_op jit(solution)/shard_map/ppermute | solution.py:89
  44.5 15.5 %collective-permute-done.8 = bf16[4,448,128]{2,1,0:T(8,128)(2,1)S(1)} collective-permute-done((bf16[4,448,128]{2,1,0:T(8,128)(2,1)S(1)}, bf16[4,448,128]{2,1,0:T(8,128)(2,1)S(1)}, u32[]{:S(2)}, u32[]{:S(2)}) %collective-permute-start.8) | collective-permute-done | bytes 458784 | tf_op jit(solution)/shard_map/ppermute | solution.py:89
  60.2 4.0 %collective-permute-done.11 = bf16[1,256,384]{2,1,0:T(8,128)(2,1)S(1)} collective-permute-done((bf16[1,256,384]{2,1,0:T(8,128)(2,1)S(1)}, bf16[1,256,384]{2,1,0:T(8,128)(2,1)S(1)}, u32[]{:S(2)}, u32[]{:S(2)}) %collective-permute-start.11) | collective-permute-done | bytes 196640 | tf_op jit(solution)/shard_map/ppermute | solution.py:89
  64.1 6.7 %collective-permute-done.12 = bf16[2,256,384]{2,1,0:T(8,128)(2,1)S(1)} collective-permute-done((bf16[2,256,384]{2,1,0:T(8,128)(2,1)S(1)}, bf16[2,256,384]{2,1,0:T(8,128)(2,1)S(1)}, u32[]{:S(2)}, u32[]{:S(2)}) %collective-permute-start.12) | collective-permute-done | bytes 393248 | tf_op jit(solution)/shard_map/ppermute | solution.py:89
  75.8 17.1 %forward.1 = (bf16[256,384]{1,0:T(8,128)(2,1)}, bf16[288,384]{1,0:T(8,128)(2,1)}, bf16[13,256,384]{2,1,0:T(8,128)(2,1)}, bf16[13,256,384]{2,1,0:T(8,128)(2,1)}, ...) custom-call(s32[62]{0:T(128)} %concatenate.30.table, ...), custom_call_target="tpu_custom_call" | custom-call | tf_op jit(solution)/shard_map/forward/pallas_call | solution.py:734
  94.0 4.7 %collective-permute-start.18 = (bf16[1,288,384]{2,1,0:T(8,128)(2,1)}, bf16[1,288,384]{2,1,0:T(8,128)(2,1)S(1)}, u32[]{:S(2)}, u32[]{:S(2)}) collective-permute-start(bf16[1,288,384]{2,1,0:T(8,128)(2,1)} %bitcast.34), channel_id=1, source_target_pairs={{0,6},{1,7},{2,4},{3,5},{4,2},{5,3},{6,0},{7,1},{8,14},{9,15},{10,... | collective-permute-start | bytes 663560 | tf_op jit(solution)/shard_map/ppermute | solution.py:89
  99.2 3.3 %collective-permute-start.20 = (bf16[1,288,384]{2,1,0:T(8,128)(2,1)}, bf16[1,288,384]{2,1,0:T(8,128)(2,1)S(1)}, u32[]{:S(2)}, u32[]{:S(2)}) collective-permute-start(bf16[1,288,384]{2,1,0:T(8,128)(2,1)} %bitcast.36), channel_id=1, source_target_pairs={{0,3},{1,2},{2,1},{3,0},{4,7},{5,6},{6,5},{7,4},{8,11},{9,10},{10,... | collective-permute-start | bytes 663560 | tf_op jit(solution)/shard_map/ppermute | solution.py:89
  102.4 2.8 %collective-permute-done.18 = bf16[1,288,384]{2,1,0:T(8,128)(2,1)S(1)} collective-permute-done((bf16[1,288,384]{2,1,0:T(8,128)(2,1)}, bf16[1,288,384]{2,1,0:T(8,128)(2,1)S(1)}, u32[]{:S(2)}, u32[]{:S(2)}) %collective-permute-start.18) | collective-permute-done | bytes 221216 | tf_op jit(solution)/shard_map/ppermute | solution.py:89
  107.2 4.1 %collective-permute-done.20 = bf16[1,288,384]{2,1,0:T(8,128)(2,1)S(1)} collective-permute-done((bf16[1,288,384]{2,1,0:T(8,128)(2,1)}, bf16[1,288,384]{2,1,0:T(8,128)(2,1)S(1)}, u32[]{:S(2)}, u32[]{:S(2)}) %collective-permute-start.20) | collective-permute-done | bytes 221216 | tf_op jit(solution)/shard_map/ppermute | solution.py:89
  113.5 8.6 %collective-permute-done.16 = bf16[1,288,384]{2,1,0:T(8,128)(2,1)S(1)} collective-permute-done((bf16[1,288,384]{2,1,0:T(8,128)(2,1)S(1)}, bf16[1,288,384]{2,1,0:T(8,128)(2,1)S(1)}, u32[]{:S(2)}, u32[]{:S(2)}) %collective-permute-start.16) | collective-permute-done | bytes 221216 | tf_op jit(solution)/shard_map/ppermute | solution.py:89
  122.4 21.1 %collective-permute-start.22 = (bf16[8,288,384]{2,1,0:T(8,128)(2,1)S(1)}, bf16[8,288,384]{2,1,0:T(8,128)(2,1)}, u32[]{:S(2)}, u32[]{:S(2)}) collective-permute-start(bf16[8,288,384]{2,1,0:T(8,128)(2,1)S(1)} %pad_maximum_fusion.refs_0_), channel_id=1, source_target_pairs={{0,8},{1,9},{2,10},{3,11},{4,12},{5,13},{6,14},{7,15},{8,0},{9,1},... | collective-permute-start | bytes 5308424 | tf_op jit(solution)/shard_map/ppermute | solution.py:89
  145.7 11.9 %middle.1 = (bf16[256,384]{1,0:T(8,128)(2,1)}, bf16[32,448,128]{2,1,0:T(8,128)(2,1)}, f32[448,128]{1,0:T(8,128)}) custom-call(s32[62]{0:T(128)} %concatenate.30.table, bf16[13,256,384]{2,1,0:T(8,128)(2,1)} %get-tuple-element.49.q_ref.refs_4_, bf16[13,256,384]{2,1,0:T(8,128)(2,1)} %get-tuple-element.52.k_ref, bf16[13,256,384]{2,1,0:T(8,128)(2,1)} %get-tuple-element.53.v_ref, ...), custom_call_target="tpu_custom_call" | custom-call | tf_op jit(solution)/shard_map/middle/pallas_call | solution.py:818
  158.6 10.9 %last.1 = (f32[256,384]{1,0:T(8,128)}, bf16[32,448,128]{2,1,0:T(8,128)(2,1)}) custom-call(s32[62]{0:T(128)} %concatenate.30.table, bf16[8,288,384]{2,1,0:T(8,128)(2,1)} %copy-done.1, bf16[8,288,384]{2,1,0:T(8,128)(2,1)} %collective-permute-done.22.refs_1_, bf16[4,288,384]{2,1,0:T(8,128)(2,1)} %copy-done.7, ...), custom_call_target="tpu_custom_call", output_to_operand_aliasing={{1}: (17, {})} | custom-call | tf_op jit(solution)/shard_map/last/pallas_call | solution.py:823
  171.3 19.6 %collective-permute-start.25 = (bf16[16,448,128]{2,1,0:T(8,128)(2,1)S(1)}, bf16[16,448,128]{2,1,0:T(8,128)(2,1)S(1)}, u32[]{:S(2)}, u32[]{:S(2)}) collective-permute-start(bf16[16,448,128]{2,1,0:T(8,128)(2,1)S(1)} %slice.83), channel_id=1, source_target_pairs={{0,8},{1,9},{2,10},{3,11},{4,12},{5,13},{6,14},{7,15},{8,0},{9,1},... | collective-permute-start | bytes 5505032 | tf_op jit(solution)/shard_map/ppermute | solution.py:89
  190.9 3.4 %collective-permute-done.25 = bf16[16,448,128]{2,1,0:T(8,128)(2,1)S(1)} collective-permute-done((bf16[16,448,128]{2,1,0:T(8,128)(2,1)S(1)}, bf16[16,448,128]{2,1,0:T(8,128)(2,1)S(1)}, u32[]{:S(2)}, u32[]{:S(2)}) %collective-permute-start.25) | collective-permute-done | bytes 1835040 | tf_op jit(solution)/shard_map/ppermute | solution.py:89
  195.1 3.4 %collective-permute-start.28 = (bf16[4,448,128]{2,1,0:T(8,128)(2,1)S(1)}, bf16[4,448,128]{2,1,0:T(8,128)(2,1)S(1)}, u32[]{:S(2)}, u32[]{:S(2)}) collective-permute-start(bf16[4,448,128]{2,1,0:T(8,128)(2,1)S(1)} %get-tuple-element.82), channel_id=1, source_target_pairs={{0,17},{1,16},{2,19},{3,18},{4,21},{5,20},{6,23},{7,22},{8,25},{9,... | collective-permute-start | bytes 1376264 | tf_op jit(solution)/shard_map/ppermute | solution.py:89
  198.4 9.9 %collective-permute-done.26 = bf16[4,448,128]{2,1,0:T(8,128)(2,1)S(1)} collective-permute-done((bf16[4,448,128]{2,1,0:T(8,128)(2,1)S(1)}, bf16[4,448,128]{2,1,0:T(8,128)(2,1)S(1)}, u32[]{:S(2)}, u32[]{:S(2)}) %collective-permute-start.26) | collective-permute-done | bytes 458784 | tf_op jit(solution)/shard_map/ppermute | solution.py:89
  208.3 9.3 %collective-permute-done.27 = bf16[4,448,128]{2,1,0:T(8,128)(2,1)S(1)} collective-permute-done((bf16[4,448,128]{2,1,0:T(8,128)(2,1)S(1)}, bf16[4,448,128]{2,1,0:T(8,128)(2,1)S(1)}, u32[]{:S(2)}, u32[]{:S(2)}) %collective-permute-start.27) | collective-permute-done | bytes 458784 | tf_op jit(solution)/shard_map/ppermute | solution.py:89
  224.6 6.8 %collective-permute-done.30 = bf16[1,448,128]{2,1,0:T(8,128)(2,1)S(1)} collective-permute-done((bf16[1,448,128]{2,1,0:T(8,128)(2,1)S(1)}, bf16[1,448,128]{2,1,0:T(8,128)(2,1)S(1)}, u32[]{:S(2)}, u32[]{:S(2)}) %collective-permute-start.30) | collective-permute-done | bytes 114720 | tf_op jit(solution)/shard_map/ppermute | solution.py:89
  247.2 2.2 collective-permute-done.37
  (130 shorter events, 70.6 us)
Async XLA Ops:
  4.1 20.0 %collective-permute-start.4 = (bf16[1,448,128]{2,1,0:T(8,128)(2,1)}, bf16[1,448,128]{2,1,0:T(8,128)(2,1)S(1)}, u32[]{:S(2)}, u32[]{:S(2)}) collective-permute-start(bf16[1,448,128]{2,1,0:T(8,128)(2,1)} %bitcast.29), channel_id=1, source_target_pairs={{0,2},{1,3},{2,0},{3,1},{4,6},{5,7},{6,4},{7,5},{8,10},{9,11},{10,... | collective-permute-start | bytes 344072 | tf_op jit(solution)/shard_map/ppermute | solution.py:89
  7.1 20.3 %collective-permute-start.5 = (bf16[1,448,128]{2,1,0:T(8,128)(2,1)}, bf16[1,448,128]{2,1,0:T(8,128)(2,1)S(1)}, u32[]{:S(2)}, u32[]{:S(2)}) collective-permute-start(bf16[1,448,128]{2,1,0:T(8,128)(2,1)} %bitcast.30), channel_id=1, source_target_pairs={{0,4},{1,5},{2,6},{3,7},{4,0},{5,1},{6,2},{7,3},{8,12},{9,13},{10,... | collective-permute-start | bytes 344072 | tf_op jit(solution)/shard_map/ppermute | solution.py:89
  9.7 18.4 %collective-permute-start.6 = (bf16[1,448,128]{2,1,0:T(8,128)(2,1)}, bf16[1,448,128]{2,1,0:T(8,128)(2,1)S(1)}, u32[]{:S(2)}, u32[]{:S(2)}) collective-permute-start(bf16[1,448,128]{2,1,0:T(8,128)(2,1)} %bitcast.31), channel_id=1, source_target_pairs={{0,6},{1,7},{2,4},{3,5},{4,2},{5,3},{6,0},{7,1},{8,14},{9,15},{10,... | collective-permute-start | bytes 344072 | tf_op jit(solution)/shard_map/ppermute | solution.py:89
  9.7 24.4 %collective-permute-start = (bf16[1,256,384]{2,1,0:T(8,128)(2,1)}, bf16[1,256,384]{2,1,0:T(8,128)(2,1)S(1)}, u32[]{:S(2)}, u32[]{:S(2)}) collective-permute-start(bf16[1,256,384]{2,1,0:T(8,128)(2,1)} %bitcast.39), channel_id=1, source_target_pairs={{0,4},{1,5},{2,6},{3,7},{4,0},{5,1},{6,2},{7,3},{8,12},{9,13},{10,... | collective-permute-start | bytes 589832 | tf_op jit(solution)/shard_map/ppermute | solution.py:89
  11.6 24.1 %collective-permute-start.1 = (bf16[1,256,384]{2,1,0:T(8,128)(2,1)}, bf16[1,256,384]{2,1,0:T(8,128)(2,1)S(1)}, u32[]{:S(2)}, u32[]{:S(2)}) collective-permute-start(bf16[1,256,384]{2,1,0:T(8,128)(2,1)} %bitcast.40), channel_id=1, source_target_pairs={{0,6},{1,7},{2,4},{3,5},{4,2},{5,3},{6,0},{7,1},{8,14},{9,15},{10,... | collective-permute-start | bytes 589832 | tf_op jit(solution)/shard_map/ppermute | solution.py:89
  24.1 13.1 %collective-permute-start.2 = (bf16[1,256,384]{2,1,0:T(8,128)(2,1)}, bf16[1,256,384]{2,1,0:T(8,128)(2,1)S(1)}, u32[]{:S(2)}, u32[]{:S(2)}) collective-permute-start(bf16[1,256,384]{2,1,0:T(8,128)(2,1)} %bitcast.41), channel_id=1, source_target_pairs={{0,2},{1,3},{2,0},{3,1},{4,6},{5,7},{6,4},{7,5},{8,10},{9,11},{10,... | collective-permute-start | bytes 589832 | tf_op jit(solution)/shard_map/ppermute | solution.py:89
  27.5 15.6 %collective-permute-start.3 = (bf16[1,256,384]{2,1,0:T(8,128)(2,1)}, bf16[1,256,384]{2,1,0:T(8,128)(2,1)S(1)}, u32[]{:S(2)}, u32[]{:S(2)}) collective-permute-start(bf16[1,256,384]{2,1,0:T(8,128)(2,1)} %bitcast.42), channel_id=1, source_target_pairs={{0,3},{1,2},{2,1},{3,0},{4,7},{5,6},{6,5},{7,4},{8,11},{9,10},{10,... | collective-permute-start | bytes 589832 | tf_op jit(solution)/shard_map/ppermute | solution.py:89
  29.1 15.3 %collective-permute-start.7 = (bf16[4,448,128]{2,1,0:T(8,128)(2,1)S(1)}, bf16[4,448,128]{2,1,0:T(8,128)(2,1)S(1)}, u32[]{:S(2)}, u32[]{:S(2)}) collective-permute-start(bf16[4,448,128]{2,1,0:T(8,128)(2,1)S(1)} %pad_maximum_fusion.4), channel_id=1, source_target_pairs={{0,16},{1,17},{2,18},{3,19},{4,20},{5,21},{6,22},{7,23},{8,24},{9,... | collective-permute-start | bytes 1376264 | tf_op jit(solution)/shard_map/ppermute | solution.py:89
  34.1 25.8 %collective-permute-start.8 = (bf16[4,448,128]{2,1,0:T(8,128)(2,1)S(1)}, bf16[4,448,128]{2,1,0:T(8,128)(2,1)S(1)}, u32[]{:S(2)}, u32[]{:S(2)}) collective-permute-start(bf16[4,448,128]{2,1,0:T(8,128)(2,1)S(1)} %pad_maximum_fusion.4), channel_id=1, source_target_pairs={{0,1},{1,0},{2,3},{3,2},{4,5},{5,4},{6,7},{7,6},{8,9},{9,8},{10,11... | collective-permute-start | bytes 1376264 | tf_op jit(solution)/shard_map/ppermute | solution.py:89
  35.7 24.3 %collective-permute-start.9 = (bf16[4,448,128]{2,1,0:T(8,128)(2,1)S(1)}, bf16[4,448,128]{2,1,0:T(8,128)(2,1)S(1)}, u32[]{:S(2)}, u32[]{:S(2)}) collective-permute-start(bf16[4,448,128]{2,1,0:T(8,128)(2,1)S(1)} %pad_maximum_fusion.4), channel_id=1, source_target_pairs={{0,17},{1,16},{2,19},{3,18},{4,21},{5,20},{6,23},{7,22},{8,25},{9,... | collective-permute-start | bytes 1376264 | tf_op jit(solution)/shard_map/ppermute | solution.py:89
  37.3 26.9 %collective-permute-start.11 = (bf16[1,256,384]{2,1,0:T(8,128)(2,1)S(1)}, bf16[1,256,384]{2,1,0:T(8,128)(2,1)S(1)}, u32[]{:S(2)}, u32[]{:S(2)}) collective-permute-start(bf16[1,256,384]{2,1,0:T(8,128)(2,1)S(1)} %bitcast.43), channel_id=1, source_target_pairs={{0,1},{1,0},{2,3},{3,2},{4,5},{5,4},{6,7},{7,6},{8,9},{9,8},{10,11... | collective-permute-start | bytes 589832 | tf_op jit(solution)/shard_map/ppermute | solution.py:89
  44.0 26.9 %collective-permute-start.12 = (bf16[2,256,384]{2,1,0:T(8,128)(2,1)S(1)}, bf16[2,256,384]{2,1,0:T(8,128)(2,1)S(1)}, u32[]{:S(2)}, u32[]{:S(2)}) collective-permute-start(bf16[2,256,384]{2,1,0:T(8,128)(2,1)S(1)} %pad_maximum_fusion.6), channel_id=1, source_target_pairs={{0,1},{1,0},{2,3},{3,2},{4,5},{5,4},{6,7},{7,6},{8,9},{9,8},{10,11... | collective-permute-start | bytes 1179656 | tf_op jit(solution)/shard_map/ppermute | solution.py:89
  60.1 15.7 %collective-permute-start.10 = (bf16[16,448,128]{2,1,0:T(8,128)(2,1)S(1)}, bf16[16,448,128]{2,1,0:T(8,128)(2,1)}, u32[]{:S(2)}, u32[]{:S(2)}) collective-permute-start(bf16[16,448,128]{2,1,0:T(8,128)(2,1)S(1)} %constant_dynamic-update-slice_fusion.refs_0_), channel_id=1, source_target_pairs={{0,8},{1,9},{2,10},{3,11},{4,12},{5,13},{6,14},{7,15},{8,0},{9,1},... | collective-permute-start | bytes 5505032 | tf_op jit(solution)/shard_map/ppermute | solution.py:89
  94.0 11.3 %collective-permute-start.18 = (bf16[1,288,384]{2,1,0:T(8,128)(2,1)}, bf16[1,288,384]{2,1,0:T(8,128)(2,1)S(1)}, u32[]{:S(2)}, u32[]{:S(2)}) collective-permute-start(bf16[1,288,384]{2,1,0:T(8,128)(2,1)} %bitcast.34), channel_id=1, source_target_pairs={{0,6},{1,7},{2,4},{3,5},{4,2},{5,3},{6,0},{7,1},{8,14},{9,15},{10,... | collective-permute-start | bytes 663560 | tf_op jit(solution)/shard_map/ppermute | solution.py:89
  99.2 12.1 %collective-permute-start.20 = (bf16[1,288,384]{2,1,0:T(8,128)(2,1)}, bf16[1,288,384]{2,1,0:T(8,128)(2,1)S(1)}, u32[]{:S(2)}, u32[]{:S(2)}) collective-permute-start(bf16[1,288,384]{2,1,0:T(8,128)(2,1)} %bitcast.36), channel_id=1, source_target_pairs={{0,3},{1,2},{2,1},{3,0},{4,7},{5,6},{6,5},{7,4},{8,11},{9,10},{10,... | collective-permute-start | bytes 663560 | tf_op jit(solution)/shard_map/ppermute | solution.py:89
  111.4 10.7 %collective-permute-start.21 = (bf16[2,288,384]{2,1,0:T(8,128)(2,1)S(1)}, bf16[2,288,384]{2,1,0:T(8,128)(2,1)S(1)}, u32[]{:S(2)}, u32[]{:S(2)}) collective-permute-start(bf16[2,288,384]{2,1,0:T(8,128)(2,1)S(1)} %pad_maximum_fusion.5), channel_id=1, source_target_pairs={{0,1},{1,0},{2,3},{3,2},{4,5},{5,4},{6,7},{7,6},{8,9},{9,8},{10,11... | collective-permute-start | bytes 1327112 | tf_op jit(solution)/shard_map/ppermute | solution.py:89
  122.4 35.2 %collective-permute-start.22 = (bf16[8,288,384]{2,1,0:T(8,128)(2,1)S(1)}, bf16[8,288,384]{2,1,0:T(8,128)(2,1)}, u32[]{:S(2)}, u32[]{:S(2)}) collective-permute-start(bf16[8,288,384]{2,1,0:T(8,128)(2,1)S(1)} %pad_maximum_fusion.refs_0_), channel_id=1, source_target_pairs={{0,8},{1,9},{2,10},{3,11},{4,12},{5,13},{6,14},{7,15},{8,0},{9,1},... | collective-permute-start | bytes 5308424 | tf_op jit(solution)/shard_map/ppermute | solution.py:89
  143.5 14.1 %collective-permute-start.23 = (bf16[4,288,384]{2,1,0:T(8,128)(2,1)S(1)}, bf16[4,288,384]{2,1,0:T(8,128)(2,1)S(1)}, u32[]{:S(2)}, u32[]{:S(2)}) collective-permute-start(bf16[4,288,384]{2,1,0:T(8,128)(2,1)S(1)} %pad_maximum_fusion.2), channel_id=1, source_target_pairs={{8,16},{9,17},{10,18},{11,19},{12,20},{13,21},{14,22},{15,23},{16,... | collective-permute-start | bytes 2654216 | tf_op jit(solution)/shard_map/ppermute | solution.py:129
  144.2 13.4 %collective-permute-start.24 = (bf16[2,288,384]{2,1,0:T(8,128)(2,1)S(1)}, bf16[2,288,384]{2,1,0:T(8,128)(2,1)}, u32[]{:S(2)}, u32[]{:S(2)}) collective-permute-start(bf16[2,288,384]{2,1,0:T(8,128)(2,1)S(1)} %pad_maximum_fusion.5), channel_id=1, source_target_pairs={{8,17},{9,16},{10,19},{11,18},{12,21},{13,20},{14,23},{15,22},{16,... | collective-permute-start | bytes 1327112 | tf_op jit(solution)/shard_map/ppermute | solution.py:130
  171.3 23.0 %collective-permute-start.25 = (bf16[16,448,128]{2,1,0:T(8,128)(2,1)S(1)}, bf16[16,448,128]{2,1,0:T(8,128)(2,1)S(1)}, u32[]{:S(2)}, u32[]{:S(2)}) collective-permute-start(bf16[16,448,128]{2,1,0:T(8,128)(2,1)S(1)} %slice.83), channel_id=1, source_target_pairs={{0,8},{1,9},{2,10},{3,11},{4,12},{5,13},{6,14},{7,15},{8,0},{9,1},... | collective-permute-start | bytes 5505032 | tf_op jit(solution)/shard_map/ppermute | solution.py:89
  194.9 13.5 %collective-permute-start.26 = (bf16[4,448,128]{2,1,0:T(8,128)(2,1)S(1)}, bf16[4,448,128]{2,1,0:T(8,128)(2,1)S(1)}, u32[]{:S(2)}, u32[]{:S(2)}) collective-permute-start(bf16[4,448,128]{2,1,0:T(8,128)(2,1)S(1)} %get-tuple-element.81), channel_id=1, source_target_pairs={{0,16},{1,17},{2,18},{3,19},{4,20},{5,21},{6,22},{7,23},{8,24},{9,... | collective-permute-start | bytes 1376264 | tf_op jit(solution)/shard_map/ppermute | solution.py:89
  195.0 22.7 %collective-permute-start.27 = (bf16[4,448,128]{2,1,0:T(8,128)(2,1)S(1)}, bf16[4,448,128]{2,1,0:T(8,128)(2,1)S(1)}, u32[]{:S(2)}, u32[]{:S(2)}) collective-permute-start(bf16[4,448,128]{2,1,0:T(8,128)(2,1)S(1)} %get-tuple-element.83), channel_id=1, source_target_pairs={{0,1},{1,0},{2,3},{3,2},{4,5},{5,4},{6,7},{7,6},{8,9},{9,8},{10,11... | collective-permute-start | bytes 1376264 | tf_op jit(solution)/shard_map/ppermute | solution.py:89
  195.1 22.6 %collective-permute-start.28 = (bf16[4,448,128]{2,1,0:T(8,128)(2,1)S(1)}, bf16[4,448,128]{2,1,0:T(8,128)(2,1)S(1)}, u32[]{:S(2)}, u32[]{:S(2)}) collective-permute-start(bf16[4,448,128]{2,1,0:T(8,128)(2,1)S(1)} %get-tuple-element.82), channel_id=1, source_target_pairs={{0,17},{1,16},{2,19},{3,18},{4,21},{5,20},{6,23},{7,22},{8,25},{9,... | collective-permute-start | bytes 1376264 | tf_op jit(solution)/shard_map/ppermute | solution.py:89
  220.3 11.1 %collective-permute-start.30 = (bf16[1,448,128]{2,1,0:T(8,128)(2,1)S(1)}, bf16[1,448,128]{2,1,0:T(8,128)(2,1)S(1)}, u32[]{:S(2)}, u32[]{:S(2)}) collective-permute-start(bf16[1,448,128]{2,1,0:T(8,128)(2,1)S(1)} %get-tuple-element.85), channel_id=1, source_target_pairs={{0,4},{1,5},{2,6},{3,7},{4,0},{5,1},{6,2},{7,3},{8,12},{9,13},{10,... | collective-permute-start | bytes 344072 | tf_op jit(solution)/shard_map/ppermute | solution.py:89
  (32 other events, 427.8 us)

commit v3 on v2

--- a/solution.py
+++ b/solution.py
@@ -94,25 +94,16 @@
             buf = jnp.concatenate([buf] + [self.send(buf, m) for m in stage], axis=0)
         return buf, self.send(buf, self.stages[-1][0])
 
-    def reduce_parts(self, blocks):
-        buf = blocks
-        for stage in reversed(self.stages):
-            split = buf.reshape((len(stage) + 1, -1) + buf.shape[1:])
-            parts = [split[0]] + [self.send(split[k + 1], m) for k, m in enumerate(stage)]
-            if stage is self.stages[0]:
-                return [part[0] for part in parts]
+    def reduce_parts(self, keep, away):
+        parts = [keep, self.send(away, self.stages[-1][0])]
+        for stage in reversed(self.stages[:-1]):
             total = parts[0].astype(WIDE)
             for part in parts[1:]:
                 total = total + part.astype(WIDE)
             buf = total.astype(LOW)
-
-    def total(self, value):
-        for stage in self.stages:
-            got = [value] + [self.send(value, m) for m in stage]
-            while len(got) > 1:
-                got = [got[k] + got[k + 1] for k in range(0, len(got), 2)]
-            value = got[0]
-        return value
+            split = buf.reshape((len(stage) + 1, -1) + buf.shape[1:])
+            parts = [split[0]] + [self.send(split[k + 1], m) for k, m in enumerate(stage)]
+        return [part[0] for part in parts]
 
     def exchange(self, block, extra=()):
         own = block[None]
@@ -130,7 +121,8 @@
             far_beside = lax.ppermute(pair, BOTH, skew)
             beside = self.send(pair, 1)
             row = jnp.concatenate([own, one, quad, beside], axis=0)
-            return [row, self.send(row, 8), far, far_beside], extra
+            home = self.send(row, 8)
+            return [row, home, far, far_beside], extra
         slots = []
         for slot in range(self.window):
             by = self.reach - slot
@@ -238,6 +230,11 @@
     return jnp.concatenate([ids, ids], axis=0)
 
 
+def scaled_query(low, weight, bias):
+    q = dot(low, weight, NN) + bias
+    return (q.astype(LOW).astype(WIDE) * SCALE).astype(LOW)
+
+
 def column_sum(x):
     return jnp.sum(x, axis=0, keepdims=True)
 
@@ -271,7 +268,69 @@
         out = jnp.where(row * LANES + lane < plan.share, out, 0.0)
         out_ref[...] = out
         sq = jnp.sum(jnp.sum(out * out, axis=0, keepdims=True), axis=1, keepdims=True)
-        sq_ref[...] = jnp.broadcast_to(sq, (8, LANES))
+        sq_ref[...] = jnp.broadcast_to(sq, (plan.count, LANES))
+
+    return kernel
+
+
+VEC = {"gain1": 0, "shift1": 1, "tbias": 2, "obias": 3, "scale1": 4, "gain2": 5, "shift2": 6}
+VEC.update({"ubias": 7, "dbias": 8, "scale2": 9})
+
+
+def unpack_kernel(plan):
+    half = plan.count // 2
+
+    def kernel(table, near, core, triple_ref, wo, wup, wdn, vec_ref, wbuf, flat, wsem):
+        def weight_copy(e, wait):
+            t = table[e]
+
+            @pl.when(t < half)
+            def _():
+                c = pltpu.make_async_copy(near.at[t], wbuf.at[e], wsem.at[e])
+                c.wait() if wait else c.start()
+
+            @pl.when(t >= half)
+            def _():
+                c = pltpu.make_async_copy(core.at[t - half], wbuf.at[e], wsem.at[e])
+                c.wait() if wait else c.start()
+
+        def start_one(e, carry):
+            weight_copy(e, False)
+            return carry
+
+        def wait_one(e, carry):
+            weight_copy(e, True)
+            return carry
+
+        lax.fori_loop(0, plan.count, start_one, 0)
+        lax.fori_loop(0, plan.count, wait_one, 0)
+        for e in range(plan.count):
+            r0 = plan.start[e]
+            block = wbuf[e].astype(WIDE)
+            if e:
+                before = flat[r0 : r0 + 1, :]
+                flat[r0 : r0 + plan.rows, :] = block
+                flat[r0 : r0 + 1, :] = before + block[0:1, :]
+            else:
+                flat[r0 : r0 + plan.rows, :] = block
+
+        def unfold(dest, name, height, width):
+            wide = width // LANES
+            step = min(height, 384)
+            for j in range(wide):
+                for i in range(0, height, step):
+                    dest[i : i + step, LANES * j : LANES * (j + 1)] = flat[
+                        pl.ds(AT[name] + i * wide + j, step, stride=wide), :
+                    ].astype(LOW)
+
+        unfold(triple_ref, "triple", D, 3 * D)
+        unfold(wo, "out", D, D)
+        unfold(wup, "up", D, FF)
+        unfold(wdn, "down", FF, D)
+        vec_ref[...] = jnp.zeros(vec_ref.shape, WIDE)
+        for name, row in VEC.items():
+            width = dict(PIECES)[name]
+            vec_ref[row : row + 1, :width] = vector(flat, AT[name], width)
 
     return kernel
 
@@ -279,21 +338,19 @@
 def forward_kernel(plan, sources):
     T = plan.tokens
     own = plan.reach
-    half = plan.count // 2
     part = plan.part
     pairs = HEADS // 2
 
     def kernel(table, *refs):
-        near, core = refs[:2]
-        wins = refs[2 : 2 + sources]
-        cot_ref, col_ref, row_ref = refs[2 + sources : 5 + sources]
+        wins = refs[:sources]
+        triple_ref, wo, wup, wdn, par_ref, cot_ref, col_ref, row_ref = refs[sources : 8 + sources]
         (
             out_ref,
             msg_ref,
             q_ref,
             k_ref,
             v_ref,
-            triple_ref,
+            norm_ref,
             normed_ref,
             mid_ref,
             act_ref,
@@ -304,93 +361,45 @@
             gbo_ref,
             vec_ref,
             stat_ref,
-            gain_ref,
             kown_ref,
             vown_ref,
-        ) = refs[5 + sources : 24 + sources]
-        wbuf, flat, xwin, wo, wup, wdn, scores, tops, sums, accs, mix, wsem, xsem = refs[24 + sources :]
+        ) = refs[8 + sources : 26 + sources]
+        xwin, scores, tops, sums, accs, mix, xsem = refs[26 + sources :]
         lo = table[plan.low_at()]
         hi = table[plan.low_at() + 1]
 
-        def weight_copy(e, wait):
-            t = table[e]
-
-            @pl.when(t < half)
-            def _():
-                c = pltpu.make_async_copy(near.at[t], wbuf.at[e], wsem.at[e])
-                c.wait() if wait else c.start()
-
-            @pl.when(t >= half)
-            def _():
-                c = pltpu.make_async_copy(core.at[t - half], wbuf.at[e], wsem.at[e])
-                c.wait() if wait else c.start()
-
-        def start_one(e, carry):
-            weight_copy(e, False)
-            return carry
-
-        lax.fori_loop(0, plan.count, start_one, 0)
+        def param(name):
+            row = VEC[name]
+            return par_ref[row : row + 1, : dict(PIECES)[name]]
+
         fetch_window(plan, table, wins, xwin, xsem, lo, hi, False)
-
-        def wait_one(e, carry):
-            weight_copy(e, True)
-            return carry
-
-        lax.fori_loop(0, plan.count, wait_one, 0)
-        for e in range(plan.count):
-            r0 = plan.start[e]
-            block = wbuf[e].astype(WIDE)
-            if e:
-                before = flat[r0 : r0 + 1, :]
-                flat[r0 : r0 + plan.rows, :] = block
-                flat[r0 : r0 + 1, :] = before + block[0:1, :]
-            else:
-                flat[r0 : r0 + plan.rows, :] = block
-
-        def unfold(dest, name, height, width):
-            wide = width // LANES
-            step = min(height, 384)
-            for j in range(wide):
-                for i in range(0, height, step):
-                    dest[i : i + step, LANES * j : LANES * (j + 1)] = flat[
-                        pl.ds(AT[name] + i * wide + j, step, stride=wide), :
-                    ].astype(LOW)
-
-        unfold(triple_ref, "triple", D, 3 * D)
-        gain1 = vector(flat, AT["gain1"], D)
-        shift1 = vector(flat, AT["shift1"], D)
-        gain_ref[...] = jnp.broadcast_to(gain1, (8, D))
-        tbias = vector(flat, AT["tbias"], 2 * D)
+        gain1 = param("gain1")
+        shift1 = param("shift1")
+        tbias = param("tbias")
         fetch_window(plan, table, wins, xwin, xsem, lo, hi, True)
 
         def project(w, carry):
             n, _ = normalized(xwin[w].astype(WIDE))
             low = (n * gain1 + shift1).astype(LOW)
-
-            @pl.when(w == own)
-            def _():
-                normed_ref[...] = low
-
-            q = dot(low, triple_ref[:, :D], NN) + tbias[:, :D]
-            q_ref[w] = (q.astype(LOW).astype(WIDE) * SCALE).astype(LOW)
-            k_ref[w] = dot(low, triple_ref[:, D : 2 * D], NN).astype(LOW)
-            v_ref[w] = (dot(low, triple_ref[:, 2 * D :], NN) + tbias[:, D:]).astype(LOW)
+            norm_ref[w] = low
+            kv = dot(low, triple_ref[:, D:], NN)
+            k_ref[w] = kv[:, :D].astype(LOW)
+            v_ref[w] = (kv[:, D:] + tbias[:, D:]).astype(LOW)
             return carry
 
         lax.fori_loop(lo, hi + 1, project, 0)
         kown_ref[...] = k_ref[own]
         vown_ref[...] = v_ref[own]
-
-        unfold(wo, "out", D, D)
-        unfold(wup, "up", D, FF)
-        unfold(wdn, "down", FF, D)
+        low = norm_ref[own]
+        normed_ref[...] = low
+        q_ref[...] = scaled_query(low, triple_ref[:, :D], tbias[:, :D])
 
         lane = lax.broadcasted_iota(jnp.int32, (part, LANES), 1)
         for c in range(T // part):
             rows = slice(part * c, part * (c + 1))
             at, to = plan.range_at(c)
             begin, finish = table[at], table[to] + 1
-            qs = [stacked(q_ref[own, rows, LANES * p : LANES * (p + 1)]) for p in range(pairs)]
+            qs = [stacked(q_ref[rows, LANES * p : LANES * (p + 1)]) for p in range(pairs)]
             ids = tiled(col_ref[rows, :], T)
             for p in range(pairs):
                 tops[p] = jnp.full((2 * part, LANES), MASKED, WIDE)
@@ -440,20 +449,20 @@
         att_low = att.astype(LOW)
         att_ref[...] = att_low
         x = xwin[own].astype(WIDE)
-        scale1 = vector(flat, AT["scale1"], D)
-        scale2 = vector(flat, AT["scale2"], D)
-        gain2 = vector(flat, AT["gain2"], D)
-        branch_one = dot(att_low, wo[...], NN) + vector(flat, AT["obias"], D)
+        scale1 = param("scale1")
+        scale2 = param("scale2")
+        gain2 = param("gain2")
+        branch_one = dot(att_low, wo[...], NN) + param("obias")
         middle = x + scale1 * branch_one
         n2, r2 = normalized(middle)
-        n2_low = (n2 * gain2 + vector(flat, AT["shift2"], D)).astype(LOW)
+        n2_low = (n2 * gain2 + param("shift2")).astype(LOW)
         n2_ref[...] = n2_low
-        pre = dot(n2_low, wup[...], NN) + vector(flat, AT["ubias"], FF)
+        pre = dot(n2_low, wup[...], NN) + param("ubias")
         cdf = 0.5 * (1.0 + lax.erf(pre * math.sqrt(0.5)))
         act_low = (pre * cdf).astype(LOW)
         act_ref[...] = act_low
         slope = cdf + pre * (jnp.exp(-0.5 * pre * pre) * (1.0 / math.sqrt(2.0 * math.pi)))
-        branch_two = dot(act_low, wdn[...], NN) + vector(flat, AT["dbias"], D)
+        branch_two = dot(act_low, wdn[...], NN) + param("dbias")
         out_ref[...] = (middle + scale2 * branch_two).astype(LOW)
 
         up = cot_ref[...].astype(WIDE)
@@ -479,15 +488,14 @@
             stats = jnp.where(lane == HEADS + 2 * p, one, stats)
             stats = jnp.where(lane == HEADS + 2 * p + 1, two, stats)
         stat_ref[...] = stats
-        flipped = jnp.transpose(stats)[0:16, :]
-        hi16 = flipped.astype(LOW)
-        rest = flipped - hi16.astype(WIDE)
-        mid16 = rest.astype(LOW)
-        low16 = (rest - mid16.astype(WIDE)).astype(LOW)
-        packed = jnp.concatenate([hi16, mid16[:, : D - T]], axis=1)
-        msg_ref[T : T + 16, :] = packed
-        packed = jnp.concatenate([mid16[:, D - T :], low16], axis=1)
-        msg_ref[T + 16 : T + 32, :] = packed
+        high = stats.astype(LOW).astype(WIDE)
+        rest = pltpu.roll(stats - high, 2 * HEADS, 1)
+        flipped = jnp.transpose(jnp.where(lane < 2 * HEADS, high, rest))
+        tail = flipped[16:24, :]
+        msg_ref[T : T + 16, 0:T] = flipped[0:16, :].astype(LOW)
+        msg_ref[T : T + 16, T:] = jnp.concatenate(
+            [tail[:, :LANES], tail[:, LANES:]], axis=0
+        ).astype(LOW)
 
         vec_ref[...] = jnp.zeros(vec_ref.shape, WIDE)
         vec_ref[0:1, :D] = column_sum(up * branch_two)
@@ -512,22 +520,58 @@
             ]
 
 
-def middle_kernel(plan):
+def query_kernel(plan):
     T = plan.tokens
-    own = plan.reach
-    base = AT["out"]
     part = plan.part
     pairs = HEADS // 2
 
     def kernel(
+        table, q_ref, k_ref, v_ref, msg_ref, stat_ref, col_ref, row_ref, gq_ref, logs, dots, accs
+    ):
+        for c in range(T // part):
+            rows = slice(part * c, part * (c + 1))
+            at, to = plan.range_at(c)
+            begin, finish = table[at], table[to] + 1
+            qs = [stacked(q_ref[rows, LANES * p : LANES * (p + 1)]) for p in range(pairs)]
+            gs = [stacked(msg_ref[rows, LANES * p : LANES * (p + 1)]) for p in range(pairs)]
+            ids = tiled(col_ref[rows, :], T)
+            for p in range(pairs):
+                for k in range(2):
+                    h = 2 * p + k
+                    half = slice(part * k, part * (k + 1))
+                    logs[p, half, :] = jnp.broadcast_to(stat_ref[rows, h : h + 1], (part, LANES))
+                    h = h + HEADS
+                    dots[p, half, :] = jnp.broadcast_to(stat_ref[rows, h : h + 1], (part, LANES))
+                accs[p] = jnp.zeros((2 * part, LANES), WIDE)
+
+            def step(w, carry, qs=qs, gs=gs, ids=ids):
+                seen = ids == row_ref[pl.ds(w, 1), :]
+                for p in range(pairs):
+                    cols = slice(LANES * p, LANES * (p + 1))
+                    key = k_ref[w, :, cols]
+                    s = jnp.where(seen, dot(qs[p], key, NT), MASKED)
+                    prob = jnp.exp(s - jnp.concatenate([logs[p]] * (T // LANES), axis=1))
+                    inner = jnp.concatenate([dots[p]] * (T // LANES), axis=1)
+                    grad = prob * (dot(gs[p], v_ref[w, :, cols], NT) - inner)
+                    accs[p] = accs[p] + dot(grad.astype(LOW), key, NN)
+                return carry
+
+            lax.fori_loop(begin, finish, step, 0)
+            for p in range(pairs):
+                gq_ref[rows, LANES * p : LANES * (p + 1)] = (unstacked(accs[p]) * SCALE).astype(LOW)
+
+    return kernel
+
+
+def weight_kernel(plan):
+    base = AT["out"]
+    half = plan.count // 2
+
+    def kernel(
         table,
-        q_ref,
-        k_ref,
-        v_ref,
-        msg_ref,
-        stat_ref,
-        col_ref,
-        row_ref,
+        norm_ref,
+        triple_ref,
+        par_ref,
         act_ref,
         pre_ref,
         gbt_ref,
@@ -535,13 +579,11 @@
         att_ref,
         gbo_ref,
         vec_ref,
-        gq_ref,
-        blocks_ref,
+        q_ref,
+        keep_ref,
+        away_ref,
         tail_ref,
         flat,
-        logs,
-        dots,
-        accs,
     ):
         fold(flat, AT["down"] - base, act_ref, gbt_ref, D)
         fold(flat, AT["up"] - base, n2_ref, pre_ref, FF)
@@ -558,39 +600,23 @@
         tail_ref[...] = flat[0 : plan.rows, :]
         for e in range(plan.first_late, plan.count):
             r0 = plan.start[e] - base
-            blocks_ref[table[e]] = flat[r0 : r0 + plan.rows, :].astype(LOW)
-
-        for c in range(T // part):
-            rows = slice(part * c, part * (c + 1))
-            at, to = plan.range_at(c)
-            begin, finish = table[at], table[to] + 1
-            qs = [stacked(q_ref[own, rows, LANES * p : LANES * (p + 1)]) for p in range(pairs)]
-            gs = [stacked(msg_ref[rows, LANES * p : LANES * (p + 1)]) for p in range(pairs)]
-            ids = tiled(col_ref[rows, :], T)
-            for p in range(pairs):
-                for k in range(2):
-                    h = 2 * p + k
-                    half = slice(part * k, part * (k + 1))
-                    logs[p, half, :] = jnp.broadcast_to(stat_ref[rows, h : h + 1], (part, LANES))
-                    h = h + HEADS
-                    dots[p, half, :] = jnp.broadcast_to(stat_ref[rows, h : h + 1], (part, LANES))
-                accs[p] = jnp.zeros((2 * part, LANES), WIDE)
-
-            def step(w, carry, qs=qs, gs=gs, ids=ids):
-                seen = ids == row_ref[pl.ds(w, 1), :]
-                for p in range(pairs):
-                    cols = slice(LANES * p, LANES * (p + 1))
-                    key = k_ref[w, :, cols]
-                    s = jnp.where(seen, dot(qs[p], key, NT), MASKED)
-                    prob = jnp.exp(s - jnp.concatenate([logs[p]] * (T // LANES), axis=1))
-                    inner = jnp.concatenate([dots[p]] * (T // LANES), axis=1)
-                    grad = prob * (dot(gs[p], v_ref[w, :, cols], NT) - inner)
-                    accs[p] = accs[p] + dot(grad.astype(LOW), key, NN)
-                return carry
-
-            lax.fori_loop(begin, finish, step, 0)
-            for p in range(pairs):
-                gq_ref[rows, LANES * p : LANES * (p + 1)] = (unstacked(accs[p]) * SCALE).astype(LOW)
+            t = table[e]
+
+            @pl.when(t < half)
+            def _(r0=r0, t=t):
+                keep_ref[t] = flat[r0 : r0 + plan.rows, :].astype(LOW)
+
+            @pl.when(t >= half)
+            def _(r0=r0, t=t):
+                away_ref[t - half] = flat[r0 : r0 + plan.rows, :].astype(LOW)
+
+        bias = par_ref[VEC["tbias"] : VEC["tbias"] + 1, :D]
+
+        def project(w, carry):
+            q_ref[w] = scaled_query(norm_ref[w], triple_ref[:, :D], bias)
+            return carry
+
+        lax.fori_loop(table[plan.low_at()], table[plan.low_at() + 1] + 1, project, 0)
 
     return kernel
 
@@ -598,6 +624,7 @@
 def last_kernel(plan, sources):
     T = plan.tokens
     early = plan.first_late
+    half = plan.count // 2
     part = plan.part
     pairs = HEADS // 2
 
@@ -614,23 +641,25 @@
             triple_ref,
             x_ref,
             mid_ref,
-            gain_ref,
+            par_ref,
             tail_ref,
             _,
+            _,
             grad_ref,
-            blocks_ref,
-        ) = refs[sources : sources + 15]
-        mwin, flat, gt, stage, stats, acck, accv, msem, osem = refs[sources + 15 :]
+            keep_ref,
+            away_ref,
+        ) = refs[sources : sources + 17]
+        mwin, flat, gt, stage, stats, spare, acck, accv, msem, osem = refs[sources + 17 :]
         lo = table[plan.low_at()]
         hi = table[plan.low_at() + 1]
         fetch_window(plan, table, wins, mwin, msem, lo, hi, False)
         fetch_window(plan, table, wins, mwin, msem, lo, hi, True)
 
         def unpack(w, carry):
-            one = mwin[w, T : T + 16, :].astype(WIDE)
-            two = mwin[w, T + 16 : T + 32, :].astype(WIDE)
-            middle = jnp.concatenate([one[:, T:], two[:, : 2 * T - D]], axis=1)
-            stats[w] = (one[:, :T] + middle) + two[:, 2 * T - D :]
+            got = mwin[w, T : T + 16, :].astype(WIDE)
+            spare[0:16, :] = got[:, :T]
+            spare[16:24, :] = jnp.concatenate([got[:8, T:], got[8:, T:]], axis=1)
+            stats[w, 0 : 2 * HEADS, :] = spare[0 : 2 * HEADS, :] + spare[2 * HEADS : 4 * HEADS, :]
             return carry
 
         lax.fori_loop(lo, hi + 1, unpack, 0)
@@ -683,13 +712,28 @@
         put_vector(flat, AT["gain1"], column_sum(gn * n))
         put_vector(flat, AT["shift1"], column_sum(gn))
         flat[AT["out"] : AT["out"] + plan.rows, :] = tail_ref[...]
+
+        def put(e, wait):
+            t = table[e]
+
+            @pl.when(t < half)
+            def _():
+                c = pltpu.make_async_copy(stage.at[e], keep_ref.at[t], osem.at[e])
+                c.wait() if wait else c.start()
+
+            @pl.when(t >= half)
+            def _():
+                c = pltpu.make_async_copy(stage.at[e], away_ref.at[t - half], osem.at[e])
+                c.wait() if wait else c.start()
+
         for e in range(early):
             r0 = plan.start[e]
             stage[e] = flat[r0 : r0 + plan.rows, :].astype(LOW)
-            pltpu.make_async_copy(stage.at[e], blocks_ref.at[table[e]], osem.at[e]).start()
-        grad_ref[...] = mid_ref[...] + norm_back(gn, gain_ref[0:1, :], n, r)
+            put(e, False)
+        gain1 = par_ref[VEC["gain1"] : VEC["gain1"] + 1, :D]
+        grad_ref[...] = mid_ref[...] + norm_back(gn, gain1, n, r)
         for e in range(early):
-            pltpu.make_async_copy(stage.at[e], blocks_ref.at[table[e]], osem.at[e]).wait()
+            put(e, True)
 
     return kernel
 
@@ -731,17 +775,39 @@
         wins, (table, columns, key_ids) = plan.exchange(inputs, (table, columns, key_ids))
         sources = len(wins)
 
+        half = pltpu.VMEM((HEADS // 2, 2 * plan.part, LANES), WIDE)
+        unpack = pl.pallas_call(
+            unpack_kernel(plan),
+            in_specs=[SMEM, ANY, ANY],
+            out_specs=[VMEM] * 5,
+            out_shape=[
+                shape((D, 3 * D), LOW),
+                shape((D, D), LOW),
+                shape((D, FF), LOW),
+                shape((FF, D), LOW),
+                shape((16, FF), WIDE),
+            ],
+            scratch_shapes=[
+                pltpu.VMEM((N, R, LANES), LOW),
+                pltpu.VMEM((plan.flat_rows, LANES), WIDE),
+                pltpu.SemaphoreType.DMA((N,)),
+            ],
+            compiler_params=limit,
+            name="unpack",
+        )
+        triple, wo, wup, wdn, params = unpack(table, near, core)
+
         outs = pl.pallas_call(
             forward_kernel(plan, sources),
-            in_specs=[SMEM, ANY, ANY] + [ANY] * sources + [VMEM] * 3,
-            out_specs=[VMEM] * 19,
+            in_specs=[SMEM] + [ANY] * sources + [VMEM] * 8,
+            out_specs=[VMEM] * 18,
             out_shape=[
                 shape((T, D), LOW),
-                shape((T + 32, D), LOW),
+                shape((T + 16, D), LOW),
+                shape((T, D), LOW),
                 shape((W, T, D), LOW),
                 shape((W, T, D), LOW),
                 shape((W, T, D), LOW),
-                shape((D, 3 * D), LOW),
                 shape((T, D), LOW),
                 shape((T, D), WIDE),
                 shape((T, FF), LOW),
@@ -752,35 +818,28 @@
                 shape((T, D), LOW),
                 shape((8, FF), WIDE),
                 shape((T, LANES), WIDE),
-                shape((8, D), WIDE),
                 shape((T, D), LOW),
                 shape((T, D), LOW),
             ],
             scratch_shapes=[
-                pltpu.VMEM((N, R, LANES), LOW),
-                pltpu.VMEM((plan.flat_rows, LANES), WIDE),
                 pltpu.VMEM((W, T, D), LOW),
-                pltpu.VMEM((D, D), LOW),
-                pltpu.VMEM((D, FF), LOW),
-                pltpu.VMEM((FF, D), LOW),
                 pltpu.VMEM((HEADS // 2, W, 2 * plan.part, T), WIDE),
-                pltpu.VMEM((HEADS // 2, 2 * plan.part, LANES), WIDE),
-                pltpu.VMEM((HEADS // 2, 2 * plan.part, LANES), WIDE),
-                pltpu.VMEM((HEADS // 2, 2 * plan.part, LANES), WIDE),
+                half,
+                half,
+                half,
                 pltpu.VMEM((T, D), WIDE),
-                pltpu.SemaphoreType.DMA((N,)),
                 pltpu.SemaphoreType.DMA((W,)),
             ],
             compiler_params=limit,
             name="forward",
-        )(table, near, core, *wins, cotangent, columns, key_ids)
+        )(table, *wins, triple, wo, wup, wdn, params, cotangent, columns, key_ids)
         (
             result,
             message,
             q,
             k,
             v,
-            triple,
+            norms,
             normed,
             gmid,
             act,
@@ -791,61 +850,70 @@
             gbo,
             vec,
             stat,
-            gain,
             k_own,
             v_own,
         ) = outs
         messages, _ = plan.exchange(message)
 
-        middle_call = pl.pallas_call(
-            middle_kernel(plan),
-            in_specs=[SMEM] + [VMEM] * 14,
-            out_specs=[VMEM] * 3,
+        query_call = pl.pallas_call(
+            query_kernel(plan),
+            in_specs=[SMEM] + [VMEM] * 7,
+            out_specs=VMEM,
+            out_shape=shape((T, D), LOW),
+            scratch_shapes=[half] * 3,
+            compiler_params=limit,
+            name="query",
+        )
+        gq = query_call(table, q, k, v, message, stat, columns, key_ids)
+        weight_call = pl.pallas_call(
+            weight_kernel(plan),
+            in_specs=[SMEM] + [VMEM] * 10,
+            out_specs=[VMEM] * 4,
             out_shape=[
-                shape((T, D), LOW),
-                shape((N, R, LANES), LOW),
+                shape((W, T, D), LOW),
+                shape((N // 2, R, LANES), LOW),
+                shape((N // 2, R, LANES), LOW),
                 shape((R, LANES), WIDE),
             ],
             scratch_shapes=[
                 pltpu.VMEM((plan.flat_rows - AT["out"] + 8, LANES), WIDE),
-                pltpu.VMEM((HEADS // 2, 2 * plan.part, LANES), WIDE),
-                pltpu.VMEM((HEADS // 2, 2 * plan.part, LANES), WIDE),
-                pltpu.VMEM((HEADS // 2, 2 * plan.part, LANES), WIDE),
             ],
             compiler_params=limit,
-            name="middle",
+            name="weight",
         )
-        gq, blocks, tail = middle_call(
-            table, q, k, v, message, stat, columns, key_ids, act, gpre, gbt, n2, att, gbo, vec
+        queries, keep, away, tail = weight_call(
+            table, norms, triple, params, act, gpre, gbt, n2, att, gbo, vec
         )
 
         late = plan.first_late
-        input_grad, blocks = pl.pallas_call(
+        input_grad, keep, away = pl.pallas_call(
             last_kernel(plan, sources),
-            in_specs=[SMEM]
-            + [ANY] * sources
-            + [VMEM] * 12
-            + [ANY],
-            out_specs=[VMEM, ANY],
-            out_shape=[shape((T, D), WIDE), shape((N, R, LANES), LOW)],
+            in_specs=[SMEM] + [ANY] * sources + [VMEM] * 12 + [ANY, ANY],
+            out_specs=[VMEM, ANY, ANY],
+            out_shape=[
+                shape((T, D), WIDE),
+                shape((N // 2, R, LANES), LOW),
+                shape((N // 2, R, LANES), LOW),
+            ],
             scratch_shapes=[
-                pltpu.VMEM((W, T + 32, D), LOW),
+                pltpu.VMEM((W, T + 16, D), LOW),
                 pltpu.VMEM((AT["out"] + R + 8, LANES), WIDE),
                 pltpu.VMEM((T, 3 * D), LOW),
                 pltpu.VMEM((late, R, LANES), LOW),
                 pltpu.VMEM((W, 16, T), WIDE),
-                pltpu.VMEM((HEADS // 2, 2 * plan.part, LANES), WIDE),
-                pltpu.VMEM((HEADS // 2, 2 * plan.part, LANES), WIDE),
+                pltpu.VMEM((24, T), WIDE),
+                half,
+                half,
                 pltpu.SemaphoreType.DMA((W,)),
                 pltpu.SemaphoreType.DMA((late,)),
             ],
-            input_output_aliases={13 + sources: 1},
+            input_output_aliases={13 + sources: 1, 14 + sources: 2},
             compiler_params=limit,
             name="last",
         )(
             table,
             *messages,
-            q,
+            queries,
             k_own,
             v_own,
             columns,
@@ -855,22 +923,24 @@
             triple,
             inputs,
             gmid,
-            gain,
+            params,
             tail,
-            blocks,
+            keep,
+            away,
         )
 
-        parts = plan.reduce_parts(blocks)
+        parts = plan.reduce_parts(keep, away)
         grad, square = pl.pallas_call(
             unshift_kernel(plan),
             in_specs=[SMEM] + [VMEM] * len(parts),
             out_specs=[VMEM, VMEM],
-            out_shape=[shape((R, LANES), WIDE), shape((8, LANES), WIDE)],
+            out_shape=[shape((R, LANES), WIDE), shape((N, LANES), WIDE)],
             scratch_shapes=[pltpu.VMEM((R + 8, LANES), WIDE)],
             name="unshift",
         )(shift, *parts)
         grad_shard = grad.reshape(-1)[: plan.share]
-        grad_norm = jnp.sqrt(plan.total(square)[0, 0])
+        squares = lax.all_to_all(square, BOTH, 0, 0, tiled=True)
+        grad_norm = jnp.sqrt(jnp.sum(squares[:, 0]))
         ceiling = CLIP_RATIO * math.sqrt(plan.share * N)
         factor = ceiling / jnp.maximum(grad_norm, ceiling)
         clipped = grad_shard * factor

time: 256 us -> 252 us (0.984)
  waiting for transfers between devices: 95.1 us -> 76.7 us
  blocking collectives: 0 us -> 9.69 us
  Pallas kernels: 43.6 us -> 50.3 us
  starting transfers between devices: 89 us -> 83.1 us
    ppermute x35 -> x28, waiting for transfers between devices: 95.1 us -> 76.7 us  [send(): return lax.ppermute(x, BOTH, [(i, i ^ mask) for i in range(self.count)])]
    all_to_all x0 -> x1, blocking collectives: none -> 9.69 us  [per_device(): squares = lax.all_to_all(square, BOTH, 0, 0, tiled=True)]
    ppermute x35 -> x28, starting transfers between devices: 85.5 us -> 78 us  [send(): return lax.ppermute(x, BOTH, [(i, i ^ mask) for i in range(self.count)])]
    pallas_call x2 -> x4, Pallas kernels: 29.1 us -> 35.8 us  [the longest x1 13.9 us: per_device(): pl.pallas_call(forward_kernel(plan, sources), in_specs=[SMEM] + [ANY] * s...]
    unnamed x40 -> x32, local copies, waits for them, and re-layouts: 3.97 us -> 7.94 us
  transfers between devices with their start and end apart: 39 -> 32, of which waited for: 22 -> 15; matrix products, arithmetic and copies ran while one was open for 5% -> 8% of each run, Pallas kernels for 5% -> 9%
where the time goes in v3:
time: 252 us; the launch traced here: 251 us
  starting transfers between devices  83.1 us (33%)
  waiting for transfers between devices  76.7 us (30%)
  Pallas kernels  50.3 us (20%)
  local copies, waits for them, and re-layouts  17.3 us (7%)
  other arithmetic  11.5 us (5%)
  blocking collectives  9.69 us (4%)
  between operations  2.79 us (1%)
    ppermute x28, starting transfers between devices, send(): return lax.ppermute(x, BOTH, [(i, i ^ mask) for i in range(self.count)])  78 us
    ppermute x28, waiting for transfers between devices, send(): return lax.ppermute(x, BOTH, [(i, i ^ mask) for i in range(self.count)])  76.7 us
    pallas_call x1, Pallas kernels, per_device(): pl.pallas_call(forward_kernel(plan, sources), in_specs=[SMEM] + [ANY] * s...  13.9 us
    pallas_call x1, Pallas kernels, per_device(): pl.pallas_call(last_kernel(plan, sources), in_specs=[SMEM] + [ANY] * sour...  10.9 us
    all_to_all x1, blocking collectives, per_device(): squares = lax.all_to_all(square, BOTH, 0, 0, tiled=True)  9.69 us
    pallas_call x1, Pallas kernels, per_device(): gq = query_call(table, q, k, v, message, stat, columns, key_ids)  8.23 us
    pallas_call x1, Pallas kernels, per_device(): weight_call(table, norms, triple, params, act, gpre, gbt, n2, att, gbo, vec)  8.08 us
    unnamed x32, local copies, waits for them, and re-layouts  7.94 us
  transfers between devices with their start and end apart: 32, of which 15 were waited for; matrix products, arithmetic and copies ran while one was open for 8% of the time, Pallas kernels for 9%

profile of v3, /device:TPU:0, one launch (start us, length us, event | category | flops | bytes accessed | tf_op | source)
XLA Modules:
  0.0 251.5 jit_solution(13380683224097600559)
XLA Ops:
  0.6 4.1 %collective-permute-start.3 = (bf16[1,256,384]{2,1,0:T(8,128)(2,1)}, bf16[1,256,384]{2,1,0:T(8,128)(2,1)S(1)}, u32[]{:S(2)}, u32[]{:S(2)}) collective-permute-start(bf16[1,256,384]{2,1,0:T(8,128)(2,1)} %bitcast.42), channel_id=1, source_target_pairs={{0,3},{1,2},{2,1},{3,0},{4,7},{5,6},{6,5},{7,4},{8,11},{9,10},{10,... | collective-permute-start | bytes 589832 | tf_op jit(solution)/shard_map/ppermute | solution.py:89
  8.6 3.6 %collective-permute-start.11 = (bf16[1,448,128]{2,1,0:T(8,128)(2,1)}, bf16[1,448,128]{2,1,0:T(8,128)(2,1)S(1)}, u32[]{:S(2)}, u32[]{:S(2)}) collective-permute-start(bf16[1,448,128]{2,1,0:T(8,128)(2,1)} %bitcast.32), channel_id=1, source_target_pairs={{0,6},{1,7},{2,4},{3,5},{4,2},{5,3},{6,0},{7,1},{8,14},{9,15},{10,... | collective-permute-start | bytes 344072 | tf_op jit(solution)/shard_map/ppermute | solution.py:89
  24.2 3.6 %collective-permute-start.1 = (bf16[1,256,384]{2,1,0:T(8,128)(2,1)}, bf16[1,256,384]{2,1,0:T(8,128)(2,1)S(1)}, u32[]{:S(2)}, u32[]{:S(2)}) collective-permute-start(bf16[1,256,384]{2,1,0:T(8,128)(2,1)} %bitcast.44), channel_id=1, source_target_pairs={{0,6},{1,7},{2,4},{3,5},{4,2},{5,3},{6,0},{7,1},{8,14},{9,15},{10,... | collective-permute-start | bytes 589832 | tf_op jit(solution)/shard_map/ppermute | solution.py:89
  34.9 8.4 %collective-permute-done = bf16[1,256,384]{2,1,0:T(8,128)(2,1)S(1)} collective-permute-done((bf16[1,256,384]{2,1,0:T(8,128)(2,1)}, bf16[1,256,384]{2,1,0:T(8,128)(2,1)S(1)}, u32[]{:S(2)}, u32[]{:S(2)}) %collective-permute-start) | collective-permute-done | bytes 196640 | tf_op jit(solution)/shard_map/ppermute | solution.py:89
  50.0 5.8 %collective-permute-done.14 = bf16[4,448,128]{2,1,0:T(8,128)(2,1)S(1)} collective-permute-done((bf16[4,448,128]{2,1,0:T(8,128)(2,1)S(1)}, bf16[4,448,128]{2,1,0:T(8,128)(2,1)S(1)}, u32[]{:S(2)}, u32[]{:S(2)}) %collective-permute-start.14) | collective-permute-done | bytes 458784 | tf_op jit(solution)/shard_map/ppermute | solution.py:89
  60.0 8.3 %collective-permute-done.5 = bf16[2,256,384]{2,1,0:T(8,128)(2,1)S(1)} collective-permute-done((bf16[2,256,384]{2,1,0:T(8,128)(2,1)}, bf16[2,256,384]{2,1,0:T(8,128)(2,1)S(1)}, u32[]{:S(2)}, u32[]{:S(2)}) %collective-permute-start.5) | collective-permute-done | bytes 393248 | tf_op jit(solution)/shard_map/ppermute | solution.py:89
  71.6 5.5 %unpack.1 = (bf16[384,1152]{1,0:T(8,128)(2,1)}, bf16[384,384]{1,0:T(8,128)(2,1)}, bf16[384,1536]{1,0:T(8,128)(2,1)}, bf16[1536,384]{1,0:T(8,128)(2,1)}, f32[16,1536]{1,0:T(8,128)}) custom-call(s32[62]{0:T(128)} %concatenate.30.table, bf16[16,448,128]{2,1,0:T(8,128)(2,1)} %constant_dynamic-update-slice_fusion.near, ...), custom_call_target="tpu_custom_call" | custom-call | tf_op jit(solution)/shard_map/unpack/pallas_call | solution.py:798
  78.4 13.9 %forward.1 = (bf16[256,384]{1,0:T(8,128)(2,1)}, bf16[272,384]{1,0:T(8,128)(2,1)}, bf16[256,384]{1,0:T(8,128)(2,1)}, bf16[13,256,384]{2,1,0:T(8,128)(2,1)}, bf16[...) custom-call(s32[62]{0:T(128)} %concatenate.30.table, ...), custom_call_target="tpu_custom_call" | custom-call | tf_op jit(solution)/shard_map/forward/pallas_call | solution.py:800
  92.3 3.8 %collective-permute-start.18 = (bf16[1,272,384]{2,1,0:T(8,128)(2,1)}, bf16[1,272,384]{2,1,0:T(8,128)(2,1)S(1)}, u32[]{:S(2)}, u32[]{:S(2)}) collective-permute-start(bf16[1,272,384]{2,1,0:T(8,128)(2,1)} %bitcast.36), channel_id=1, source_target_pairs={{0,6},{1,7},{2,4},{3,5},{4,2},{5,3},{6,0},{7,1},{8,14},{9,15},{10,... | collective-permute-start | bytes 626696 | tf_op jit(solution)/shard_map/ppermute | solution.py:89
  96.1 3.7 %collective-permute-start.17 = (bf16[1,272,384]{2,1,0:T(8,128)(2,1)}, bf16[1,272,384]{2,1,0:T(8,128)(2,1)S(1)}, u32[]{:S(2)}, u32[]{:S(2)}) collective-permute-start(bf16[1,272,384]{2,1,0:T(8,128)(2,1)} %bitcast.37), channel_id=1, source_target_pairs={{0,4},{1,5},{2,6},{3,7},{4,0},{5,1},{6,2},{7,3},{8,12},{9,13},{10,... | collective-permute-start | bytes 626696 | tf_op jit(solution)/shard_map/ppermute | solution.py:89
  99.8 5.0 %collective-permute-start.20 = (bf16[1,272,384]{2,1,0:T(8,128)(2,1)}, bf16[1,272,384]{2,1,0:T(8,128)(2,1)S(1)}, u32[]{:S(2)}, u32[]{:S(2)}) collective-permute-start(bf16[1,272,384]{2,1,0:T(8,128)(2,1)} %bitcast.38), channel_id=1, source_target_pairs={{0,3},{1,2},{2,1},{3,0},{4,7},{5,6},{6,5},{7,4},{8,11},{9,10},{10,... | collective-permute-start | bytes 626696 | tf_op jit(solution)/shard_map/ppermute | solution.py:89
  108.8 5.6 %collective-permute-done.19 = bf16[1,272,384]{2,1,0:T(8,128)(2,1)S(1)} collective-permute-done((bf16[1,272,384]{2,1,0:T(8,128)(2,1)}, bf16[1,272,384]{2,1,0:T(8,128)(2,1)S(1)}, u32[]{:S(2)}, u32[]{:S(2)}) %collective-permute-start.19) | collective-permute-done | bytes 208928 | tf_op jit(solution)/shard_map/ppermute | solution.py:89
  117.7 10.4 %collective-permute-done.16 = bf16[1,272,384]{2,1,0:T(8,128)(2,1)S(1)} collective-permute-done((bf16[1,272,384]{2,1,0:T(8,128)(2,1)S(1)}, bf16[1,272,384]{2,1,0:T(8,128)(2,1)S(1)}, u32[]{:S(2)}, u32[]{:S(2)}) %collective-permute-start.16) | collective-permute-done | bytes 208928 | tf_op jit(solution)/shard_map/ppermute | solution.py:89
  128.4 8.1 %collective-permute-start.22 = (bf16[8,272,384]{2,1,0:T(8,128)(2,1)S(1)}, bf16[8,272,384]{2,1,0:T(8,128)(2,1)}, u32[]{:S(2)}, u32[]{:S(2)}) collective-permute-start(bf16[8,272,384]{2,1,0:T(8,128)(2,1)S(1)} %pad_maximum_fusion.refs_0_), channel_id=1, source_target_pairs={{0,8},{1,9},{2,10},{3,11},{4,12},{5,13},{6,14},{7,15},{8,0},{9,1},... | collective-permute-start | bytes 5013512 | tf_op jit(solution)/shard_map/ppermute | solution.py:89
  138.7 8.2 %query.1.refs_9_ = bf16[256,384]{1,0:T(8,128)(2,1)} custom-call(s32[62]{0:T(128)} %concatenate.30.table, bf16[256,384]{1,0:T(8,128)(2,1)} %get-tuple-element.71.q_ref, bf16[13,256,384]{2,1,0:T(8,128)(2,1)} %get-tuple-element.72.k_ref, bf16[13,256,384]{2,1,0:T(8,128)(2,1)} %get-tuple-element.73.v_ref, bf16[272,384]{1,0:T(8,128)(2,1)} %get-tuple-element.57.msg_ref, ...), custom_call_target="tpu_custom_call" | custom-call | tf_op jit(solution)/shard_map/query/pallas_call | solution.py:867
  146.9 8.1 %weight.1 = (bf16[13,256,384]{2,1,0:T(8,128)(2,1)}, bf16[16,448,128]{2,1,0:T(8,128)(2,1)}, bf16[16,448,128]{2,1,0:T(8,128)(2,1)}, f32[448,128]{1,0:T(8,128)}) custom-call(s32[62]{0:T(128)} %concatenate.30.table, bf16[13,256,384]{2,1,0:T(8,128)(2,1)} %get-tuple-element.60.norm_ref, bf16[384,1152]{1,0:T(8,128)(2,1)} %get-tuple-element.49.refs_4_.triple_ref.refs_11_, ...), custom_call_target="tpu_custom_call" | custom-call | tf_op jit(solution)/shard_map/weight/pallas_call | solution.py:884
  156.0 10.9 %last.1 = (f32[256,384]{1,0:T(8,128)}, bf16[16,448,128]{2,1,0:T(8,128)(2,1)}, bf16[16,448,128]{2,1,0:T(8,128)(2,1)}) custom-call(s32[62]{0:T(128)} %concatenate.30.table, bf16[8,272,384]{2,1,0:T(8,128)(2,1)} %copy-done, bf16[8,272,384]{2,1,0:T(8,128)(2,1)} %collective-permute-done.22.refs_1_, ...), custom_call_target="tpu_custom_call", output_to_operand_aliasing={{1}: (17, {}), {2}: (18, {})} | custom-call | tf_op jit(solution)/shard_map/last/pallas_call | solution.py:889
  166.9 23.3 %collective-permute-start.25 = (bf16[16,448,128]{2,1,0:T(8,128)(2,1)}, bf16[16,448,128]{2,1,0:T(8,128)(2,1)S(1)}, u32[]{:S(2)}, u32[]{:S(2)}) collective-permute-start(bf16[16,448,128]{2,1,0:T(8,128)(2,1)} %get-tuple-element.82), channel_id=1, source_target_pairs={{0,8},{1,9},{2,10},{3,11},{4,12},{5,13},{6,14},{7,15},{8,0},{9,1},... | collective-permute-start | bytes 5505032 | tf_op jit(solution)/shard_map/ppermute | solution.py:89
  190.2 3.6 %collective-permute-done.25 = bf16[16,448,128]{2,1,0:T(8,128)(2,1)S(1)} collective-permute-done((bf16[16,448,128]{2,1,0:T(8,128)(2,1)}, bf16[16,448,128]{2,1,0:T(8,128)(2,1)S(1)}, u32[]{:S(2)}, u32[]{:S(2)}) %collective-permute-start.25) | collective-permute-done | bytes 1835040 | tf_op jit(solution)/shard_map/ppermute | solution.py:89
  199.5 9.9 %collective-permute-done.26 = bf16[4,448,128]{2,1,0:T(8,128)(2,1)S(1)} collective-permute-done((bf16[4,448,128]{2,1,0:T(8,128)(2,1)S(1)}, bf16[4,448,128]{2,1,0:T(8,128)(2,1)S(1)}, u32[]{:S(2)}, u32[]{:S(2)}) %collective-permute-start.26) | collective-permute-done | bytes 458784 | tf_op jit(solution)/shard_map/ppermute | solution.py:89
  209.4 7.1 %collective-permute-done.28 = bf16[4,448,128]{2,1,0:T(8,128)(2,1)S(1)} collective-permute-done((bf16[4,448,128]{2,1,0:T(8,128)(2,1)S(1)}, bf16[4,448,128]{2,1,0:T(8,128)(2,1)S(1)}, u32[]{:S(2)}, u32[]{:S(2)}) %collective-permute-start.28) | collective-permute-done | bytes 458784 | tf_op jit(solution)/shard_map/ppermute | solution.py:89
  220.5 5.9 %collective-permute-start.30 = (bf16[1,448,128]{2,1,0:T(8,128)(2,1)S(1)}, bf16[1,448,128]{2,1,0:T(8,128)(2,1)S(1)}, u32[]{:S(2)}, u32[]{:S(2)}) collective-permute-start(bf16[1,448,128]{2,1,0:T(8,128)(2,1)S(1)} %get-tuple-element.97), channel_id=1, source_target_pairs={{0,4},{1,5},{2,6},{3,7},{4,0},{5,1},{6,2},{7,3},{8,12},{9,13},{10,... | collective-permute-start | bytes 344072 | tf_op jit(solution)/shard_map/ppermute | solution.py:89
  227.8 7.0 %collective-permute-done.30 = bf16[1,448,128]{2,1,0:T(8,128)(2,1)S(1)} collective-permute-done((bf16[1,448,128]{2,1,0:T(8,128)(2,1)S(1)}, bf16[1,448,128]{2,1,0:T(8,128)(2,1)S(1)}, u32[]{:S(2)}, u32[]{:S(2)}) %collective-permute-start.30) | collective-permute-done | bytes 114720 | tf_op jit(solution)/shard_map/ppermute | solution.py:89
  237.4 9.7 %all_to_all.12 = f32[32,1,128]{2,1,0:T(1,128)S(1)} all-to-all(f32[32,1,128]{2,1,0:T(1,128)} %bitcast.53), channel_id=1, replica_groups=mesh['dp'=4,'fsdp'=8] {'dp','fsdp'}, dimensions={0} | all-to-all | bytes 32768 | tf_op jit(solution)/shard_map/all_to_all | solution.py:942
  (107 shorter events, 65.0 us)
Async XLA Ops:
  0.6 44.9 %collective-permute-start.3 = (bf16[1,256,384]{2,1,0:T(8,128)(2,1)}, bf16[1,256,384]{2,1,0:T(8,128)(2,1)S(1)}, u32[]{:S(2)}, u32[]{:S(2)}) collective-permute-start(bf16[1,256,384]{2,1,0:T(8,128)(2,1)} %bitcast.42), channel_id=1, source_target_pairs={{0,3},{1,2},{2,1},{3,0},{4,7},{5,6},{6,5},{7,4},{8,11},{9,10},{10,... | collective-permute-start | bytes 589832 | tf_op jit(solution)/shard_map/ppermute | solution.py:89
  4.7 42.3 %collective-permute-start.2 = (bf16[1,256,384]{2,1,0:T(8,128)(2,1)}, bf16[1,256,384]{2,1,0:T(8,128)(2,1)S(1)}, u32[]{:S(2)}, u32[]{:S(2)}) collective-permute-start(bf16[1,256,384]{2,1,0:T(8,128)(2,1)} %bitcast.43), channel_id=1, source_target_pairs={{0,2},{1,3},{2,0},{3,1},{4,6},{5,7},{6,4},{7,5},{8,10},{9,11},{10,... | collective-permute-start | bytes 589832 | tf_op jit(solution)/shard_map/ppermute | solution.py:89
  8.6 15.6 %collective-permute-start.11 = (bf16[1,448,128]{2,1,0:T(8,128)(2,1)}, bf16[1,448,128]{2,1,0:T(8,128)(2,1)S(1)}, u32[]{:S(2)}, u32[]{:S(2)}) collective-permute-start(bf16[1,448,128]{2,1,0:T(8,128)(2,1)} %bitcast.32), channel_id=1, source_target_pairs={{0,6},{1,7},{2,4},{3,5},{4,2},{5,3},{6,0},{7,1},{8,14},{9,15},{10,... | collective-permute-start | bytes 344072 | tf_op jit(solution)/shard_map/ppermute | solution.py:89
  12.2 15.7 %collective-permute-start.10 = (bf16[1,448,128]{2,1,0:T(8,128)(2,1)}, bf16[1,448,128]{2,1,0:T(8,128)(2,1)S(1)}, u32[]{:S(2)}, u32[]{:S(2)}) collective-permute-start(bf16[1,448,128]{2,1,0:T(8,128)(2,1)} %bitcast.33), channel_id=1, source_target_pairs={{0,4},{1,5},{2,6},{3,7},{4,0},{5,1},{6,2},{7,3},{8,12},{9,13},{10,... | collective-permute-start | bytes 344072 | tf_op jit(solution)/shard_map/ppermute | solution.py:89
  12.2 15.7 %collective-permute-start.9 = (bf16[1,448,128]{2,1,0:T(8,128)(2,1)}, bf16[1,448,128]{2,1,0:T(8,128)(2,1)S(1)}, u32[]{:S(2)}, u32[]{:S(2)}) collective-permute-start(bf16[1,448,128]{2,1,0:T(8,128)(2,1)} %bitcast.34), channel_id=1, source_target_pairs={{0,2},{1,3},{2,0},{3,1},{4,6},{5,7},{6,4},{7,5},{8,10},{9,11},{10,... | collective-permute-start | bytes 344072 | tf_op jit(solution)/shard_map/ppermute | solution.py:89
  27.8 15.4 %collective-permute-start = (bf16[1,256,384]{2,1,0:T(8,128)(2,1)}, bf16[1,256,384]{2,1,0:T(8,128)(2,1)S(1)}, u32[]{:S(2)}, u32[]{:S(2)}) collective-permute-start(bf16[1,256,384]{2,1,0:T(8,128)(2,1)} %bitcast.45), channel_id=1, source_target_pairs={{0,4},{1,5},{2,6},{3,7},{4,0},{5,1},{6,2},{7,3},{8,12},{9,13},{10,... | collective-permute-start | bytes 589832 | tf_op jit(solution)/shard_map/ppermute | solution.py:89
  28.8 19.6 %collective-permute-start.12 = (bf16[4,448,128]{2,1,0:T(8,128)(2,1)S(1)}, bf16[4,448,128]{2,1,0:T(8,128)(2,1)S(1)}, u32[]{:S(2)}, u32[]{:S(2)}) collective-permute-start(bf16[4,448,128]{2,1,0:T(8,128)(2,1)S(1)} %pad_maximum_fusion.4), channel_id=1, source_target_pairs={{0,16},{1,17},{2,18},{3,19},{4,20},{5,21},{6,22},{7,23},{8,24},{9,... | collective-permute-start | bytes 1376264 | tf_op jit(solution)/shard_map/ppermute | solution.py:89
  33.8 15.5 %collective-permute-start.13 = (bf16[4,448,128]{2,1,0:T(8,128)(2,1)S(1)}, bf16[4,448,128]{2,1,0:T(8,128)(2,1)S(1)}, u32[]{:S(2)}, u32[]{:S(2)}) collective-permute-start(bf16[4,448,128]{2,1,0:T(8,128)(2,1)S(1)} %pad_maximum_fusion.4), channel_id=1, source_target_pairs={{0,1},{1,0},{2,3},{3,2},{4,5},{5,4},{6,7},{7,6},{8,9},{9,8},{10,11... | collective-permute-start | bytes 1376264 | tf_op jit(solution)/shard_map/ppermute | solution.py:89
  43.3 12.5 %collective-permute-start.14 = (bf16[4,448,128]{2,1,0:T(8,128)(2,1)S(1)}, bf16[4,448,128]{2,1,0:T(8,128)(2,1)S(1)}, u32[]{:S(2)}, u32[]{:S(2)}) collective-permute-start(bf16[4,448,128]{2,1,0:T(8,128)(2,1)S(1)} %pad_maximum_fusion.4), channel_id=1, source_target_pairs={{0,17},{1,16},{2,19},{3,18},{4,21},{5,20},{6,23},{7,22},{8,25},{9,... | collective-permute-start | bytes 1376264 | tf_op jit(solution)/shard_map/ppermute | solution.py:89
  45.5 14.5 %collective-permute-start.4 = (bf16[1,256,384]{2,1,0:T(8,128)(2,1)S(1)}, bf16[1,256,384]{2,1,0:T(8,128)(2,1)S(1)}, u32[]{:S(2)}, u32[]{:S(2)}) collective-permute-start(bf16[1,256,384]{2,1,0:T(8,128)(2,1)S(1)} %bitcast.46), channel_id=1, source_target_pairs={{0,1},{1,0},{2,3},{3,2},{4,5},{5,4},{6,7},{7,6},{8,9},{9,8},{10,11... | collective-permute-start | bytes 589832 | tf_op jit(solution)/shard_map/ppermute | solution.py:89
  47.9 20.5 %collective-permute-start.5 = (bf16[2,256,384]{2,1,0:T(8,128)(2,1)}, bf16[2,256,384]{2,1,0:T(8,128)(2,1)S(1)}, u32[]{:S(2)}, u32[]{:S(2)}) collective-permute-start(bf16[2,256,384]{2,1,0:T(8,128)(2,1)} %pad_maximum_fusion.6), channel_id=1, source_target_pairs={{0,1},{1,0},{2,3},{3,2},{4,5},{5,4},{6,7},{7,6},{8,9},{9,8},{10,11... | collective-permute-start | bytes 1179656 | tf_op jit(solution)/shard_map/ppermute | solution.py:89
  56.6 15.0 %collective-permute-start.15 = (bf16[16,448,128]{2,1,0:T(8,128)(2,1)}, bf16[16,448,128]{2,1,0:T(8,128)(2,1)}, u32[]{:S(2)}, u32[]{:S(2)}) collective-permute-start(bf16[16,448,128]{2,1,0:T(8,128)(2,1)} %constant_dynamic-update-slice_fusion.near), channel_id=1, source_target_pairs={{0,8},{1,9},{2,10},{3,11},{4,12},{5,13},{6,14},{7,15},{8,0},{9,1},... | collective-permute-start | bytes 5505032 | tf_op jit(solution)/shard_map/ppermute | solution.py:89
  92.3 15.8 %collective-permute-start.18 = (bf16[1,272,384]{2,1,0:T(8,128)(2,1)}, bf16[1,272,384]{2,1,0:T(8,128)(2,1)S(1)}, u32[]{:S(2)}, u32[]{:S(2)}) collective-permute-start(bf16[1,272,384]{2,1,0:T(8,128)(2,1)} %bitcast.36), channel_id=1, source_target_pairs={{0,6},{1,7},{2,4},{3,5},{4,2},{5,3},{6,0},{7,1},{8,14},{9,15},{10,... | collective-permute-start | bytes 626696 | tf_op jit(solution)/shard_map/ppermute | solution.py:89
  96.1 12.1 %collective-permute-start.17 = (bf16[1,272,384]{2,1,0:T(8,128)(2,1)}, bf16[1,272,384]{2,1,0:T(8,128)(2,1)S(1)}, u32[]{:S(2)}, u32[]{:S(2)}) collective-permute-start(bf16[1,272,384]{2,1,0:T(8,128)(2,1)} %bitcast.37), channel_id=1, source_target_pairs={{0,4},{1,5},{2,6},{3,7},{4,0},{5,1},{6,2},{7,3},{8,12},{9,13},{10,... | collective-permute-start | bytes 626696 | tf_op jit(solution)/shard_map/ppermute | solution.py:89
  114.5 13.7 %collective-permute-start.21 = (bf16[2,272,384]{2,1,0:T(8,128)(2,1)S(1)}, bf16[2,272,384]{2,1,0:T(8,128)(2,1)S(1)}, u32[]{:S(2)}, u32[]{:S(2)}) collective-permute-start(bf16[2,272,384]{2,1,0:T(8,128)(2,1)S(1)} %pad_maximum_fusion.5), channel_id=1, source_target_pairs={{0,1},{1,0},{2,3},{3,2},{4,5},{5,4},{6,7},{7,6},{8,9},{9,8},{10,11... | collective-permute-start | bytes 1253384 | tf_op jit(solution)/shard_map/ppermute | solution.py:89
  117.7 10.5 %collective-permute-start.16 = (bf16[1,272,384]{2,1,0:T(8,128)(2,1)S(1)}, bf16[1,272,384]{2,1,0:T(8,128)(2,1)S(1)}, u32[]{:S(2)}, u32[]{:S(2)}) collective-permute-start(bf16[1,272,384]{2,1,0:T(8,128)(2,1)S(1)} %bitcast.40), channel_id=1, source_target_pairs={{0,1},{1,0},{2,3},{3,2},{4,5},{5,4},{6,7},{7,6},{8,9},{9,8},{10,11... | collective-permute-start | bytes 626696 | tf_op jit(solution)/shard_map/ppermute | solution.py:89
  128.4 26.6 %collective-permute-start.22 = (bf16[8,272,384]{2,1,0:T(8,128)(2,1)S(1)}, bf16[8,272,384]{2,1,0:T(8,128)(2,1)}, u32[]{:S(2)}, u32[]{:S(2)}) collective-permute-start(bf16[8,272,384]{2,1,0:T(8,128)(2,1)S(1)} %pad_maximum_fusion.refs_0_), channel_id=1, source_target_pairs={{0,8},{1,9},{2,10},{3,11},{4,12},{5,13},{6,14},{7,15},{8,0},{9,1},... | collective-permute-start | bytes 5013512 | tf_op jit(solution)/shard_map/ppermute | solution.py:89
  136.5 18.5 %collective-permute-start.23 = (bf16[4,272,384]{2,1,0:T(8,128)(2,1)S(1)}, bf16[4,272,384]{2,1,0:T(8,128)(2,1)S(1)}, u32[]{:S(2)}, u32[]{:S(2)}) collective-permute-start(bf16[4,272,384]{2,1,0:T(8,128)(2,1)S(1)} %pad_maximum_fusion.2), channel_id=1, source_target_pairs={{8,16},{9,17},{10,18},{11,19},{12,20},{13,21},{14,22},{15,23},{16,... | collective-permute-start | bytes 2506760 | tf_op jit(solution)/shard_map/ppermute | solution.py:120
  137.2 17.7 %collective-permute-start.24 = (bf16[2,272,384]{2,1,0:T(8,128)(2,1)S(1)}, bf16[2,272,384]{2,1,0:T(8,128)(2,1)}, u32[]{:S(2)}, u32[]{:S(2)}) collective-permute-start(bf16[2,272,384]{2,1,0:T(8,128)(2,1)S(1)} %pad_maximum_fusion.5), channel_id=1, source_target_pairs={{8,17},{9,16},{10,19},{11,18},{12,21},{13,20},{14,23},{15,22},{16,... | collective-permute-start | bytes 1253384 | tf_op jit(solution)/shard_map/ppermute | solution.py:121
  166.9 26.9 %collective-permute-start.25 = (bf16[16,448,128]{2,1,0:T(8,128)(2,1)}, bf16[16,448,128]{2,1,0:T(8,128)(2,1)S(1)}, u32[]{:S(2)}, u32[]{:S(2)}) collective-permute-start(bf16[16,448,128]{2,1,0:T(8,128)(2,1)} %get-tuple-element.82), channel_id=1, source_target_pairs={{0,8},{1,9},{2,10},{3,11},{4,12},{5,13},{6,14},{7,15},{8,0},{9,1},... | collective-permute-start | bytes 5505032 | tf_op jit(solution)/shard_map/ppermute | solution.py:89
  195.9 13.5 %collective-permute-start.26 = (bf16[4,448,128]{2,1,0:T(8,128)(2,1)S(1)}, bf16[4,448,128]{2,1,0:T(8,128)(2,1)S(1)}, u32[]{:S(2)}, u32[]{:S(2)}) collective-permute-start(bf16[4,448,128]{2,1,0:T(8,128)(2,1)S(1)} %get-tuple-element.93), channel_id=1, source_target_pairs={{0,16},{1,17},{2,18},{3,19},{4,20},{5,21},{6,22},{7,23},{8,24},{9,... | collective-permute-start | bytes 1376264 | tf_op jit(solution)/shard_map/ppermute | solution.py:89
  196.0 20.5 %collective-permute-start.28 = (bf16[4,448,128]{2,1,0:T(8,128)(2,1)S(1)}, bf16[4,448,128]{2,1,0:T(8,128)(2,1)S(1)}, u32[]{:S(2)}, u32[]{:S(2)}) collective-permute-start(bf16[4,448,128]{2,1,0:T(8,128)(2,1)S(1)} %get-tuple-element.94), channel_id=1, source_target_pairs={{0,17},{1,16},{2,19},{3,18},{4,21},{5,20},{6,23},{7,22},{8,25},{9,... | collective-permute-start | bytes 1376264 | tf_op jit(solution)/shard_map/ppermute | solution.py:89
  196.1 23.5 %collective-permute-start.27 = (bf16[4,448,128]{2,1,0:T(8,128)(2,1)S(1)}, bf16[4,448,128]{2,1,0:T(8,128)(2,1)S(1)}, u32[]{:S(2)}, u32[]{:S(2)}) collective-permute-start(bf16[4,448,128]{2,1,0:T(8,128)(2,1)S(1)} %get-tuple-element.95), channel_id=1, source_target_pairs={{0,1},{1,0},{2,3},{3,2},{4,5},{5,4},{6,7},{7,6},{8,9},{9,8},{10,11... | collective-permute-start | bytes 1376264 | tf_op jit(solution)/shard_map/ppermute | solution.py:89
  220.5 14.3 %collective-permute-start.30 = (bf16[1,448,128]{2,1,0:T(8,128)(2,1)S(1)}, bf16[1,448,128]{2,1,0:T(8,128)(2,1)S(1)}, u32[]{:S(2)}, u32[]{:S(2)}) collective-permute-start(bf16[1,448,128]{2,1,0:T(8,128)(2,1)S(1)} %get-tuple-element.97), channel_id=1, source_target_pairs={{0,4},{1,5},{2,6},{3,7},{4,0},{5,1},{6,2},{7,3},{8,12},{9,13},{10,... | collective-permute-start | bytes 344072 | tf_op jit(solution)/shard_map/ppermute | solution.py:89
  (21 other events, 339.1 us)

commit v4 on v3

--- a/solution.py
+++ b/solution.py
@@ -68,7 +68,7 @@
         self.rows = -(-self.rows // 16) * 16
         self.start = [e * share // LANES for e in range(self.count)]
         self.tokens = tokens
-        self.part = tokens
+        self.part = tokens // 2
         self.reach = (IMG - 2 + tokens) // tokens
         self.window = 2 * self.reach + 1
         self.grouped = dp == 4 and fsdp == 8 and self.reach <= 6
@@ -88,11 +88,17 @@
     def send(self, x, mask):
         return lax.ppermute(x, BOTH, [(i, i ^ mask) for i in range(self.count)])
 
-    def spread(self, own):
+    def spread(self, own, extra):
         buf = own[None]
-        for stage in self.stages[:-1]:
-            buf = jnp.concatenate([buf] + [self.send(buf, m) for m in stage], axis=0)
-        return buf, self.send(buf, self.stages[-1][0])
+        for level, stage in enumerate(self.stages[:-1]):
+            parts = [buf]
+            for m in stage:
+                parts.append(self.send(buf, m))
+            buf = jnp.concatenate(parts, axis=0)
+            if level == 0:
+                buf, extra = lax.optimization_barrier((buf, extra))
+        core = self.send(buf, self.stages[-1][0])
+        return buf, core, extra
 
     def reduce_parts(self, keep, away):
         parts = [keep, self.send(away, self.stages[-1][0])]
@@ -105,7 +111,7 @@
             parts = [split[0]] + [self.send(split[k + 1], m) for k, m in enumerate(stage)]
         return [part[0] for part in parts]
 
-    def exchange(self, block, extra=()):
+    def exchange(self, block):
         own = block[None]
         if self.grouped:
             hops = []
@@ -114,21 +120,22 @@
             one, two, three, four, six = hops
             pair = jnp.concatenate([four, six], axis=0)
             quad = jnp.concatenate([two, three, four, six], axis=0)
-            pair, quad, extra = lax.optimization_barrier((pair, quad, extra))
+            row = jnp.concatenate([own, one, quad], axis=0)
+            pair, quad, row = lax.optimization_barrier((pair, quad, row))
             across = [(8 + j, 16 + j) for j in range(8)] + [(16 + j, 8 + j) for j in range(8)]
             skew = [(a, b ^ 1) for a, b in across]
             far = lax.ppermute(quad, BOTH, across)
             far_beside = lax.ppermute(pair, BOTH, skew)
             beside = self.send(pair, 1)
-            row = jnp.concatenate([own, one, quad, beside], axis=0)
             home = self.send(row, 8)
-            return [row, home, far, far_beside], extra
+            home_beside = self.send(beside, 8)
+            return [row, beside, home, home_beside, far, far_beside]
         slots = []
         for slot in range(self.window):
             by = self.reach - slot
             pairs = [(i, i + by) for i in range(self.count) if 0 <= i + by < self.count]
             slots.append(own if by == 0 else lax.ppermute(own, BOTH, pairs))
-        return [jnp.concatenate(slots, axis=0)], extra
+        return [jnp.concatenate(slots, axis=0)]
 
     def table(self, device, spans, key_ids):
         e = jnp.arange(self.count, dtype=jnp.int32)
@@ -143,8 +150,8 @@
             pos = jnp.where(mask == 6, 5, jnp.where(mask == 5, 6, mask))
             cross = (other >> 3) ^ (device >> 3)
             late = pos >= 6
-            source = jnp.where(cross == 0, 0, jnp.where(cross == 1, 1, jnp.where(late, 3, 2)))
-            index = jnp.where(source >= 2, jnp.where(late, pos - 6, pos - 2), pos)
+            source = jnp.where(cross == 0, 0, jnp.where(cross == 1, 2, 4)) + jnp.where(late, 1, 0)
+            index = jnp.where(late, pos - 6, jnp.where(source == 4, pos - 2, pos))
         else:
             source = jnp.zeros_like(slot)
             index = slot
@@ -225,9 +232,45 @@
     return jnp.where(left, x[:half], x[half:])
 
 
+def halves(x):
+    part = x.shape[0] // 2
+    return jnp.concatenate([stacked(x[:part]), stacked(x[part:])], axis=0)
+
+
+def whole(x):
+    part = x.shape[0] // 2
+    return jnp.concatenate([unstacked(x[:part]), unstacked(x[part:])], axis=0)
+
+
 def tiled(ids, width):
+    part = ids.shape[0] // 2
     ids = jnp.concatenate([ids] * (width // LANES), axis=1)
-    return jnp.concatenate([ids, ids], axis=0)
+    return jnp.concatenate([ids[:part], ids[:part], ids[part:], ids[part:]], axis=0)
+
+
+def sweep(plan, table, body):
+    (a, b), (c, d) = plan.range_at(0), plan.range_at(1)
+    rows = 2 * plan.part
+
+    def loop(begin, finish, rows):
+        def step(w, carry):
+            body(w, rows)
+            return carry
+
+        lax.fori_loop(begin, finish, step, 0)
+
+    loop(table[a], table[c], slice(0, rows))
+    loop(table[c], table[b] + 1, slice(0, 2 * rows))
+    loop(table[b] + 1, table[d] + 1, slice(rows, 2 * rows))
+
+
+def block_copies(source, dest, sems, lo, hi, wait):
+    def step(slot, carry):
+        copy = pltpu.make_async_copy(source.at[slot], dest.at[slot], sems.at[slot])
+        copy.wait() if wait else copy.start()
+        return carry
+
+    lax.fori_loop(lo, hi + 1, step, 0)
 
 
 def scaled_query(low, weight, bias):
@@ -364,7 +407,7 @@
             kown_ref,
             vown_ref,
         ) = refs[8 + sources : 26 + sources]
-        xwin, scores, tops, sums, accs, mix, xsem = refs[26 + sources :]
+        xwin, n_buf, k_buf, v_buf, scores, tops, sums, accs, mix, xsem, ksem = refs[26 + sources :]
         lo = table[plan.low_at()]
         hi = table[plan.low_at() + 1]
 
@@ -378,73 +421,73 @@
         tbias = param("tbias")
         fetch_window(plan, table, wins, xwin, xsem, lo, hi, True)
 
+        saved = [(n_buf, norm_ref), (k_buf, k_ref), (v_buf, v_ref)]
+
         def project(w, carry):
             n, _ = normalized(xwin[w].astype(WIDE))
             low = (n * gain1 + shift1).astype(LOW)
-            norm_ref[w] = low
+            n_buf[w] = low
             kv = dot(low, triple_ref[:, D:], NN)
-            k_ref[w] = kv[:, :D].astype(LOW)
-            v_ref[w] = (kv[:, D:] + tbias[:, D:]).astype(LOW)
+            k_buf[w] = kv[:, :D].astype(LOW)
+            v_buf[w] = (kv[:, D:] + tbias[:, D:]).astype(LOW)
+            for i, (buf, ref) in enumerate(saved):
+                pltpu.make_async_copy(buf.at[w], ref.at[w], ksem.at[i, w]).start()
             return carry
 
         lax.fori_loop(lo, hi + 1, project, 0)
-        kown_ref[...] = k_ref[own]
-        vown_ref[...] = v_ref[own]
-        low = norm_ref[own]
+        kown_ref[...] = k_buf[own]
+        vown_ref[...] = v_buf[own]
+        low = n_buf[own]
         normed_ref[...] = low
         q_ref[...] = scaled_query(low, triple_ref[:, :D], tbias[:, :D])
 
-        lane = lax.broadcasted_iota(jnp.int32, (part, LANES), 1)
-        for c in range(T // part):
-            rows = slice(part * c, part * (c + 1))
-            at, to = plan.range_at(c)
-            begin, finish = table[at], table[to] + 1
-            qs = [stacked(q_ref[rows, LANES * p : LANES * (p + 1)]) for p in range(pairs)]
-            ids = tiled(col_ref[rows, :], T)
+        lane = lax.broadcasted_iota(jnp.int32, (T, LANES), 1)
+        qs = [halves(q_ref[:, LANES * p : LANES * (p + 1)]) for p in range(pairs)]
+        ids = tiled(col_ref[...], T)
+        for p in range(pairs):
+            tops[p] = jnp.full((2 * T, LANES), MASKED, WIDE)
+            sums[p] = jnp.zeros((2 * T, LANES), WIDE)
+            accs[p] = jnp.zeros((2 * T, LANES), WIDE)
+
+        def first(w, rows):
+            seen = ids[rows] == row_ref[pl.ds(w, 1), :]
             for p in range(pairs):
-                tops[p] = jnp.full((2 * part, LANES), MASKED, WIDE)
-                sums[p] = jnp.zeros((2 * part, LANES), WIDE)
-                accs[p] = jnp.zeros((2 * part, LANES), WIDE)
-
-            def first(w, carry, qs=qs, ids=ids):
-                seen = ids == row_ref[pl.ds(w, 1), :]
-                for p in range(pairs):
-                    s = dot(qs[p], k_ref[w, :, LANES * p : LANES * (p + 1)], NT)
-                    s = jnp.where(seen, s, MASKED)
-                    scores[p, w] = s
-                    top = tops[p]
-                    for j in range(0, T, LANES):
-                        top = jnp.maximum(top, s[:, j : j + LANES])
-                    tops[p] = top
-                return carry
-
-            lax.fori_loop(begin, finish, first, 0)
+                s = dot(qs[p][rows], k_buf[w, :, LANES * p : LANES * (p + 1)], NT)
+                s = jnp.where(seen, s, MASKED)
+                scores[p, w, rows, :] = s
+                top = tops[p, rows, :]
+                for j in range(0, T, LANES):
+                    top = jnp.maximum(top, s[:, j : j + LANES])
+                tops[p, rows, :] = top
+
+        sweep(plan, table, first)
+        for p in range(pairs):
+            top = jnp.max(tops[p], axis=1, keepdims=True)
+            tops[p] = jnp.broadcast_to(top, (2 * T, LANES))
+
+        def second(w, rows):
             for p in range(pairs):
-                top = jnp.max(tops[p], axis=1, keepdims=True)
-                tops[p] = jnp.broadcast_to(top, (2 * part, LANES))
-
-            def second(w, carry):
-                for p in range(pairs):
-                    top = jnp.concatenate([tops[p]] * (T // LANES), axis=1)
-                    e = jnp.exp(scores[p, w] - top)
-                    total = sums[p]
-                    for j in range(0, T, LANES):
-                        total = total + e[:, j : j + LANES]
-                    sums[p] = total
-                    value = v_ref[w, :, LANES * p : LANES * (p + 1)]
-                    accs[p] = accs[p] + dot(e.astype(LOW), value, NN)
-                return carry
-
-            lax.fori_loop(begin, finish, second, 0)
-            stats = jnp.zeros((part, LANES), WIDE)
-            for p in range(pairs):
-                total = jnp.sum(sums[p], axis=1, keepdims=True)
-                mixed = accs[p] / total
-                mix[rows, LANES * p : LANES * (p + 1)] = unstacked(mixed)
-                log = tops[p] + jnp.log(total)
-                stats = jnp.where(lane == 2 * p, log[:part], stats)
-                stats = jnp.where(lane == 2 * p + 1, log[part:], stats)
-            stat_ref[rows, :] = stats
+                top = jnp.concatenate([tops[p, rows, :]] * (T // LANES), axis=1)
+                e = jnp.exp(scores[p, w, rows, :] - top)
+                total = sums[p, rows, :]
+                for j in range(0, T, LANES):
+                    total = total + e[:, j : j + LANES]
+                sums[p, rows, :] = total
+                value = v_buf[w, :, LANES * p : LANES * (p + 1)]
+                accs[p, rows, :] = accs[p, rows, :] + dot(e.astype(LOW), value, NN)
+
+        sweep(plan, table, second)
+        stats = jnp.zeros((T, LANES), WIDE)
+        for p in range(pairs):
+            total = jnp.sum(sums[p], axis=1, keepdims=True)
+            mix[:, LANES * p : LANES * (p + 1)] = whole(accs[p] / total)
+            log = tops[p] + jnp.log(total)
+            for k in range(2):
+                at = part * k
+                column = jnp.concatenate(
+                    [log[at : at + part], log[2 * part + at : 3 * part + at]], axis=0
+                )
+                stats = jnp.where(lane == 2 * p + k, column, stats)
         att = mix[...]
         att_low = att.astype(LOW)
         att_ref[...] = att_low
@@ -478,8 +521,6 @@
         gatt = dot(gbo, wo[...], NT).astype(LOW)
         msg_ref[0:T, :] = gatt
         inner = gatt.astype(WIDE) * att
-        stats = stat_ref[...]
-        lane = lax.broadcasted_iota(jnp.int32, (T, LANES), 1)
         left = lane < HEAD_DIM
         for p in range(HEADS // 2):
             piece = inner[:, LANES * p : LANES * (p + 1)]
@@ -505,6 +546,8 @@
         vec_ref[4:5, :D] = column_sum(gn2)
         vec_ref[5:6, :D] = column_sum(gmid * branch_one)
         vec_ref[6:7, :D] = column_sum(gbo.astype(WIDE))
+        for i, (buf, ref) in enumerate(saved):
+            block_copies(buf, ref, ksem.at[i], lo, hi, True)
 
     return kernel
 
@@ -526,39 +569,57 @@
     pairs = HEADS // 2
 
     def kernel(
-        table, q_ref, k_ref, v_ref, msg_ref, stat_ref, col_ref, row_ref, gq_ref, logs, dots, accs
+        table,
+        q_ref,
+        k_ref,
+        v_ref,
+        msg_ref,
+        stat_ref,
+        col_ref,
+        row_ref,
+        gq_ref,
+        logs,
+        dots,
+        accs,
+        k_buf,
+        v_buf,
+        ksem,
+        vsem,
     ):
-        for c in range(T // part):
-            rows = slice(part * c, part * (c + 1))
-            at, to = plan.range_at(c)
-            begin, finish = table[at], table[to] + 1
-            qs = [stacked(q_ref[rows, LANES * p : LANES * (p + 1)]) for p in range(pairs)]
-            gs = [stacked(msg_ref[rows, LANES * p : LANES * (p + 1)]) for p in range(pairs)]
-            ids = tiled(col_ref[rows, :], T)
+        lo = table[plan.low_at()]
+        hi = table[plan.low_at() + 1]
+        block_copies(k_ref, k_buf, ksem, lo, hi, False)
+        block_copies(v_ref, v_buf, vsem, lo, hi, False)
+        qs = [halves(q_ref[:, LANES * p : LANES * (p + 1)]) for p in range(pairs)]
+        gs = [halves(msg_ref[0:T, LANES * p : LANES * (p + 1)]) for p in range(pairs)]
+        ids = tiled(col_ref[...], T)
+        for p in range(pairs):
+            for k in range(2):
+                for c in range(2):
+                    rows = slice(part * c, part * (c + 1))
+                    to = slice(part * (2 * c + k), part * (2 * c + k + 1))
+                    h = 2 * p + k
+                    logs[p, to, :] = jnp.broadcast_to(stat_ref[rows, h : h + 1], (part, LANES))
+                    h = h + HEADS
+                    dots[p, to, :] = jnp.broadcast_to(stat_ref[rows, h : h + 1], (part, LANES))
+            accs[p] = jnp.zeros((2 * T, LANES), WIDE)
+        block_copies(k_ref, k_buf, ksem, lo, hi, True)
+        block_copies(v_ref, v_buf, vsem, lo, hi, True)
+
+        def step(w, rows):
+            seen = ids[rows] == row_ref[pl.ds(w, 1), :]
             for p in range(pairs):
-                for k in range(2):
-                    h = 2 * p + k
-                    half = slice(part * k, part * (k + 1))
-                    logs[p, half, :] = jnp.broadcast_to(stat_ref[rows, h : h + 1], (part, LANES))
-                    h = h + HEADS
-                    dots[p, half, :] = jnp.broadcast_to(stat_ref[rows, h : h + 1], (part, LANES))
-                accs[p] = jnp.zeros((2 * part, LANES), WIDE)
-
-            def step(w, carry, qs=qs, gs=gs, ids=ids):
-                seen = ids == row_ref[pl.ds(w, 1), :]
-                for p in range(pairs):
-                    cols = slice(LANES * p, LANES * (p + 1))
-                    key = k_ref[w, :, cols]
-                    s = jnp.where(seen, dot(qs[p], key, NT), MASKED)
-                    prob = jnp.exp(s - jnp.concatenate([logs[p]] * (T // LANES), axis=1))
-                    inner = jnp.concatenate([dots[p]] * (T // LANES), axis=1)
-                    grad = prob * (dot(gs[p], v_ref[w, :, cols], NT) - inner)
-                    accs[p] = accs[p] + dot(grad.astype(LOW), key, NN)
-                return carry
-
-            lax.fori_loop(begin, finish, step, 0)
-            for p in range(pairs):
-                gq_ref[rows, LANES * p : LANES * (p + 1)] = (unstacked(accs[p]) * SCALE).astype(LOW)
+                cols = slice(LANES * p, LANES * (p + 1))
+                key = k_buf[w, :, cols]
+                s = jnp.where(seen, dot(qs[p][rows], key, NT), MASKED)
+                prob = jnp.exp(s - jnp.concatenate([logs[p, rows, :]] * (T // LANES), axis=1))
+                inner = jnp.concatenate([dots[p, rows, :]] * (T // LANES), axis=1)
+                grad = prob * (dot(gs[p][rows], v_buf[w, :, cols], NT) - inner)
+                accs[p, rows, :] = accs[p, rows, :] + dot(grad.astype(LOW), key, NN)
+
+        sweep(plan, table, step)
+        for p in range(pairs):
+            gq_ref[:, LANES * p : LANES * (p + 1)] = (whole(accs[p]) * SCALE).astype(LOW)
 
     return kernel
 
@@ -649,11 +710,21 @@
             keep_ref,
             away_ref,
         ) = refs[sources : sources + 17]
-        mwin, flat, gt, stage, stats, spare, acck, accv, msem, osem = refs[sources + 17 :]
+        mwin, q_buf, flat, gt, stage, stats, spare, acck, accv, msem, qsem, osem = refs[
+            sources + 17 :
+        ]
         lo = table[plan.low_at()]
         hi = table[plan.low_at() + 1]
         fetch_window(plan, table, wins, mwin, msem, lo, hi, False)
+        block_copies(q_ref, q_buf, qsem, lo, hi, False)
+        ks = [halves(k_ref[:, LANES * p : LANES * (p + 1)]) for p in range(pairs)]
+        vs = [halves(v_ref[:, LANES * p : LANES * (p + 1)]) for p in range(pairs)]
+        ids = tiled(col_ref[...], T)
+        for p in range(pairs):
+            acck[p] = jnp.zeros((2 * T, LANES), WIDE)
+            accv[p] = jnp.zeros((2 * T, LANES), WIDE)
         fetch_window(plan, table, wins, mwin, msem, lo, hi, True)
+        block_copies(q_ref, q_buf, qsem, lo, hi, True)
 
         def unpack(w, carry):
             got = mwin[w, T : T + 16, :].astype(WIDE)
@@ -663,46 +734,29 @@
             return carry
 
         lax.fori_loop(lo, hi + 1, unpack, 0)
-        for c in range(T // part):
-            rows = slice(part * c, part * (c + 1))
-            at, to = plan.range_at(c)
-            begin, finish = table[at], table[to] + 1
-            ks = [stacked(k_ref[rows, LANES * p : LANES * (p + 1)]) for p in range(pairs)]
-            vs = [stacked(v_ref[rows, LANES * p : LANES * (p + 1)]) for p in range(pairs)]
-            ids = tiled(col_ref[rows, :], T)
+
+        def step(w, rows):
+            seen = ids[rows] == row_ref[pl.ds(w, 1), :]
+            copies = (rows.stop - rows.start) // (2 * part)
+
+            def pair_rows(h):
+                two = [jnp.broadcast_to(stats[w, h + k : h + k + 1, :], (part, T)) for k in range(2)]
+                return jnp.concatenate(two * copies, axis=0)
+
             for p in range(pairs):
-                acck[p] = jnp.zeros((2 * part, LANES), WIDE)
-                accv[p] = jnp.zeros((2 * part, LANES), WIDE)
-
-            def step(w, carry, ks=ks, vs=vs, ids=ids):
-                seen = ids == row_ref[pl.ds(w, 1), :]
-
-                def pair_rows(h):
-                    return jnp.concatenate(
-                        [
-                            jnp.broadcast_to(stats[w, h + k : h + k + 1, :], (part, T))
-                            for k in range(2)
-                        ],
-                        axis=0,
-                    )
-
-                for p in range(pairs):
-                    cols = slice(LANES * p, LANES * (p + 1))
-                    q = q_ref[w, :, cols]
-                    g = mwin[w, 0:T, cols]
-                    s = jnp.where(seen, dot(ks[p], q, NT), MASKED)
-                    prob = jnp.exp(s - pair_rows(2 * p))
-                    grad = prob * (dot(vs[p], g, NT) - pair_rows(HEADS + 2 * p))
-                    acck[p] = acck[p] + dot(grad.astype(LOW), q, NN)
-                    accv[p] = accv[p] + dot(prob.astype(LOW), g, NN)
-                return carry
-
-            lax.fori_loop(begin, finish, step, 0)
-            for p in range(pairs):
-                gt[rows, D + LANES * p : D + LANES * (p + 1)] = unstacked(acck[p]).astype(LOW)
-                gt[rows, 2 * D + LANES * p : 2 * D + LANES * (p + 1)] = unstacked(accv[p]).astype(
-                    LOW
-                )
+                cols = slice(LANES * p, LANES * (p + 1))
+                q = q_buf[w, :, cols]
+                g = mwin[w, 0:T, cols]
+                s = jnp.where(seen, dot(ks[p][rows], q, NT), MASKED)
+                prob = jnp.exp(s - pair_rows(2 * p))
+                grad = prob * (dot(vs[p][rows], g, NT) - pair_rows(HEADS + 2 * p))
+                acck[p, rows, :] = acck[p, rows, :] + dot(grad.astype(LOW), q, NN)
+                accv[p, rows, :] = accv[p, rows, :] + dot(prob.astype(LOW), g, NN)
+
+        sweep(plan, table, step)
+        for p in range(pairs):
+            gt[:, D + LANES * p : D + LANES * (p + 1)] = whole(acck[p]).astype(LOW)
+            gt[:, 2 * D + LANES * p : 2 * D + LANES * (p + 1)] = whole(accv[p]).astype(LOW)
         gt[:, :D] = gq_ref[...]
         fold(flat, AT["triple"], normed_ref, gt, 3 * D)
         put_vector(flat, AT["tbias"], column_sum(gt[:, :D].astype(WIDE)))
@@ -757,12 +811,6 @@
     def per_device(inputs, cotangent, master, first_moment, second_moment, image_ids, spans):
         device = lax.axis_index(BOTH).astype(jnp.int32)
         shift = ((device * plan.share) % LANES).reshape(1).astype(jnp.int32)
-        padded = jnp.pad(image_ids, (plan.reach * T, plan.reach * T), constant_values=-1)
-        key_ids = lax.dynamic_slice_in_dim(padded, device * T, W * T, 0).reshape(W, T)
-        table = plan.table(device, spans, key_ids)
-        own_ids = key_ids[plan.reach]
-        columns = jnp.broadcast_to(own_ids[:, None], (T, LANES))
-
         shifted = pl.pallas_call(
             shift_kernel(plan),
             in_specs=[SMEM, VMEM],
@@ -771,11 +819,16 @@
             scratch_shapes=[pltpu.VMEM((R + 8, LANES), WIDE)],
             name="shift",
         )(shift, jnp.pad(master, (0, R * LANES - plan.share)).reshape(R, LANES))
-        near, core = plan.spread(shifted)
-        wins, (table, columns, key_ids) = plan.exchange(inputs, (table, columns, key_ids))
+        near, core, (image_ids, spans) = plan.spread(shifted, (image_ids, spans))
+        padded = jnp.pad(image_ids, (plan.reach * T, plan.reach * T), constant_values=-1)
+        key_ids = lax.dynamic_slice_in_dim(padded, device * T, W * T, 0).reshape(W, T)
+        table = plan.table(device, spans, key_ids)
+        own_ids = key_ids[plan.reach]
+        columns = jnp.broadcast_to(own_ids[:, None], (T, LANES))
+        wins = plan.exchange(inputs)
         sources = len(wins)
 
-        half = pltpu.VMEM((HEADS // 2, 2 * plan.part, LANES), WIDE)
+        half = pltpu.VMEM((HEADS // 2, 2 * T, LANES), WIDE)
         unpack = pl.pallas_call(
             unpack_kernel(plan),
             in_specs=[SMEM, ANY, ANY],
@@ -800,7 +853,7 @@
         outs = pl.pallas_call(
             forward_kernel(plan, sources),
             in_specs=[SMEM] + [ANY] * sources + [VMEM] * 8,
-            out_specs=[VMEM] * 18,
+            out_specs=[VMEM] * 3 + [ANY] * 3 + [VMEM] * 12,
             out_shape=[
                 shape((T, D), LOW),
                 shape((T + 16, D), LOW),
@@ -823,12 +876,16 @@
             ],
             scratch_shapes=[
                 pltpu.VMEM((W, T, D), LOW),
-                pltpu.VMEM((HEADS // 2, W, 2 * plan.part, T), WIDE),
+                pltpu.VMEM((W, T, D), LOW),
+                pltpu.VMEM((W, T, D), LOW),
+                pltpu.VMEM((W, T, D), LOW),
+                pltpu.VMEM((HEADS // 2, W, 2 * T, T), WIDE),
                 half,
                 half,
                 half,
                 pltpu.VMEM((T, D), WIDE),
                 pltpu.SemaphoreType.DMA((W,)),
+                pltpu.SemaphoreType.DMA((3, W)),
             ],
             compiler_params=limit,
             name="forward",
@@ -853,14 +910,22 @@
             k_own,
             v_own,
         ) = outs
-        messages, _ = plan.exchange(message)
+        messages = plan.exchange(message)
 
         query_call = pl.pallas_call(
             query_kernel(plan),
-            in_specs=[SMEM] + [VMEM] * 7,
+            in_specs=[SMEM, VMEM, ANY, ANY] + [VMEM] * 4,
             out_specs=VMEM,
             out_shape=shape((T, D), LOW),
-            scratch_shapes=[half] * 3,
+            scratch_shapes=[
+                half,
+                half,
+                half,
+                pltpu.VMEM((W, T, D), LOW),
+                pltpu.VMEM((W, T, D), LOW),
+                pltpu.SemaphoreType.DMA((W,)),
+                pltpu.SemaphoreType.DMA((W,)),
+            ],
             compiler_params=limit,
             name="query",
         )
@@ -888,7 +953,7 @@
         late = plan.first_late
         input_grad, keep, away = pl.pallas_call(
             last_kernel(plan, sources),
-            in_specs=[SMEM] + [ANY] * sources + [VMEM] * 12 + [ANY, ANY],
+            in_specs=[SMEM] + [ANY] * (sources + 1) + [VMEM] * 11 + [ANY, ANY],
             out_specs=[VMEM, ANY, ANY],
             out_shape=[
                 shape((T, D), WIDE),
@@ -897,6 +962,7 @@
             ],
             scratch_shapes=[
                 pltpu.VMEM((W, T + 16, D), LOW),
+                pltpu.VMEM((W, T, D), LOW),
                 pltpu.VMEM((AT["out"] + R + 8, LANES), WIDE),
                 pltpu.VMEM((T, 3 * D), LOW),
                 pltpu.VMEM((late, R, LANES), LOW),
@@ -904,6 +970,7 @@
                 pltpu.VMEM((24, T), WIDE),
                 half,
                 half,
+                pltpu.SemaphoreType.DMA((W,)),
                 pltpu.SemaphoreType.DMA((W,)),
                 pltpu.SemaphoreType.DMA((late,)),
             ],

time: 252 us -> 237 us (0.940)
  starting transfers between devices: 83.1 us -> 69.4 us
  local copies, waits for them, and re-layouts: 17.3 us -> 8.46 us
  waiting for transfers between devices: 76.7 us -> 84.8 us
    ppermute x28 -> x30, starting transfers between devices: 78 us -> 64.3 us  [send(): return lax.ppermute(x, BOTH, [(i, i ^ mask) for i in range(self.count)])]
    ppermute x28 -> x30, waiting for transfers between devices: 76.7 us -> 84.8 us  [send(): return lax.ppermute(x, BOTH, [(i, i ^ mask) for i in range(self.count)])]
    unnamed x32 -> x43, local copies, waits for them, and re-layouts: 7.94 us -> 3.47 us
  transfers between devices with their start and end apart: 32 -> 34, of which waited for: 15 -> 14; matrix products, arithmetic and copies ran while one was open for 8% -> 4% of each run, Pallas kernels for 9% -> 9%
where the time goes in v4:
time: 237 us; the launch traced here: 236 us
  waiting for transfers between devices  84.8 us (36%)
  starting transfers between devices  69.4 us (29%)
  Pallas kernels  50.4 us (21%)
  other arithmetic  10.3 us (4%)
  blocking collectives  9.69 us (4%)
  local copies, waits for them, and re-layouts  8.46 us (4%)
  between operations  2.99 us (1%)
    ppermute x30, waiting for transfers between devices, send(): return lax.ppermute(x, BOTH, [(i, i ^ mask) for i in range(self.count)])  84.8 us
    ppermute x30, starting transfers between devices, send(): return lax.ppermute(x, BOTH, [(i, i ^ mask) for i in range(self.count)])  64.3 us
    pallas_call x1, Pallas kernels, per_device(): pl.pallas_call(forward_kernel(plan, sources), in_specs=[SMEM] + [ANY] * s...  15 us
    pallas_call x1, Pallas kernels, per_device(): pl.pallas_call(last_kernel(plan, sources), in_specs=[SMEM] + [ANY] * (sou...  10.4 us
    all_to_all x1, blocking collectives, per_device(): squares = lax.all_to_all(square, BOTH, 0, 0, tiled=True)  9.69 us
    pallas_call x1, Pallas kernels, per_device(): weight_call(table, norms, triple, params, act, gpre, gbt, n2, att, gbo, vec)  8.09 us
    pallas_call x1, Pallas kernels, per_device(): gq = query_call(table, q, k, v, message, stat, columns, key_ids)  7.71 us
    pallas_call x1, Pallas kernels, per_device(): triple, wo, wup, wdn, params = unpack(table, near, core)  5.56 us
  transfers between devices with their start and end apart: 34, of which 14 were waited for; matrix products, arithmetic and copies ran while one was open for 4% of the time, Pallas kernels for 9%

profile of v4, /device:TPU:0, one launch (start us, length us, event | category | flops | bytes accessed | tf_op | source)
XLA Modules:
  0.0 236.1 jit_solution(14553261349373358768)
XLA Ops:
  4.1 5.1 %collective-permute-start.2 = (bf16[1,448,128]{2,1,0:T(8,128)(2,1)}, bf16[1,448,128]{2,1,0:T(8,128)(2,1)S(1)}, u32[]{:S(2)}, u32[]{:S(2)}) collective-permute-start(bf16[1,448,128]{2,1,0:T(8,128)(2,1)} %bitcast.31), channel_id=1, source_target_pairs={{0,6},{1,7},{2,4},{3,5},{4,2},{5,3},{6,0},{7,1},{8,14},{9,15},{10,... | collective-permute-start | bytes 344072 | tf_op jit(solution)/shard_map/ppermute | solution.py:89
  13.5 5.7 %collective-permute-done.1 = bf16[1,448,128]{2,1,0:T(8,128)(2,1)S(1)} collective-permute-done((bf16[1,448,128]{2,1,0:T(8,128)(2,1)}, bf16[1,448,128]{2,1,0:T(8,128)(2,1)S(1)}, u32[]{:S(2)}, u32[]{:S(2)}) %collective-permute-start.1) | collective-permute-done | bytes 114720 | tf_op jit(solution)/shard_map/ppermute | solution.py:89
  25.0 10.0 %collective-permute-done.13 = bf16[4,448,128]{2,1,0:T(8,128)(2,1)S(1)} collective-permute-done((bf16[4,448,128]{2,1,0:T(8,128)(2,1)S(1)}, bf16[4,448,128]{2,1,0:T(8,128)(2,1)S(1)}, u32[]{:S(2)}, u32[]{:S(2)}) %collective-permute-start.13) | collective-permute-done | bytes 458784 | tf_op jit(solution)/shard_map/ppermute | solution.py:89
  37.5 5.3 %collective-permute-start.3 = (bf16[1,256,384]{2,1,0:T(8,128)(2,1)S(1)}, bf16[1,256,384]{2,1,0:T(8,128)(2,1)S(1)}, u32[]{:S(2)}, u32[]{:S(2)}) collective-permute-start(bf16[1,256,384]{2,1,0:T(8,128)(2,1)S(1)} %bitcast.30), channel_id=1, source_target_pairs={{0,4},{1,5},{2,6},{3,7},{4,0},{5,1},{6,2},{7,3},{8,12},{9,13},{10,... | collective-permute-start | bytes 589832 | tf_op jit(solution)/shard_map/ppermute | solution.py:89
  43.2 3.3 %collective-permute-done.3 = bf16[1,256,384]{2,1,0:T(8,128)(2,1)S(1)} collective-permute-done((bf16[1,256,384]{2,1,0:T(8,128)(2,1)S(1)}, bf16[1,256,384]{2,1,0:T(8,128)(2,1)S(1)}, u32[]{:S(2)}, u32[]{:S(2)}) %collective-permute-start.3) | collective-permute-done | bytes 196640 | tf_op jit(solution)/shard_map/ppermute | solution.py:89
  54.1 6.4 %collective-permute-done.8.refs_1_ = bf16[2,256,384]{2,1,0:T(8,128)(2,1)} collective-permute-done((bf16[2,256,384]{2,1,0:T(8,128)(2,1)}, bf16[2,256,384]{2,1,0:T(8,128)(2,1)}, u32[]{:S(2)}, u32[]{:S(2)}) %collective-permute-start.8) | collective-permute-done | bytes 393248 | tf_op jit(solution)/shard_map/ppermute | solution.py:89
  63.1 5.6 %unpack.1 = (bf16[384,1152]{1,0:T(8,128)(2,1)}, bf16[384,384]{1,0:T(8,128)(2,1)}, bf16[384,1536]{1,0:T(8,128)(2,1)}, bf16[1536,384]{1,0:T(8,128)(2,1)}, f32[16,1536]{1,0:T(8,128)}) custom-call(s32[64]{0:T(128)} %concatenate.30.table, bf16[16,448,128]{2,1,0:T(8,128)(2,1)} %copy-done, bf16[16,448,128]{2,1,0:T(8,128)(2,1)} %collective-permute-done.16.core), custom_call_target="tpu_custom_call" | custom-call | tf_op jit(solution)/shard_map/unpack/pallas_call | solution.py:851
  69.5 15.0 %forward.1 = (bf16[256,384]{1,0:T(8,128)(2,1)}, bf16[272,384]{1,0:T(8,128)(2,1)}, bf16[256,384]{1,0:T(8,128)(2,1)}, bf16[13,256,384]{2,1,0:T(8,128)(2,1)}, bf16[...) custom-call(s32[64]{0:T(128)} %concatenate.30.table, ...), custom_call_target="tpu_custom_call" | custom-call | tf_op jit(solution)/shard_map/forward/pallas_call | solution.py:853
  86.3 9.5 %collective-permute-start.20 = (bf16[1,272,384]{2,1,0:T(8,128)(2,1)}, bf16[1,272,384]{2,1,0:T(8,128)(2,1)S(1)}, u32[]{:S(2)}, u32[]{:S(2)}) collective-permute-start(bf16[1,272,384]{2,1,0:T(8,128)(2,1)} %bitcast.22), channel_id=1, source_target_pairs={{0,3},{1,2},{2,1},{3,0},{4,7},{5,6},{6,5},{7,4},{8,11},{9,10},{10,... | collective-permute-start | bytes 626696 | tf_op jit(solution)/shard_map/ppermute | solution.py:89
  100.3 10.3 %collective-permute-done.18 = bf16[1,272,384]{2,1,0:T(8,128)(2,1)S(1)} collective-permute-done((bf16[1,272,384]{2,1,0:T(8,128)(2,1)}, bf16[1,272,384]{2,1,0:T(8,128)(2,1)S(1)}, u32[]{:S(2)}, u32[]{:S(2)}) %collective-permute-start.18) | collective-permute-done | bytes 208928 | tf_op jit(solution)/shard_map/ppermute | solution.py:89
  110.6 7.5 %collective-permute-done.17 = bf16[1,272,384]{2,1,0:T(8,128)(2,1)S(1)} collective-permute-done((bf16[1,272,384]{2,1,0:T(8,128)(2,1)}, bf16[1,272,384]{2,1,0:T(8,128)(2,1)S(1)}, u32[]{:S(2)}, u32[]{:S(2)}) %collective-permute-start.17) | collective-permute-done | bytes 208928 | tf_op jit(solution)/shard_map/ppermute | solution.py:89
  123.4 8.3 %collective-permute-done.22.refs_1_ = bf16[2,272,384]{2,1,0:T(8,128)(2,1)} collective-permute-done((bf16[2,272,384]{2,1,0:T(8,128)(2,1)S(1)}, bf16[2,272,384]{2,1,0:T(8,128)(2,1)}, u32[]{:S(2)}, u32[]{:S(2)}) %collective-permute-start.22) | collective-permute-done | bytes 417824 | tf_op jit(solution)/shard_map/ppermute | solution.py:89
  131.7 7.7 %query.1.refs_11_ = bf16[256,384]{1,0:T(8,128)(2,1)} custom-call(s32[64]{0:T(128)} %concatenate.30.table, bf16[256,384]{1,0:T(8,128)(2,1)} %get-tuple-element.75.q_ref, bf16[13,256,384]{2,1,0:T(8,128)(2,1)} %get-tuple-element.76.k_ref, bf16[13,256,384]{2,1,0:T(8,128)(2,1)} %get-tuple-element.77.v_ref, bf16[272,384]{1,0:T(8,128)(2,1)} %get-tuple-element.60.msg_ref, ...), custom_call_target="tpu_custom_call" | custom-call | tf_op jit(solution)/shard_map/query/pallas_call | solution.py:932
  139.4 8.1 %weight.1 = (bf16[13,256,384]{2,1,0:T(8,128)(2,1)}, bf16[16,448,128]{2,1,0:T(8,128)(2,1)}, bf16[16,448,128]{2,1,0:T(8,128)(2,1)}, f32[448,128]{1,0:T(8,128)}) custom-call(s32[64]{0:T(128)} %concatenate.30.table, bf16[13,256,384]{2,1,0:T(8,128)(2,1)} %get-tuple-element.64.norm_ref, bf16[384,1152]{1,0:T(8,128)(2,1)} %get-tuple-element.54.refs_6_.triple_ref.refs_13_, ...), custom_call_target="tpu_custom_call" | custom-call | tf_op jit(solution)/shard_map/weight/pallas_call | solution.py:949
  148.9 10.4 %last.1 = (f32[256,384]{1,0:T(8,128)}, bf16[16,448,128]{2,1,0:T(8,128)(2,1)}, bf16[16,448,128]{2,1,0:T(8,128)(2,1)}) custom-call(s32[64]{0:T(128)} %concatenate.30.table, bf16[6,272,384]{2,1,0:T(8,128)(2,1)} %copy-done.1, bf16[2,272,384]{2,1,0:T(8,128)(2,1)} %collective-permute-done.22.refs_1_, ...), custom_call_target="tpu_custom_call", output_to_operand_aliasing={{1}: (19, {}), {2}: (20, {})} | custom-call | tf_op jit(solution)/shard_map/last/pallas_call | solution.py:954
  159.3 16.6 %collective-permute-start.27 = (bf16[16,448,128]{2,1,0:T(8,128)(2,1)}, bf16[16,448,128]{2,1,0:T(8,128)(2,1)S(1)}, u32[]{:S(2)}, u32[]{:S(2)}) collective-permute-start(bf16[16,448,128]{2,1,0:T(8,128)(2,1)} %get-tuple-element.86), channel_id=1, source_target_pairs={{0,8},{1,9},{2,10},{3,11},{4,12},{5,13},{6,14},{7,15},{8,0},{9,1},... | collective-permute-start | bytes 5505032 | tf_op jit(solution)/shard_map/ppermute | solution.py:89
  175.9 3.6 %collective-permute-done.27 = bf16[16,448,128]{2,1,0:T(8,128)(2,1)S(1)} collective-permute-done((bf16[16,448,128]{2,1,0:T(8,128)(2,1)}, bf16[16,448,128]{2,1,0:T(8,128)(2,1)S(1)}, u32[]{:S(2)}, u32[]{:S(2)}) %collective-permute-start.27) | collective-permute-done | bytes 1835040 | tf_op jit(solution)/shard_map/ppermute | solution.py:89
  182.0 3.2 %collective-permute-start.29 = (bf16[4,448,128]{2,1,0:T(8,128)(2,1)S(1)}, bf16[4,448,128]{2,1,0:T(8,128)(2,1)S(1)}, u32[]{:S(2)}, u32[]{:S(2)}) collective-permute-start(bf16[4,448,128]{2,1,0:T(8,128)(2,1)S(1)} %get-tuple-element.101), channel_id=1, source_target_pairs={{0,1},{1,0},{2,3},{3,2},{4,5},{5,4},{6,7},{7,6},{8,9},{9,8},{10,11... | collective-permute-start | bytes 1376264 | tf_op jit(solution)/shard_map/ppermute | solution.py:89
  185.2 9.9 %collective-permute-done.28 = bf16[4,448,128]{2,1,0:T(8,128)(2,1)S(1)} collective-permute-done((bf16[4,448,128]{2,1,0:T(8,128)(2,1)S(1)}, bf16[4,448,128]{2,1,0:T(8,128)(2,1)S(1)}, u32[]{:S(2)}, u32[]{:S(2)}) %collective-permute-start.28) | collective-permute-done | bytes 458784 | tf_op jit(solution)/shard_map/ppermute | solution.py:89
  195.1 7.1 %collective-permute-done.30 = bf16[4,448,128]{2,1,0:T(8,128)(2,1)S(1)} collective-permute-done((bf16[4,448,128]{2,1,0:T(8,128)(2,1)S(1)}, bf16[4,448,128]{2,1,0:T(8,128)(2,1)S(1)}, u32[]{:S(2)}, u32[]{:S(2)}) %collective-permute-start.30) | collective-permute-done | bytes 458784 | tf_op jit(solution)/shard_map/ppermute | solution.py:89
  206.2 3.5 %collective-permute-start.32 = (bf16[1,448,128]{2,1,0:T(8,128)(2,1)S(1)}, bf16[1,448,128]{2,1,0:T(8,128)(2,1)S(1)}, u32[]{:S(2)}, u32[]{:S(2)}) collective-permute-start(bf16[1,448,128]{2,1,0:T(8,128)(2,1)S(1)} %get-tuple-element.103), channel_id=1, source_target_pairs={{0,4},{1,5},{2,6},{3,7},{4,0},{5,1},{6,2},{7,3},{8,12},{9,13},{10,... | collective-permute-start | bytes 344072 | tf_op jit(solution)/shard_map/ppermute | solution.py:89
  210.6 3.5 %collective-permute-done.33 = bf16[1,448,128]{2,1,0:T(8,128)(2,1)S(1)} collective-permute-done((bf16[1,448,128]{2,1,0:T(8,128)(2,1)S(1)}, bf16[1,448,128]{2,1,0:T(8,128)(2,1)S(1)}, u32[]{:S(2)}, u32[]{:S(2)}) %collective-permute-start.33) | collective-permute-done | bytes 114720 | tf_op jit(solution)/shard_map/ppermute | solution.py:89
  214.2 5.2 %collective-permute-done.32 = bf16[1,448,128]{2,1,0:T(8,128)(2,1)S(1)} collective-permute-done((bf16[1,448,128]{2,1,0:T(8,128)(2,1)S(1)}, bf16[1,448,128]{2,1,0:T(8,128)(2,1)S(1)}, u32[]{:S(2)}, u32[]{:S(2)}) %collective-permute-start.32) | collective-permute-done | bytes 114720 | tf_op jit(solution)/shard_map/ppermute | solution.py:89
  222.0 9.7 %all_to_all.12 = f32[32,1,128]{2,1,0:T(1,128)S(1)} all-to-all(f32[32,1,128]{2,1,0:T(1,128)} %bitcast.40), channel_id=1, replica_groups=mesh['dp'=4,'fsdp'=8] {'dp','fsdp'}, dimensions={0} | all-to-all | bytes 32768 | tf_op jit(solution)/shard_map/all_to_all | solution.py:1009
  (124 shorter events, 52.5 us)
Async XLA Ops:
  9.7 14.1 %collective-permute-start.7 = (bf16[1,256,384]{2,1,0:T(8,128)(2,1)}, bf16[1,256,384]{2,1,0:T(8,128)(2,1)S(1)}, u32[]{:S(2)}, u32[]{:S(2)}) collective-permute-start(bf16[1,256,384]{2,1,0:T(8,128)(2,1)} %bitcast.26), channel_id=1, source_target_pairs={{0,1},{1,0},{2,3},{3,2},{4,5},{5,4},{6,7},{7,6},{8,9},{9,8},{10,11... | collective-permute-start | bytes 589832 | tf_op jit(solution)/shard_map/ppermute | solution.py:89
  11.5 31.7 %collective-permute-start.6 = (bf16[1,256,384]{2,1,0:T(8,128)(2,1)}, bf16[1,256,384]{2,1,0:T(8,128)(2,1)S(1)}, u32[]{:S(2)}, u32[]{:S(2)}) collective-permute-start(bf16[1,256,384]{2,1,0:T(8,128)(2,1)} %bitcast.27), channel_id=1, source_target_pairs={{0,3},{1,2},{2,1},{3,0},{4,7},{5,6},{6,5},{7,4},{8,11},{9,10},{10,... | collective-permute-start | bytes 589832 | tf_op jit(solution)/shard_map/ppermute | solution.py:89
  20.1 17.4 %collective-permute-start.14 = (bf16[4,448,128]{2,1,0:T(8,128)(2,1)S(1)}, bf16[4,448,128]{2,1,0:T(8,128)(2,1)S(1)}, u32[]{:S(2)}, u32[]{:S(2)}) collective-permute-start(bf16[4,448,128]{2,1,0:T(8,128)(2,1)S(1)} %pad_maximum_fusion.2), channel_id=1, source_target_pairs={{0,1},{1,0},{2,3},{3,2},{4,5},{5,4},{6,7},{7,6},{8,9},{9,8},{10,11... | collective-permute-start | bytes 1376264 | tf_op jit(solution)/shard_map/ppermute | solution.py:89
  21.7 13.4 %collective-permute-start.13 = (bf16[4,448,128]{2,1,0:T(8,128)(2,1)S(1)}, bf16[4,448,128]{2,1,0:T(8,128)(2,1)S(1)}, u32[]{:S(2)}, u32[]{:S(2)}) collective-permute-start(bf16[4,448,128]{2,1,0:T(8,128)(2,1)S(1)} %pad_maximum_fusion.2), channel_id=1, source_target_pairs={{0,16},{1,17},{2,18},{3,19},{4,20},{5,21},{6,22},{7,23},{8,24},{9,... | collective-permute-start | bytes 1376264 | tf_op jit(solution)/shard_map/ppermute | solution.py:89
  23.2 19.7 %collective-permute-start.15 = (bf16[4,448,128]{2,1,0:T(8,128)(2,1)S(1)}, bf16[4,448,128]{2,1,0:T(8,128)(2,1)S(1)}, u32[]{:S(2)}, u32[]{:S(2)}) collective-permute-start(bf16[4,448,128]{2,1,0:T(8,128)(2,1)S(1)} %pad_maximum_fusion.2), channel_id=1, source_target_pairs={{0,17},{1,16},{2,19},{3,18},{4,21},{5,20},{6,23},{7,22},{8,25},{9,... | collective-permute-start | bytes 1376264 | tf_op jit(solution)/shard_map/ppermute | solution.py:89
  23.8 19.3 %collective-permute-start.5 = (bf16[1,256,384]{2,1,0:T(8,128)(2,1)S(1)}, bf16[1,256,384]{2,1,0:T(8,128)(2,1)S(1)}, u32[]{:S(2)}, u32[]{:S(2)}) collective-permute-start(bf16[1,256,384]{2,1,0:T(8,128)(2,1)S(1)} %bitcast.28), channel_id=1, source_target_pairs={{0,2},{1,3},{2,0},{3,1},{4,6},{5,7},{6,4},{7,5},{8,10},{9,11},{10,... | collective-permute-start | bytes 589832 | tf_op jit(solution)/shard_map/ppermute | solution.py:89
  43.0 20.1 %collective-permute-start.16 = (bf16[16,448,128]{2,1,0:T(8,128)(2,1)S(1)}, bf16[16,448,128]{2,1,0:T(8,128)(2,1)}, u32[]{:S(2)}, u32[]{:S(2)}) collective-permute-start(bf16[16,448,128]{2,1,0:T(8,128)(2,1)S(1)} %constant_dynamic-update-slice_fusion.6.near), channel_id=1, source_target_pairs={{0,8},{1,9},{2,10},{3,11},{4,12},{5,13},{6,14},{7,15},{8,0},{9,1},... | collective-permute-start | bytes 5505032 | tf_op jit(solution)/shard_map/ppermute | solution.py:89
  48.5 20.3 %collective-permute-start.9 = (bf16[6,256,384]{2,1,0:T(8,128)(2,1)S(1)}, bf16[6,256,384]{2,1,0:T(8,128)(2,1)}, u32[]{:S(2)}, u32[]{:S(2)}) collective-permute-start(bf16[6,256,384]{2,1,0:T(8,128)(2,1)S(1)} %constant_dynamic-update-slice_fusion.refs_0_), channel_id=1, source_target_pairs={{0,8},{1,9},{2,10},{3,11},{4,12},{5,13},{6,14},{7,15},{8,0},{9,1},... | collective-permute-start | bytes 3538952 | tf_op jit(solution)/shard_map/ppermute | solution.py:89
  50.4 18.3 %collective-permute-start.11 = (bf16[4,256,384]{2,1,0:T(8,128)(2,1)}, bf16[4,256,384]{2,1,0:T(8,128)(2,1)}, u32[]{:S(2)}, u32[]{:S(2)}) collective-permute-start(bf16[4,256,384]{2,1,0:T(8,128)(2,1)} %pad_maximum_fusion.1), channel_id=1, source_target_pairs={{8,16},{9,17},{10,18},{11,19},{12,20},{13,21},{14,22},{15,23},{16,... | collective-permute-start | bytes 2359304 | tf_op jit(solution)/shard_map/ppermute | solution.py:127
  52.7 15.9 %collective-permute-start.12 = (bf16[2,256,384]{2,1,0:T(8,128)(2,1)}, bf16[2,256,384]{2,1,0:T(8,128)(2,1)}, u32[]{:S(2)}, u32[]{:S(2)}) collective-permute-start(bf16[2,256,384]{2,1,0:T(8,128)(2,1)} %pad_maximum_fusion.4), channel_id=1, source_target_pairs={{8,17},{9,16},{10,19},{11,18},{12,21},{13,20},{14,23},{15,22},{16,... | collective-permute-start | bytes 1179656 | tf_op jit(solution)/shard_map/ppermute | solution.py:128
  84.5 34.7 %collective-permute-start.21 = (bf16[1,272,384]{2,1,0:T(8,128)(2,1)}, bf16[1,272,384]{2,1,0:T(8,128)(2,1)S(1)}, u32[]{:S(2)}, u32[]{:S(2)}) collective-permute-start(bf16[1,272,384]{2,1,0:T(8,128)(2,1)} %bitcast.21), channel_id=1, source_target_pairs={{0,1},{1,0},{2,3},{3,2},{4,5},{5,4},{6,7},{7,6},{8,9},{9,8},{10,11... | collective-permute-start | bytes 626696 | tf_op jit(solution)/shard_map/ppermute | solution.py:89
  86.3 31.9 %collective-permute-start.20 = (bf16[1,272,384]{2,1,0:T(8,128)(2,1)}, bf16[1,272,384]{2,1,0:T(8,128)(2,1)S(1)}, u32[]{:S(2)}, u32[]{:S(2)}) collective-permute-start(bf16[1,272,384]{2,1,0:T(8,128)(2,1)} %bitcast.22), channel_id=1, source_target_pairs={{0,3},{1,2},{2,1},{3,0},{4,7},{5,6},{6,5},{7,4},{8,11},{9,10},{10,... | collective-permute-start | bytes 626696 | tf_op jit(solution)/shard_map/ppermute | solution.py:89
  95.9 22.3 %collective-permute-start.19 = (bf16[1,272,384]{2,1,0:T(8,128)(2,1)}, bf16[1,272,384]{2,1,0:T(8,128)(2,1)S(1)}, u32[]{:S(2)}, u32[]{:S(2)}) collective-permute-start(bf16[1,272,384]{2,1,0:T(8,128)(2,1)} %bitcast.23), channel_id=1, source_target_pairs={{0,2},{1,3},{2,0},{3,1},{4,6},{5,7},{6,4},{7,5},{8,10},{9,11},{10,... | collective-permute-start | bytes 626696 | tf_op jit(solution)/shard_map/ppermute | solution.py:89
  96.3 14.3 %collective-permute-start.18 = (bf16[1,272,384]{2,1,0:T(8,128)(2,1)}, bf16[1,272,384]{2,1,0:T(8,128)(2,1)S(1)}, u32[]{:S(2)}, u32[]{:S(2)}) collective-permute-start(bf16[1,272,384]{2,1,0:T(8,128)(2,1)} %bitcast.24), channel_id=1, source_target_pairs={{0,6},{1,7},{2,4},{3,5},{4,2},{5,3},{6,0},{7,1},{8,14},{9,15},{10,... | collective-permute-start | bytes 626696 | tf_op jit(solution)/shard_map/ppermute | solution.py:89
  98.8 19.3 %collective-permute-start.17 = (bf16[1,272,384]{2,1,0:T(8,128)(2,1)}, bf16[1,272,384]{2,1,0:T(8,128)(2,1)S(1)}, u32[]{:S(2)}, u32[]{:S(2)}) collective-permute-start(bf16[1,272,384]{2,1,0:T(8,128)(2,1)} %bitcast.25), channel_id=1, source_target_pairs={{0,4},{1,5},{2,6},{3,7},{4,0},{5,1},{6,2},{7,3},{8,12},{9,13},{10,... | collective-permute-start | bytes 626696 | tf_op jit(solution)/shard_map/ppermute | solution.py:89
  119.5 28.1 %collective-permute-start.23 = (bf16[6,272,384]{2,1,0:T(8,128)(2,1)S(1)}, bf16[6,272,384]{2,1,0:T(8,128)(2,1)S(1)}, u32[]{:S(2)}, u32[]{:S(2)}) collective-permute-start(bf16[6,272,384]{2,1,0:T(8,128)(2,1)S(1)} %constant_dynamic-update-slice_fusion.10.refs_0_), channel_id=1, source_target_pairs={{0,8},{1,9},{2,10},{3,11},{4,12},{5,13},{6,14},{7,15},{8,0},{9,1},... | collective-permute-start | bytes 3760136 | tf_op jit(solution)/shard_map/ppermute | solution.py:89
  121.3 26.3 %collective-permute-start.25 = (bf16[4,272,384]{2,1,0:T(8,128)(2,1)}, bf16[4,272,384]{2,1,0:T(8,128)(2,1)S(1)}, u32[]{:S(2)}, u32[]{:S(2)}) collective-permute-start(bf16[4,272,384]{2,1,0:T(8,128)(2,1)} %pad_maximum_fusion), channel_id=1, source_target_pairs={{8,16},{9,17},{10,18},{11,19},{12,20},{13,21},{14,22},{15,23},{16,... | collective-permute-start | bytes 2506760 | tf_op jit(solution)/shard_map/ppermute | solution.py:127
  122.0 25.5 %collective-permute-start.26 = (bf16[2,272,384]{2,1,0:T(8,128)(2,1)S(1)}, bf16[2,272,384]{2,1,0:T(8,128)(2,1)}, u32[]{:S(2)}, u32[]{:S(2)}) collective-permute-start(bf16[2,272,384]{2,1,0:T(8,128)(2,1)S(1)} %pad_maximum_fusion.3), channel_id=1, source_target_pairs={{8,17},{9,16},{10,19},{11,18},{12,21},{13,20},{14,23},{15,22},{16,... | collective-permute-start | bytes 1253384 | tf_op jit(solution)/shard_map/ppermute | solution.py:128
  131.7 15.8 %collective-permute-start.24 = (bf16[2,272,384]{2,1,0:T(8,128)(2,1)}, bf16[2,272,384]{2,1,0:T(8,128)(2,1)}, u32[]{:S(2)}, u32[]{:S(2)}) collective-permute-start(bf16[2,272,384]{2,1,0:T(8,128)(2,1)} %collective-permute-done.22.refs_1_), channel_id=1, source_target_pairs={{0,8},{1,9},{2,10},{3,11},{4,12},{5,13},{6,14},{7,15},{8,0},{9,1},... | collective-permute-start | bytes 1253384 | tf_op jit(solution)/shard_map/ppermute | solution.py:89
  159.3 20.3 %collective-permute-start.27 = (bf16[16,448,128]{2,1,0:T(8,128)(2,1)}, bf16[16,448,128]{2,1,0:T(8,128)(2,1)S(1)}, u32[]{:S(2)}, u32[]{:S(2)}) collective-permute-start(bf16[16,448,128]{2,1,0:T(8,128)(2,1)} %get-tuple-element.86), channel_id=1, source_target_pairs={{0,8},{1,9},{2,10},{3,11},{4,12},{5,13},{6,14},{7,15},{8,0},{9,1},... | collective-permute-start | bytes 5505032 | tf_op jit(solution)/shard_map/ppermute | solution.py:89
  181.6 13.5 %collective-permute-start.28 = (bf16[4,448,128]{2,1,0:T(8,128)(2,1)S(1)}, bf16[4,448,128]{2,1,0:T(8,128)(2,1)S(1)}, u32[]{:S(2)}, u32[]{:S(2)}) collective-permute-start(bf16[4,448,128]{2,1,0:T(8,128)(2,1)S(1)} %get-tuple-element.99), channel_id=1, source_target_pairs={{0,16},{1,17},{2,18},{3,19},{4,20},{5,21},{6,22},{7,23},{8,24},{9,... | collective-permute-start | bytes 1376264 | tf_op jit(solution)/shard_map/ppermute | solution.py:89
  182.0 20.2 %collective-permute-start.30 = (bf16[4,448,128]{2,1,0:T(8,128)(2,1)S(1)}, bf16[4,448,128]{2,1,0:T(8,128)(2,1)S(1)}, u32[]{:S(2)}, u32[]{:S(2)}) collective-permute-start(bf16[4,448,128]{2,1,0:T(8,128)(2,1)S(1)} %get-tuple-element.100), channel_id=1, source_target_pairs={{0,17},{1,16},{2,19},{3,18},{4,21},{5,20},{6,23},{7,22},{8,25},{9,... | collective-permute-start | bytes 1376264 | tf_op jit(solution)/shard_map/ppermute | solution.py:89
  182.0 23.3 %collective-permute-start.29 = (bf16[4,448,128]{2,1,0:T(8,128)(2,1)S(1)}, bf16[4,448,128]{2,1,0:T(8,128)(2,1)S(1)}, u32[]{:S(2)}, u32[]{:S(2)}) collective-permute-start(bf16[4,448,128]{2,1,0:T(8,128)(2,1)S(1)} %get-tuple-element.101), channel_id=1, source_target_pairs={{0,1},{1,0},{2,3},{3,2},{4,5},{5,4},{6,7},{7,6},{8,9},{9,8},{10,11... | collective-permute-start | bytes 1376264 | tf_op jit(solution)/shard_map/ppermute | solution.py:89
  206.2 13.2 %collective-permute-start.32 = (bf16[1,448,128]{2,1,0:T(8,128)(2,1)S(1)}, bf16[1,448,128]{2,1,0:T(8,128)(2,1)S(1)}, u32[]{:S(2)}, u32[]{:S(2)}) collective-permute-start(bf16[1,448,128]{2,1,0:T(8,128)(2,1)S(1)} %get-tuple-element.103), channel_id=1, source_target_pairs={{0,4},{1,5},{2,6},{3,7},{4,0},{5,1},{6,2},{7,3},{8,12},{9,13},{10,... | collective-permute-start | bytes 344072 | tf_op jit(solution)/shard_map/ppermute | solution.py:89
  (25 other events, 272.5 us)

commit v5 on v4

--- a/solution.py
+++ b/solution.py
@@ -66,6 +66,7 @@
         self.share = share
         self.rows = -(-(2 * (LANES - 1) + share) // LANES)
         self.rows = -(-self.rows // 16) * 16
+        self.cut = self.rows * 3 // 64 * 16
         self.start = [e * share // LANES for e in range(self.count)]
         self.tokens = tokens
         self.part = tokens // 2
@@ -101,14 +102,29 @@
         return buf, core, extra
 
     def reduce_parts(self, keep, away):
-        parts = [keep, self.send(away, self.stages[-1][0])]
-        for stage in reversed(self.stages[:-1]):
+        def added(parts):
             total = parts[0].astype(WIDE)
             for part in parts[1:]:
                 total = total + part.astype(WIDE)
-            buf = total.astype(LOW)
-            split = buf.reshape((len(stage) + 1, -1) + buf.shape[1:])
-            parts = [split[0]] + [self.send(split[k + 1], m) for k, m in enumerate(stage)]
+            return total.astype(LOW)
+
+        def one(buf, axis, level):
+            parts = [lax.index_in_dim(buf, 0, axis, keepdims=False)]
+            for k, m in enumerate(self.stages[level]):
+                parts.append(self.send(lax.index_in_dim(buf, k + 1, axis, keepdims=False), m))
+            return parts
+
+        buf = added([keep, self.send(away, self.stages[-1][0])])
+        if self.grouped:
+            buf = buf.reshape((len(self.stages[1]) + 1, len(self.stages[0]) + 1) + buf.shape[1:])
+            lead, rest = buf[:, :, : self.cut], buf[:, :, self.cut :]
+            lead = one(lead, 0, 1)
+            rest = one(rest, 1, 0)
+            return one(added(lead), 0, 0) + one(added(rest), 0, 1)
+        for level in reversed(range(len(self.stages) - 1)):
+            buf = buf.reshape((len(self.stages[level]) + 1, -1) + buf.shape[1:])
+            parts = one(buf, 0, level)
+            buf = added(parts)
         return [part[0] for part in parts]
 
     def exchange(self, block):
@@ -264,6 +280,12 @@
     loop(table[b] + 1, table[d] + 1, slice(rows, 2 * rows))
 
 
+def launch(source, dest, sem):
+    copy = pltpu.make_async_copy(source, dest, sem)
+    copy.start()
+    return copy
+
+
 def block_copies(source, dest, sems, lo, hi, wait):
     def step(slot, carry):
         copy = pltpu.make_async_copy(source.at[slot], dest.at[slot], sems.at[slot])
@@ -299,10 +321,19 @@
     def kernel(table, *refs):
         parts, (out_ref, sq_ref, pad) = refs[:-3], refs[-3:]
         s = table[0]
-        got = [p[...].astype(WIDE) for p in parts]
-        while len(got) > 1:
-            got = [got[k] + got[k + 1] for k in range(0, len(got), 2)]
-        y = pltpu.roll(got[0], LANES - s, 1)
+
+        def total(parts):
+            got = [p[...].astype(WIDE) for p in parts]
+            while len(got) > 1:
+                got = [got[k] + got[k + 1] for k in range(0, len(got), 2)]
+            return got[0]
+
+        if plan.grouped:
+            lead = len(plan.stages[0]) + 1
+            y = jnp.concatenate([total(parts[:lead]), total(parts[lead:])], axis=0)
+        else:
+            y = total(parts)
+        y = pltpu.roll(y, LANES - s, 1)
         pad[0 : plan.rows, :] = y
         pad[plan.rows :, :] = jnp.zeros((8, LANES), WIDE)
         lane = lax.broadcasted_iota(jnp.int32, y.shape, 1)
@@ -386,7 +417,9 @@
 
     def kernel(table, *refs):
         wins = refs[:sources]
-        triple_ref, wo, wup, wdn, par_ref, cot_ref, col_ref, row_ref = refs[sources : 8 + sources]
+        triple_ref, wo_ref, wup_ref, wdn_ref, par_ref, cot_ref, col_ref, row_ref = refs[
+            sources : 8 + sources
+        ]
         (
             out_ref,
             msg_ref,
@@ -407,7 +440,8 @@
             kown_ref,
             vown_ref,
         ) = refs[8 + sources : 26 + sources]
-        xwin, n_buf, k_buf, v_buf, scores, tops, sums, accs, mix, xsem, ksem = refs[26 + sources :]
+        xwin, n_buf, k_buf, v_buf, scores, tops, sums, accs, mix = refs[26 + sources : 35 + sources]
+        wo, wup, wdn, act_buf, pre_buf, xsem, ksem, osem = refs[35 + sources :]
         lo = table[plan.low_at()]
         hi = table[plan.low_at() + 1]
 
@@ -416,6 +450,8 @@
             return par_ref[row : row + 1, : dict(PIECES)[name]]
 
         fetch_window(plan, table, wins, xwin, xsem, lo, hi, False)
+        pairs_in = [(wo_ref, wo), (wup_ref, wup), (wdn_ref, wdn)]
+        loads = [launch(a, b, osem.at[i]) for i, (a, b) in enumerate(pairs_in)]
         gain1 = param("gain1")
         shift1 = param("shift1")
         tbias = param("tbias")
@@ -489,6 +525,8 @@
                 )
                 stats = jnp.where(lane == 2 * p + k, column, stats)
         att = mix[...]
+        for load in loads:
+            load.wait()
         att_low = att.astype(LOW)
         att_ref[...] = att_low
         x = xwin[own].astype(WIDE)
@@ -503,7 +541,8 @@
         pre = dot(n2_low, wup[...], NN) + param("ubias")
         cdf = 0.5 * (1.0 + lax.erf(pre * math.sqrt(0.5)))
         act_low = (pre * cdf).astype(LOW)
-        act_ref[...] = act_low
+        act_buf[...] = act_low
+        saves = [launch(act_buf, act_ref, osem.at[3])]
         slope = cdf + pre * (jnp.exp(-0.5 * pre * pre) * (1.0 / math.sqrt(2.0 * math.pi)))
         branch_two = dot(act_low, wdn[...], NN) + param("dbias")
         out_ref[...] = (middle + scale2 * branch_two).astype(LOW)
@@ -512,7 +551,8 @@
         gbt = (scale2 * up).astype(LOW)
         gbt_ref[...] = gbt
         gpre = (dot(gbt, wdn[...], NT) * slope).astype(LOW)
-        pre_ref[...] = gpre
+        pre_buf[...] = gpre
+        saves.append(launch(pre_buf, pre_ref, osem.at[4]))
         gn2 = dot(gpre, wup[...], NT)
         gmid = up + norm_back(gn2, gain2, n2, r2)
         mid_ref[...] = gmid
@@ -548,6 +588,8 @@
         vec_ref[6:7, :D] = column_sum(gbo.astype(WIDE))
         for i, (buf, ref) in enumerate(saved):
             block_copies(buf, ref, ksem.at[i], lo, hi, True)
+        for save in saves:
+            save.wait()
 
     return kernel
 
@@ -645,7 +687,16 @@
         away_ref,
         tail_ref,
         flat,
+        stage,
+        n_buf,
+        q_buf,
+        nsem,
+        qsem,
+        ssem,
     ):
+        lo = table[plan.low_at()]
+        hi = table[plan.low_at() + 1]
+        block_copies(norm_ref, n_buf, nsem, lo, hi, False)
         fold(flat, AT["down"] - base, act_ref, gbt_ref, D)
         fold(flat, AT["up"] - base, n2_ref, pre_ref, FF)
         fold(flat, AT["out"] - base, att_ref, gbo_ref, D)
@@ -659,25 +710,42 @@
         end = ALL_ROWS - base
         flat[end:, :] = jnp.zeros((flat.shape[0] - end, LANES), WIDE)
         tail_ref[...] = flat[0 : plan.rows, :]
+
+        def put(e, wait):
+            t = table[e]
+            i = e - plan.first_late
+
+            @pl.when(t < half)
+            def _():
+                c = pltpu.make_async_copy(stage.at[i], keep_ref.at[t], ssem.at[i])
+                c.wait() if wait else c.start()
+
+            @pl.when(t >= half)
+            def _():
+                c = pltpu.make_async_copy(stage.at[i], away_ref.at[t - half], ssem.at[i])
+                c.wait() if wait else c.start()
+
         for e in range(plan.first_late, plan.count):
             r0 = plan.start[e] - base
-            t = table[e]
-
-            @pl.when(t < half)
-            def _(r0=r0, t=t):
-                keep_ref[t] = flat[r0 : r0 + plan.rows, :].astype(LOW)
-
-            @pl.when(t >= half)
-            def _(r0=r0, t=t):
-                away_ref[t - half] = flat[r0 : r0 + plan.rows, :].astype(LOW)
+            stage[e - plan.first_late] = flat[r0 : r0 + plan.rows, :].astype(LOW)
+            put(e, False)
 
         bias = par_ref[VEC["tbias"] : VEC["tbias"] + 1, :D]
+        block_copies(norm_ref, n_buf, nsem, lo, hi, True)
 
         def project(w, carry):
-            q_ref[w] = scaled_query(norm_ref[w], triple_ref[:, :D], bias)
+            q_buf[w] = scaled_query(n_buf[w], triple_ref[:, :D], bias)
+            pltpu.make_async_copy(q_buf.at[w], q_ref.at[w], qsem.at[w]).start()
             return carry
 
-        lax.fori_loop(table[plan.low_at()], table[plan.low_at() + 1] + 1, project, 0)
+        lax.fori_loop(lo, hi + 1, project, 0)
+        block_copies(q_buf, q_ref, qsem, lo, hi, True)
+
+        def finish(e, carry):
+            put(e, True)
+            return carry
+
+        lax.fori_loop(plan.first_late, plan.count, finish, 0)
 
     return kernel
 
@@ -699,7 +767,7 @@
             row_ref,
             gq_ref,
             normed_ref,
-            triple_ref,
+            triple_any,
             x_ref,
             mid_ref,
             par_ref,
@@ -710,13 +778,14 @@
             keep_ref,
             away_ref,
         ) = refs[sources : sources + 17]
-        mwin, q_buf, flat, gt, stage, stats, spare, acck, accv, msem, qsem, osem = refs[
+        mwin, q_buf, triple_ref, flat, gt, stage, stats, spare, acck, accv, msem, qsem, tsem, osem = refs[
             sources + 17 :
         ]
         lo = table[plan.low_at()]
         hi = table[plan.low_at() + 1]
         fetch_window(plan, table, wins, mwin, msem, lo, hi, False)
         block_copies(q_ref, q_buf, qsem, lo, hi, False)
+        load = launch(triple_any, triple_ref, tsem.at[0])
         ks = [halves(k_ref[:, LANES * p : LANES * (p + 1)]) for p in range(pairs)]
         vs = [halves(v_ref[:, LANES * p : LANES * (p + 1)]) for p in range(pairs)]
         ids = tiled(col_ref[...], T)
@@ -761,6 +830,7 @@
         fold(flat, AT["triple"], normed_ref, gt, 3 * D)
         put_vector(flat, AT["tbias"], column_sum(gt[:, :D].astype(WIDE)))
         put_vector(flat, AT["tbias"] + D // LANES, column_sum(gt[:, 2 * D :].astype(WIDE)))
+        load.wait()
         gn = dot(gt[...], triple_ref[...], NT)
         n, r = normalized(x_ref[...].astype(WIDE))
         put_vector(flat, AT["gain1"], column_sum(gn * n))
@@ -852,8 +922,8 @@
 
         outs = pl.pallas_call(
             forward_kernel(plan, sources),
-            in_specs=[SMEM] + [ANY] * sources + [VMEM] * 8,
-            out_specs=[VMEM] * 3 + [ANY] * 3 + [VMEM] * 12,
+            in_specs=[SMEM] + [ANY] * sources + [VMEM] + [ANY] * 3 + [VMEM] * 4,
+            out_specs=[VMEM] * 3 + [ANY] * 3 + [VMEM] * 2 + [ANY] * 2 + [VMEM] * 8,
             out_shape=[
                 shape((T, D), LOW),
                 shape((T + 16, D), LOW),
@@ -884,8 +954,14 @@
                 half,
                 half,
                 pltpu.VMEM((T, D), WIDE),
+                pltpu.VMEM((D, D), LOW),
+                pltpu.VMEM((D, FF), LOW),
+                pltpu.VMEM((FF, D), LOW),
+                pltpu.VMEM((T, FF), LOW),
+                pltpu.VMEM((T, FF), LOW),
                 pltpu.SemaphoreType.DMA((W,)),
                 pltpu.SemaphoreType.DMA((3, W)),
+                pltpu.SemaphoreType.DMA((5,)),
             ],
             compiler_params=limit,
             name="forward",
@@ -932,8 +1008,8 @@
         gq = query_call(table, q, k, v, message, stat, columns, key_ids)
         weight_call = pl.pallas_call(
             weight_kernel(plan),
-            in_specs=[SMEM] + [VMEM] * 10,
-            out_specs=[VMEM] * 4,
+            in_specs=[SMEM, ANY] + [VMEM] * 9,
+            out_specs=[ANY] * 3 + [VMEM],
             out_shape=[
                 shape((W, T, D), LOW),
                 shape((N // 2, R, LANES), LOW),
@@ -942,6 +1018,12 @@
             ],
             scratch_shapes=[
                 pltpu.VMEM((plan.flat_rows - AT["out"] + 8, LANES), WIDE),
+                pltpu.VMEM((N - plan.first_late, R, LANES), LOW),
+                pltpu.VMEM((W, T, D), LOW),
+                pltpu.VMEM((W, T, D), LOW),
+                pltpu.SemaphoreType.DMA((W,)),
+                pltpu.SemaphoreType.DMA((W,)),
+                pltpu.SemaphoreType.DMA((N - plan.first_late,)),
             ],
             compiler_params=limit,
             name="weight",
@@ -953,7 +1035,7 @@
         late = plan.first_late
         input_grad, keep, away = pl.pallas_call(
             last_kernel(plan, sources),
-            in_specs=[SMEM] + [ANY] * (sources + 1) + [VMEM] * 11 + [ANY, ANY],
+            in_specs=[SMEM] + [ANY] * (sources + 1) + [VMEM] * 6 + [ANY] + [VMEM] * 4 + [ANY, ANY],
             out_specs=[VMEM, ANY, ANY],
             out_shape=[
                 shape((T, D), WIDE),
@@ -963,6 +1045,7 @@
             scratch_shapes=[
                 pltpu.VMEM((W, T + 16, D), LOW),
                 pltpu.VMEM((W, T, D), LOW),
+                pltpu.VMEM((D, 3 * D), LOW),
                 pltpu.VMEM((AT["out"] + R + 8, LANES), WIDE),
                 pltpu.VMEM((T, 3 * D), LOW),
                 pltpu.VMEM((late, R, LANES), LOW),
@@ -972,6 +1055,7 @@
                 half,
                 pltpu.SemaphoreType.DMA((W,)),
                 pltpu.SemaphoreType.DMA((W,)),
+                pltpu.SemaphoreType.DMA((1,)),
                 pltpu.SemaphoreType.DMA((late,)),
             ],
             input_output_aliases={13 + sources: 1, 14 + sources: 2},

time: 237 us -> 235 us (level)
  waiting for transfers between devices: 84.8 us -> 77.9 us
  starting transfers between devices: 69.4 us -> 76 us
  Pallas kernels: 50.4 us -> 47.9 us
    ppermute x30 -> x36, waiting for transfers between devices: 84.8 us -> 77.9 us  [send(): return lax.ppermute(x, BOTH, [(i, i ^ mask) for i in range(self.count)])]
    ppermute x30 -> x36, starting transfers between devices: 64.3 us -> 70.9 us  [send(): return lax.ppermute(x, BOTH, [(i, i ^ mask) for i in range(self.count)])]
  transfers between devices with their start and end apart: 34 -> 40, of which waited for: 14 -> 15; matrix products, arithmetic and copies ran while one was open for 4% -> 4% of each run, Pallas kernels for 9% -> 8%
where the time goes in v5:
time: 235 us; the launch traced here: 234 us
  waiting for transfers between devices  77.9 us (33%)
  starting transfers between devices  76 us (32%)
  Pallas kernels  47.9 us (20%)
  other arithmetic  10.3 us (4%)
  blocking collectives  9.72 us (4%)
  local copies, waits for them, and re-layouts  9.06 us (4%)
  between operations  3.08 us (1%)
    ppermute x36, waiting for transfers between devices, send(): return lax.ppermute(x, BOTH, [(i, i ^ mask) for i in range(self.count)])  77.9 us
    ppermute x36, starting transfers between devices, send(): return lax.ppermute(x, BOTH, [(i, i ^ mask) for i in range(self.count)])  70.9 us
    pallas_call x1, Pallas kernels, per_device(): pl.pallas_call(forward_kernel(plan, sources), in_specs=[SMEM] + [ANY] * s...  14 us
    pallas_call x1, Pallas kernels, per_device(): pl.pallas_call(last_kernel(plan, sources), in_specs=[SMEM] + [ANY] * (sou...  10.4 us
    all_to_all x1, blocking collectives, per_device(): squares = lax.all_to_all(square, BOTH, 0, 0, tiled=True)  9.72 us
    pallas_call x1, Pallas kernels, per_device(): gq = query_call(table, q, k, v, message, stat, columns, key_ids)  7.7 us
    pallas_call x1, Pallas kernels, per_device(): weight_call(table, norms, triple, params, act, gpre, gbt, n2, att, gbo, vec)  6.61 us
    pallas_call x1, Pallas kernels, per_device(): triple, wo, wup, wdn, params = unpack(table, near, core)  5.53 us
  transfers between devices with their start and end apart: 40, of which 15 were waited for; matrix products, arithmetic and copies ran while one was open for 4% of the time, Pallas kernels for 8%

profile of v5, /device:TPU:0, one launch (start us, length us, event | category | flops | bytes accessed | tf_op | source)
XLA Modules:
  0.0 234.0 jit_solution(4013841387546530973)
XLA Ops:
  4.1 5.1 %collective-permute-start.2 = (bf16[1,448,128]{2,1,0:T(8,128)(2,1)}, bf16[1,448,128]{2,1,0:T(8,128)(2,1)S(1)}, u32[]{:S(2)}, u32[]{:S(2)}) collective-permute-start(bf16[1,448,128]{2,1,0:T(8,128)(2,1)} %bitcast.77), channel_id=1, source_target_pairs={{0,6},{1,7},{2,4},{3,5},{4,2},{5,3},{6,0},{7,1},{8,14},{9,15},{10,... | collective-permute-start | bytes 344072 | tf_op jit(solution)/shard_map/ppermute | solution.py:90
  13.5 5.7 %collective-permute-done.1 = bf16[1,448,128]{2,1,0:T(8,128)(2,1)S(1)} collective-permute-done((bf16[1,448,128]{2,1,0:T(8,128)(2,1)}, bf16[1,448,128]{2,1,0:T(8,128)(2,1)S(1)}, u32[]{:S(2)}, u32[]{:S(2)}) %collective-permute-start.1) | collective-permute-done | bytes 114720 | tf_op jit(solution)/shard_map/ppermute | solution.py:90
  25.0 10.0 %collective-permute-done.13 = bf16[4,448,128]{2,1,0:T(8,128)(2,1)S(1)} collective-permute-done((bf16[4,448,128]{2,1,0:T(8,128)(2,1)S(1)}, bf16[4,448,128]{2,1,0:T(8,128)(2,1)S(1)}, u32[]{:S(2)}, u32[]{:S(2)}) %collective-permute-start.13) | collective-permute-done | bytes 458784 | tf_op jit(solution)/shard_map/ppermute | solution.py:90
  37.5 5.3 %collective-permute-start.3 = (bf16[1,256,384]{2,1,0:T(8,128)(2,1)S(1)}, bf16[1,256,384]{2,1,0:T(8,128)(2,1)S(1)}, u32[]{:S(2)}, u32[]{:S(2)}) collective-permute-start(bf16[1,256,384]{2,1,0:T(8,128)(2,1)S(1)} %bitcast.76), channel_id=1, source_target_pairs={{0,4},{1,5},{2,6},{3,7},{4,0},{5,1},{6,2},{7,3},{8,12},{9,13},{10,... | collective-permute-start | bytes 589832 | tf_op jit(solution)/shard_map/ppermute | solution.py:90
  43.2 3.3 %collective-permute-done.3 = bf16[1,256,384]{2,1,0:T(8,128)(2,1)S(1)} collective-permute-done((bf16[1,256,384]{2,1,0:T(8,128)(2,1)S(1)}, bf16[1,256,384]{2,1,0:T(8,128)(2,1)S(1)}, u32[]{:S(2)}, u32[]{:S(2)}) %collective-permute-start.3) | collective-permute-done | bytes 196640 | tf_op jit(solution)/shard_map/ppermute | solution.py:90
  54.2 6.3 %collective-permute-done.8.refs_1_ = bf16[2,256,384]{2,1,0:T(8,128)(2,1)} collective-permute-done((bf16[2,256,384]{2,1,0:T(8,128)(2,1)}, bf16[2,256,384]{2,1,0:T(8,128)(2,1)}, u32[]{:S(2)}, u32[]{:S(2)}) %collective-permute-start.8) | collective-permute-done | bytes 393248 | tf_op jit(solution)/shard_map/ppermute | solution.py:90
  63.1 5.5 %unpack.1 = (bf16[384,1152]{1,0:T(8,128)(2,1)}, bf16[384,384]{1,0:T(8,128)(2,1)}, bf16[384,1536]{1,0:T(8,128)(2,1)}, bf16[1536,384]{1,0:T(8,128)(2,1)}, f32[16,1536]{1,0:T(8,128)}) custom-call(s32[64]{0:T(128)} %concatenate.30.table, bf16[16,448,128]{2,1,0:T(8,128)(2,1)} %copy-done, bf16[16,448,128]{2,1,0:T(8,128)(2,1)} %collective-permute-done.16.core), custom_call_target="tpu_custom_call" | custom-call | tf_op jit(solution)/shard_map/unpack/pallas_call | solution.py:921
  69.4 14.0 %forward.1 = (bf16[256,384]{1,0:T(8,128)(2,1)}, bf16[272,384]{1,0:T(8,128)(2,1)}, bf16[256,384]{1,0:T(8,128)(2,1)}, bf16[13,256,384]{2,1,0:T(8,128)(2,1)}, bf16[...) custom-call(s32[64]{0:T(128)} %concatenate.30.table, ...), custom_call_target="tpu_custom_call" | custom-call | tf_op jit(solution)/shard_map/forward/pallas_call | solution.py:923
  85.2 9.5 %collective-permute-start.20 = (bf16[1,272,384]{2,1,0:T(8,128)(2,1)}, bf16[1,272,384]{2,1,0:T(8,128)(2,1)S(1)}, u32[]{:S(2)}, u32[]{:S(2)}) collective-permute-start(bf16[1,272,384]{2,1,0:T(8,128)(2,1)} %bitcast.68), channel_id=1, source_target_pairs={{0,3},{1,2},{2,1},{3,0},{4,7},{5,6},{6,5},{7,4},{8,11},{9,10},{10,... | collective-permute-start | bytes 626696 | tf_op jit(solution)/shard_map/ppermute | solution.py:90
  99.2 10.3 %collective-permute-done.18 = bf16[1,272,384]{2,1,0:T(8,128)(2,1)S(1)} collective-permute-done((bf16[1,272,384]{2,1,0:T(8,128)(2,1)}, bf16[1,272,384]{2,1,0:T(8,128)(2,1)S(1)}, u32[]{:S(2)}, u32[]{:S(2)}) %collective-permute-start.18) | collective-permute-done | bytes 208928 | tf_op jit(solution)/shard_map/ppermute | solution.py:90
  109.5 7.5 %collective-permute-done.17 = bf16[1,272,384]{2,1,0:T(8,128)(2,1)S(1)} collective-permute-done((bf16[1,272,384]{2,1,0:T(8,128)(2,1)}, bf16[1,272,384]{2,1,0:T(8,128)(2,1)S(1)}, u32[]{:S(2)}, u32[]{:S(2)}) %collective-permute-start.17) | collective-permute-done | bytes 208928 | tf_op jit(solution)/shard_map/ppermute | solution.py:90
  122.4 8.3 %collective-permute-done.22.refs_1_ = bf16[2,272,384]{2,1,0:T(8,128)(2,1)} collective-permute-done((bf16[2,272,384]{2,1,0:T(8,128)(2,1)S(1)}, bf16[2,272,384]{2,1,0:T(8,128)(2,1)}, u32[]{:S(2)}, u32[]{:S(2)}) %collective-permute-start.22) | collective-permute-done | bytes 417824 | tf_op jit(solution)/shard_map/ppermute | solution.py:90
  130.6 7.7 %query.1.refs_11_ = bf16[256,384]{1,0:T(8,128)(2,1)} custom-call(s32[64]{0:T(128)} %concatenate.30.table, bf16[256,384]{1,0:T(8,128)(2,1)} %get-tuple-element.75.q_ref, bf16[13,256,384]{2,1,0:T(8,128)(2,1)} %get-tuple-element.76.k_ref, bf16[13,256,384]{2,1,0:T(8,128)(2,1)} %get-tuple-element.77.v_ref, bf16[272,384]{1,0:T(8,128)(2,1)} %get-tuple-element.60.msg_ref, ...), custom_call_target="tpu_custom_call" | custom-call | tf_op jit(solution)/shard_map/query/pallas_call | solution.py:1008
  138.3 6.6 %weight.1 = (bf16[13,256,384]{2,1,0:T(8,128)(2,1)}, bf16[16,448,128]{2,1,0:T(8,128)(2,1)}, bf16[16,448,128]{2,1,0:T(8,128)(2,1)}, f32[448,128]{1,0:T(8,128)}) custom-call(s32[64]{0:T(128)} %concatenate.30.table, bf16[13,256,384]{2,1,0:T(8,128)(2,1)} %get-tuple-element.64.norm_ref, bf16[384,1152]{1,0:T(8,128)(2,1)} %get-tuple-element.54.refs_6_.triple_ref.refs_13_, ...), custom_call_target="tpu_custom_call" | custom-call | tf_op jit(solution)/shard_map/weight/pallas_call | solution.py:1031
  146.3 10.4 %last.1 = (f32[256,384]{1,0:T(8,128)}, bf16[16,448,128]{2,1,0:T(8,128)(2,1)}, bf16[16,448,128]{2,1,0:T(8,128)(2,1)}) custom-call(s32[64]{0:T(128)} %concatenate.30.table, bf16[6,272,384]{2,1,0:T(8,128)(2,1)} %copy-done.1, bf16[2,272,384]{2,1,0:T(8,128)(2,1)} %collective-permute-done.22.refs_1_, ...), custom_call_target="tpu_custom_call", output_to_operand_aliasing={{1}: (19, {}), {2}: (20, {})} | custom-call | tf_op jit(solution)/shard_map/last/pallas_call | solution.py:1036
  156.8 16.7 %collective-permute-start.27 = (bf16[16,448,128]{2,1,0:T(8,128)(2,1)}, bf16[16,448,128]{2,1,0:T(8,128)(2,1)S(1)}, u32[]{:S(2)}, u32[]{:S(2)}) collective-permute-start(bf16[16,448,128]{2,1,0:T(8,128)(2,1)} %get-tuple-element.86), channel_id=1, source_target_pairs={{0,8},{1,9},{2,10},{3,11},{4,12},{5,13},{6,14},{7,15},{8,0},{9,1},... | collective-permute-start | bytes 5505032 | tf_op jit(solution)/shard_map/ppermute | solution.py:90
  173.5 3.6 %collective-permute-done.27 = bf16[16,448,128]{2,1,0:T(8,128)(2,1)S(1)} collective-permute-done((bf16[16,448,128]{2,1,0:T(8,128)(2,1)}, bf16[16,448,128]{2,1,0:T(8,128)(2,1)S(1)}, u32[]{:S(2)}, u32[]{:S(2)}) %collective-permute-start.27) | collective-permute-done | bytes 1835040 | tf_op jit(solution)/shard_map/ppermute | solution.py:90
  179.3 4.3 %collective-permute-start.36 = (bf16[4,112,128]{2,1,0:T(8,128)(2,1)S(1)}, bf16[4,112,128]{2,1,0:T(8,128)(2,1)S(1)}, u32[]{:S(2)}, u32[]{:S(2)}) collective-permute-start(bf16[4,112,128]{2,1,0:T(8,128)(2,1)S(1)} %get-tuple-element.101), channel_id=1, source_target_pairs={{0,6},{1,7},{2,4},{3,5},{4,2},{5,3},{6,0},{7,1},{8,14},{9,15},{10,... | collective-permute-start | bytes 344072 | tf_op jit(solution)/shard_map/ppermute | solution.py:90
  187.3 3.9 %collective-permute-done.35 = bf16[4,112,128]{2,1,0:T(8,128)(2,1)S(1)} collective-permute-done((bf16[4,112,128]{2,1,0:T(8,128)(2,1)S(1)}, bf16[4,112,128]{2,1,0:T(8,128)(2,1)S(1)}, u32[]{:S(2)}, u32[]{:S(2)}) %collective-permute-start.35) | collective-permute-done | bytes 114720 | tf_op jit(solution)/shard_map/ppermute | solution.py:90
  191.3 3.4 %collective-permute-done.28 = bf16[4,336,128]{2,1,0:T(8,128)(2,1)S(1)} collective-permute-done((bf16[4,336,128]{2,1,0:T(8,128)(2,1)S(1)}, bf16[4,336,128]{2,1,0:T(8,128)(2,1)S(1)}, u32[]{:S(2)}, u32[]{:S(2)}) %collective-permute-start.28) | collective-permute-done | bytes 344096 | tf_op jit(solution)/shard_map/ppermute | solution.py:90
  194.7 6.5 %collective-permute-done.30 = bf16[4,336,128]{2,1,0:T(8,128)(2,1)S(1)} collective-permute-done((bf16[4,336,128]{2,1,0:T(8,128)(2,1)S(1)}, bf16[4,336,128]{2,1,0:T(8,128)(2,1)S(1)}, u32[]{:S(2)}, u32[]{:S(2)}) %collective-permute-start.30) | collective-permute-done | bytes 344096 | tf_op jit(solution)/shard_map/ppermute | solution.py:90
  210.3 3.1 %collective-permute-done.39.refs_7_ = bf16[112,128]{1,0:T(8,128)(2,1)S(1)} collective-permute-done((bf16[112,128]{1,0:T(8,128)(2,1)S(1)}, bf16[112,128]{1,0:T(8,128)(2,1)S(1)}, u32[]{:S(2)}, u32[]{:S(2)}) %collective-permute-start.39) | collective-permute-done | bytes 28704 | tf_op jit(solution)/shard_map/ppermute | solution.py:90
  213.6 3.6 %collective-permute-done.37.refs_5_ = bf16[112,128]{1,0:T(8,128)(2,1)S(1)} collective-permute-done((bf16[112,128]{1,0:T(8,128)(2,1)S(1)}, bf16[112,128]{1,0:T(8,128)(2,1)S(1)}, u32[]{:S(2)}, u32[]{:S(2)}) %collective-permute-start.37) | collective-permute-done | bytes 28704 | tf_op jit(solution)/shard_map/ppermute | solution.py:90
  219.9 9.7 %all_to_all.12 = f32[32,1,128]{2,1,0:T(1,128)S(1)} all-to-all(f32[32,1,128]{2,1,0:T(1,128)} %bitcast.83), channel_id=1, replica_groups=mesh['dp'=4,'fsdp'=8] {'dp','fsdp'}, dimensions={0} | all-to-all | bytes 32768 | tf_op jit(solution)/shard_map/all_to_all | solution.py:1093
  (145 shorter events, 60.5 us)
Async XLA Ops:
  9.7 14.1 %collective-permute-start.7 = (bf16[1,256,384]{2,1,0:T(8,128)(2,1)}, bf16[1,256,384]{2,1,0:T(8,128)(2,1)S(1)}, u32[]{:S(2)}, u32[]{:S(2)}) collective-permute-start(bf16[1,256,384]{2,1,0:T(8,128)(2,1)} %bitcast.72), channel_id=1, source_target_pairs={{0,1},{1,0},{2,3},{3,2},{4,5},{5,4},{6,7},{7,6},{8,9},{9,8},{10,11... | collective-permute-start | bytes 589832 | tf_op jit(solution)/shard_map/ppermute | solution.py:90
  11.5 31.7 %collective-permute-start.6 = (bf16[1,256,384]{2,1,0:T(8,128)(2,1)}, bf16[1,256,384]{2,1,0:T(8,128)(2,1)S(1)}, u32[]{:S(2)}, u32[]{:S(2)}) collective-permute-start(bf16[1,256,384]{2,1,0:T(8,128)(2,1)} %bitcast.73), channel_id=1, source_target_pairs={{0,3},{1,2},{2,1},{3,0},{4,7},{5,6},{6,5},{7,4},{8,11},{9,10},{10,... | collective-permute-start | bytes 589832 | tf_op jit(solution)/shard_map/ppermute | solution.py:90
  20.1 17.4 %collective-permute-start.14 = (bf16[4,448,128]{2,1,0:T(8,128)(2,1)S(1)}, bf16[4,448,128]{2,1,0:T(8,128)(2,1)S(1)}, u32[]{:S(2)}, u32[]{:S(2)}) collective-permute-start(bf16[4,448,128]{2,1,0:T(8,128)(2,1)S(1)} %pad_maximum_fusion.2), channel_id=1, source_target_pairs={{0,1},{1,0},{2,3},{3,2},{4,5},{5,4},{6,7},{7,6},{8,9},{9,8},{10,11... | collective-permute-start | bytes 1376264 | tf_op jit(solution)/shard_map/ppermute | solution.py:90
  21.7 13.4 %collective-permute-start.13 = (bf16[4,448,128]{2,1,0:T(8,128)(2,1)S(1)}, bf16[4,448,128]{2,1,0:T(8,128)(2,1)S(1)}, u32[]{:S(2)}, u32[]{:S(2)}) collective-permute-start(bf16[4,448,128]{2,1,0:T(8,128)(2,1)S(1)} %pad_maximum_fusion.2), channel_id=1, source_target_pairs={{0,16},{1,17},{2,18},{3,19},{4,20},{5,21},{6,22},{7,23},{8,24},{9,... | collective-permute-start | bytes 1376264 | tf_op jit(solution)/shard_map/ppermute | solution.py:90
  23.2 19.7 %collective-permute-start.15 = (bf16[4,448,128]{2,1,0:T(8,128)(2,1)S(1)}, bf16[4,448,128]{2,1,0:T(8,128)(2,1)S(1)}, u32[]{:S(2)}, u32[]{:S(2)}) collective-permute-start(bf16[4,448,128]{2,1,0:T(8,128)(2,1)S(1)} %pad_maximum_fusion.2), channel_id=1, source_target_pairs={{0,17},{1,16},{2,19},{3,18},{4,21},{5,20},{6,23},{7,22},{8,25},{9,... | collective-permute-start | bytes 1376264 | tf_op jit(solution)/shard_map/ppermute | solution.py:90
  23.8 19.3 %collective-permute-start.5 = (bf16[1,256,384]{2,1,0:T(8,128)(2,1)S(1)}, bf16[1,256,384]{2,1,0:T(8,128)(2,1)S(1)}, u32[]{:S(2)}, u32[]{:S(2)}) collective-permute-start(bf16[1,256,384]{2,1,0:T(8,128)(2,1)S(1)} %bitcast.74), channel_id=1, source_target_pairs={{0,2},{1,3},{2,0},{3,1},{4,6},{5,7},{6,4},{7,5},{8,10},{9,11},{10,... | collective-permute-start | bytes 589832 | tf_op jit(solution)/shard_map/ppermute | solution.py:90
  43.0 20.1 %collective-permute-start.16 = (bf16[16,448,128]{2,1,0:T(8,128)(2,1)S(1)}, bf16[16,448,128]{2,1,0:T(8,128)(2,1)}, u32[]{:S(2)}, u32[]{:S(2)}) collective-permute-start(bf16[16,448,128]{2,1,0:T(8,128)(2,1)S(1)} %constant_dynamic-update-slice_fusion.6.near), channel_id=1, source_target_pairs={{0,8},{1,9},{2,10},{3,11},{4,12},{5,13},{6,14},{7,15},{8,0},{9,1},... | collective-permute-start | bytes 5505032 | tf_op jit(solution)/shard_map/ppermute | solution.py:90
  48.4 20.2 %collective-permute-start.9 = (bf16[6,256,384]{2,1,0:T(8,128)(2,1)S(1)}, bf16[6,256,384]{2,1,0:T(8,128)(2,1)}, u32[]{:S(2)}, u32[]{:S(2)}) collective-permute-start(bf16[6,256,384]{2,1,0:T(8,128)(2,1)S(1)} %constant_dynamic-update-slice_fusion.refs_0_), channel_id=1, source_target_pairs={{0,8},{1,9},{2,10},{3,11},{4,12},{5,13},{6,14},{7,15},{8,0},{9,1},... | collective-permute-start | bytes 3538952 | tf_op jit(solution)/shard_map/ppermute | solution.py:90
  50.4 18.3 %collective-permute-start.11 = (bf16[4,256,384]{2,1,0:T(8,128)(2,1)}, bf16[4,256,384]{2,1,0:T(8,128)(2,1)}, u32[]{:S(2)}, u32[]{:S(2)}) collective-permute-start(bf16[4,256,384]{2,1,0:T(8,128)(2,1)} %pad_maximum_fusion.1), channel_id=1, source_target_pairs={{8,16},{9,17},{10,18},{11,19},{12,20},{13,21},{14,22},{15,23},{16,... | collective-permute-start | bytes 2359304 | tf_op jit(solution)/shard_map/ppermute | solution.py:143
  52.7 15.9 %collective-permute-start.12 = (bf16[2,256,384]{2,1,0:T(8,128)(2,1)}, bf16[2,256,384]{2,1,0:T(8,128)(2,1)}, u32[]{:S(2)}, u32[]{:S(2)}) collective-permute-start(bf16[2,256,384]{2,1,0:T(8,128)(2,1)} %pad_maximum_fusion.4), channel_id=1, source_target_pairs={{8,17},{9,16},{10,19},{11,18},{12,21},{13,20},{14,23},{15,22},{16,... | collective-permute-start | bytes 1179656 | tf_op jit(solution)/shard_map/ppermute | solution.py:144
  83.4 34.7 %collective-permute-start.21 = (bf16[1,272,384]{2,1,0:T(8,128)(2,1)}, bf16[1,272,384]{2,1,0:T(8,128)(2,1)S(1)}, u32[]{:S(2)}, u32[]{:S(2)}) collective-permute-start(bf16[1,272,384]{2,1,0:T(8,128)(2,1)} %bitcast.67), channel_id=1, source_target_pairs={{0,1},{1,0},{2,3},{3,2},{4,5},{5,4},{6,7},{7,6},{8,9},{9,8},{10,11... | collective-permute-start | bytes 626696 | tf_op jit(solution)/shard_map/ppermute | solution.py:90
  85.2 31.9 %collective-permute-start.20 = (bf16[1,272,384]{2,1,0:T(8,128)(2,1)}, bf16[1,272,384]{2,1,0:T(8,128)(2,1)S(1)}, u32[]{:S(2)}, u32[]{:S(2)}) collective-permute-start(bf16[1,272,384]{2,1,0:T(8,128)(2,1)} %bitcast.68), channel_id=1, source_target_pairs={{0,3},{1,2},{2,1},{3,0},{4,7},{5,6},{6,5},{7,4},{8,11},{9,10},{10,... | collective-permute-start | bytes 626696 | tf_op jit(solution)/shard_map/ppermute | solution.py:90
  94.8 22.4 %collective-permute-start.19 = (bf16[1,272,384]{2,1,0:T(8,128)(2,1)}, bf16[1,272,384]{2,1,0:T(8,128)(2,1)S(1)}, u32[]{:S(2)}, u32[]{:S(2)}) collective-permute-start(bf16[1,272,384]{2,1,0:T(8,128)(2,1)} %bitcast.69), channel_id=1, source_target_pairs={{0,2},{1,3},{2,0},{3,1},{4,6},{5,7},{6,4},{7,5},{8,10},{9,11},{10,... | collective-permute-start | bytes 626696 | tf_op jit(solution)/shard_map/ppermute | solution.py:90
  95.2 14.3 %collective-permute-start.18 = (bf16[1,272,384]{2,1,0:T(8,128)(2,1)}, bf16[1,272,384]{2,1,0:T(8,128)(2,1)S(1)}, u32[]{:S(2)}, u32[]{:S(2)}) collective-permute-start(bf16[1,272,384]{2,1,0:T(8,128)(2,1)} %bitcast.70), channel_id=1, source_target_pairs={{0,6},{1,7},{2,4},{3,5},{4,2},{5,3},{6,0},{7,1},{8,14},{9,15},{10,... | collective-permute-start | bytes 626696 | tf_op jit(solution)/shard_map/ppermute | solution.py:90
  97.8 19.3 %collective-permute-start.17 = (bf16[1,272,384]{2,1,0:T(8,128)(2,1)}, bf16[1,272,384]{2,1,0:T(8,128)(2,1)S(1)}, u32[]{:S(2)}, u32[]{:S(2)}) collective-permute-start(bf16[1,272,384]{2,1,0:T(8,128)(2,1)} %bitcast.71), channel_id=1, source_target_pairs={{0,4},{1,5},{2,6},{3,7},{4,0},{5,1},{6,2},{7,3},{8,12},{9,13},{10,... | collective-permute-start | bytes 626696 | tf_op jit(solution)/shard_map/ppermute | solution.py:90
  118.4 26.6 %collective-permute-start.23 = (bf16[6,272,384]{2,1,0:T(8,128)(2,1)S(1)}, bf16[6,272,384]{2,1,0:T(8,128)(2,1)S(1)}, u32[]{:S(2)}, u32[]{:S(2)}) collective-permute-start(bf16[6,272,384]{2,1,0:T(8,128)(2,1)S(1)} %constant_dynamic-update-slice_fusion.10.refs_0_), channel_id=1, source_target_pairs={{0,8},{1,9},{2,10},{3,11},{4,12},{5,13},{6,14},{7,15},{8,0},{9,1},... | collective-permute-start | bytes 3760136 | tf_op jit(solution)/shard_map/ppermute | solution.py:90
  118.5 12.1 %collective-permute-start.22 = (bf16[2,272,384]{2,1,0:T(8,128)(2,1)S(1)}, bf16[2,272,384]{2,1,0:T(8,128)(2,1)}, u32[]{:S(2)}, u32[]{:S(2)}) collective-permute-start(bf16[2,272,384]{2,1,0:T(8,128)(2,1)S(1)} %pad_maximum_fusion.3), channel_id=1, source_target_pairs={{0,1},{1,0},{2,3},{3,2},{4,5},{5,4},{6,7},{7,6},{8,9},{9,8},{10,11... | collective-permute-start | bytes 1253384 | tf_op jit(solution)/shard_map/ppermute | solution.py:90
  120.2 24.8 %collective-permute-start.25 = (bf16[4,272,384]{2,1,0:T(8,128)(2,1)}, bf16[4,272,384]{2,1,0:T(8,128)(2,1)S(1)}, u32[]{:S(2)}, u32[]{:S(2)}) collective-permute-start(bf16[4,272,384]{2,1,0:T(8,128)(2,1)} %pad_maximum_fusion), channel_id=1, source_target_pairs={{8,16},{9,17},{10,18},{11,19},{12,20},{13,21},{14,22},{15,23},{16,... | collective-permute-start | bytes 2506760 | tf_op jit(solution)/shard_map/ppermute | solution.py:143
  120.9 24.0 %collective-permute-start.26 = (bf16[2,272,384]{2,1,0:T(8,128)(2,1)S(1)}, bf16[2,272,384]{2,1,0:T(8,128)(2,1)}, u32[]{:S(2)}, u32[]{:S(2)}) collective-permute-start(bf16[2,272,384]{2,1,0:T(8,128)(2,1)S(1)} %pad_maximum_fusion.3), channel_id=1, source_target_pairs={{8,17},{9,16},{10,19},{11,18},{12,21},{13,20},{14,23},{15,22},{16,... | collective-permute-start | bytes 1253384 | tf_op jit(solution)/shard_map/ppermute | solution.py:144
  130.6 14.4 %collective-permute-start.24 = (bf16[2,272,384]{2,1,0:T(8,128)(2,1)}, bf16[2,272,384]{2,1,0:T(8,128)(2,1)}, u32[]{:S(2)}, u32[]{:S(2)}) collective-permute-start(bf16[2,272,384]{2,1,0:T(8,128)(2,1)} %collective-permute-done.22.refs_1_), channel_id=1, source_target_pairs={{0,8},{1,9},{2,10},{3,11},{4,12},{5,13},{6,14},{7,15},{8,0},{9,1},... | collective-permute-start | bytes 1253384 | tf_op jit(solution)/shard_map/ppermute | solution.py:90
  156.8 20.3 %collective-permute-start.27 = (bf16[16,448,128]{2,1,0:T(8,128)(2,1)}, bf16[16,448,128]{2,1,0:T(8,128)(2,1)S(1)}, u32[]{:S(2)}, u32[]{:S(2)}) collective-permute-start(bf16[16,448,128]{2,1,0:T(8,128)(2,1)} %get-tuple-element.86), channel_id=1, source_target_pairs={{0,8},{1,9},{2,10},{3,11},{4,12},{5,13},{6,14},{7,15},{8,0},{9,1},... | collective-permute-start | bytes 5505032 | tf_op jit(solution)/shard_map/ppermute | solution.py:90
  184.1 17.1 %collective-permute-start.30 = (bf16[4,336,128]{2,1,0:T(8,128)(2,1)S(1)}, bf16[4,336,128]{2,1,0:T(8,128)(2,1)S(1)}, u32[]{:S(2)}, u32[]{:S(2)}) collective-permute-start(bf16[4,336,128]{2,1,0:T(8,128)(2,1)S(1)} %get-tuple-element.103), channel_id=1, source_target_pairs={{0,17},{1,16},{2,19},{3,18},{4,21},{5,20},{6,23},{7,22},{8,25},{9,... | collective-permute-start | bytes 1032200 | tf_op jit(solution)/shard_map/ppermute | solution.py:90
  185.9 16.7 %collective-permute-start.29 = (bf16[4,336,128]{2,1,0:T(8,128)(2,1)S(1)}, bf16[4,336,128]{2,1,0:T(8,128)(2,1)S(1)}, u32[]{:S(2)}, u32[]{:S(2)}) collective-permute-start(bf16[4,336,128]{2,1,0:T(8,128)(2,1)S(1)} %get-tuple-element.104), channel_id=1, source_target_pairs={{0,1},{1,0},{2,3},{3,2},{4,5},{5,4},{6,7},{7,6},{8,9},{9,8},{10,11... | collective-permute-start | bytes 1032200 | tf_op jit(solution)/shard_map/ppermute | solution.py:90
  203.5 13.8 %collective-permute-start.33 = (bf16[336,128]{1,0:T(8,128)(2,1)S(1)}, bf16[336,128]{1,0:T(8,128)(2,1)S(1)}, u32[]{:S(2)}, u32[]{:S(2)}) collective-permute-start(bf16[336,128]{1,0:T(8,128)(2,1)S(1)} %get-tuple-element.105), channel_id=1, source_target_pairs={{0,6},{1,7},{2,4},{3,5},{4,2},{5,3},{6,0},{7,1},{8,14},{9,15},{10,... | collective-permute-start | bytes 258056 | tf_op jit(solution)/shard_map/ppermute | solution.py:90
  (34 other events, 360.5 us)

commit v6 on v5

--- a/solution.py
+++ b/solution.py
@@ -108,24 +108,28 @@
                 total = total + part.astype(WIDE)
             return total.astype(LOW)
 
-        def one(buf, axis, level):
-            parts = [lax.index_in_dim(buf, 0, axis, keepdims=False)]
+        def one(pieces, level):
+            parts = [pieces[0]]
             for k, m in enumerate(self.stages[level]):
-                parts.append(self.send(lax.index_in_dim(buf, k + 1, axis, keepdims=False), m))
+                parts.append(self.send(pieces[k + 1], m))
             return parts
 
-        buf = added([keep, self.send(away, self.stages[-1][0])])
+        got = [keep, self.send(away, self.stages[-1][0])]
         if self.grouped:
-            buf = buf.reshape((len(self.stages[1]) + 1, len(self.stages[0]) + 1) + buf.shape[1:])
-            lead, rest = buf[:, :, : self.cut], buf[:, :, self.cut :]
-            lead = one(lead, 0, 1)
-            rest = one(rest, 1, 0)
-            return one(added(lead), 0, 0) + one(added(rest), 0, 1)
+            wide, deep = len(self.stages[1]) + 1, len(self.stages[0]) + 1
+            got = [x.reshape((wide, deep) + x.shape[1:]) for x in got]
+            lead = [added([x[k, :, : self.cut] for x in got]) for k in range(wide)]
+            rest = [added([x[:, k, self.cut :] for x in got]) for k in range(deep)]
+            lead = one(lead, 1)
+            rest = one(rest, 0)
+            lead = [added([x[k] for x in lead]) for k in range(deep)]
+            rest = [added([x[k] for x in rest]) for k in range(wide)]
+            return one(lead, 0) + one(rest, 1)
         for level in reversed(range(len(self.stages) - 1)):
-            buf = buf.reshape((len(self.stages[level]) + 1, -1) + buf.shape[1:])
-            parts = one(buf, 0, level)
-            buf = added(parts)
-        return [part[0] for part in parts]
+            count = len(self.stages[level]) + 1
+            got = [x.reshape((count, -1) + x.shape[1:]) for x in got]
+            got = one([added([x[k] for x in got]) for k in range(count)], level)
+        return [part[0] for part in got]
 
     def exchange(self, block):
         own = block[None]
@@ -136,16 +140,16 @@
             one, two, three, four, six = hops
             pair = jnp.concatenate([four, six], axis=0)
             quad = jnp.concatenate([two, three, four, six], axis=0)
-            row = jnp.concatenate([own, one, quad], axis=0)
-            pair, quad, row = lax.optimization_barrier((pair, quad, row))
-            across = [(8 + j, 16 + j) for j in range(8)] + [(16 + j, 8 + j) for j in range(8)]
-            skew = [(a, b ^ 1) for a, b in across]
+            pair, quad = lax.optimization_barrier((pair, quad))
+            across = [(8 + j, 16 + j) for j in range(6)] + [(16 + j, 8 + j) for j in range(2, 8)]
+            skew = [(8 + j, 16 + (j ^ 1)) for j in range(4)]
+            skew += [(16 + j, 8 + (j ^ 1)) for j in range(4, 8)]
             far = lax.ppermute(quad, BOTH, across)
             far_beside = lax.ppermute(pair, BOTH, skew)
             beside = self.send(pair, 1)
-            home = self.send(row, 8)
+            home = self.send(quad, 8)
             home_beside = self.send(beside, 8)
-            return [row, beside, home, home_beside, far, far_beside]
+            return [own, one, quad, beside, home, home_beside, far, far_beside]
         slots = []
         for slot in range(self.window):
             by = self.reach - slot
@@ -163,11 +167,12 @@
         if self.grouped:
             other = device - self.reach + slot
             mask = (other ^ device) & 7
-            pos = jnp.where(mask == 6, 5, jnp.where(mask == 5, 6, mask))
+            late = (mask == 5) | (mask == 7)
+            index = jnp.where(late, mask >> 2 & mask >> 1, jnp.where(mask == 6, 3, mask - 2))
+            index = jnp.where(mask < 2, 0, index)
+            group = jnp.where(mask < 2, mask, jnp.where(late, 3, 2))
             cross = (other >> 3) ^ (device >> 3)
-            late = pos >= 6
-            source = jnp.where(cross == 0, 0, jnp.where(cross == 1, 2, 4)) + jnp.where(late, 1, 0)
-            index = jnp.where(late, pos - 6, jnp.where(source == 4, pos - 2, pos))
+            source = group + jnp.where(cross == 0, 0, jnp.where(cross == 1, 2, 4))
         else:
             source = jnp.zeros_like(slot)
             index = slot
@@ -197,6 +202,9 @@
 
 def fetch_window(plan, table, sources, dest, sems, lo, hi, wait):
     def step(slot, carry):
+        if wait:
+            pltpu.make_async_copy(sources[0].at[0], dest.at[slot], sems.at[slot]).wait()
+            return carry
         for k, source in enumerate(sources):
 
             @pl.when(table[plan.source_at(slot)] == k)
@@ -204,10 +212,7 @@
                 copy = pltpu.make_async_copy(
                     source.at[table[plan.index_at(slot)]], dest.at[slot], sems.at[slot]
                 )
-                if wait:
-                    copy.wait()
-                else:
-                    copy.start()
+                copy.start()
 
         return carry
 
@@ -354,7 +359,24 @@
 def unpack_kernel(plan):
     half = plan.count // 2
 
-    def kernel(table, near, core, triple_ref, wo, wup, wdn, vec_ref, wbuf, flat, wsem):
+    def kernel(
+        table,
+        near,
+        core,
+        triple_ref,
+        wo_ref,
+        wup_ref,
+        wdn_ref,
+        vec_ref,
+        wbuf,
+        flat,
+        triple,
+        wo,
+        wup,
+        wdn,
+        wsem,
+        osem,
+    ):
         def weight_copy(e, wait):
             t = table[e]
 
@@ -372,13 +394,9 @@
             weight_copy(e, False)
             return carry
 
-        def wait_one(e, carry):
+        lax.fori_loop(0, plan.count, start_one, 0)
+        for e in range(plan.count):
             weight_copy(e, True)
-            return carry
-
-        lax.fori_loop(0, plan.count, start_one, 0)
-        lax.fori_loop(0, plan.count, wait_one, 0)
-        for e in range(plan.count):
             r0 = plan.start[e]
             block = wbuf[e].astype(WIDE)
             if e:
@@ -397,14 +415,20 @@
                         pl.ds(AT[name] + i * wide + j, step, stride=wide), :
                     ].astype(LOW)
 
-        unfold(triple_ref, "triple", D, 3 * D)
+        unfold(wup, "up", D, FF)
+        saves = [launch(wup, wup_ref, osem.at[0])]
+        unfold(wdn, "down", FF, D)
+        saves.append(launch(wdn, wdn_ref, osem.at[1]))
+        unfold(triple, "triple", D, 3 * D)
+        saves.append(launch(triple, triple_ref, osem.at[2]))
         unfold(wo, "out", D, D)
-        unfold(wup, "up", D, FF)
-        unfold(wdn, "down", FF, D)
+        saves.append(launch(wo, wo_ref, osem.at[3]))
         vec_ref[...] = jnp.zeros(vec_ref.shape, WIDE)
         for name, row in VEC.items():
             width = dict(PIECES)[name]
             vec_ref[row : row + 1, :width] = vector(flat, AT[name], width)
+        for save in saves:
+            save.wait()
 
     return kernel
 
@@ -902,7 +926,7 @@
         unpack = pl.pallas_call(
             unpack_kernel(plan),
             in_specs=[SMEM, ANY, ANY],
-            out_specs=[VMEM] * 5,
+            out_specs=[ANY] * 4 + [VMEM],
             out_shape=[
                 shape((D, 3 * D), LOW),
                 shape((D, D), LOW),
@@ -913,7 +937,12 @@
             scratch_shapes=[
                 pltpu.VMEM((N, R, LANES), LOW),
                 pltpu.VMEM((plan.flat_rows, LANES), WIDE),
+                pltpu.VMEM((D, 3 * D), LOW),
+                pltpu.VMEM((D, D), LOW),
+                pltpu.VMEM((D, FF), LOW),
+                pltpu.VMEM((FF, D), LOW),
                 pltpu.SemaphoreType.DMA((N,)),
+                pltpu.SemaphoreType.DMA((4,)),
             ],
             compiler_params=limit,
             name="unpack",

time: 235 us -> 243 us (1.034)
  starting transfers between devices: 76 us -> 81.3 us
  waiting for transfers between devices: 77.9 us -> 80.6 us
  local copies, waits for them, and re-layouts: 9.06 us -> 6.56 us
    ppermute x36, starting transfers between devices: 70.9 us -> 77.8 us  [send(): return lax.ppermute(x, BOTH, [(i, i ^ mask) for i in range(self.count)])]
    ppermute x36, waiting for transfers between devices: 77.9 us -> 80.6 us  [send(): return lax.ppermute(x, BOTH, [(i, i ^ mask) for i in range(self.count)])]
  transfers between devices with their start and end apart: 40 -> 40, of which waited for: 15 -> 18; matrix products, arithmetic and copies ran while one was open for 4% -> 4% of each run, Pallas kernels for 8% -> 8%
where the time goes in v6:
time: 243 us
  starting transfers between devices  81.3 us (33%)
  waiting for transfers between devices  80.6 us (33%)
  Pallas kernels  48.1 us (20%)
  other arithmetic  12.4 us (5%)
  blocking collectives  10.8 us (4%)
  local copies, waits for them, and re-layouts  6.56 us (3%)
  between operations  3.01 us (1%)
    ppermute x36, waiting for transfers between devices, send(): return lax.ppermute(x, BOTH, [(i, i ^ mask) for i in range(self.count)])  80.6 us
    ppermute x36, starting transfers between devices, send(): return lax.ppermute(x, BOTH, [(i, i ^ mask) for i in range(self.count)])  77.8 us
    pallas_call x1, Pallas kernels, per_device(): pl.pallas_call(forward_kernel(plan, sources), in_specs=[SMEM] + [ANY] * s...  14 us
    all_to_all x1, blocking collectives, per_device(): squares = lax.all_to_all(square, BOTH, 0, 0, tiled=True)  10.8 us
    pallas_call x1, Pallas kernels, per_device(): pl.pallas_call(last_kernel(plan, sources), in_specs=[SMEM] + [ANY] * (sou...  10.4 us
    pallas_call x1, Pallas kernels, per_device(): gq = query_call(table, q, k, v, message, stat, columns, key_ids)  7.68 us
    pallas_call x1, Pallas kernels, per_device(): weight_call(table, norms, triple, params, act, gpre, gbt, n2, att, gbo, vec)  6.6 us
    pallas_call x1, Pallas kernels, per_device(): triple, wo, wup, wdn, params = unpack(table, near, core)  5.73 us
  transfers between devices with their start and end apart: 40, of which 18 were waited for; matrix products, arithmetic and copies ran while one was open for 4% of the time, Pallas kernels for 8%

profile of v6, /device:TPU:0, one launch (start us, length us, event | category | flops | bytes accessed | tf_op | source)
XLA Modules:
  0.0 242.7 jit_solution(6660825680370823866)
XLA Ops:
  4.0 5.1 %collective-permute-start.2 = (bf16[1,448,128]{2,1,0:T(8,128)(2,1)}, bf16[1,448,128]{2,1,0:T(8,128)(2,1)S(1)}, u32[]{:S(2)}, u32[]{:S(2)}) collective-permute-start(bf16[1,448,128]{2,1,0:T(8,128)(2,1)} %bitcast.100), channel_id=1, source_target_pairs={{0,6},{1,7},{2,4},{3,5},{4,2},{5,3},{6,0},{7,1},{8,14},{9,15},{10,... | collective-permute-start | bytes 344072 | tf_op jit(solution)/shard_map/ppermute | solution.py:90
  9.7 3.7 %collective-permute-done.2 = bf16[1,448,128]{2,1,0:T(8,128)(2,1)S(1)} collective-permute-done((bf16[1,448,128]{2,1,0:T(8,128)(2,1)}, bf16[1,448,128]{2,1,0:T(8,128)(2,1)S(1)}, u32[]{:S(2)}, u32[]{:S(2)}) %collective-permute-start.2) | collective-permute-done | bytes 114720 | tf_op jit(solution)/shard_map/ppermute | solution.py:90
  13.4 5.6 %collective-permute-done.1 = bf16[1,448,128]{2,1,0:T(8,128)(2,1)S(1)} collective-permute-done((bf16[1,448,128]{2,1,0:T(8,128)(2,1)}, bf16[1,448,128]{2,1,0:T(8,128)(2,1)S(1)}, u32[]{:S(2)}, u32[]{:S(2)}) %collective-permute-start.1) | collective-permute-done | bytes 114720 | tf_op jit(solution)/shard_map/ppermute | solution.py:90
  23.5 9.9 %collective-permute-done.13 = bf16[4,448,128]{2,1,0:T(8,128)(2,1)S(1)} collective-permute-done((bf16[4,448,128]{2,1,0:T(8,128)(2,1)S(1)}, bf16[4,448,128]{2,1,0:T(8,128)(2,1)S(1)}, u32[]{:S(2)}, u32[]{:S(2)}) %collective-permute-start.13) | collective-permute-done | bytes 458784 | tf_op jit(solution)/shard_map/ppermute | solution.py:90
  33.5 9.2 %collective-permute-done.14 = bf16[4,448,128]{2,1,0:T(8,128)(2,1)S(1)} collective-permute-done((bf16[4,448,128]{2,1,0:T(8,128)(2,1)S(1)}, bf16[4,448,128]{2,1,0:T(8,128)(2,1)S(1)}, u32[]{:S(2)}, u32[]{:S(2)}) %collective-permute-start.14) | collective-permute-done | bytes 458784 | tf_op jit(solution)/shard_map/ppermute | solution.py:90
  48.4 4.4 %collective-permute-done.5 = bf16[1,256,384]{2,1,0:T(8,128)(2,1)S(1)} collective-permute-done((bf16[1,256,384]{2,1,0:T(8,128)(2,1)S(1)}, bf16[1,256,384]{2,1,0:T(8,128)(2,1)S(1)}, u32[]{:S(2)}, u32[]{:S(2)}) %collective-permute-start.5) | collective-permute-done | bytes 196640 | tf_op jit(solution)/shard_map/ppermute | solution.py:90
  52.7 9.7 %collective-permute-done.4 = bf16[1,256,384]{2,1,0:T(8,128)(2,1)S(1)} collective-permute-done((bf16[1,256,384]{2,1,0:T(8,128)(2,1)S(1)}, bf16[1,256,384]{2,1,0:T(8,128)(2,1)S(1)}, u32[]{:S(2)}, u32[]{:S(2)}) %collective-permute-start.4) | collective-permute-done | bytes 196640 | tf_op jit(solution)/shard_map/ppermute | solution.py:90
  72.4 5.0 %collective-permute-done.8.refs_3_ = bf16[2,256,384]{2,1,0:T(8,128)(2,1)} collective-permute-done((bf16[2,256,384]{2,1,0:T(8,128)(2,1)}, bf16[2,256,384]{2,1,0:T(8,128)(2,1)}, u32[]{:S(2)}, u32[]{:S(2)}) %collective-permute-start.8) | collective-permute-done | bytes 393248 | tf_op jit(solution)/shard_map/ppermute | solution.py:90
  81.5 5.7 %unpack.1 = (bf16[384,1152]{1,0:T(8,128)(2,1)}, bf16[384,384]{1,0:T(8,128)(2,1)}, bf16[384,1536]{1,0:T(8,128)(2,1)}, bf16[1536,384]{1,0:T(8,128)(2,1)}, f32[16,1536]{1,0:T(8,128)}) custom-call(s32[64]{0:T(128)} %concatenate.22.table, bf16[16,448,128]{2,1,0:T(8,128)(2,1)} %copy-done.2, bf16[16,448,128]{2,1,0:T(8,128)(2,1)} %collective-permute-done.16.core), custom_call_target="tpu_custom_call" | custom-call | tf_op jit(solution)/shard_map/unpack/pallas_call | solution.py:950
  88.3 14.0 %forward.1 = (bf16[256,384]{1,0:T(8,128)(2,1)}, bf16[272,384]{1,0:T(8,128)(2,1)}, bf16[256,384]{1,0:T(8,128)(2,1)}, bf16[13,256,384]{2,1,0:T(8,128)(2,1)}, bf16[...) custom-call(s32[64]{0:T(128)} %concatenate.22.table, ...), custom_call_target="tpu_custom_call" | custom-call | tf_op jit(solution)/shard_map/forward/pallas_call | solution.py:952
  102.3 7.1 %collective-permute-start.19 = (bf16[1,272,384]{2,1,0:T(8,128)(2,1)}, bf16[1,272,384]{2,1,0:T(8,128)(2,1)S(1)}, u32[]{:S(2)}, u32[]{:S(2)}) collective-permute-start(bf16[1,272,384]{2,1,0:T(8,128)(2,1)} %bitcast.88), channel_id=1, source_target_pairs={{0,6},{1,7},{2,4},{3,5},{4,2},{5,3},{6,0},{7,1},{8,14},{9,15},{10,... | collective-permute-start | bytes 626696 | tf_op jit(solution)/shard_map/ppermute | solution.py:90
  114.2 12.3 %collective-permute-done.18 = bf16[1,272,384]{2,1,0:T(8,128)(2,1)S(1)} collective-permute-done((bf16[1,272,384]{2,1,0:T(8,128)(2,1)}, bf16[1,272,384]{2,1,0:T(8,128)(2,1)S(1)}, u32[]{:S(2)}, u32[]{:S(2)}) %collective-permute-start.18) | collective-permute-done | bytes 208928 | tf_op jit(solution)/shard_map/ppermute | solution.py:90
  131.9 5.2 %collective-permute-start.23 = (bf16[4,272,384]{2,1,0:T(8,128)(2,1)S(1)}, bf16[4,272,384]{2,1,0:T(8,128)(2,1)S(1)}, u32[]{:S(2)}, u32[]{:S(2)}) collective-permute-start(bf16[4,272,384]{2,1,0:T(8,128)(2,1)S(1)} %pad_maximum_fusion.refs_2_), channel_id=1, source_target_pairs={{0,8},{1,9},{2,10},{3,11},{4,12},{5,13},{6,14},{7,15},{8,0},{9,1},... | collective-permute-start | bytes 2506760 | tf_op jit(solution)/shard_map/ppermute | solution.py:90
  137.7 3.8 %collective-permute-done.22.refs_3_ = bf16[2,272,384]{2,1,0:T(8,128)(2,1)S(1)} collective-permute-done((bf16[2,272,384]{2,1,0:T(8,128)(2,1)}, bf16[2,272,384]{2,1,0:T(8,128)(2,1)S(1)}, u32[]{:S(2)}, u32[]{:S(2)}) %collective-permute-start.22) | collective-permute-done | bytes 417824 | tf_op jit(solution)/shard_map/ppermute | solution.py:90
  143.2 7.7 %query.1.refs_13_ = bf16[256,384]{1,0:T(8,128)(2,1)} custom-call(s32[64]{0:T(128)} %concatenate.22.table, bf16[256,384]{1,0:T(8,128)(2,1)} %get-tuple-element.71.q_ref, bf16[13,256,384]{2,1,0:T(8,128)(2,1)} %get-tuple-element.72.k_ref, bf16[13,256,384]{2,1,0:T(8,128)(2,1)} %get-tuple-element.73.v_ref, bf16[272,384]{1,0:T(8,128)(2,1)} %get-tuple-element.57.msg_ref, ...), custom_call_target="tpu_custom_call" | custom-call | tf_op jit(solution)/shard_map/query/pallas_call | solution.py:1037
  150.9 6.6 %weight.1 = (bf16[13,256,384]{2,1,0:T(8,128)(2,1)}, bf16[16,448,128]{2,1,0:T(8,128)(2,1)}, bf16[16,448,128]{2,1,0:T(8,128)(2,1)}, f32[448,128]{1,0:T(8,128)}) custom-call(s32[64]{0:T(128)} %concatenate.22.table, bf16[13,256,384]{2,1,0:T(8,128)(2,1)} %get-tuple-element.60.norm_ref, bf16[384,1152]{1,0:T(8,128)(2,1)} %get-tuple-element.51.refs_8_.triple_ref.refs_15_, ...), custom_call_target="tpu_custom_call" | custom-call | tf_op jit(solution)/shard_map/weight/pallas_call | solution.py:1060
  159.0 10.4 %last.1 = (f32[256,384]{1,0:T(8,128)}, bf16[16,448,128]{2,1,0:T(8,128)(2,1)}, bf16[16,448,128]{2,1,0:T(8,128)(2,1)}) custom-call(s32[64]{0:T(128)} %concatenate.22.table, bf16[1,272,384]{2,1,0:T(8,128)(2,1)} %bitcast.92, bf16[1,272,384]{2,1,0:T(8,128)(2,1)} %collective-permute-done.17.refs_1_, ...), custom_call_target="tpu_custom_call", output_to_operand_aliasing={{1}: (21, {}), {2}: (22, {})} | custom-call | tf_op jit(solution)/shard_map/last/pallas_call | solution.py:1065
  169.4 16.5 %collective-permute-start.27 = (bf16[16,448,128]{2,1,0:T(8,128)(2,1)}, bf16[16,448,128]{2,1,0:T(8,128)(2,1)S(1)}, u32[]{:S(2)}, u32[]{:S(2)}) collective-permute-start(bf16[16,448,128]{2,1,0:T(8,128)(2,1)} %get-tuple-element.82), channel_id=1, source_target_pairs={{0,8},{1,9},{2,10},{3,11},{4,12},{5,13},{6,14},{7,15},{8,0},{9,1},... | collective-permute-start | bytes 5505032 | tf_op jit(solution)/shard_map/ppermute | solution.py:90
  186.0 3.6 %collective-permute-done.27 = bf16[16,448,128]{2,1,0:T(8,128)(2,1)S(1)} collective-permute-done((bf16[16,448,128]{2,1,0:T(8,128)(2,1)}, bf16[16,448,128]{2,1,0:T(8,128)(2,1)S(1)}, u32[]{:S(2)}, u32[]{:S(2)}) %collective-permute-start.27) | collective-permute-done | bytes 1835040 | tf_op jit(solution)/shard_map/ppermute | solution.py:90
  191.4 4.4 %collective-permute-start.29 = (bf16[4,336,128]{2,1,0:T(8,128)(2,1)S(1)}, bf16[4,336,128]{2,1,0:T(8,128)(2,1)S(1)}, u32[]{:S(2)}, u32[]{:S(2)}) collective-permute-start(bf16[4,336,128]{2,1,0:T(8,128)(2,1)S(1)} %get-tuple-element.101), channel_id=1, source_target_pairs={{0,1},{1,0},{2,3},{3,2},{4,5},{5,4},{6,7},{7,6},{8,9},{9,8},{10,11... | collective-permute-start | bytes 1032200 | tf_op jit(solution)/shard_map/ppermute | solution.py:90
  197.1 3.8 %collective-permute-start.35 = (bf16[4,112,128]{2,1,0:T(8,128)(2,1)S(1)}, bf16[4,112,128]{2,1,0:T(8,128)(2,1)S(1)}, u32[]{:S(2)}, u32[]{:S(2)}) collective-permute-start(bf16[4,112,128]{2,1,0:T(8,128)(2,1)S(1)} %get-tuple-element.97), channel_id=1, source_target_pairs={{0,4},{1,5},{2,6},{3,7},{4,0},{5,1},{6,2},{7,3},{8,12},{9,13},{10,... | collective-permute-start | bytes 344072 | tf_op jit(solution)/shard_map/ppermute | solution.py:90
  206.6 3.4 %collective-permute-done.29 = bf16[4,336,128]{2,1,0:T(8,128)(2,1)S(1)} collective-permute-done((bf16[4,336,128]{2,1,0:T(8,128)(2,1)S(1)}, bf16[4,336,128]{2,1,0:T(8,128)(2,1)S(1)}, u32[]{:S(2)}, u32[]{:S(2)}) %collective-permute-start.29) | collective-permute-done | bytes 344096 | tf_op jit(solution)/shard_map/ppermute | solution.py:90
  211.2 4.5 %collective-permute-start.32 = (bf16[336,128]{1,0:T(8,128)(2,1)S(1)}, bf16[336,128]{1,0:T(8,128)(2,1)S(1)}, u32[]{:S(2)}, u32[]{:S(2)}) collective-permute-start(bf16[336,128]{1,0:T(8,128)(2,1)S(1)} %get-tuple-element.104), channel_id=1, source_target_pairs={{0,4},{1,5},{2,6},{3,7},{4,0},{5,1},{6,2},{7,3},{8,12},{9,13},{10,... | collective-permute-start | bytes 258056 | tf_op jit(solution)/shard_map/ppermute | solution.py:90
  227.6 10.8 %all_to_all.12 = f32[32,1,128]{2,1,0:T(1,128)S(1)} all-to-all(f32[32,1,128]{2,1,0:T(1,128)} %bitcast.106), channel_id=1, replica_groups=mesh['dp'=4,'fsdp'=8] {'dp','fsdp'}, dimensions={0} | all-to-all | bytes 32768 | tf_op jit(solution)/shard_map/all_to_all | solution.py:1122
  (140 shorter events, 67.3 us)
Async XLA Ops:
  21.5 21.1 %collective-permute-start.14 = (bf16[4,448,128]{2,1,0:T(8,128)(2,1)S(1)}, bf16[4,448,128]{2,1,0:T(8,128)(2,1)S(1)}, u32[]{:S(2)}, u32[]{:S(2)}) collective-permute-start(bf16[4,448,128]{2,1,0:T(8,128)(2,1)S(1)} %pad_maximum_fusion.2), channel_id=1, source_target_pairs={{0,1},{1,0},{2,3},{3,2},{4,5},{5,4},{6,7},{7,6},{8,9},{9,8},{10,11... | collective-permute-start | bytes 1376264 | tf_op jit(solution)/shard_map/ppermute | solution.py:90
  23.0 19.7 %collective-permute-start.15 = (bf16[4,448,128]{2,1,0:T(8,128)(2,1)S(1)}, bf16[4,448,128]{2,1,0:T(8,128)(2,1)S(1)}, u32[]{:S(2)}, u32[]{:S(2)}) collective-permute-start(bf16[4,448,128]{2,1,0:T(8,128)(2,1)S(1)} %pad_maximum_fusion.2), channel_id=1, source_target_pairs={{0,17},{1,16},{2,19},{3,18},{4,21},{5,20},{6,23},{7,22},{8,25},{9,... | collective-permute-start | bytes 1376264 | tf_op jit(solution)/shard_map/ppermute | solution.py:90
  42.8 35.0 %collective-permute-start.16 = (bf16[16,448,128]{2,1,0:T(8,128)(2,1)S(1)}, bf16[16,448,128]{2,1,0:T(8,128)(2,1)}, u32[]{:S(2)}, u32[]{:S(2)}) collective-permute-start(bf16[16,448,128]{2,1,0:T(8,128)(2,1)S(1)} %constant_dynamic-update-slice_fusion.near), channel_id=1, source_target_pairs={{0,8},{1,9},{2,10},{3,11},{4,12},{5,13},{6,14},{7,15},{8,0},{9,1},... | collective-permute-start | bytes 5505032 | tf_op jit(solution)/shard_map/ppermute | solution.py:90
  45.3 17.1 %collective-permute-start.4 = (bf16[1,256,384]{2,1,0:T(8,128)(2,1)S(1)}, bf16[1,256,384]{2,1,0:T(8,128)(2,1)S(1)}, u32[]{:S(2)}, u32[]{:S(2)}) collective-permute-start(bf16[1,256,384]{2,1,0:T(8,128)(2,1)S(1)} %bitcast.97), channel_id=1, source_target_pairs={{0,4},{1,5},{2,6},{3,7},{4,0},{5,1},{6,2},{7,3},{8,12},{9,13},{10,... | collective-permute-start | bytes 589832 | tf_op jit(solution)/shard_map/ppermute | solution.py:90
  45.3 17.9 %collective-permute-start.7 = (bf16[1,256,384]{2,1,0:T(8,128)(2,1)S(1)}, bf16[1,256,384]{2,1,0:T(8,128)(2,1)S(1)}, u32[]{:S(2)}, u32[]{:S(2)}) collective-permute-start(bf16[1,256,384]{2,1,0:T(8,128)(2,1)S(1)} %bitcast.98), channel_id=1, source_target_pairs={{0,3},{1,2},{2,1},{3,0},{4,7},{5,6},{6,5},{7,4},{8,11},{9,10},{10,... | collective-permute-start | bytes 589832 | tf_op jit(solution)/shard_map/ppermute | solution.py:90
  48.3 16.5 %collective-permute-start.6 = (bf16[1,256,384]{2,1,0:T(8,128)(2,1)S(1)}, bf16[1,256,384]{2,1,0:T(8,128)(2,1)}, u32[]{:S(2)}, u32[]{:S(2)}) collective-permute-start(bf16[1,256,384]{2,1,0:T(8,128)(2,1)S(1)} %bitcast.99), channel_id=1, source_target_pairs={{0,2},{1,3},{2,0},{3,1},{4,6},{5,7},{6,4},{7,5},{8,10},{9,11},{10,... | collective-permute-start | bytes 589832 | tf_op jit(solution)/shard_map/ppermute | solution.py:90
  67.5 19.8 %collective-permute-start.11 = (bf16[4,256,384]{2,1,0:T(8,128)(2,1)S(1)}, bf16[4,256,384]{2,1,0:T(8,128)(2,1)S(1)}, u32[]{:S(2)}, u32[]{:S(2)}) collective-permute-start(bf16[4,256,384]{2,1,0:T(8,128)(2,1)S(1)} %pad_maximum_fusion.1.refs_2_), channel_id=1, source_target_pairs={{8,16},{9,17},{10,18},{11,19},{12,20},{13,21},{18,10},{19,11},{20,... | collective-permute-start | bytes 2359304 | tf_op jit(solution)/shard_map/ppermute | solution.py:147
  68.2 19.1 %collective-permute-start.9 = (bf16[4,256,384]{2,1,0:T(8,128)(2,1)S(1)}, bf16[4,256,384]{2,1,0:T(8,128)(2,1)}, u32[]{:S(2)}, u32[]{:S(2)}) collective-permute-start(bf16[4,256,384]{2,1,0:T(8,128)(2,1)S(1)} %pad_maximum_fusion.1.refs_2_), channel_id=1, source_target_pairs={{0,8},{1,9},{2,10},{3,11},{4,12},{5,13},{6,14},{7,15},{8,0},{9,1},... | collective-permute-start | bytes 2359304 | tf_op jit(solution)/shard_map/ppermute | solution.py:90
  71.0 16.3 %collective-permute-start.12 = (bf16[2,256,384]{2,1,0:T(8,128)(2,1)}, bf16[2,256,384]{2,1,0:T(8,128)(2,1)}, u32[]{:S(2)}, u32[]{:S(2)}) collective-permute-start(bf16[2,256,384]{2,1,0:T(8,128)(2,1)} %pad_maximum_fusion.4), channel_id=1, source_target_pairs={{8,17},{9,16},{10,19},{11,18},{20,13},{21,12},{22,15},{23,14}} | collective-permute-start | bytes 1179656 | tf_op jit(solution)/shard_map/ppermute | solution.py:148
  109.4 17.1 %collective-permute-start.18 = (bf16[1,272,384]{2,1,0:T(8,128)(2,1)}, bf16[1,272,384]{2,1,0:T(8,128)(2,1)S(1)}, u32[]{:S(2)}, u32[]{:S(2)}) collective-permute-start(bf16[1,272,384]{2,1,0:T(8,128)(2,1)} %bitcast.89), channel_id=1, source_target_pairs={{0,4},{1,5},{2,6},{3,7},{4,0},{5,1},{6,2},{7,3},{8,12},{9,13},{10,... | collective-permute-start | bytes 626696 | tf_op jit(solution)/shard_map/ppermute | solution.py:90
  109.4 17.9 %collective-permute-start.21 = (bf16[1,272,384]{2,1,0:T(8,128)(2,1)}, bf16[1,272,384]{2,1,0:T(8,128)(2,1)S(1)}, u32[]{:S(2)}, u32[]{:S(2)}) collective-permute-start(bf16[1,272,384]{2,1,0:T(8,128)(2,1)} %bitcast.90), channel_id=1, source_target_pairs={{0,3},{1,2},{2,1},{3,0},{4,7},{5,6},{6,5},{7,4},{8,11},{9,10},{10,... | collective-permute-start | bytes 626696 | tf_op jit(solution)/shard_map/ppermute | solution.py:90
  111.0 16.6 %collective-permute-start.20 = (bf16[1,272,384]{2,1,0:T(8,128)(2,1)}, bf16[1,272,384]{2,1,0:T(8,128)(2,1)S(1)}, u32[]{:S(2)}, u32[]{:S(2)}) collective-permute-start(bf16[1,272,384]{2,1,0:T(8,128)(2,1)} %bitcast.91), channel_id=1, source_target_pairs={{0,2},{1,3},{2,0},{3,1},{4,6},{5,7},{6,4},{7,5},{8,10},{9,11},{10,... | collective-permute-start | bytes 626696 | tf_op jit(solution)/shard_map/ppermute | solution.py:90
  131.2 26.4 %collective-permute-start.25 = (bf16[4,272,384]{2,1,0:T(8,128)(2,1)S(1)}, bf16[4,272,384]{2,1,0:T(8,128)(2,1)S(1)}, u32[]{:S(2)}, u32[]{:S(2)}) collective-permute-start(bf16[4,272,384]{2,1,0:T(8,128)(2,1)S(1)} %pad_maximum_fusion.refs_2_), channel_id=1, source_target_pairs={{8,16},{9,17},{10,18},{11,19},{12,20},{13,21},{18,10},{19,11},{20,... | collective-permute-start | bytes 2506760 | tf_op jit(solution)/shard_map/ppermute | solution.py:147
  131.9 25.7 %collective-permute-start.23 = (bf16[4,272,384]{2,1,0:T(8,128)(2,1)S(1)}, bf16[4,272,384]{2,1,0:T(8,128)(2,1)S(1)}, u32[]{:S(2)}, u32[]{:S(2)}) collective-permute-start(bf16[4,272,384]{2,1,0:T(8,128)(2,1)S(1)} %pad_maximum_fusion.refs_2_), channel_id=1, source_target_pairs={{0,8},{1,9},{2,10},{3,11},{4,12},{5,13},{6,14},{7,15},{8,0},{9,1},... | collective-permute-start | bytes 2506760 | tf_op jit(solution)/shard_map/ppermute | solution.py:90
  137.1 20.4 %collective-permute-start.26 = (bf16[2,272,384]{2,1,0:T(8,128)(2,1)}, bf16[2,272,384]{2,1,0:T(8,128)(2,1)S(1)}, u32[]{:S(2)}, u32[]{:S(2)}) collective-permute-start(bf16[2,272,384]{2,1,0:T(8,128)(2,1)} %pad_maximum_fusion.3), channel_id=1, source_target_pairs={{8,17},{9,16},{10,19},{11,18},{20,13},{21,12},{22,15},{23,14}} | collective-permute-start | bytes 1253384 | tf_op jit(solution)/shard_map/ppermute | solution.py:148
  141.6 15.9 %collective-permute-start.24 = (bf16[2,272,384]{2,1,0:T(8,128)(2,1)S(1)}, bf16[2,272,384]{2,1,0:T(8,128)(2,1)S(1)}, u32[]{:S(2)}, u32[]{:S(2)}) collective-permute-start(bf16[2,272,384]{2,1,0:T(8,128)(2,1)S(1)} %collective-permute-done.22.refs_3_), channel_id=1, source_target_pairs={{0,8},{1,9},{2,10},{3,11},{4,12},{5,13},{6,14},{7,15},{8,0},{9,1},... | collective-permute-start | bytes 1253384 | tf_op jit(solution)/shard_map/ppermute | solution.py:90
  141.6 15.9 %collective-permute-start.17 = (bf16[1,272,384]{2,1,0:T(8,128)(2,1)S(1)}, bf16[1,272,384]{2,1,0:T(8,128)(2,1)}, u32[]{:S(2)}, u32[]{:S(2)}) collective-permute-start(bf16[1,272,384]{2,1,0:T(8,128)(2,1)S(1)} %bitcast.93), channel_id=1, source_target_pairs={{0,1},{1,0},{2,3},{3,2},{4,5},{5,4},{6,7},{7,6},{8,9},{9,8},{10,11... | collective-permute-start | bytes 626696 | tf_op jit(solution)/shard_map/ppermute | solution.py:90
  169.4 20.2 %collective-permute-start.27 = (bf16[16,448,128]{2,1,0:T(8,128)(2,1)}, bf16[16,448,128]{2,1,0:T(8,128)(2,1)S(1)}, u32[]{:S(2)}, u32[]{:S(2)}) collective-permute-start(bf16[16,448,128]{2,1,0:T(8,128)(2,1)} %get-tuple-element.82), channel_id=1, source_target_pairs={{0,8},{1,9},{2,10},{3,11},{4,12},{5,13},{6,14},{7,15},{8,0},{9,1},... | collective-permute-start | bytes 5505032 | tf_op jit(solution)/shard_map/ppermute | solution.py:90
  191.4 18.6 %collective-permute-start.29 = (bf16[4,336,128]{2,1,0:T(8,128)(2,1)S(1)}, bf16[4,336,128]{2,1,0:T(8,128)(2,1)S(1)}, u32[]{:S(2)}, u32[]{:S(2)}) collective-permute-start(bf16[4,336,128]{2,1,0:T(8,128)(2,1)S(1)} %get-tuple-element.101), channel_id=1, source_target_pairs={{0,1},{1,0},{2,3},{3,2},{4,5},{5,4},{6,7},{7,6},{8,9},{9,8},{10,11... | collective-permute-start | bytes 1032200 | tf_op jit(solution)/shard_map/ppermute | solution.py:90
  195.8 14.5 %collective-permute-start.28 = (bf16[4,336,128]{2,1,0:T(8,128)(2,1)S(1)}, bf16[4,336,128]{2,1,0:T(8,128)(2,1)S(1)}, u32[]{:S(2)}, u32[]{:S(2)}) collective-permute-start(bf16[4,336,128]{2,1,0:T(8,128)(2,1)S(1)} %get-tuple-element.102), channel_id=1, source_target_pairs={{0,16},{1,17},{2,18},{3,19},{4,20},{5,21},{6,22},{7,23},{8,24},{9,... | collective-permute-start | bytes 1032200 | tf_op jit(solution)/shard_map/ppermute | solution.py:90
  197.1 18.6 %collective-permute-start.36 = (bf16[4,112,128]{2,1,0:T(8,128)(2,1)S(1)}, bf16[4,112,128]{2,1,0:T(8,128)(2,1)S(1)}, u32[]{:S(2)}, u32[]{:S(2)}) collective-permute-start(bf16[4,112,128]{2,1,0:T(8,128)(2,1)S(1)} %get-tuple-element.96), channel_id=1, source_target_pairs={{0,6},{1,7},{2,4},{3,5},{4,2},{5,3},{6,0},{7,1},{8,14},{9,15},{10,... | collective-permute-start | bytes 344072 | tf_op jit(solution)/shard_map/ppermute | solution.py:90
  197.1 18.5 %collective-permute-start.35 = (bf16[4,112,128]{2,1,0:T(8,128)(2,1)S(1)}, bf16[4,112,128]{2,1,0:T(8,128)(2,1)S(1)}, u32[]{:S(2)}, u32[]{:S(2)}) collective-permute-start(bf16[4,112,128]{2,1,0:T(8,128)(2,1)S(1)} %get-tuple-element.97), channel_id=1, source_target_pairs={{0,4},{1,5},{2,6},{3,7},{4,0},{5,1},{6,2},{7,3},{8,12},{9,13},{10,... | collective-permute-start | bytes 344072 | tf_op jit(solution)/shard_map/ppermute | solution.py:90
  211.1 13.8 %collective-permute-start.33 = (bf16[336,128]{1,0:T(8,128)(2,1)S(1)}, bf16[336,128]{1,0:T(8,128)(2,1)S(1)}, u32[]{:S(2)}, u32[]{:S(2)}) collective-permute-start(bf16[336,128]{1,0:T(8,128)(2,1)S(1)} %get-tuple-element.103), channel_id=1, source_target_pairs={{0,6},{1,7},{2,4},{3,5},{4,2},{5,3},{6,0},{7,1},{8,14},{9,15},{10,... | collective-permute-start | bytes 258056 | tf_op jit(solution)/shard_map/ppermute | solution.py:90
  211.2 13.8 %collective-permute-start.32 = (bf16[336,128]{1,0:T(8,128)(2,1)S(1)}, bf16[336,128]{1,0:T(8,128)(2,1)S(1)}, u32[]{:S(2)}, u32[]{:S(2)}) collective-permute-start(bf16[336,128]{1,0:T(8,128)(2,1)S(1)} %get-tuple-element.104), channel_id=1, source_target_pairs={{0,4},{1,5},{2,6},{3,7},{4,0},{5,1},{6,2},{7,3},{8,12},{9,13},{10,... | collective-permute-start | bytes 258056 | tf_op jit(solution)/shard_map/ppermute | solution.py:90
  (39 other events, 521.0 us)

commit v7 on v6

--- a/solution.py
+++ b/solution.py
@@ -66,7 +66,7 @@
         self.share = share
         self.rows = -(-(2 * (LANES - 1) + share) // LANES)
         self.rows = -(-self.rows // 16) * 16
-        self.cut = self.rows * 3 // 64 * 16
+        self.cut = self.rows * 11 // 16 // 16 * 16
         self.start = [e * share // LANES for e in range(self.count)]
         self.tokens = tokens
         self.part = tokens // 2
@@ -1046,7 +1046,7 @@
                 shape((R, LANES), WIDE),
             ],
             scratch_shapes=[
-                pltpu.VMEM((plan.flat_rows - AT["out"] + 8, LANES), WIDE),
+                pltpu.VMEM((-(-(plan.flat_rows - AT["out"]) // 8) * 8 + 8, LANES), WIDE),
                 pltpu.VMEM((N - plan.first_late, R, LANES), LOW),
                 pltpu.VMEM((W, T, D), LOW),
                 pltpu.VMEM((W, T, D), LOW),
@@ -1075,7 +1075,7 @@
                 pltpu.VMEM((W, T + 16, D), LOW),
                 pltpu.VMEM((W, T, D), LOW),
                 pltpu.VMEM((D, 3 * D), LOW),
-                pltpu.VMEM((AT["out"] + R + 8, LANES), WIDE),
+                pltpu.VMEM((-(-(AT["out"] + R) // 8) * 8 + 8, LANES), WIDE),
                 pltpu.VMEM((T, 3 * D), LOW),
                 pltpu.VMEM((late, R, LANES), LOW),
                 pltpu.VMEM((W, 16, T), WIDE),

time: 243 us -> 242 us (level)
  no operation moved by 1% of the time
where the time goes in v7:
time: 242 us; the launch traced here: 241 us
  starting transfers between devices  81.4 us (34%)
  waiting for transfers between devices  79.2 us (33%)
  Pallas kernels  48.1 us (20%)
  other arithmetic  12.4 us (5%)
  blocking collectives  10.8 us (4%)
  local copies, waits for them, and re-layouts  6.56 us (3%)
  between operations  3.03 us (1%)
    ppermute x36, waiting for transfers between devices, send(): return lax.ppermute(x, BOTH, [(i, i ^ mask) for i in range(self.count)])  79.2 us
    ppermute x36, starting transfers between devices, send(): return lax.ppermute(x, BOTH, [(i, i ^ mask) for i in range(self.count)])  77.9 us
    pallas_call x1, Pallas kernels, per_device(): pl.pallas_call(forward_kernel(plan, sources), in_specs=[SMEM] + [ANY] * s...  14 us
    all_to_all x1, blocking collectives, per_device(): squares = lax.all_to_all(square, BOTH, 0, 0, tiled=True)  10.8 us
    pallas_call x1, Pallas kernels, per_device(): pl.pallas_call(last_kernel(plan, sources), in_specs=[SMEM] + [ANY] * (sou...  10.4 us
    pallas_call x1, Pallas kernels, per_device(): gq = query_call(table, q, k, v, message, stat, columns, key_ids)  7.68 us
    pallas_call x1, Pallas kernels, per_device(): weight_call(table, norms, triple, params, act, gpre, gbt, n2, att, gbo, vec)  6.6 us
    pallas_call x1, Pallas kernels, per_device(): triple, wo, wup, wdn, params = unpack(table, near, core)  5.73 us
  transfers between devices with their start and end apart: 40, of which 18 were waited for; matrix products, arithmetic and copies ran while one was open for 4% of the time, Pallas kernels for 8%

profile of v7, /device:TPU:0, one launch (start us, length us, event | category | flops | bytes accessed | tf_op | source)
XLA Modules:
  0.0 241.5 jit_solution(11138660031631930621)
XLA Ops:
  4.0 5.1 %collective-permute-start.2 = (bf16[1,448,128]{2,1,0:T(8,128)(2,1)}, bf16[1,448,128]{2,1,0:T(8,128)(2,1)S(1)}, u32[]{:S(2)}, u32[]{:S(2)}) collective-permute-start(bf16[1,448,128]{2,1,0:T(8,128)(2,1)} %bitcast.100), channel_id=1, source_target_pairs={{0,6},{1,7},{2,4},{3,5},{4,2},{5,3},{6,0},{7,1},{8,14},{9,15},{10,... | collective-permute-start | bytes 344072 | tf_op jit(solution)/shard_map/ppermute | solution.py:90
  9.7 3.7 %collective-permute-done.2 = bf16[1,448,128]{2,1,0:T(8,128)(2,1)S(1)} collective-permute-done((bf16[1,448,128]{2,1,0:T(8,128)(2,1)}, bf16[1,448,128]{2,1,0:T(8,128)(2,1)S(1)}, u32[]{:S(2)}, u32[]{:S(2)}) %collective-permute-start.2) | collective-permute-done | bytes 114720 | tf_op jit(solution)/shard_map/ppermute | solution.py:90
  13.4 5.6 %collective-permute-done.1 = bf16[1,448,128]{2,1,0:T(8,128)(2,1)S(1)} collective-permute-done((bf16[1,448,128]{2,1,0:T(8,128)(2,1)}, bf16[1,448,128]{2,1,0:T(8,128)(2,1)S(1)}, u32[]{:S(2)}, u32[]{:S(2)}) %collective-permute-start.1) | collective-permute-done | bytes 114720 | tf_op jit(solution)/shard_map/ppermute | solution.py:90
  23.5 9.9 %collective-permute-done.13 = bf16[4,448,128]{2,1,0:T(8,128)(2,1)S(1)} collective-permute-done((bf16[4,448,128]{2,1,0:T(8,128)(2,1)S(1)}, bf16[4,448,128]{2,1,0:T(8,128)(2,1)S(1)}, u32[]{:S(2)}, u32[]{:S(2)}) %collective-permute-start.13) | collective-permute-done | bytes 458784 | tf_op jit(solution)/shard_map/ppermute | solution.py:90
  33.5 9.2 %collective-permute-done.14 = bf16[4,448,128]{2,1,0:T(8,128)(2,1)S(1)} collective-permute-done((bf16[4,448,128]{2,1,0:T(8,128)(2,1)S(1)}, bf16[4,448,128]{2,1,0:T(8,128)(2,1)S(1)}, u32[]{:S(2)}, u32[]{:S(2)}) %collective-permute-start.14) | collective-permute-done | bytes 458784 | tf_op jit(solution)/shard_map/ppermute | solution.py:90
  48.4 4.4 %collective-permute-done.5 = bf16[1,256,384]{2,1,0:T(8,128)(2,1)S(1)} collective-permute-done((bf16[1,256,384]{2,1,0:T(8,128)(2,1)S(1)}, bf16[1,256,384]{2,1,0:T(8,128)(2,1)S(1)}, u32[]{:S(2)}, u32[]{:S(2)}) %collective-permute-start.5) | collective-permute-done | bytes 196640 | tf_op jit(solution)/shard_map/ppermute | solution.py:90
  52.7 9.7 %collective-permute-done.4 = bf16[1,256,384]{2,1,0:T(8,128)(2,1)S(1)} collective-permute-done((bf16[1,256,384]{2,1,0:T(8,128)(2,1)S(1)}, bf16[1,256,384]{2,1,0:T(8,128)(2,1)S(1)}, u32[]{:S(2)}, u32[]{:S(2)}) %collective-permute-start.4) | collective-permute-done | bytes 196640 | tf_op jit(solution)/shard_map/ppermute | solution.py:90
  72.4 5.0 %collective-permute-done.8.refs_3_ = bf16[2,256,384]{2,1,0:T(8,128)(2,1)} collective-permute-done((bf16[2,256,384]{2,1,0:T(8,128)(2,1)}, bf16[2,256,384]{2,1,0:T(8,128)(2,1)}, u32[]{:S(2)}, u32[]{:S(2)}) %collective-permute-start.8) | collective-permute-done | bytes 393248 | tf_op jit(solution)/shard_map/ppermute | solution.py:90
  81.5 5.7 %unpack.1 = (bf16[384,1152]{1,0:T(8,128)(2,1)}, bf16[384,384]{1,0:T(8,128)(2,1)}, bf16[384,1536]{1,0:T(8,128)(2,1)}, bf16[1536,384]{1,0:T(8,128)(2,1)}, f32[16,1536]{1,0:T(8,128)}) custom-call(s32[64]{0:T(128)} %concatenate.22.table, bf16[16,448,128]{2,1,0:T(8,128)(2,1)} %copy-done.2, bf16[16,448,128]{2,1,0:T(8,128)(2,1)} %collective-permute-done.16.core), custom_call_target="tpu_custom_call" | custom-call | tf_op jit(solution)/shard_map/unpack/pallas_call | solution.py:950
  88.3 14.0 %forward.1 = (bf16[256,384]{1,0:T(8,128)(2,1)}, bf16[272,384]{1,0:T(8,128)(2,1)}, bf16[256,384]{1,0:T(8,128)(2,1)}, bf16[13,256,384]{2,1,0:T(8,128)(2,1)}, bf16[...) custom-call(s32[64]{0:T(128)} %concatenate.22.table, ...), custom_call_target="tpu_custom_call" | custom-call | tf_op jit(solution)/shard_map/forward/pallas_call | solution.py:952
  102.3 7.1 %collective-permute-start.19 = (bf16[1,272,384]{2,1,0:T(8,128)(2,1)}, bf16[1,272,384]{2,1,0:T(8,128)(2,1)S(1)}, u32[]{:S(2)}, u32[]{:S(2)}) collective-permute-start(bf16[1,272,384]{2,1,0:T(8,128)(2,1)} %bitcast.88), channel_id=1, source_target_pairs={{0,6},{1,7},{2,4},{3,5},{4,2},{5,3},{6,0},{7,1},{8,14},{9,15},{10,... | collective-permute-start | bytes 626696 | tf_op jit(solution)/shard_map/ppermute | solution.py:90
  114.2 12.3 %collective-permute-done.18 = bf16[1,272,384]{2,1,0:T(8,128)(2,1)S(1)} collective-permute-done((bf16[1,272,384]{2,1,0:T(8,128)(2,1)}, bf16[1,272,384]{2,1,0:T(8,128)(2,1)S(1)}, u32[]{:S(2)}, u32[]{:S(2)}) %collective-permute-start.18) | collective-permute-done | bytes 208928 | tf_op jit(solution)/shard_map/ppermute | solution.py:90
  127.8 3.4 %collective-permute-start.22 = (bf16[2,272,384]{2,1,0:T(8,128)(2,1)}, bf16[2,272,384]{2,1,0:T(8,128)(2,1)S(1)}, u32[]{:S(2)}, u32[]{:S(2)}) collective-permute-start(bf16[2,272,384]{2,1,0:T(8,128)(2,1)} %pad_maximum_fusion.3), channel_id=1, source_target_pairs={{0,1},{1,0},{2,3},{3,2},{4,5},{5,4},{6,7},{7,6},{8,9},{9,8},{10,11... | collective-permute-start | bytes 1253384 | tf_op jit(solution)/shard_map/ppermute | solution.py:90
  131.9 5.2 %collective-permute-start.23 = (bf16[4,272,384]{2,1,0:T(8,128)(2,1)S(1)}, bf16[4,272,384]{2,1,0:T(8,128)(2,1)S(1)}, u32[]{:S(2)}, u32[]{:S(2)}) collective-permute-start(bf16[4,272,384]{2,1,0:T(8,128)(2,1)S(1)} %pad_maximum_fusion.refs_2_), channel_id=1, source_target_pairs={{0,8},{1,9},{2,10},{3,11},{4,12},{5,13},{6,14},{7,15},{8,0},{9,1},... | collective-permute-start | bytes 2506760 | tf_op jit(solution)/shard_map/ppermute | solution.py:90
  137.7 3.8 %collective-permute-done.22.refs_3_ = bf16[2,272,384]{2,1,0:T(8,128)(2,1)S(1)} collective-permute-done((bf16[2,272,384]{2,1,0:T(8,128)(2,1)}, bf16[2,272,384]{2,1,0:T(8,128)(2,1)S(1)}, u32[]{:S(2)}, u32[]{:S(2)}) %collective-permute-start.22) | collective-permute-done | bytes 417824 | tf_op jit(solution)/shard_map/ppermute | solution.py:90
  143.2 7.7 %query.1.refs_13_ = bf16[256,384]{1,0:T(8,128)(2,1)} custom-call(s32[64]{0:T(128)} %concatenate.22.table, bf16[256,384]{1,0:T(8,128)(2,1)} %get-tuple-element.71.q_ref, bf16[13,256,384]{2,1,0:T(8,128)(2,1)} %get-tuple-element.72.k_ref, bf16[13,256,384]{2,1,0:T(8,128)(2,1)} %get-tuple-element.73.v_ref, bf16[272,384]{1,0:T(8,128)(2,1)} %get-tuple-element.57.msg_ref, ...), custom_call_target="tpu_custom_call" | custom-call | tf_op jit(solution)/shard_map/query/pallas_call | solution.py:1037
  150.9 6.6 %weight.1 = (bf16[13,256,384]{2,1,0:T(8,128)(2,1)}, bf16[16,448,128]{2,1,0:T(8,128)(2,1)}, bf16[16,448,128]{2,1,0:T(8,128)(2,1)}, f32[448,128]{1,0:T(8,128)}) custom-call(s32[64]{0:T(128)} %concatenate.22.table, bf16[13,256,384]{2,1,0:T(8,128)(2,1)} %get-tuple-element.60.norm_ref, bf16[384,1152]{1,0:T(8,128)(2,1)} %get-tuple-element.51.refs_8_.triple_ref.refs_15_, ...), custom_call_target="tpu_custom_call" | custom-call | tf_op jit(solution)/shard_map/weight/pallas_call | solution.py:1060
  159.0 10.4 %last.1 = (f32[256,384]{1,0:T(8,128)}, bf16[16,448,128]{2,1,0:T(8,128)(2,1)}, bf16[16,448,128]{2,1,0:T(8,128)(2,1)}) custom-call(s32[64]{0:T(128)} %concatenate.22.table, bf16[1,272,384]{2,1,0:T(8,128)(2,1)} %bitcast.92, bf16[1,272,384]{2,1,0:T(8,128)(2,1)} %collective-permute-done.17.refs_1_, ...), custom_call_target="tpu_custom_call", output_to_operand_aliasing={{1}: (21, {}), {2}: (22, {})} | custom-call | tf_op jit(solution)/shard_map/last/pallas_call | solution.py:1065
  169.4 16.5 %collective-permute-start.27 = (bf16[16,448,128]{2,1,0:T(8,128)(2,1)}, bf16[16,448,128]{2,1,0:T(8,128)(2,1)S(1)}, u32[]{:S(2)}, u32[]{:S(2)}) collective-permute-start(bf16[16,448,128]{2,1,0:T(8,128)(2,1)} %get-tuple-element.82), channel_id=1, source_target_pairs={{0,8},{1,9},{2,10},{3,11},{4,12},{5,13},{6,14},{7,15},{8,0},{9,1},... | collective-permute-start | bytes 5505032 | tf_op jit(solution)/shard_map/ppermute | solution.py:90
  186.0 3.6 %collective-permute-done.27 = bf16[16,448,128]{2,1,0:T(8,128)(2,1)S(1)} collective-permute-done((bf16[16,448,128]{2,1,0:T(8,128)(2,1)}, bf16[16,448,128]{2,1,0:T(8,128)(2,1)S(1)}, u32[]{:S(2)}, u32[]{:S(2)}) %collective-permute-start.27) | collective-permute-done | bytes 1835040 | tf_op jit(solution)/shard_map/ppermute | solution.py:90
  191.3 4.4 %collective-permute-start.29 = (bf16[4,304,128]{2,1,0:T(8,128)(2,1)S(1)}, bf16[4,304,128]{2,1,0:T(8,128)(2,1)S(1)}, u32[]{:S(2)}, u32[]{:S(2)}) collective-permute-start(bf16[4,304,128]{2,1,0:T(8,128)(2,1)S(1)} %get-tuple-element.101), channel_id=1, source_target_pairs={{0,1},{1,0},{2,3},{3,2},{4,5},{5,4},{6,7},{7,6},{8,9},{9,8},{10,11... | collective-permute-start | bytes 933896 | tf_op jit(solution)/shard_map/ppermute | solution.py:90
  197.1 3.9 %collective-permute-start.35 = (bf16[4,144,128]{2,1,0:T(8,128)(2,1)S(1)}, bf16[4,144,128]{2,1,0:T(8,128)(2,1)S(1)}, u32[]{:S(2)}, u32[]{:S(2)}) collective-permute-start(bf16[4,144,128]{2,1,0:T(8,128)(2,1)S(1)} %get-tuple-element.97), channel_id=1, source_target_pairs={{0,4},{1,5},{2,6},{3,7},{4,0},{5,1},{6,2},{7,3},{8,12},{9,13},{10,... | collective-permute-start | bytes 442376 | tf_op jit(solution)/shard_map/ppermute | solution.py:90
  209.7 4.5 %collective-permute-start.32 = (bf16[304,128]{1,0:T(8,128)(2,1)S(1)}, bf16[304,128]{1,0:T(8,128)(2,1)S(1)}, u32[]{:S(2)}, u32[]{:S(2)}) collective-permute-start(bf16[304,128]{1,0:T(8,128)(2,1)S(1)} %get-tuple-element.104), channel_id=1, source_target_pairs={{0,4},{1,5},{2,6},{3,7},{4,0},{5,1},{6,2},{7,3},{8,12},{9,13},{10,... | collective-permute-start | bytes 233480 | tf_op jit(solution)/shard_map/ppermute | solution.py:90
  226.3 10.8 %all_to_all.12 = f32[32,1,128]{2,1,0:T(1,128)S(1)} all-to-all(f32[32,1,128]{2,1,0:T(1,128)} %bitcast.106), channel_id=1, replica_groups=mesh['dp'=4,'fsdp'=8] {'dp','fsdp'}, dimensions={0} | all-to-all | bytes 32768 | tf_op jit(solution)/shard_map/all_to_all | solution.py:1122
  (140 shorter events, 66.0 us)
Async XLA Ops:
  21.5 21.1 %collective-permute-start.14 = (bf16[4,448,128]{2,1,0:T(8,128)(2,1)S(1)}, bf16[4,448,128]{2,1,0:T(8,128)(2,1)S(1)}, u32[]{:S(2)}, u32[]{:S(2)}) collective-permute-start(bf16[4,448,128]{2,1,0:T(8,128)(2,1)S(1)} %pad_maximum_fusion.2), channel_id=1, source_target_pairs={{0,1},{1,0},{2,3},{3,2},{4,5},{5,4},{6,7},{7,6},{8,9},{9,8},{10,11... | collective-permute-start | bytes 1376264 | tf_op jit(solution)/shard_map/ppermute | solution.py:90
  23.0 19.7 %collective-permute-start.15 = (bf16[4,448,128]{2,1,0:T(8,128)(2,1)S(1)}, bf16[4,448,128]{2,1,0:T(8,128)(2,1)S(1)}, u32[]{:S(2)}, u32[]{:S(2)}) collective-permute-start(bf16[4,448,128]{2,1,0:T(8,128)(2,1)S(1)} %pad_maximum_fusion.2), channel_id=1, source_target_pairs={{0,17},{1,16},{2,19},{3,18},{4,21},{5,20},{6,23},{7,22},{8,25},{9,... | collective-permute-start | bytes 1376264 | tf_op jit(solution)/shard_map/ppermute | solution.py:90
  42.8 35.0 %collective-permute-start.16 = (bf16[16,448,128]{2,1,0:T(8,128)(2,1)S(1)}, bf16[16,448,128]{2,1,0:T(8,128)(2,1)}, u32[]{:S(2)}, u32[]{:S(2)}) collective-permute-start(bf16[16,448,128]{2,1,0:T(8,128)(2,1)S(1)} %constant_dynamic-update-slice_fusion.near), channel_id=1, source_target_pairs={{0,8},{1,9},{2,10},{3,11},{4,12},{5,13},{6,14},{7,15},{8,0},{9,1},... | collective-permute-start | bytes 5505032 | tf_op jit(solution)/shard_map/ppermute | solution.py:90
  45.3 17.1 %collective-permute-start.4 = (bf16[1,256,384]{2,1,0:T(8,128)(2,1)S(1)}, bf16[1,256,384]{2,1,0:T(8,128)(2,1)S(1)}, u32[]{:S(2)}, u32[]{:S(2)}) collective-permute-start(bf16[1,256,384]{2,1,0:T(8,128)(2,1)S(1)} %bitcast.97), channel_id=1, source_target_pairs={{0,4},{1,5},{2,6},{3,7},{4,0},{5,1},{6,2},{7,3},{8,12},{9,13},{10,... | collective-permute-start | bytes 589832 | tf_op jit(solution)/shard_map/ppermute | solution.py:90
  45.3 17.9 %collective-permute-start.7 = (bf16[1,256,384]{2,1,0:T(8,128)(2,1)S(1)}, bf16[1,256,384]{2,1,0:T(8,128)(2,1)S(1)}, u32[]{:S(2)}, u32[]{:S(2)}) collective-permute-start(bf16[1,256,384]{2,1,0:T(8,128)(2,1)S(1)} %bitcast.98), channel_id=1, source_target_pairs={{0,3},{1,2},{2,1},{3,0},{4,7},{5,6},{6,5},{7,4},{8,11},{9,10},{10,... | collective-permute-start | bytes 589832 | tf_op jit(solution)/shard_map/ppermute | solution.py:90
  48.3 16.5 %collective-permute-start.6 = (bf16[1,256,384]{2,1,0:T(8,128)(2,1)S(1)}, bf16[1,256,384]{2,1,0:T(8,128)(2,1)}, u32[]{:S(2)}, u32[]{:S(2)}) collective-permute-start(bf16[1,256,384]{2,1,0:T(8,128)(2,1)S(1)} %bitcast.99), channel_id=1, source_target_pairs={{0,2},{1,3},{2,0},{3,1},{4,6},{5,7},{6,4},{7,5},{8,10},{9,11},{10,... | collective-permute-start | bytes 589832 | tf_op jit(solution)/shard_map/ppermute | solution.py:90
  67.5 19.8 %collective-permute-start.11 = (bf16[4,256,384]{2,1,0:T(8,128)(2,1)S(1)}, bf16[4,256,384]{2,1,0:T(8,128)(2,1)S(1)}, u32[]{:S(2)}, u32[]{:S(2)}) collective-permute-start(bf16[4,256,384]{2,1,0:T(8,128)(2,1)S(1)} %pad_maximum_fusion.1.refs_2_), channel_id=1, source_target_pairs={{8,16},{9,17},{10,18},{11,19},{12,20},{13,21},{18,10},{19,11},{20,... | collective-permute-start | bytes 2359304 | tf_op jit(solution)/shard_map/ppermute | solution.py:147
  68.2 19.1 %collective-permute-start.9 = (bf16[4,256,384]{2,1,0:T(8,128)(2,1)S(1)}, bf16[4,256,384]{2,1,0:T(8,128)(2,1)}, u32[]{:S(2)}, u32[]{:S(2)}) collective-permute-start(bf16[4,256,384]{2,1,0:T(8,128)(2,1)S(1)} %pad_maximum_fusion.1.refs_2_), channel_id=1, source_target_pairs={{0,8},{1,9},{2,10},{3,11},{4,12},{5,13},{6,14},{7,15},{8,0},{9,1},... | collective-permute-start | bytes 2359304 | tf_op jit(solution)/shard_map/ppermute | solution.py:90
  71.0 16.3 %collective-permute-start.12 = (bf16[2,256,384]{2,1,0:T(8,128)(2,1)}, bf16[2,256,384]{2,1,0:T(8,128)(2,1)}, u32[]{:S(2)}, u32[]{:S(2)}) collective-permute-start(bf16[2,256,384]{2,1,0:T(8,128)(2,1)} %pad_maximum_fusion.4), channel_id=1, source_target_pairs={{8,17},{9,16},{10,19},{11,18},{20,13},{21,12},{22,15},{23,14}} | collective-permute-start | bytes 1179656 | tf_op jit(solution)/shard_map/ppermute | solution.py:148
  109.4 17.1 %collective-permute-start.18 = (bf16[1,272,384]{2,1,0:T(8,128)(2,1)}, bf16[1,272,384]{2,1,0:T(8,128)(2,1)S(1)}, u32[]{:S(2)}, u32[]{:S(2)}) collective-permute-start(bf16[1,272,384]{2,1,0:T(8,128)(2,1)} %bitcast.89), channel_id=1, source_target_pairs={{0,4},{1,5},{2,6},{3,7},{4,0},{5,1},{6,2},{7,3},{8,12},{9,13},{10,... | collective-permute-start | bytes 626696 | tf_op jit(solution)/shard_map/ppermute | solution.py:90
  109.4 17.9 %collective-permute-start.21 = (bf16[1,272,384]{2,1,0:T(8,128)(2,1)}, bf16[1,272,384]{2,1,0:T(8,128)(2,1)S(1)}, u32[]{:S(2)}, u32[]{:S(2)}) collective-permute-start(bf16[1,272,384]{2,1,0:T(8,128)(2,1)} %bitcast.90), channel_id=1, source_target_pairs={{0,3},{1,2},{2,1},{3,0},{4,7},{5,6},{6,5},{7,4},{8,11},{9,10},{10,... | collective-permute-start | bytes 626696 | tf_op jit(solution)/shard_map/ppermute | solution.py:90
  111.0 16.6 %collective-permute-start.20 = (bf16[1,272,384]{2,1,0:T(8,128)(2,1)}, bf16[1,272,384]{2,1,0:T(8,128)(2,1)S(1)}, u32[]{:S(2)}, u32[]{:S(2)}) collective-permute-start(bf16[1,272,384]{2,1,0:T(8,128)(2,1)} %bitcast.91), channel_id=1, source_target_pairs={{0,2},{1,3},{2,0},{3,1},{4,6},{5,7},{6,4},{7,5},{8,10},{9,11},{10,... | collective-permute-start | bytes 626696 | tf_op jit(solution)/shard_map/ppermute | solution.py:90
  127.8 13.8 %collective-permute-start.22 = (bf16[2,272,384]{2,1,0:T(8,128)(2,1)}, bf16[2,272,384]{2,1,0:T(8,128)(2,1)S(1)}, u32[]{:S(2)}, u32[]{:S(2)}) collective-permute-start(bf16[2,272,384]{2,1,0:T(8,128)(2,1)} %pad_maximum_fusion.3), channel_id=1, source_target_pairs={{0,1},{1,0},{2,3},{3,2},{4,5},{5,4},{6,7},{7,6},{8,9},{9,8},{10,11... | collective-permute-start | bytes 1253384 | tf_op jit(solution)/shard_map/ppermute | solution.py:90
  131.2 26.4 %collective-permute-start.25 = (bf16[4,272,384]{2,1,0:T(8,128)(2,1)S(1)}, bf16[4,272,384]{2,1,0:T(8,128)(2,1)S(1)}, u32[]{:S(2)}, u32[]{:S(2)}) collective-permute-start(bf16[4,272,384]{2,1,0:T(8,128)(2,1)S(1)} %pad_maximum_fusion.refs_2_), channel_id=1, source_target_pairs={{8,16},{9,17},{10,18},{11,19},{12,20},{13,21},{18,10},{19,11},{20,... | collective-permute-start | bytes 2506760 | tf_op jit(solution)/shard_map/ppermute | solution.py:147
  131.9 25.7 %collective-permute-start.23 = (bf16[4,272,384]{2,1,0:T(8,128)(2,1)S(1)}, bf16[4,272,384]{2,1,0:T(8,128)(2,1)S(1)}, u32[]{:S(2)}, u32[]{:S(2)}) collective-permute-start(bf16[4,272,384]{2,1,0:T(8,128)(2,1)S(1)} %pad_maximum_fusion.refs_2_), channel_id=1, source_target_pairs={{0,8},{1,9},{2,10},{3,11},{4,12},{5,13},{6,14},{7,15},{8,0},{9,1},... | collective-permute-start | bytes 2506760 | tf_op jit(solution)/shard_map/ppermute | solution.py:90
  137.1 20.4 %collective-permute-start.26 = (bf16[2,272,384]{2,1,0:T(8,128)(2,1)}, bf16[2,272,384]{2,1,0:T(8,128)(2,1)S(1)}, u32[]{:S(2)}, u32[]{:S(2)}) collective-permute-start(bf16[2,272,384]{2,1,0:T(8,128)(2,1)} %pad_maximum_fusion.3), channel_id=1, source_target_pairs={{8,17},{9,16},{10,19},{11,18},{20,13},{21,12},{22,15},{23,14}} | collective-permute-start | bytes 1253384 | tf_op jit(solution)/shard_map/ppermute | solution.py:148
  141.6 15.9 %collective-permute-start.24 = (bf16[2,272,384]{2,1,0:T(8,128)(2,1)S(1)}, bf16[2,272,384]{2,1,0:T(8,128)(2,1)S(1)}, u32[]{:S(2)}, u32[]{:S(2)}) collective-permute-start(bf16[2,272,384]{2,1,0:T(8,128)(2,1)S(1)} %collective-permute-done.22.refs_3_), channel_id=1, source_target_pairs={{0,8},{1,9},{2,10},{3,11},{4,12},{5,13},{6,14},{7,15},{8,0},{9,1},... | collective-permute-start | bytes 1253384 | tf_op jit(solution)/shard_map/ppermute | solution.py:90
  141.6 15.9 %collective-permute-start.17 = (bf16[1,272,384]{2,1,0:T(8,128)(2,1)S(1)}, bf16[1,272,384]{2,1,0:T(8,128)(2,1)}, u32[]{:S(2)}, u32[]{:S(2)}) collective-permute-start(bf16[1,272,384]{2,1,0:T(8,128)(2,1)S(1)} %bitcast.93), channel_id=1, source_target_pairs={{0,1},{1,0},{2,3},{3,2},{4,5},{5,4},{6,7},{7,6},{8,9},{9,8},{10,11... | collective-permute-start | bytes 626696 | tf_op jit(solution)/shard_map/ppermute | solution.py:90
  169.4 20.2 %collective-permute-start.27 = (bf16[16,448,128]{2,1,0:T(8,128)(2,1)}, bf16[16,448,128]{2,1,0:T(8,128)(2,1)S(1)}, u32[]{:S(2)}, u32[]{:S(2)}) collective-permute-start(bf16[16,448,128]{2,1,0:T(8,128)(2,1)} %get-tuple-element.82), channel_id=1, source_target_pairs={{0,8},{1,9},{2,10},{3,11},{4,12},{5,13},{6,14},{7,15},{8,0},{9,1},... | collective-permute-start | bytes 5505032 | tf_op jit(solution)/shard_map/ppermute | solution.py:90
  191.3 17.2 %collective-permute-start.29 = (bf16[4,304,128]{2,1,0:T(8,128)(2,1)S(1)}, bf16[4,304,128]{2,1,0:T(8,128)(2,1)S(1)}, u32[]{:S(2)}, u32[]{:S(2)}) collective-permute-start(bf16[4,304,128]{2,1,0:T(8,128)(2,1)S(1)} %get-tuple-element.101), channel_id=1, source_target_pairs={{0,1},{1,0},{2,3},{3,2},{4,5},{5,4},{6,7},{7,6},{8,9},{9,8},{10,11... | collective-permute-start | bytes 933896 | tf_op jit(solution)/shard_map/ppermute | solution.py:90
  197.0 17.1 %collective-permute-start.36 = (bf16[4,144,128]{2,1,0:T(8,128)(2,1)S(1)}, bf16[4,144,128]{2,1,0:T(8,128)(2,1)S(1)}, u32[]{:S(2)}, u32[]{:S(2)}) collective-permute-start(bf16[4,144,128]{2,1,0:T(8,128)(2,1)S(1)} %get-tuple-element.96), channel_id=1, source_target_pairs={{0,6},{1,7},{2,4},{3,5},{4,2},{5,3},{6,0},{7,1},{8,14},{9,15},{10,... | collective-permute-start | bytes 442376 | tf_op jit(solution)/shard_map/ppermute | solution.py:90
  197.1 17.0 %collective-permute-start.35 = (bf16[4,144,128]{2,1,0:T(8,128)(2,1)S(1)}, bf16[4,144,128]{2,1,0:T(8,128)(2,1)S(1)}, u32[]{:S(2)}, u32[]{:S(2)}) collective-permute-start(bf16[4,144,128]{2,1,0:T(8,128)(2,1)S(1)} %get-tuple-element.97), channel_id=1, source_target_pairs={{0,4},{1,5},{2,6},{3,7},{4,0},{5,1},{6,2},{7,3},{8,12},{9,13},{10,... | collective-permute-start | bytes 442376 | tf_op jit(solution)/shard_map/ppermute | solution.py:90
  209.7 14.0 %collective-permute-start.33 = (bf16[304,128]{1,0:T(8,128)(2,1)S(1)}, bf16[304,128]{1,0:T(8,128)(2,1)S(1)}, u32[]{:S(2)}, u32[]{:S(2)}) collective-permute-start(bf16[304,128]{1,0:T(8,128)(2,1)S(1)} %get-tuple-element.103), channel_id=1, source_target_pairs={{0,6},{1,7},{2,4},{3,5},{4,2},{5,3},{6,0},{7,1},{8,14},{9,15},{10,... | collective-permute-start | bytes 233480 | tf_op jit(solution)/shard_map/ppermute | solution.py:90
  209.7 14.0 %collective-permute-start.32 = (bf16[304,128]{1,0:T(8,128)(2,1)S(1)}, bf16[304,128]{1,0:T(8,128)(2,1)S(1)}, u32[]{:S(2)}, u32[]{:S(2)}) collective-permute-start(bf16[304,128]{1,0:T(8,128)(2,1)S(1)} %get-tuple-element.104), channel_id=1, source_target_pairs={{0,4},{1,5},{2,6},{3,7},{4,0},{5,1},{6,2},{7,3},{8,12},{9,13},{10,... | collective-permute-start | bytes 233480 | tf_op jit(solution)/shard_map/ppermute | solution.py:90
  (39 other events, 512.0 us)
